TPU v7x, 32 devices: a whole 2x2x4 slice. The times are simulated.
32 devices in a mesh: dp: 8 (over z, y), seq: 4 (over x, core).
Axes of the slice: x: 2, y: 2, z: 4, core: 2. Of those that a mesh axis runs over, the one named last changes fastest.
Arguments:
- hidden: bfloat16 [2, 8, 1024, 1536], P(None, 'dp', 'seq'), may hold values from -6 to 6
- in_weight: bfloat16 [1536, 6448], P(('dp', 'seq')), may hold values from -0.15625 to 0.15625
- out_weight: bfloat16 [3072, 1536], P(('dp', 'seq')), may hold values from -0.109375 to 0.109375
- conv_weight: bfloat16 [3328, 4], P(('dp', 'seq')), may hold values from -3 to 3
- conv_bias: bfloat16 [3328], P(('dp', 'seq')), may hold values from -3 to 3
- norm_gain: bfloat16 [1536], P(('dp', 'seq')), may hold values from 0.099609375 to 1.8984375
- gate_gain: bfloat16 [3072], P(('dp', 'seq')), may hold values from 0.099609375 to 1.8984375
- step_bias: float32 [48], replicated, may hold values from -4 to -1
- decay_rate: float32 [48], replicated, may hold values from 0.00048828125 to 1
- skip_gain: float32 [48], replicated, may hold values from 0.5 to 2
- cotangent: bfloat16 [2, 8, 1024, 1536], P(None, 'dp', 'seq'), may hold values from -6 to 6
Outputs:
- block_out: bfloat16 [2, 8, 1024, 1536], P(None, 'dp', 'seq')
- grad_hidden: float32 [2, 8, 1024, 1536], P(None, 'dp', 'seq')
- grad_in_weight: float32 [1536, 6448], P(('dp', 'seq'))
- grad_out_weight: float32 [3072, 1536], P(('dp', 'seq'))
- grad_conv_weight: float32 [3328, 4], P(('dp', 'seq'))
- grad_conv_bias: float32 [3328], P(('dp', 'seq'))
- grad_norm_gain: float32 [1536], P(('dp', 'seq'))
- grad_gate_gain: float32 [3072], P(('dp', 'seq'))
- grad_step_bias: float32 [48], replicated
- grad_decay_rate: float32 [48], replicated
- grad_skip_gain: float32 [48], replicated
All inputs are finite; a program needn't handle non-finite values.
Results may differ from a plain program's by a relative error of at most 0.008.
The roundings to bfloat16 on the way count: a program that leaves them out, or rounds other values in their place, can miss the bound.
Values may be sent and summed in bfloat16 or wider, within the bound.
No kernel may reach another device: no remote copies, remote signals or barrier semaphores. Data moves between devices by JAX's collectives and lax.ppermute only.
A program may use at most 320 MiB of HBM per device.

v0:
```python
import jax
import jax.numpy as jnp
from jax import lax
from jax.sharding import PartitionSpec as P

DI = 3072
H = 48
P_SIZE = 64
N = 128
KCONV = 4
CONV = 3328


epsilon = 1e-05
highest = lax.Precision.HIGHEST


def passed_along(block, axis, distance):
    devices = range(lax.axis_size(axis))
    route = [(i - distance, i) for i in devices if i - distance in devices]
    return lax.ppermute(block, axis, route)


def prefix(value, axis, combine, identity):
    devices, mine = (lax.axis_size(axis), lax.axis_index(axis))
    everything = jax.tree.map(
        lambda part, kind: lax.all_gather(part.astype(kind), axis),
        value,
        (jnp.bfloat16, jnp.bfloat16),
    )
    start = jax.tree.map(
        lambda part, zero: jnp.broadcast_to(jnp.asarray(zero, part.dtype), part.shape),
        value,
        identity,
    )

    def lap(k, before):
        reached = k < mine
        new = combine(
            before, jax.tree.map(lambda part, own: part[k].astype(own.dtype), everything, value)
        )
        return jax.tree.map(lambda a, b: jnp.where(reached, a, b), new, before)

    return lax.fori_loop(0, devices, lap, start)


def carried_in(value, axis, join, neutral):
    count = lax.axis_size(axis)
    place = lax.axis_index(axis)
    ahead = count - 1 - place
    gathered = jax.tree.map(
        lambda a, kind: lax.all_gather(a.astype(kind), axis),
        value,
        jax.tree.map(lambda a: jnp.bfloat16 if a.dtype == jnp.float32 else a.dtype, value),
    )
    state = jax.tree.map(lambda a, e: jnp.zeros_like(a) + jnp.asarray(e, a.dtype), value, neutral)

    def one(lap, state):
        source = count - 1 - lap
        return join(
            state,
            jax.tree.map(
                lambda a, own: lax.dynamic_index_in_dim(a, source, 0, False).astype(own.dtype),
                gathered,
                value,
            ),
        )

    return lax.fori_loop(0, ahead, one, state)


def rms_scale(values, gain_vec):
    return (
        values * lax.rsqrt(jnp.mean(values * values, axis=-1, keepdims=True) + epsilon) * gain_vec
    )


def convolve(padded, conv_taps, conv_shift, block_rows):
    summed = conv_shift
    for tap_index in range(conv_taps.shape[1]):
        summed = (
            summed + conv_taps[:, tap_index] * padded[..., tap_index : tap_index + block_rows, :]
        )
    return summed


def split_parts(act, dt_raw, step_bias, decay_rate):
    x_heads = act[..., :DI].reshape(act.shape[:-1] + (H, P_SIZE))
    b_state = act[..., DI : DI + N]
    c_state = act[..., DI + N :]
    dt_step = jax.nn.softplus(dt_raw + step_bias)
    log_decay = jnp.cumsum(-decay_rate * dt_step, axis=-2)
    return (x_heads, b_state, c_state, dt_step, log_decay)


def group_states(x_heads, b_state, dt_step, log_decay):
    tail_weights = jnp.exp(log_decay[:, -1:, :] - log_decay) * dt_step
    weighted = x_heads * tail_weights[..., None]
    states = jnp.einsum("sun,suhp->shnp", b_state, weighted, precision=highest)
    return (jnp.exp(log_decay[:, -1, :]), states)


def group_outputs(
    gate_z, x_heads, b_state, c_state, dt_step, log_decay, entering, gate_vec, skip_gain
):
    block_count, block_rows = (x_heads.shape[0], x_heads.shape[1])
    scores = jnp.einsum("stn,sun->stu", c_state, b_state, precision=highest)
    decay_heads = jnp.transpose(log_decay, (0, 2, 1))
    log_diff = decay_heads[:, :, :, None] - decay_heads[:, :, None, :]
    causal = lax.broadcasted_iota(jnp.int32, (block_rows, block_rows), 0) >= lax.broadcasted_iota(
        jnp.int32, (block_rows, block_rows), 1
    )
    decay_mat = jnp.exp(jnp.where(causal, log_diff, -jnp.inf))
    mixing = decay_mat * scores[:, None, :, :] * jnp.transpose(dt_step, (0, 2, 1))[:, :, None, :]
    inner_sum = jnp.einsum("shtu,suhp->sthp", mixing, x_heads, precision=highest)
    carried = (
        jnp.einsum("stn,shnp->sthp", c_state, entering, precision=highest)
        * jnp.exp(log_decay)[..., None]
    )
    ssd_sum = inner_sum + carried + skip_gain[:, None] * x_heads
    flat_ssd = ssd_sum.reshape(block_count, block_rows, DI)
    gated = flat_ssd * jax.nn.silu(gate_z)
    return rms_scale(gated, gate_vec)


def prepare(proj_blocks, halo_rows, conv_taps, conv_shift, step_bias, decay_rate):
    block_rows = proj_blocks.shape[1]
    xbc_part = proj_blocks[:, :, DI : DI + CONV]
    padded = jnp.concatenate([halo_rows, xbc_part], axis=1)
    act = jax.nn.silu(convolve(padded, conv_taps, conv_shift, block_rows))
    return split_parts(act, proj_blocks[:, :, DI + CONV :], step_bias, decay_rate)


def finish(proj_blocks, ssd_parts, entering, gate_vec, skip_gain):
    return group_outputs(proj_blocks[:, :, :DI], *ssd_parts, entering, gate_vec, skip_gain).reshape(
        -1, DI
    )


def combine_links(earlier, later_part):
    return (
        earlier[0] * later_part[0],
        later_part[0][:, :, None, None] * earlier[1] + later_part[1],
    )


def contract_rows(left_mat, right_mat):
    return lax.dot_general(
        left_mat, right_mat, (((0,), (0,)), ((), ())), preferred_element_type=jnp.float32
    )


def contract_cols(left_mat, right_mat):
    return lax.dot_general(
        left_mat, right_mat, (((1,), (1,)), ((), ())), preferred_element_type=jnp.float32
    )


def body(
    hidden,
    in_weight,
    out_weight,
    conv_weight,
    conv_bias,
    norm_gain,
    gate_gain,
    step_bias,
    decay_rate,
    skip_gain,
    cotangent,
):
    shards = (in_weight, out_weight, conv_weight, conv_bias, norm_gain, gate_gain)
    micro_count, seq_count, block_rows = (hidden.shape[0], hidden.shape[1], hidden.shape[2])
    token_rows = seq_count * block_rows
    outputs_list = []
    grad_rows_list = []
    shard_totals = None
    head_totals = (jnp.zeros_like(step_bias), jnp.zeros_like(decay_rate), jnp.zeros_like(skip_gain))
    for micro in range(micro_count):
        gathered = (
            lax.all_gather(shards[0], ("dp", "seq"), axis=0, tiled=True),
            lax.all_gather(shards[1], ("dp", "seq"), axis=0, tiled=True),
            lax.all_gather(shards[2], ("dp", "seq"), axis=0, tiled=True),
            lax.all_gather(shards[3], ("dp", "seq"), axis=0, tiled=True),
            lax.all_gather(shards[4], ("dp", "seq"), axis=0, tiled=True),
            lax.all_gather(shards[5], ("dp", "seq"), axis=0, tiled=True),
        )
        w_in, w_out = (gathered[0], gathered[1])
        conv_taps = gathered[2].astype(jnp.float32)
        conv_shift = gathered[3].astype(jnp.float32)
        norm_vec = gathered[4].astype(jnp.float32)
        gate_vec = gathered[5].astype(jnp.float32)
        inputs_f = hidden[micro].astype(jnp.float32).reshape(token_rows, -1)
        normed = rms_scale(inputs_f, norm_vec).astype(jnp.bfloat16)
        projected = jnp.dot(normed, w_in, preferred_element_type=jnp.float32)
        proj_blocks = projected.reshape(seq_count, block_rows, -1)
        rim_rows = proj_blocks[:, block_rows - (KCONV - 1) :, DI : DI + CONV]
        halo_rows = passed_along(rim_rows.astype(jnp.bfloat16), "seq", 1).astype(rim_rows.dtype)
        ssd_parts = prepare(proj_blocks, halo_rows, conv_taps, conv_shift, step_bias, decay_rate)
        decays, states = group_states(ssd_parts[0], ssd_parts[1], ssd_parts[3], ssd_parts[4])
        identity = (jnp.ones_like(decays), jnp.zeros_like(states))
        entering = prefix((decays, states), "seq", combine_links, identity)[1]
        finished = finish(proj_blocks, ssd_parts, entering, gate_vec, skip_gain)
        finished_low = finished.astype(jnp.bfloat16)
        result = inputs_f + jnp.dot(finished_low, w_out, preferred_element_type=jnp.float32)
        outputs_list.append(result.astype(jnp.bfloat16).reshape(seq_count, block_rows, -1))
        gathered = (
            lax.all_gather(shards[0], ("dp", "seq"), axis=0, tiled=True),
            lax.all_gather(shards[1], ("dp", "seq"), axis=0, tiled=True),
            lax.all_gather(shards[2], ("dp", "seq"), axis=0, tiled=True),
            lax.all_gather(shards[3], ("dp", "seq"), axis=0, tiled=True),
            lax.all_gather(shards[4], ("dp", "seq"), axis=0, tiled=True),
            lax.all_gather(shards[5], ("dp", "seq"), axis=0, tiled=True),
        )
        w_in, w_out = (gathered[0], gathered[1])
        cot_low = cotangent[micro].reshape(token_rows, -1)
        grad_out = contract_rows(finished_low, cot_low)
        grad_finished = contract_cols(cot_low, w_out)
        _, pull_finish = jax.vjp(finish, proj_blocks, ssd_parts, entering, gate_vec, skip_gain)
        grad_proj_a, grad_parts_a, grad_enter, grad_gate, grad_skip = pull_finish(grad_finished)
        later_grads = carried_in((decays, grad_enter), "seq", combine_links, identity)[1]
        grad_decays = jnp.sum(later_grads * entering, axis=(2, 3))
        _, pull_states = jax.vjp(
            group_states, ssd_parts[0], ssd_parts[1], ssd_parts[3], ssd_parts[4]
        )
        grad_x, grad_b, grad_dt, grad_log = pull_states((grad_decays, later_grads))
        grad_parts = (
            grad_parts_a[0] + grad_x,
            grad_parts_a[1] + grad_b,
            grad_parts_a[2],
            grad_parts_a[3] + grad_dt,
            grad_parts_a[4] + grad_log,
        )
        _, pull_prepare = jax.vjp(
            prepare, proj_blocks, halo_rows, conv_taps, conv_shift, step_bias, decay_rate
        )
        grad_proj_b, grad_halo, grad_taps, grad_shift, grad_bias, grad_rate = pull_prepare(
            grad_parts
        )
        back_rows = passed_along(grad_halo.astype(jnp.bfloat16), "seq", -1).astype(grad_halo.dtype)
        total_cols = proj_blocks.shape[2]
        edge_grad = jnp.pad(
            back_rows, ((0, 0), (block_rows - (KCONV - 1), 0), (DI, total_cols - DI - CONV))
        )
        grad_proj = (
            (grad_proj_a + grad_proj_b + edge_grad).reshape(token_rows, -1).astype(jnp.bfloat16)
        )
        grad_in = contract_rows(normed, grad_proj)
        grad_normed = contract_cols(grad_proj, w_in)
        _, pull_norm = jax.vjp(rms_scale, inputs_f, norm_vec)
        grad_inputs, grad_norm = pull_norm(grad_normed)
        grad_rows_list.append(
            (cot_low.astype(jnp.float32) + grad_inputs).reshape(seq_count, block_rows, -1)
        )
        head_totals = (
            head_totals[0] + grad_bias,
            head_totals[1] + grad_rate,
            head_totals[2] + grad_skip,
        )
        gradients = (grad_in, grad_out, grad_taps, grad_shift, grad_norm, grad_gate)
        summed = (
            lax.psum_scatter(gradients[0], ("dp", "seq"), scatter_dimension=0, tiled=True),
            lax.psum_scatter(gradients[1], ("dp", "seq"), scatter_dimension=0, tiled=True),
            lax.psum_scatter(gradients[2], ("dp", "seq"), scatter_dimension=0, tiled=True),
            lax.psum_scatter(gradients[3], ("dp", "seq"), scatter_dimension=0, tiled=True),
            lax.psum_scatter(gradients[4], ("dp", "seq"), scatter_dimension=0, tiled=True),
            lax.psum_scatter(gradients[5], ("dp", "seq"), scatter_dimension=0, tiled=True),
        )
        if shard_totals is None:
            shard_totals = summed
        else:
            shard_totals = jax.tree.map(jnp.add, shard_totals, summed)
    head_sums = lax.psum((head_totals[0], head_totals[1], head_totals[2]), ("dp", "seq"))
    return (
        jnp.stack(outputs_list, 0),
        jnp.stack(grad_rows_list, 0),
        shard_totals[0],
        shard_totals[1],
        shard_totals[2],
        shard_totals[3],
        shard_totals[4],
        shard_totals[5],
        head_sums[0],
        head_sums[1],
        head_sums[2],
    )


def solution(mesh):
    in_specs = (
        P(None, "dp", "seq", None),
        P(("dp", "seq"), None),
        P(("dp", "seq"), None),
        P(("dp", "seq"), None),
        P(("dp", "seq")),
        P(("dp", "seq")),
        P(("dp", "seq")),
        P(),
        P(),
        P(),
        P(None, "dp", "seq", None),
    )
    out_specs = (
        P(None, "dp", "seq", None),
        P(None, "dp", "seq", None),
        P(("dp", "seq"), None),
        P(("dp", "seq"), None),
        P(("dp", "seq"), None),
        P(("dp", "seq")),
        P(("dp", "seq")),
        P(("dp", "seq")),
        P(),
        P(),
        P(),
    )
    return jax.shard_map(body, mesh=mesh, in_specs=in_specs, out_specs=out_specs, check_vma=False)
```

profile of v0, /device:TPU:0, one launch (start us, length us, event | category | flops | bytes accessed | tf_op | source)
XLA Modules:
  0.0 1524.3 jit_solution(8590487744954955340)
XLA Ops:
  10.5 43.2 %all-reduce.42 = (bf16[1536]{0:T(1024)(128)(2,1)S(1)}, bf16[3328]{0:T(1024)(128)(2,1)S(1)}, bf16[3072]{0:T(1024)(128)(2,1)}) all-reduce(bf16[1536]{0:T(1024)(128)(2,1)S(1)} %dynamic-update-slice.1, bf16[3328]{0:T(1024)(128)(2,1)S(1)} %dynamic-update-slice, ...), channel_id=1, replica_groups=mesh['dp'=8,'seq'=4] {'dp','seq'}, use_global_device_ids=true, to_apply=%add.35 | all-reduce | flops 7936 | bytes 31744
  54.4 40.9 %all-gather.4 = bf16[32,104,4]{1,2,0:T(4,128)(2,1)S(1)} all-gather(bf16[1,104,4]{1,2,0:T(4,128)(2,1)} %bitcast.677), channel_id=1, replica_groups=mesh['dp'=8,'seq'=4] {'dp','seq'}, dimensions={0}, use_global_device_ids=true | all-gather | bytes 27456 | tf_op jit(solution)/shard_map/all_gather | solution.py:183
  99.2 46.4 %all-gather.12.cloned.1.call-done = bf16[1536,6448]{1,0:T(8,128)(2,1)} async-done(((bf16[48,6448]{1,0:T(8,128)(2,1)}), bf16[1536,6448]{1,0:T(8,128)(2,1)}) %all-gather.12.cloned.1.call-update) | async-done | bytes 19808272 | tf_op jit(solution)/shard_map/all_gather | solution.py:181
  145.6 10.1 convolution_bitcast_fusion.1
  155.8 12.2 convolution_bitcast_fusion
  184.9 4.1 slice.186
  195.0 14.7 fusion.51
  209.7 3.8 slice_multiply_fusion
  217.1 5.4 fusion.123
  225.5 3.9 copy.374
  229.5 5.4 slice_multiply_fusion.1
  237.4 4.9 fusion.122
  262.6 5.0 all_gather.73
  267.7 5.0 all_gather.68
  284.4 36.7 %while.59 = (s32[]{:T(128)}, f32[1,48,128,64]{3,2,1,0:T(8,128)}, s32[]{:T(128)}, bf16[4,1,48]{2,1,0:T(2,128)(2,1)S(1)}, bf16[4,1,48,128,64]{3,4,2,0,1:T(8,128)(2,1)}, /*index=5*/s32[]{:T(128)}, s32[]{:T(128)}) while((s32[]{:T(128)}, f32[1,48,128,64]{3,2,1,0:T(8,128)}, s32[]{:T(128)}, bf16[4,1,48]{2,1,0:T(2,128)(2,1)S(1)}, ...), condition=%wide.region_10.11_spmd.clone, body=%wide.region_9.10_spmd.clone.sunk | while | flops 1966132 | bytes 7078481 | solution.py:44
  289.0 3.9 fusion.292
  297.5 4.8 fusion.292
  306.8 5.0 fusion.292
  316.3 4.8 fusion.292
  324.4 4.2 fusion.194
  328.7 15.5 %fusion.60 = f32[1,256,48,64]{1,3,2,0:T(8,128)} fusion(f32[1,256,48,64]{1,3,2,0:T(8,128)S(1)} %bitcast.619, f32[256,48,64]{0,2,1:T(8,128)S(1)} %bitcast.637, f32[256,48,64]{0,2,1:T(8,128)S(1)} %bitcast.620, f32[48,256]{1,0:T(8,128)S(1)} %copy-done.83, f32[256,256]{1,0:T(8,128)S(1)} %copy-done.52, f32[48,256]{1,0:T(8,128)S(1)} %copy-done.85, ...), kind=kOutput, calls=%fused_computation.112 | convolution fusion | flops 2431647744 | bytes 13058240 | tf_op jit(solution)/shard_map/shtu,suhp->sthp/dot_general | solution.py:115
  347.8 30.1 %while.58 = (s32[]{:T(128)}, f32[1,48,128,64]{3,2,1,0:T(8,128)S(1)}, s32[]{:T(128)}, bf16[4,1,48]{2,1,0:T(2,128)(2,1)S(1)}, bf16[4,1,48,128,64]{3,4,2,0,1:T(8,128)(2,1)}, /*index=5*/s32[]{:T(128)}, s32[]{:T(128)}) while((s32[]{:T(128)}, f32[1,48,128,64]{3,2,1,0:T(8,128)S(1)}, s32[]{:T(128)}, bf16[4,1,48]{2,1,0:T(2,128)(2,1)S(1)}, ...), condition=%wide.region_4.5_spmd.clone, body=%wide.region_3.4_spmd.clone.sunk | while | flops 1966132 | bytes 7078481 | solution.py:44
  380.4 4.2 fusion.203
  384.7 15.5 %fusion.61 = f32[1,256,48,64]{1,3,2,0:T(8,128)} fusion(f32[1,256,48,64]{1,3,2,0:T(8,128)S(1)} %bitcast.646, f32[256,48,64]{0,2,1:T(8,128)S(1)} %bitcast.639, f32[256,48,64]{0,2,1:T(8,128)S(1)} %bitcast.647, f32[48,256]{1,0:T(8,128)S(1)} %copy-done.82, f32[256,256]{1,0:T(8,128)S(1)} %fusion.200, f32[48,256]{1,0:T(8,128)S(1)} %copy-done.84, ...), kind=kOutput, calls=%fused_computation.114 | convolution fusion | flops 2431647744 | bytes 13058240 | tf_op jit(solution)/shard_map/shtu,suhp->sthp/dot_general | solution.py:115
  403.7 5.5 multiply_reduce_fusion.18
  409.3 4.6 multiply_reduce_fusion.19
  413.9 9.3 fusion.63
  423.2 13.8 multiply_reduce_fusion.13
  437.0 7.4 multiply_reduce_fusion.12
  448.0 5.0 mul.1182
  456.5 15.8 %fusion.258 = f32[48,256,256]{2,1,0:T(8,128)} fusion(f32[48,64,256]{2,1,0:T(8,128)} %bitcast.621, f32[256,48,64]{0,2,1:T(8,128)} %bitcast.617), kind=kOutput, calls=%fused_computation.395 | convolution fusion | flops 2415919104 | bytes 18874368 | tf_op jit(solution)/shard_map/transpose(jvp(shtu,suhp->sthp))/dot_general | solution.py:115
  475.9 5.0 mul.1132
  484.6 5.4 fusion.124
  494.5 27.6 %fusion.15 = (f32[48,256]{1,0:T(8,128)}, f32[48,256]{1,0:T(8,128)}, f32[48,256]{1,0:T(8,128)}, f32[256,256]{1,0:T(8,128)S(1)}, f32[256,256]{1,0:T(8,128)}, /*ind...) fusion(f32[48,256]{1,0:T(8,128)} %copy.371, f32[256,256]{1,0:T(8,128)} %copy-done.50, ...), kind=kOutput, calls=%fused_computation.35 | convolution fusion | flops 2497503232 | bytes 20480000 | tf_op jit(solution)/shard_map/transpose(jvp(shtu,suhp->sthp))/dot_general | solution.py:115
  540.2 12.5 convolution_bitcast_fusion.4
  554.7 4.4 fusion.125
  560.5 11.9 convolution_bitcast_fusion.5
  574.4 8.0 fusion.150
  582.8 19.8 %while.56 = (s32[]{:T(128)}, f32[1,48,128,64]{3,2,1,0:T(8,128)S(1)}, s32[]{:T(128)}, bf16[4,1,48]{2,1,0:T(2,128)(2,1)S(1)}, bf16[4,1,48,128,64]{3,4,2,0,1:T(8,12...) while((s32[]{:T(128)}, f32[1,48,128,64]{3,2,1,0:T(8,128)S(1)}, s32[]{:T(128)}, ...), condition=%wide.region_15.16_spmd, body=%wide.region_14.15_spmd.sunk | while | flops 1179702 | bytes 7078523 | solution.py:69
  605.4 7.6 fusion.70
  615.1 28.9 %while.57 = (s32[]{:T(128)}, f32[1,48,128,64]{3,2,1,0:T(8,128)}, s32[]{:T(128)}, bf16[4,1,48]{2,1,0:T(2,128)(2,1)}, bf16[4,1,48,128,64]{3,4,2,0,1:T(8,128)(2,1)}...) while((s32[]{:T(128)}, f32[1,48,128,64]{3,2,1,0:T(8,128)}, s32[]{:T(128)}, ...), condition=%wide.region_29.31_spmd, body=%wide.region_28.30_spmd.sunk | while | flops 1179702 | bytes 7078523 | solution.py:69
  620.2 4.4 convert_add_fusion.7
  629.8 4.4 convert_add_fusion.7
  639.4 4.4 convert_add_fusion.7
  644.0 10.4 fusion.64
  672.6 14.4 fusion.58
  687.0 4.0 copy.433
  691.0 13.6 fusion.134
  704.6 13.1 fusion.59
  721.4 12.5 fusion.137
  735.1 9.7 multiply_reduce_fusion.6
  745.0 6.1 multiply_reduce_fusion.10
  751.1 5.5 broadcast_multiply_fusion
  756.7 6.0 pad_add_fusion
  777.9 11.4 fusion.243
  789.4 13.7 fusion.105
  803.7 12.7 convolution_add_fusion.1
  817.4 22.2 %fusion.143 = f32[1536,6448]{1,0:T(8,128)} fusion(f32[1536]{0:T(1024)S(1)} %copy-done.49, f32[256]{0:T(256)S(1)} %copy-done.91, bf16[2,1,256,1536]{3,2,1,0:T(8,128)(2,1)} %param.20, f32[1,256,3328]{2,1,0:T(8,128)} %split.18, f32[1,256,48]{2,1,0:T(8,128)S(1)} %copy-done.40, f32[1,256,3072]{2,1,0:T(8,128)} %get-tuple-element.669, ...), kind=kOutput, calls=%fused_computation.226 | convolution fusion | flops 5080739840 | bytes 47032832 | tf_op jit(solution)/shard_map/dot_general | solution.py:148
  839.5 27.9 %convolution_add_fusion = f32[1536,6448]{1,0:T(8,128)} fusion(f32[1536,6448]{1,0:T(8,128)} %fusion.143, f32[256]{0:T(256)S(1)} %copy-done.87, f32[1536]{0:T(1024)S(1)} %copy-done.49, bf16[2,1,256,1536]{3,2,1,0:T(8,128)(2,1)} %param.20, f32[1,256,3328]{2,1,0:T(8,128)} %copy-done.19, f32[1,256,48]{2,1,0:T(8,128)S(1)} %copy-done.39, ...), kind=kOutput, calls=%fused_computation.14 | convolution fusion | flops 5090643968 | bytes 87147520 | tf_op jit(solution)/shard_map/dot_general | solution.py:148
  867.5 6.6 fusion.80
  874.1 6.5 fusion.81
  885.9 41.8 %all-reduce.45.cloned.1.call-done = (f32[3328,4]{0,1:T(4,128)}, f32[3328]{0:T(1024)}, f32[1536]{0:T(1024)}, f32[3072]{0:T(1024)}, f32[48]{0:T(128)}, /*index=5*/f32[48]{0:T(128)}, f32[48]{0:T(128)}) async-done(((f32[3328,4]{0,1:T(4,128)}, f32[3328]{0:T(1024)}, f32[1536]{0:T(1024)}, f32[3072]{0:T(1024)}, f32[48]{0:T(128)}, /*index=5*/f32[48]{0:T(128)}, f32[48]{0:T(128)}), (f32[3328,4]{0,1:T(4,128)}, ...) | async-done | bytes 85584
  932.9 209.6 %reduce-scatter.6.cloned.1.call-done = f32[96,1536]{1,0:T(8,128)} async-done(((f32[3072,1536]{1,0:T(8,128)}), f32[96,1536]{1,0:T(8,128)}) %reduce-scatter.6.cloned.1.call-update) | async-done | bytes 589840 | tf_op jit(solution)/shard_map/reduce_scatter | solution.py:263
  1142.5 371.6 %reduce-scatter.4.cloned.1.call-done = f32[48,6448]{1,0:T(8,128)} async-done(((f32[1536,6448]{1,0:T(8,128)}), f32[48,6448]{1,0:T(8,128)}) %reduce-scatter.4.cloned.1.call-update) | async-done | bytes 1238032 | tf_op jit(solution)/shard_map/reduce_scatter | solution.py:262
  (464 shorter events, 268.7 us)
Async XLA Ops:
  7.2 138.4 %all-gather.12.cloned.1.call-start = ((), (), s32[]{:S(2)}) async-start(), calls=%async_computation.2 | async-start | bytes 20680704 | tf_op jit(solution)/shard_map/all_gather | solution.py:181
  7.9 276.5 %all-gather.18.cloned.1.call-start = ((), (), s32[]{:S(2)}) async-start(), calls=%async_computation.5 | async-start | bytes 3932160 | tf_op jit(solution)/shard_map/all_gather | solution.py:27
  53.8 101.9 %copy-start.48 = (f32[1536]{0:T(1024)}, f32[1536]{0:T(1024)S(1)}, u32[]{:S(2)}) copy-start(f32[1536]{0:T(1024)S(1)} %convert_element_type.301) | copy-start | bytes 18436
  54.4 113.6 %copy-start.110 = (f32[48]{0:T(128)}, f32[48]{0:T(128)S(1)}, u32[]{:S(2)}) copy-start(f32[48]{0:T(128)S(1)} %neg.55) | copy-start | bytes 580
  96.8 98.1 %copy-start.61 = (f32[3328]{0:T(1024)}, f32[3328]{0:T(1024)S(1)}, u32[]{:S(2)}) copy-start(f32[3328]{0:T(1024)S(1)} %get-tuple-element.589) | copy-start | bytes 39940
  96.8 98.1 %copy-start.63 = (f32[3328]{0:T(1024)}, f32[3328]{0:T(1024)S(1)}, u32[]{:S(2)}) copy-start(f32[3328]{0:T(1024)S(1)} %get-tuple-element.590) | copy-start | bytes 39940
  96.8 98.2 %copy-start.65 = (f32[3328]{0:T(1024)}, f32[3328]{0:T(1024)S(1)}, u32[]{:S(2)}) copy-start(f32[3328]{0:T(1024)S(1)} %get-tuple-element.591) | copy-start | bytes 39940
  98.6 57.1 %copy-start.100 = (f32[256]{0:T(256)}, f32[256]{0:T(256)S(1)}, u32[]{:S(2)}) copy-start(f32[256]{0:T(256)S(1)} %get-tuple-element.584) | copy-start | bytes 3076
  99.1 56.6 %copy-start.90 = (f32[256]{0:T(256)}, f32[256]{0:T(256)S(1)}, u32[]{:S(2)}) copy-start(f32[256]{0:T(256)S(1)} %fusion.224) | copy-start | bytes 3076
  99.1 56.6 %copy-start.86 = (f32[256]{0:T(256)}, f32[256]{0:T(256)S(1)}, u32[]{:S(2)}) copy-start(f32[256]{0:T(256)S(1)} %fusion.226) | copy-start | bytes 3076
  99.1 56.6 %copy-start.14 = (bf16[2,1,256,1536]{3,2,1,0:T(8,128)(2,1)S(1)}, bf16[2,1,256,1536]{3,2,1,0:T(8,128)(2,1)}, u32[]{:S(2)}) copy-start(bf16[2,1,256,1536]{3,2,1,0:T(8,128)(2,1)} %param.20) | copy-start | bytes 4718596
  155.7 12.3 copy-start.13
  155.8 15.0 copy-start.92
  174.7 14.3 copy-start.94
  175.4 13.6 copy-start.30
  175.9 13.1 copy-start.104
  176.0 13.0 copy-start.96
  177.2 11.8 copy-start.106
  177.2 17.7 %collective-permute-start = (bf16[1,3,3328]{2,1,0:T(4,128)(2,1)S(1)}, bf16[1,3,3328]{2,1,0:T(4,128)(2,1)S(1)}, u32[]{:S(2)}, u32[]{:S(2)}) collective-permute-start(bf16[1,3,3328]{2,1,0:T(4,128)(2,1)S(1)} %slice.455), channel_id=1, source_target_pairs={{0,1},{1,2},{2,3},{4,5},{5,6},{6,7},{8,9},{9,10},{10,11},{12,13},{... | collective-permute-start | bytes 59912 | tf_op jit(solution)/shard_map/ppermute | solution.py:21
  179.4 15.5 %collective-permute-start.1 = (bf16[1,3,3328]{2,1,0:T(4,128)(2,1)S(1)}, bf16[1,3,3328]{2,1,0:T(4,128)(2,1)S(1)}, u32[]{:S(2)}, u32[]{:S(2)}) collective-permute-start(bf16[1,3,3328]{2,1,0:T(4,128)(2,1)S(1)} %slice.454), channel_id=1, source_target_pairs={{0,1},{1,2},{2,3},{4,5},{5,6},{6,7},{8,9},{9,10},{10,11},{12,13},{... | collective-permute-start | bytes 59912 | tf_op jit(solution)/shard_map/ppermute | solution.py:21
  194.9 14.8 copy-start.44
  194.9 14.8 copy-start.46
  194.9 14.8 copy-start.27
  222.5 125.3 %all-gather.16.cloned.1.call-start = ((), (), s32[]{:S(2)}) async-start(), calls=%async_computation.4 | async-start | bytes 3932160 | tf_op jit(solution)/shard_map/all_gather | solution.py:27
  237.4 10.4 copy-start.43
  237.4 12.7 copy-start.95
  237.4 13.4 copy-start.42
  242.3 171.6 %all-gather.14.cloned.1.call-start = ((), (), s32[]{:S(2)}) async-start(), calls=%async_computation.3 | async-start | bytes 9732096 | tf_op jit(solution)/shard_map/all_gather | solution.py:182
  242.9 339.5 %all-gather.20.cloned.1.call-start = ((), (), s32[]{:S(2)}) async-start(), calls=%async_computation.6 | async-start | bytes 3932160 | tf_op jit(solution)/shard_map/all_gather | solution.py:52
  259.1 13.6 copy-start.53
  259.1 14.3 copy-start.54
  284.4 100.2 %copy-start.50 = (f32[256,256]{1,0:T(8,128)}, f32[256,256]{1,0:T(8,128)S(1)}, u32[]{:S(2)}) copy-start(f32[256,256]{1,0:T(8,128)S(1)} %fusion.200) | copy-start | bytes 786436
  328.6 15.6 %copy-start.23 = (f32[256,3072]{0,1}, f32[256,3072]{0,1:S(1)}, u32[]{:S(2)}) copy-start(f32[256,3072]{0,1:S(1)} %fusion.194) | copy-start | bytes 9437188
  377.9 182.6 %copy-start.1 = (f32[1,48,128,64]{3,2,1,0:T(8,128)}, f32[1,48,128,64]{3,2,1,0:T(8,128)S(1)}, u32[]{:S(2)}) copy-start(f32[1,48,128,64]{3,2,1,0:T(8,128)S(1)} %get-tuple-element.371) | copy-start | bytes 4718596
  384.6 15.6 %copy-start.24 = (f32[256,3072]{0,1}, f32[256,3072]{0,1:S(1)}, u32[]{:S(2)}) copy-start(f32[256,3072]{0,1:S(1)} %fusion.203) | copy-start | bytes 9437188
  409.3 27.7 %copy-start.88 = (f32[256]{0:T(256)}, f32[256]{0:T(256)S(1)}, u32[]{:S(2)}) copy-start(f32[256]{0:T(256)S(1)} %fusion.227) | copy-start | bytes 3076
  413.9 160.5 %copy-start.102 = (f32[256]{0:T(256)}, f32[256]{0:T(256)S(1)}, u32[]{:S(2)}) copy-start(f32[256]{0:T(256)S(1)} %fusion.225) | copy-start | bytes 3076
  490.0 123.0 %all-gather.22.cloned.1.call-start = ((), (), s32[]{:S(2)}) async-start(), calls=%async_computation.7 | async-start | bytes 3932160 | tf_op jit(solution)/shard_map/all_gather | solution.py:52
  540.2 12.6 copy-start.37
  540.2 14.5 copy-start.11
  559.1 368.6 %all-reduce.45.cloned.1.call-start = ((), (), s32[]{:S(2)}) async-start(), calls=%async_computation.10 | async-start | bytes 183296
  560.5 13.9 copy-start.16
  560.5 13.9 copy-start.28
  644.0 10.5 copy-start
  644.0 10.5 copy-start.2
  655.0 17.6 %copy-start.114 = (f32[48]{0:T(128)S(1)}, f32[48]{0:T(128)}, u32[]{:S(2)}) copy-start(f32[48]{0:T(128)} %param.29) | copy-start | bytes 580
  687.0 17.6 %copy-start.57 = (f32[256,48]{0,1:T(8,128)S(1)}, f32[256,48]{0,1:T(8,128)}, u32[]{:S(2)}) copy-start(f32[256,48]{0,1:T(8,128)} %copy-done.56) | copy-start | bytes 147460
  691.0 13.6 copy-start.22
  691.0 13.6 copy-start.34
  691.0 13.6 copy-start.51
  721.4 13.7 copy-start.47
  735.1 9.9 copy-start.20
  756.6 9.9 copy-start.75
  756.6 10.5 copy-start.74
  763.3 14.6 collective-permute-start.3
  775.5 13.9 collective-permute-start.2
  777.9 11.4 copy-start.49
  777.9 11.4 copy-start.87
  777.9 11.4 copy-start.91
  789.4 14.3 copy-start.4
  789.4 14.3 copy-start.89
  803.7 338.8 %reduce-scatter.6.cloned.1.call-start = ((), (), s32[]{:S(2)}) async-start(), calls=%async_computation.9 | async-start | bytes 19464192 | tf_op jit(solution)/shard_map/reduce_scatter | solution.py:263
  816.5 23.1 %copy-start.39 = (f32[1,256,48]{2,1,0:T(8,128)S(1)}, f32[1,256,48]{2,1,0:T(8,128)}, u32[]{:S(2)}) copy-start(f32[1,256,48]{2,1,0:T(8,128)} %get-tuple-element.672) | copy-start | bytes 147460
  816.5 697.6 %reduce-scatter.4.cloned.1.call-start = ((), (), s32[]{:S(2)}) async-start(), calls=%async_computation.8 | async-start | bytes 41361408 | tf_op jit(solution)/shard_map/reduce_scatter | solution.py:262
  (64 other events, 340.5 us)
Sparse Core Ops, SparseCore 0:
  10.9 134.6 all-gather.11
  222.6 25.7 all-gather.17
  250.0 28.5 all-gather.15
  281.4 82.0 all-gather.13
  490.1 26.2 all-gather.19
  559.3 26.1 all-gather.21
  803.8 123.9 all-reduce.44
  934.7 207.7 reduce-scatter.5
  1149.5 364.5 reduce-scatter.3
where the time goes:
time: 1530 us; the launch traced here: 1520 us
  waiting for transfers between devices  671 us (44%)
  matrix products  365 us (24%)
  local copies, waits for them, and re-layouts  195 us (13%)
  other arithmetic  174 us (11%)
  blocking collectives  94.2 us (6%)
  between operations  15.6 us (1%)
    reduce_scatter x1, waiting for transfers between devices, body(): lax.psum_scatter(gradients[0], ('dp', 'seq'), scatter_dimension=0, tiled=...  372 us
    reduce_scatter x1, waiting for transfers between devices, body(): lax.psum_scatter(gradients[1], ('dp', 'seq'), scatter_dimension=0, tiled=...  210 us
    dot_general x6, matrix products, group_outputs(): jnp.einsum('shtu,suhp->sthp', mixing, x_heads, precision=highest)  102 us
    dot_general x4, matrix products, contract_rows(): lax.dot_general(left_mat, right_mat, (((0,), (0,)), ((), ())), preferred_...  70.8 us
    dot_general x6, matrix products, group_states(): states = jnp.einsum('sun,suhp->shnp', b_state, weighted, precision=highest)  54.4 us
    dot_general x4, matrix products, contract_cols(): lax.dot_general(left_mat, right_mat, (((1,), (1,)), ((), ())), preferred_...  48.1 us
    all_gather x1, waiting for transfers between devices, body(): lax.all_gather(shards[0], ('dp', 'seq'), axis=0, tiled=True)  46.4 us
    unnamed x1, blocking collectives  43.2 us
  transfers between devices with their start and end apart: 13, of which 4 were waited for; matrix products, arithmetic and copies ran while one was open for 28% of the time, Pallas kernels for 0%

commit v1 on v0

v1 whole, which is shorter than its diff:
```python
import functools

import jax
import jax.numpy as jnp
import numpy as np
from jax import lax
from jax.experimental import pallas as pl
from jax.experimental.pallas import tpu as pltpu
from jax.sharding import Mesh
from jax.sharding import PartitionSpec as P

DI = 3072
H = 48
PS = 64
N = 128
KC = 4
CONV = 3328
D = 1536
T = 256
HH = H // 2
W = DI // 2
XC = W + 2 * N
XP = XC + 128
EPS = 1e-05
NEG = -1e30
f32 = jnp.float32
bf16 = jnp.bfloat16
HIGH = lax.Precision.HIGHEST
ALL = ("za", "zb", "zl", "s", "c")
Z = ("za", "zb")
MB_ = 1 << 20


def nn(a, b):
    return lax.dot_general(a, b, (((1,), (0,)), ((), ())), preferred_element_type=f32)


def nt(a, b):
    return lax.dot_general(a, b, (((1,), (1,)), ((), ())), preferred_element_type=f32)


def tn(a, b):
    return lax.dot_general(a, b, (((0,), (0,)), ((), ())), preferred_element_type=f32)


def halves(v):
    high = v.astype(bf16)
    return high, (v - high.astype(f32)).astype(bf16)


def fine(dot, a, b):
    (ah, al), (bh, bl) = halves(a), halves(b)
    return dot(ah, bh) + (dot(ah, bl) + dot(al, bh))


def iota(shape, dim):
    return lax.broadcasted_iota(jnp.int32, shape, dim)


def spread(cols, first, heads):
    rows = cols.shape[0]
    head = iota((rows, heads * PS), 1) // PS
    out = jnp.broadcast_to(cols[:, first : first + 1], (rows, heads * PS))
    for i in range(1, heads):
        out = jnp.where(head == i, cols[:, first + i : first + i + 1], out)
    return out


def per_head(values, first):
    lanes = values.shape[1]
    place = (iota((lanes, 128), 0) // PS + first == iota((lanes, 128), 1)).astype(bf16)
    high, low = halves(values)
    return nn(high, place) + nn(low, place)


def row_sum(values):
    return jnp.sum(values, axis=0, keepdims=True)


def conv_taps(pad_ref, cw_ref, lanes):
    total = cw_ref[4:5, lanes]
    for k in range(KC):
        total = total + cw_ref[k : k + 1, lanes] * pad_ref[pl.ds(5 + k, T), lanes]
    return total


def softplus(v):
    return jnp.maximum(v, 0.0) + jnp.log1p(jnp.exp(-jnp.abs(v)))


def params(**kw):
    return pltpu.CompilerParams(vmem_limit_bytes=40 * MB_, **kw)


def cost(flops, nbytes, trans=0):
    return pl.CostEstimate(flops=int(flops), bytes_accessed=int(nbytes), transcendentals=int(trans))


def states_kernel(xbc, halo, cw, hp, x, bc, s, dt, ld, ldt, st0, comb, dec, pad, tail, carry, xw):
    j = pl.program_id(0)
    m, b = j // 2, j % 2
    before = jnp.where(b == 0, halo[pl.ds(8 * m, 8), :XC], tail[...])
    pad[0:8] = before
    pad[8 : 8 + T] = xbc[:, :XC]
    tail[...] = xbc[T - 8 : T, :XC]
    step = softplus(xbc[:, XC:XP] + hp[0:1, :])
    step = jnp.where(iota((T, 128), 1) < HH, step, 0.0)
    tri = (iota((T, T), 0) >= iota((T, T), 1)).astype(f32)
    logd = jnp.dot(tri, -hp[1:2, :] * step, precision=HIGH, preferred_element_type=f32)
    dt[...] = step
    ld[...] = logd
    ldt[0] = logd.T[:32]
    tailw = jnp.exp(logd[T - 1 : T] - logd) * step
    lanes = slice(W, XC)
    a = conv_taps(pad, cw, lanes)
    act = a * lax.logistic(a)
    bc[...] = act
    s[...] = fine(nt, act[:, N:], act[:, :N])
    for i in range(W // 128):
        lanes = slice(128 * i, 128 * i + 128)
        a = conv_taps(pad, cw, lanes)
        act_x = a * lax.logistic(a)
        x[:, lanes] = act_x
        xw[:, lanes] = (act_x * spread(tailw, 2 * i, 2)).astype(bf16)
    st = tn(act[:, :N].astype(bf16), xw[...])
    last = jnp.exp(logd[T - 8 : T])
    decay = jnp.concatenate([spread(last, 4 * i, 4) for i in range(W // 256)], axis=1)[7:8]
    dec[0] = jnp.broadcast_to(decay, (8, W))

    @pl.when(b == 0)
    def _():
        st0[0] = st
        carry[...] = st

    @pl.when(b == 1)
    def _():
        comb[0] = (decay * carry[...] + st).astype(bf16)


def block_states(xbc, cw, hp, micros):
    blocks = 2 * micros
    rows = blocks * T
    blk = lambda j: (j % 2) * micros + j // 2
    out = lambda *sh: jax.ShapeDtypeStruct(sh, f32)
    whole = lambda a: pl.BlockSpec(a.shape, lambda j: (0, 0))
    return pl.pallas_call(
        states_kernel,
        name="block_states",
        grid=(blocks,),
        in_specs=[
            pl.BlockSpec((T, XP), lambda j: (blk(j), 0)),
            pl.BlockSpec((8 * micros, XP), lambda j: (rows // (8 * micros), 0)),
            whole(cw),
            whole(hp),
        ],
        out_specs=[
            pl.BlockSpec((T, W), lambda j: (blk(j), 0)),
            pl.BlockSpec((T, 2 * N), lambda j: (blk(j), 0)),
            pl.BlockSpec((T, T), lambda j: (blk(j), 0)),
            pl.BlockSpec((T, 128), lambda j: (blk(j), 0)),
            pl.BlockSpec((T, 128), lambda j: (blk(j), 0)),
            pl.BlockSpec((1, 32, T), lambda j: (blk(j), 0, 0)),
            pl.BlockSpec((1, N, W), lambda j: (j // 2, 0, 0)),
            pl.BlockSpec((1, N, W), lambda j: (j // 2, 0, 0)),
            pl.BlockSpec((1, 8, W), lambda j: (blk(j), 0, 0)),
        ],
        out_shape=[
            out(rows, W),
            out(rows, 2 * N),
            out(rows, T),
            out(rows, 128),
            out(rows, 128),
            out(blocks, 32, T),
            out(micros, N, W),
            jax.ShapeDtypeStruct((micros, N, W), bf16),
            out(blocks, 8, W),
        ],
        scratch_shapes=[
            pltpu.VMEM((T + 8, XC), f32),
            pltpu.VMEM((8, XC), f32),
            pltpu.VMEM((N, W), f32),
            pltpu.VMEM((T, W), bf16),
        ],
        compiler_params=params(),
        cost_estimate=cost(blocks * 2 * T * N * W, rows * (XP + W + 800) * 4, rows * XC * 2),
    )(xbc, xbc, cw, hp)


def inner_kernel(s, ld, ldt, dt, x, skip, y):
    g = pl.program_id(1)
    causal = iota((T, T), 0) >= iota((T, T), 1)
    head = iota((T, 256), 1) // PS
    shift = lax.rem(128 - 4 * g, 128)
    logd = pltpu.roll(ld[...], shift, 1)
    step = pltpu.roll(dt[...], shift, 1)
    tile = x[...]
    xdt = tile * spread(step, 0, 4)
    scores = s[...]
    total = skip[0:1, :] * tile
    for i in range(4):
        gap = logd[:, i : i + 1] - ldt[0, pl.ds(4 * g + i, 1), :]
        mixing = (jnp.exp(jnp.where(causal, gap, NEG)) * scores).astype(bf16)
        total = total + nn(mixing, jnp.where(head == i, xdt, 0.0).astype(bf16))
    y[...] = total


def inner_part(s, ld, ldt, dt, x, skip_row):
    rows = x.shape[0]
    blocks, groups = rows // T, W // 256
    return pl.pallas_call(
        inner_kernel,
        name="inner_part",
        grid=(blocks, groups),
        in_specs=[
            pl.BlockSpec((T, T), lambda j, g: (j, 0)),
            pl.BlockSpec((T, 128), lambda j, g: (j, 0)),
            pl.BlockSpec((1, 32, T), lambda j, g: (j, 0, 0)),
            pl.BlockSpec((T, 128), lambda j, g: (j, 0)),
            pl.BlockSpec((T, 256), lambda j, g: (j, g)),
            pl.BlockSpec((8, 256), lambda j, g: (0, g)),
        ],
        out_specs=pl.BlockSpec((T, 256), lambda j, g: (j, g)),
        out_shape=jax.ShapeDtypeStruct((rows, W), f32),
        compiler_params=params(),
        cost_estimate=cost(
            blocks * HH * 2 * T * T * 256, rows * (2 * W + 1024) * 4, blocks * HH * T * T
        ),
    )(s, ld, ldt, dt, x, skip_row)


def gate_kernel(yin, bc, e, ld, z, y, sums):
    grow = jnp.exp(ld[...])
    cst = bc[:, N:].astype(bf16)
    squares = jnp.zeros((T, 256), f32)
    for i in range(W // 256):
        lanes = slice(256 * i, 256 * i + 256)
        out = yin[:, lanes] + spread(grow, 4 * i, 4) * nn(cst, e[0, :, lanes])
        y[:, lanes] = out
        zt = z[:, lanes]
        g = out * (zt * lax.logistic(zt))
        squares = squares + g * g
    sums[...] = jnp.broadcast_to(jnp.sum(squares, axis=1, keepdims=True), (T, 128))


def gate_part(yin, bc, e, ld, z):
    rows = yin.shape[0]
    blocks = rows // T
    row = lambda c: pl.BlockSpec((T, c), lambda j: (j, 0))
    return pl.pallas_call(
        gate_kernel,
        name="gate_part",
        grid=(blocks,),
        in_specs=[
            row(W),
            row(2 * N),
            pl.BlockSpec((1, N, W), lambda j: (j, 0, 0)),
            row(128),
            row(W),
        ],
        out_specs=[row(W), row(128)],
        out_shape=[
            jax.ShapeDtypeStruct((rows, W), f32),
            jax.ShapeDtypeStruct((rows, 128), f32),
        ],
        input_output_aliases={0: 0},
        compiler_params=params(),
        cost_estimate=cost(2 * rows * N * W, rows * W * 4 * 3, rows * W * 2),
    )(yin, bc, e, ld, z)


def gate_back_kernel(y, z, gfin, x, sums, dots, bc, e, ld, gain, skip, dz, dy, dc, de, dl, ggain, gskip, dye):
    j = pl.program_id(0)

    @pl.when(j == 0)
    def _():
        ggain[...] = jnp.zeros_like(ggain)
        gskip[...] = jnp.zeros_like(gskip)

    r = lax.rsqrt(sums[:, 0:1] * (1.0 / DI) + EPS)
    coef = r * r * dots[:, 0:1] * (1.0 / DI)
    grow = jnp.exp(ld[...])
    dlog = jnp.zeros((T, 128), f32)
    dcs = jnp.zeros((T, N), f32)
    for i in range(W // 256):
        lanes = slice(256 * i, 256 * i + 256)
        zt, yt, gf = z[:, lanes], y[:, lanes], gfin[:, lanes]
        sg = lax.logistic(zt)
        silu = zt * sg
        g = yt * silu
        gr = g * r
        ggain[0:1, lanes] += row_sum(gf * gr)
        dg = r * (gf * gain[0:1, lanes]) - g * coef
        dyt = dg * silu
        dz[:, lanes] = (dg * yt * (sg * (1.0 + zt * (1.0 - sg)))).astype(bf16)
        dy[:, lanes] = dyt.astype(bf16)
        xt = x[:, lanes]
        gskip[0:1, lanes] += row_sum(dyt * xt)
        dlog = dlog + per_head(dyt * (yt - skip[0:1, lanes] * xt), 4 * i)
        high, low = halves(dyt * spread(grow, 4 * i, 4))
        dye[:, lanes] = high
        dcs = dcs + (nt(high, e[0, :, lanes]) + nt(low, e[0, :, lanes]))
    dl[...] = dlog
    dc[...] = dcs
    de[0] = tn(bc[:, N:].astype(bf16), dye[...])


def gate_back(y, z, gfin, x, sums, dots, bc, e, ld, gain, skip_row):
    rows = y.shape[0]
    blocks = rows // T
    row = lambda c: pl.BlockSpec((T, c), lambda j: (j, 0))
    fixed = pl.BlockSpec((8, W), lambda j: (0, 0))
    state = pl.BlockSpec((1, N, W), lambda j: (j, 0, 0))
    sh = jax.ShapeDtypeStruct
    return pl.pallas_call(
        gate_back_kernel,
        name="gate_back",
        grid=(blocks,),
        in_specs=[row(W), row(W), row(W), row(W), row(128), row(128), row(2 * N), state, row(128), fixed, fixed],
        out_specs=[row(W), row(W), row(N), state, row(128), fixed, fixed],
        out_shape=[
            sh((rows, W), bf16),
            sh((rows, W), bf16),
            sh((rows, N), f32),
            sh((blocks, N, W), f32),
            sh((rows, 128), f32),
            sh((8, W), f32),
            sh((8, W), f32),
        ],
        scratch_shapes=[pltpu.VMEM((T, W), bf16)],
        compiler_params=params(),
        cost_estimate=cost(8 * rows * N * W, rows * W * 24, rows * W * 2),
    )(y, z, gfin, x, sums, dots, bc, e, ld, gain, skip_row)


def inner_back_kernel(s, bc, ld, ldt, dt, x, dy, skip, dx, xv, dbc, st, dst):
    g = pl.program_id(1)

    @pl.when(g == 0)
    def _():
        st[...] = s[...].T
        dst[...] = jnp.zeros_like(dst)
        xv[...] = jnp.zeros_like(xv)

    causal = iota((T, T), 1) >= iota((T, T), 0)
    head = iota((T, 256), 1) // PS
    shift = lax.rem(128 - 4 * g, 128)
    logd = pltpu.roll(ld[...], shift, 1)
    steps = spread(pltpu.roll(dt[...], shift, 1), 0, 4)
    tile = x[...]
    xdt = tile * steps
    dyt = dy[...]
    scores = st[...]
    total = jnp.zeros((T, 256), f32)
    gscore = jnp.zeros((T, T), f32)
    for i in range(4):
        gap = ldt[0, pl.ds(4 * g + i, 1), :] - logd[:, i : i + 1]
        decay = jnp.exp(jnp.where(causal, gap, NEG))
        mine = head == i
        total = total + nn((decay * scores).astype(bf16), jnp.where(mine, dyt, jnp.zeros_like(dyt)))
        gscore = gscore + nt(jnp.where(mine, xdt, 0.0).astype(bf16), dyt) * decay
    dst[...] += gscore
    dx[...] = total * steps + skip[0:1, :] * dyt.astype(f32)
    xv[...] += per_head(tile * total, 4 * g)

    @pl.when(g == pl.num_programs(1) - 1)
    def _():
        dbc[:, :N] = fine(nn, dst[...], bc[:, N:])
        dbc[:, N:] = fine(tn, dst[...], bc[:, :N])


def inner_back(s, bc, ld, ldt, dt, x, dy, skip_row):
    rows = x.shape[0]
    blocks, groups = rows // T, W // 256
    row = lambda c: pl.BlockSpec((T, c), lambda j, g: (j, 0))
    tile = pl.BlockSpec((T, 256), lambda j, g: (j, g))
    sh = jax.ShapeDtypeStruct
    return pl.pallas_call(
        inner_back_kernel,
        name="inner_back",
        grid=(blocks, groups),
        in_specs=[
            row(T),
            row(2 * N),
            row(128),
            pl.BlockSpec((1, 32, T), lambda j, g: (j, 0, 0)),
            row(128),
            tile,
            tile,
            pl.BlockSpec((8, 256), lambda j, g: (0, g)),
        ],
        out_specs=[tile, row(128), row(2 * N)],
        out_shape=[sh((rows, W), f32), sh((rows, 128), f32), sh((rows, 2 * N), f32)],
        scratch_shapes=[pltpu.VMEM((T, T), f32), pltpu.VMEM((T, T), f32)],
        compiler_params=params(),
        cost_estimate=cost(
            2 * blocks * HH * 2 * T * T * 256, rows * (2 * W + 1024) * 4, blocks * HH * T * T
        ),
    )(s, bc, ld, ldt, dt, x, dy, skip_row)


def conv_back_kernel(
    micros, xbc, prev, x, dxi, xv, dbc, bc, dt, ld, later, e, dc, dla, cw, hp,
    gp, gcw, ghp, pad, dpre, nxt, edge,
):
    p = pl.program_id(0)
    b = 1 - p % 2

    @pl.when(p == 0)
    def _():
        gcw[...] = jnp.zeros_like(gcw)
        ghp[...] = jnp.zeros_like(ghp)

    @pl.when(p == 2 * micros)
    def _():
        gp[0 : 8 * micros] = edge[...].astype(bf16)

    @pl.when(p < 2 * micros)
    def _():
        pad[0:8] = prev[:, :XC]
        pad[8 : 8 + T] = xbc[:, :XC]
        dpre[0:8] = jnp.zeros((8, XC), f32)
        dpre[8 + T : 16 + T] = jnp.where(b == 1, 0.0, nxt[...])
        step, logd = dt[...], ld[...]
        fade = jnp.exp(logd[T - 1 : T] - logd)
        tailw = fade * step
        bst = bc[:, :N].astype(bf16)

        def through_conv(grad, lanes):
            a = conv_taps(pad, cw, lanes)
            sg = lax.logistic(a)
            d = grad * (sg * (1.0 + a * (1.0 - sg)))
            dpre[8 : 8 + T, lanes] = d
            gcw[4:5, lanes] += row_sum(d)
            for k in range(KC):
                gcw[k : k + 1, lanes] += row_sum(d * pad[pl.ds(5 + k, T), lanes])
            total = cw[0:1, lanes] * dpre[pl.ds(11, T), lanes]
            rim = cw[0:1, lanes] * dpre[pl.ds(3, 8), lanes]
            for k in range(1, KC):
                total = total + cw[k : k + 1, lanes] * dpre[pl.ds(11 - k, T), lanes]
                rim = rim + cw[k : k + 1, lanes] * dpre[pl.ds(3 - k, 8), lanes]
            gp[:, lanes] = total.astype(bf16)
            nxt[:, lanes] = d[0:8]

            @pl.when(b == 0)
            def _():
                edge[pl.ds(pl.multiple_of(8 * (p // 2), 8), 8), lanes] = rim

        dw = jnp.zeros((T, 128), f32)
        dbs = jnp.zeros((T, N), f32)
        ddec = jnp.zeros((8, 128), f32)
        for i in range(W // 256):
            lanes = slice(256 * i, 256 * i + 256)
            lat = later[0, :, lanes]
            spreadw = spread(tailw, 4 * i, 4)
            xt = x[:, lanes]
            bl = nn(bst, lat)
            dw = dw + per_head(xt * bl, 4 * i)
            high, low = halves(xt * spreadw)
            dbs = dbs + (nt(high, lat) + nt(low, lat))
            both = row_sum(lat.astype(f32) * e[0, :, lanes].astype(f32))
            ddec = ddec + per_head(jnp.broadcast_to(both, (8, 256)), 4 * i)
            through_conv(dxi[:, lanes] + bl * spreadw, lanes)
        through_conv(
            jnp.concatenate([dbc[:, :N] + dbs, dbc[:, N:] + dc[...]], axis=1), slice(W, XC)
        )
        q = dw * tailw
        dlog = dla[...] - step * xv[...] - q
        dlast = row_sum(q) + ddec[0:1] * jnp.exp(logd[T - 1 : T])
        dlog = dlog + jnp.where(iota((T, 128), 0) == T - 1, dlast, 0.0)
        tri = (iota((T, T), 1) >= iota((T, T), 0)).astype(f32)
        dcum = jnp.dot(tri, dlog, precision=HIGH, preferred_element_type=f32)
        dstep = xv[...] + dw * fade - hp[1:2, :] * dcum
        draw = dstep * lax.logistic(xbc[:, XC:XP] + hp[0:1, :])
        draw = jnp.where(iota((T, 128), 1) < HH, draw, 0.0)
        ghp[0:1] += row_sum(draw)
        ghp[1:2] -= row_sum(dcum * step)
        gp[:, XC:XP] = draw.astype(bf16)

        @pl.when(b == 0)
        def _():
            edge[pl.ds(pl.multiple_of(8 * (p // 2), 8), 8), XC:XP] = jnp.zeros((8, 128), f32)


def conv_back(xbc, x, dxi, xv, dbc, bc, dt, ld, later, e, dc, dla, cw, hp, micros):
    blocks = 2 * micros
    rows = blocks * T
    blk = lambda p: jnp.where(p < blocks, (1 - p % 2) * micros + p // 2, micros - 1)
    row = lambda c: pl.BlockSpec((T, c), lambda p: (blk(p), 0))
    whole = lambda a: pl.BlockSpec(a.shape, lambda p: (0, 0))
    state = pl.BlockSpec((1, N, W), lambda p: (blk(p), 0, 0))

    def before(p):
        k = blk(p)
        return (jnp.where(k >= micros, (k - micros + 1) * (T // 8) - 1, rows // 8 + k), 0)

    return pl.pallas_call(
        functools.partial(conv_back_kernel, micros),
        name="conv_back",
        grid=(blocks + 1,),
        in_specs=[
            row(XP),
            pl.BlockSpec((8, XP), before),
            row(W), row(W), row(128), row(2 * N), row(2 * N), row(128), row(128),
            state, state, row(N), row(128), whole(cw), whole(hp),
        ],
        out_specs=[
            pl.BlockSpec((T, XP), lambda p: (jnp.where(p < blocks, blk(p), blocks), 0)),
            pl.BlockSpec((8, XC), lambda p: (0, 0)),
            pl.BlockSpec((8, 128), lambda p: (0, 0)),
        ],
        out_shape=[
            jax.ShapeDtypeStruct((rows + 8 * micros, XP), bf16),
            jax.ShapeDtypeStruct((8, XC), f32),
            jax.ShapeDtypeStruct((8, 128), f32),
        ],
        scratch_shapes=[
            pltpu.VMEM((T + 8, XC), f32),
            pltpu.VMEM((T + 16, XC), f32),
            pltpu.VMEM((8, XC), f32),
            pltpu.VMEM((8 * micros, XP), f32),
        ],
        compiler_params=pltpu.CompilerParams(vmem_limit_bytes=58 * MB_),
        cost_estimate=cost(6 * rows * N * W, rows * W * 18, rows * XC * 2),
    )(xbc, xbc, x, dxi, xv, dbc, bc, dt, ld, later, e, dc, dla, cw, hp)


AXIS = {"z": Z, "l": "zl", "s": "s"}
RING = 4
CHIPS = 16


def hop(value, axis):
    n = RING if axis == "z" else 2
    return lax.ppermute(value, AXIS[axis], [(i, (i + 1) % n) for i in range(n)])


def fence(groups, *values):
    held = [{k: g.live[k] for k in g.live} for g in groups]
    held, values = lax.optimization_barrier((held, values))
    for g, h in zip(groups, held):
        g.live.update(h)
    return values


def after(groups, *values):
    values, _ = lax.optimization_barrier((values, [v for g in groups for v in g.sent]))
    for g in groups:
        g.sent = ()
    return values


class Moves:
    sent = ()

    def send(self, value, axis):
        self.sent = [*self.sent, value]
        return hop(value, axis)


class RingFirst(Moves):
    def __init__(self, own, a, b):
        self.a, self.b = a, b
        self.live = {"g0": own}
        self.n = 1
        self.parts = []

    def z(self):
        self.live[f"g{self.n}"] = self.send(self.live[f"g{self.n - 1}"], "z")
        self.n += 1

    def first(self, h):
        pair = jnp.stack([self.live.pop(f"g{2 * h}"), self.live[f"g{2 * h + 1}"]], 0)
        if h:
            self.live.pop("g3")
        self.live[f"p{h}"] = pair
        self.live[f"q{h}"] = self.send(pair, self.a)

    def second(self, h):
        four = jnp.concatenate([self.live.pop(f"p{h}"), self.live.pop(f"q{h}")], 0)
        self.parts += [four, self.send(four, self.b)]

    def entry(self, kz, kl, ks):
        ka, kb = (kl, ks) if self.a == "l" else (ks, kl)
        return (kz // 2) * 2 + kb, ka * 2 + kz % 2


class RingLast(Moves):
    def __init__(self, own, a, b):
        self.a, self.b = a, b
        self.live = {"p": own[None]}
        self.parts = []

    def step(self, axis):
        self.live["p"] = jnp.concatenate([self.live["p"], self.send(self.live["p"], axis)], 0)

    def z(self):
        if not self.parts:
            self.parts = [self.live["p"]]
        self.live["p"] = self.send(self.live["p"], "z")
        self.parts.append(self.live["p"])

    def entry(self, kz, kl, ks):
        ka, kb = (kl, ks) if self.a == "l" else (ks, kl)
        return kz, kb * 2 + ka


class ExchangeFirst(Moves):
    def __init__(self, a, b):
        self.a, self.b = a, b
        self.live = {}

    def load(self, parts):
        for h in range(2):
            self.live[f"k{h}"], self.live[f"s{h}"] = parts[2 * h], parts[2 * h + 1]

    def second(self, h):
        got = self.send(self.live.pop(f"s{h}"), self.b)
        self.live[f"r{h}"] = got

    def first(self, h):
        total = self.live.pop(f"r{h}").astype(f32) + self.live.pop(f"k{h}").astype(f32)
        self.live[f"m{h}"] = total[:2].astype(bf16)
        self.live[f"n{h}"] = self.send(total[2:].astype(bf16), self.a)

    def ring(self, k):
        if k in (0, 2):
            h = k // 2
            both = self.live.pop(f"m{h}").astype(f32) + self.live.pop(f"n{h}").astype(f32)
            term, self.live["w"] = both[0], both[1].astype(bf16)
        else:
            term = self.live.pop("w").astype(f32)
        if k:
            term = term + self.live.pop("t").astype(f32)
        if k == 3:
            return term
        self.live["t"] = self.send(term.astype(bf16), "z")

    def entry(self, kz, kl, ks):
        ka, kb = (kl, ks) if self.a == "l" else (ks, kl)
        h, at = ((0, kz - 1) if kz in (1, 2) else (1, (kz + 1) % 4))
        return 2 * h + kb, ka * 2 + at


def move_kernel(table, r, out_of, where, *refs):
    sems = refs[-1]
    refs = refs[:-1]
    whole = refs[-1] if out_of else refs[0]
    arrays = refs[:-1] if out_of else refs[1:]
    copies = []
    for n, (array, entry, k, lane, width) in enumerate(table):
        row = pl.multiple_of(where[k] * r, 16)
        place = whole.at[pl.ds(row, r), lane : lane + width]
        piece = arrays[array].at[entry]
        pair = (piece, place) if out_of else (place, piece)
        copies.append(pltpu.make_async_copy(*pair, sems.at[n]))
    for c in copies:
        c.start()
    for c in copies:
        c.wait()


def move(groups, where, r, widths, whole=None, parts=None):
    table = []
    for g, group in enumerate(groups):
        for k in range(CHIPS):
            array, entry = group.entry(k // 4, k // 2 % 2, k % 2)
            table.append((4 * g + array, entry, k, sum(widths[:g]), widths[g]))
    wide = sum(widths)
    shapes = [jax.ShapeDtypeStruct((4, r, w), bf16) for w in widths for _ in range(4)]
    joined = jax.ShapeDtypeStruct((CHIPS * r, wide), bf16)
    given = parts if parts else [whole]
    any_ = pl.BlockSpec(memory_space=pl.ANY)
    return pl.pallas_call(
        functools.partial(move_kernel, tuple(table), r, parts is not None),
        name="join" if parts else "deal",
        in_specs=[pl.BlockSpec(memory_space=pltpu.SMEM)] + [any_] * len(given),
        out_specs=any_ if parts else [any_] * len(shapes),
        out_shape=joined if parts else shapes,
        scratch_shapes=[pltpu.SemaphoreType.DMA((len(table),))],
        compiler_params=pltpu.CompilerParams(vmem_limit_bytes=MB_),
        cost_estimate=cost(0, 4 * CHIPS * r * wide),
    )(where, *given)


def join(groups, where, r, widths):
    return move(groups, where, r, widths, parts=[p for g in groups for p in g.parts])


def deal(groups, where, r, widths, whole):
    parts = move(groups, where, r, widths, whole=whole)
    for g, group in enumerate(groups):
        group.load(parts[4 * g : 4 * g + 4])


def swap(value, axis="c"):
    return lax.ppermute(value, axis, [(0, 1), (1, 0)])


def two(mine, other, at):
    return jnp.where(at == 0, jnp.stack([mine, other]), jnp.stack([other, mine]))


def cols(value, *widths):
    out, at = [], 0
    for w in widths:
        out.append(value[:, at : at + w])
        at += w
    return out


class Plain:
    def __init__(self, axes):
        self.axes = axes

    def gather(self, piece):
        return lax.all_gather(piece, self.axes, axis=0, tiled=True)

    def reduce(self, grad):
        return lax.psum_scatter(grad, self.axes, scatter_dimension=0, tiled=True).astype(f32)


def body(
    hidden, in_weight, out_weight, conv_weight, conv_bias, norm_gain, gate_gain,
    step_bias, decay_rate, skip_gain, cotangent,
):
    nz, nl, ns = lax.axis_size(Z), lax.axis_size("zl"), lax.axis_size("s")
    core = lax.axis_index("c")
    micros = hidden.shape[0]
    rows = micros * 2 * T
    r_in, r_out = in_weight.shape[0], out_weight.shape[0]
    r = 2 * r_in
    fast = (nz, nl, ns) == (RING, 2, 2) and r % 16 == 0 and r_out == r
    onward = [(i, i + 1) for i in range(ns - 1)]
    backward = [(i + 1, i) for i in range(ns - 1)]
    turn = [(a * 2 + b, b * 2 + a) for a in range(2) for b in range(2)]

    def cut(k):
        return jnp.concatenate(
            [
                in_weight[:, DI + k * W : DI + (k + 1) * W],
                in_weight[:, 2 * DI : 2 * DI + 2 * N],
                jnp.pad(in_weight[:, DI + CONV + k * HH : DI + CONV + (k + 1) * HH], ((0, 0), (0, 128 - HH))),
                in_weight[:, k * W : (k + 1) * W],
            ],
            axis=1,
        )

    cuts = jnp.stack([cut(0), cut(1)])
    theirs = swap(lax.dynamic_index_in_dim(cuts, 1 - core, 0, False))
    chip_rows = two(lax.dynamic_index_in_dim(cuts, core, 0, False), theirs, core).reshape(r, -1)
    w_own = lax.ppermute(out_weight, ("za", "c"), turn)

    ins = Plain(ALL[:4])
    outs = Plain(("zb", "zl", "s", "za"))

    n_c = conv_bias.shape[0]
    packed = jnp.concatenate([conv_weight.T.reshape(-1), conv_bias, norm_gain, gate_gain])

    def spread_out(small, a, at):
        mine, other = (jnp.expand_dims(v, at) for v in (small, swap(small, a)))
        here = lax.axis_index(a) == 0
        return jnp.where(here, jnp.concatenate([mine, other], at), jnp.concatenate([other, mine], at))

    hid_own = hidden.reshape(micros, T, D)
    cot_own = cotangent.reshape(micros, T, D)
    hid_other, cot_other = swap(hid_own), swap(cot_own)

    def chip_tokens(mine, other):
        return two(mine, other, core).reshape(rows, D)

    def rim_of(tokens):
        return lax.ppermute(tokens.reshape(2, micros, T, D)[1, :, T - 8 :], "s", onward)

    if fast:
        back = jnp.arange(CHIPS)
        kz = (lax.axis_index(Z) - back // 4) % RING
        kl = (lax.axis_index("zl") - back // 2) % 2
        ks = (lax.axis_index("s") - back) % 2
        in_place = ((kz * 2 + kl) * 2 + ks).astype(jnp.int32)
        out_place = ((((kz % 2) * 2 + kl) * 2 + ks) * 2 + kz // 2).astype(jnp.int32)
        x_cols, z_cols, o_cols = (896, 1024), (768, 768), (768, 768)
        small = spread_out(packed, "za", 0)
        small = spread_out(small, "zb", 1)
        chip_rows, small = lax.optimization_barrier((chip_rows, small))
        own = cols(chip_rows, *x_cols, *z_cols)
        gx_ = [RingFirst(own[0], "s", "l"), RingFirst(own[1], "l", "s")]
        gz_ = [RingFirst(own[2], "s", "l"), RingFirst(own[3], "l", "s")]
        own = cols(w_own, *o_cols)
        go_ = [RingLast(own[0], "s", "l"), RingLast(own[1], "l", "s")]
        every = gx_ + gz_ + go_
        small = spread_out(small, "zl", 2)
        for g in gx_:
            g.z()
        for g in go_:
            g.step(g.a)
        small, hid_other, cot_other = fence(every, small, hid_other, cot_other)
        small = spread_out(small, "s", 3)
        for g in gx_:
            g.z()
            g.first(0)
        for g in go_:
            g.step(g.b)
        hid_own_, hid_other = after(every, hid_own, hid_other)
        hid_all = chip_tokens(hid_own_, hid_other)
        rim = rim_of(hid_all)
        small, rim, hid_all = fence(every, small, rim, hid_all)
        for g in gx_:
            g.z()
            g.second(0)
        for g in gz_:
            g.z()
        small, cot_own_, cot_other = after(every, small, cot_own, cot_other)
        small = spread_out(small, "c", 4).reshape(-1, packed.shape[0])
        cot_all = chip_tokens(cot_own_, cot_other)
        small, cot_all = fence(every, small, cot_all)
        for g in gx_:
            g.first(1)
        for g in gz_:
            g.z()
        for g in go_:
            g.z()
        (small,) = fence(gx_ + gz_, small)
        for g in gx_:
            g.second(1)
        for g in gz_:
            g.z()
        small, hid_all, rim = after(gx_ + gz_, small, hid_all, rim)
    else:
        small = lax.all_gather(packed, ALL)
        hid_all, cot_all = chip_tokens(hid_own, hid_other), chip_tokens(cot_own, cot_other)
        rim = rim_of(hid_all)
        w_x, w_z = ins.gather(chip_rows[:, :XP]), ins.gather(chip_rows[:, XP:])

    rim = jnp.where(iota(rim.shape, 1) >= 5, rim, jnp.zeros_like(rim)).reshape(8 * micros, D)
    tok_f = jnp.concatenate([hid_all, rim], axis=0).astype(f32)
    scale = lax.rsqrt(jnp.mean(tok_f * tok_f, axis=-1, keepdims=True) + EPS)
    devices = small.shape[0]
    taps = small[:, : KC * n_c].reshape(devices, KC, n_c).transpose(1, 0, 2).reshape(KC, CONV)
    bias = small[:, KC * n_c : (KC + 1) * n_c].reshape(1, CONV)
    norm_vec = small[:, (KC + 1) * n_c : (KC + 1) * n_c + r_in].reshape(D).astype(f32)
    gate_vec = small[:, (KC + 1) * n_c + r_in :].reshape(1, DI)
    conv_all = jnp.concatenate([taps, bias, jnp.zeros((3, CONV), bf16)], 0).astype(f32)
    cw = jnp.concatenate(
        [lax.dynamic_slice_in_dim(conv_all, core * W, W, 1), conv_all[:, DI:]], axis=1
    )
    gain = jnp.broadcast_to(lax.dynamic_slice_in_dim(gate_vec, core * W, W, 1).astype(f32), (8, W))
    heads = jnp.stack([step_bias, decay_rate, skip_gain])
    heads = lax.dynamic_slice_in_dim(heads, core * HH, HH, 1)
    hp = jnp.pad(heads, ((0, 5), (0, 128 - HH)))
    skip_row = jnp.broadcast_to(jnp.repeat(heads[2], PS)[None], (8, W))
    normed = (tok_f * scale * norm_vec).astype(bf16)

    if fast:
        normed, cw, hp, gain, skip_row = fence(every, normed, cw, hp, gain, skip_row)
        for g in gz_:
            g.first(0)
        for g in go_:
            g.z()
        (normed,) = after(gz_ + go_, normed)
        w_x = join(gx_, in_place, r, x_cols)
    xbc = nn(normed, w_x)
    if fast:
        (xbc,) = fence(gz_, xbc)
        for g in gz_:
            g.second(0)
            g.first(1)
        (xbc,) = after(gz_, xbc)
    else:
        w_o = outs.gather(w_own)
    x, bc, s, dt, ld, ldt, st0, comb, dec = block_states(xbc, cw, hp, micros)
    dec = dec[:, 0].reshape(2, micros, 1, W)
    if fast:
        comb, s = fence(gz_ + go_, comb, s)
        for g in gz_:
            g.second(1)
        for g in go_:
            g.z()
        (s,) = after(gz_ + go_, s)
    if ns == 2:
        first = lax.ppermute(comb, "s", onward)
    else:
        first = jnp.zeros_like(comb)
        chip_decay = dec[0] * dec[1]
        for _ in range(ns - 1):
            out = (chip_decay * first.astype(f32) + comb.astype(f32)).astype(bf16)
            first = lax.ppermute(out, "s", onward)
    yin = inner_part(s, ld, ldt, dt, x, skip_row)
    second = (dec[0] * first.astype(f32) + st0).astype(bf16)
    entering = jnp.stack([first, second], 0).reshape(2 * micros, N, W)
    if fast:
        w_z = join(gz_, in_place, r, z_cols)
    z = nn(normed[:rows], w_z)
    y, sums = gate_part(yin, bc, entering, ld, z)
    sums = sums + swap(sums)
    root = lax.rsqrt(sums[:, :1] * (1.0 / DI) + EPS)
    exact = y * (z * lax.logistic(z)) * root * gain[:1]
    fin = exact.astype(bf16)
    g_out = tn(fin, cot_all).astype(bf16)
    if fast:
        so_ = [ExchangeFirst("s", "l"), ExchangeFirst("l", "s")]
        deal(so_, out_place, r, o_cols, g_out)
        (cot_all,) = fence(so_, cot_all)
        for g in so_:
            g.second(0)
        (cot_all,) = after(so_, cot_all)
        w_o = join(go_, out_place, r, o_cols)

    gfin = nt(cot_all, w_o)
    dots = jnp.sum(gfin * exact, axis=1)
    if fast:
        dots, gfin = fence(so_, dots, gfin)
        for g in so_:
            g.second(1)
            g.first(0)
        (y,) = after(so_, y)
    dots = dots + swap(dots)
    dots = jnp.broadcast_to(dots[:, None], (rows, 128))
    dz, dy, dc, de, dla, ggain, gskip = gate_back(
        y, z, gfin, x, sums, dots, bc, entering, ld, gain, skip_row
    )
    de = de.reshape(2, micros, N, W)
    if ns == 2:
        given = (de[0] + dec[0] * de[1]).astype(bf16)
        dz, given = lax.optimization_barrier((dz, given))
        later1 = lax.ppermute(given, "s", backward)
    else:
        later1 = jnp.zeros((micros, N, W), bf16)
        for _ in range(ns - 1):
            out = de[0] + dec[0] * (de[1] + dec[1] * later1.astype(f32))
            later1 = lax.ppermute(out.astype(bf16), "s", backward)
    gz = tn(normed[:rows], dz).astype(bf16)
    if fast:
        sz_ = [ExchangeFirst("s", "l"), ExchangeFirst("l", "s")]
        deal(sz_, in_place, r, z_cols, gz)
        (dy,) = fence(so_ + sz_, dy)
        for g in so_:
            g.first(1)
            g.ring(0)
        for g in sz_:
            g.second(0)
        (dy,) = after(so_ + sz_, dy)

    dxi, xv, dbc = inner_back(s, bc, ld, ldt, dt, x, dy, skip_row)
    later0 = (de[1] + dec[1] * later1.astype(f32)).astype(bf16)
    later = jnp.stack([later0, later1], 0).reshape(2 * micros, N, W)
    if fast:
        dxi, later = fence(so_ + sz_, dxi, later)
        for g in so_:
            g.ring(1)
        for g in sz_:
            g.second(1)
            g.first(0)
        (dxi,) = after(so_ + sz_, dxi)
    gp, gcw, ghp = conv_back(
        xbc, x, dxi, xv, dbc, bc, dt, ld, later, entering, dc, dla, cw, hp, micros
    )
    if fast:
        (gp,) = fence(so_ + sz_, gp)
        for g in sz_:
            g.first(1)
            g.ring(0)
        for g in so_:
            g.ring(2)
        (gp,) = after(so_ + sz_, gp)
    gx = tn(normed, gp).astype(bf16)
    if fast:
        sx_ = [ExchangeFirst("s", "l"), ExchangeFirst("l", "s")]
        deal(sx_, in_place, r, x_cols, gx)
        (gp,) = fence(so_ + sz_ + sx_, gp)
        for g in sx_:
            g.second(0)
        for g in sz_:
            g.ring(1)
        (gp,) = after(sx_ + sz_, gp)
        g_out = jnp.concatenate([g.ring(3) for g in so_], axis=1)
    else:
        g_out = outs.reduce(g_out)

    gn = nt(gp, w_x)
    edge = lax.ppermute(gn[rows:].astype(bf16), "s", backward).reshape(1, micros, 8, D)
    gn = (gn[:rows] + nt(dz, w_z)).reshape(2, micros, T, D)
    if fast:
        gn, edge, fin, g_out = fence(sz_ + sx_, gn, edge, fin, g_out)
        for g in sx_:
            g.second(1)
            g.first(0)
        for g in sz_:
            g.ring(2)
        gn, fin = after(sx_ + sz_, gn, fin)
    edge = jnp.where(iota(edge.shape, 2) >= 5, edge.astype(f32), 0.0)
    gn = gn + jnp.pad(edge, ((1, 0), (0, 0), (T - 8, 0), (0, 0)))
    give = lax.dynamic_index_in_dim(gn, 1 - core, 0, False).astype(bf16)
    keep = lax.dynamic_index_in_dim(gn, core, 0, False)
    gn = keep + swap(give).astype(f32)
    hid_f = hid_own.astype(f32)
    own_scale = lax.rsqrt(jnp.mean(hid_f * hid_f, axis=-1, keepdims=True) + EPS)
    unit = hid_f * own_scale
    gq = gn * norm_vec
    g_hid = cot_own.astype(f32) + own_scale * (
        gq - unit * jnp.mean(gq * unit, axis=-1, keepdims=True)
    )
    g_norm = jnp.sum(gn * unit, axis=(0, 1))

    partial_out = nn(fin, w_o).reshape(2, micros, T, D)
    give = lax.dynamic_index_in_dim(partial_out, 1 - core, 0, False).astype(bf16)
    keep = lax.dynamic_index_in_dim(partial_out, core, 0, False)
    given_out = swap(give)

    wide = lambda v: jnp.pad(v, ((0, 0), (0, XC - v.shape[1])))
    tiny = jnp.concatenate(
        [
            gcw[:5], wide(ggain[:1]), wide(gskip[:1]), wide(ghp[:2].reshape(1, 256)),
            wide(g_norm[None]), jnp.zeros((7, XC), f32),
        ],
        axis=0,
    )
    if fast:
        tiny, g_hid, given_out, keep = fence(sz_ + sx_, tiny, g_hid, given_out, keep)
        tiny = tiny + swap(tiny, "zb")
        for g in sx_:
            g.first(1)
            g.ring(0)
        gz = jnp.concatenate([g.ring(3) for g in sz_], axis=1)
    block_out = (hid_own.astype(f32) + keep + given_out.astype(f32)).astype(bf16)

    def exchanged(g):
        g = g.reshape(2, r_in, -1)
        mine = lax.dynamic_index_in_dim(g, core, 0, False)
        return two(mine, swap(lax.dynamic_index_in_dim(g, 1 - core, 0, False)), core)

    if fast:
        tiny, block_out, gz, g_out = fence(sx_, tiny, block_out, gz, g_out)
        tiny = tiny + swap(tiny, "za")
        for g in sx_:
            g.ring(1)
        g_out = lax.ppermute(g_out, ("za", "c"), turn)
        gz = exchanged(gz)
        tiny, g_out, gz = fence(sx_, tiny, g_out, gz)
        tiny = tiny + swap(tiny, "s")
        for g in sx_:
            g.ring(2)
        tiny = tiny + swap(tiny, "zl")
        (tiny,) = fence(sx_, tiny)
        gx = jnp.concatenate([g.ring(3) for g in sx_], axis=1)
    else:
        tiny = lax.psum(tiny, ALL[:4])
        gx, gz = ins.reduce(gx), ins.reduce(gz)
        g_out = lax.ppermute(g_out, ("za", "c"), turn)
        gz = exchanged(gz)
    gx = exchanged(gx)
    both = two(tiny, swap(tiny), core)
    g_conv = jnp.concatenate([both[0, :5, :W], both[1, :5, :W], both[0, :5, W:] + both[1, :5, W:]], axis=1)
    me = lax.axis_index(ALL)
    g_conv = lax.dynamic_slice_in_dim(g_conv, me * n_c, n_c, 1)
    g_norm = lax.dynamic_slice_in_dim(both[0, 8, :D] + both[1, 8, :D], me * r_in, r_in)
    g_gate = both[:, 5, :W].reshape(-1)
    g_gate = lax.dynamic_slice_in_dim(g_gate, me * r_out, r_out)
    g_skip = both[:, 6, :W].reshape(H, PS).sum(-1)
    g_bias = both[:, 7, :HH].reshape(-1)
    g_rate = both[:, 7, 128 : 128 + HH].reshape(-1)
    g_in = jnp.concatenate(
        [
            gz[0], gz[1],
            gx[0, :, :W], gx[1, :, :W],
            gx[0, :, W:XC] + gx[1, :, W:XC],
            gx[0, :, XC : XC + HH], gx[1, :, XC : XC + HH],
        ],
        axis=1,
    )
    return (
        block_out.reshape(hidden.shape),
        g_hid.reshape(hidden.shape),
        g_in,
        g_out,
        g_conv[:KC].T,
        g_conv[KC],
        g_norm,
        g_gate,
        g_bias,
        g_rate,
        g_skip,
    )


def solution(mesh):
    dp, seq = mesh.shape["dp"], mesh.shape["seq"]
    split = Mesh(mesh.devices.reshape(2, dp // 4, 2, seq // 2, 2), ALL)
    token = P(None, ("za", "zb", "zl"), ("s", "c"), None)
    in_specs = (token, P(ALL, None), P(ALL, None), P(ALL, None), P(ALL), P(ALL), P(ALL), P(), P(), P(), token)
    out_specs = (token, token, P(ALL, None), P(ALL, None), P(ALL, None), P(ALL), P(ALL), P(ALL), P(), P(), P())
    return jax.shard_map(body, mesh=split, in_specs=in_specs, out_specs=out_specs, check_vma=False)
```

time: 1530 us -> 596 us (0.39)
  waiting for transfers between devices: 671 us -> 161 us
  matrix products: 365 us -> 63.7 us
  local copies, waits for them, and re-layouts: 195 us -> 47.6 us
  Pallas kernels: 0 us -> 129 us
  starting transfers between devices: 8.95 us -> 111 us
  other arithmetic: 174 us -> 72 us
  blocking collectives: 94.2 us -> 0 us
    reduce_scatter x2 -> x0, waiting for transfers between devices: 581 us -> none  [the longest x1 372 us: body(): lax.psum_scatter(gradients[0], ('dp', 'seq'), scatter_dimension=0, tiled=...]
    dot_general x34 -> x9, matrix products: 357 us -> 63.7 us  [the longest x3 23 us: nt(): lax.dot_general(a, b, (((1,), (1,)), ((), ())), preferred_element_type=f32)]
    ppermute x4 -> x105, waiting for transfers between devices: 0.01 us -> 161 us  [the longest x80 112 us: hop(): return lax.ppermute(value, AXIS[axis], [(i, (i + 1) % n) for i in range(n)])]
    pallas_call x0 -> x12, Pallas kernels: none -> 129 us  [the longest x1 34.1 us: conv_back(): pl.pallas_call(functools.partial(conv_back_kernel, micros), name='conv_ba...]
    ppermute x4 -> x105, starting transfers between devices: 8.42 us -> 111 us  [the longest x80 80.6 us: hop(): return lax.ppermute(value, AXIS[axis], [(i, (i + 1) % n) for i in range(n)])]
    dynamic_slice x28 -> x5, local copies, waits for them, and re-layouts: 63.2 us -> 0.78 us  [the longest x1 0.58 us: body(): g_gate = lax.dynamic_slice_in_dim(g_gate, me * r_out, r_out)]
    all_gather x3 -> x0, blocking collectives: 50.9 us -> none  [the longest x1 40.9 us: body(): lax.all_gather(shards[2], ('dp', 'seq'), axis=0, tiled=True)]
    all_gather x6 -> x0, waiting for transfers between devices: 46.5 us -> none  [the longest x1 46.4 us: body(): lax.all_gather(shards[0], ('dp', 'seq'), axis=0, tiled=True)]
  transfers between devices with their start and end apart: 13 -> 105, of which waited for: 4 -> 29; matrix products, arithmetic and copies ran while one was open for 28% -> 25% of each run, Pallas kernels for 0% -> 22%
where the time goes in v1:
time: 596 us; the launch traced here: 587 us
  waiting for transfers between devices  161 us (27%)
  Pallas kernels  129 us (22%)
  starting transfers between devices  111 us (19%)
  other arithmetic  72 us (12%)
  matrix products  63.7 us (11%)
  local copies, waits for them, and re-layouts  47.6 us (8%)
    ppermute x80, waiting for transfers between devices, hop(): return lax.ppermute(value, AXIS[axis], [(i, (i + 1) % n) for i in range(n)])  112 us
    ppermute x80, starting transfers between devices, hop(): return lax.ppermute(value, AXIS[axis], [(i, (i + 1) % n) for i in range(n)])  80.6 us
    ppermute x19, waiting for transfers between devices, swap(): return lax.ppermute(value, axis, [(0, 1), (1, 0)])  42.2 us
    pallas_call x1, Pallas kernels, conv_back(): pl.pallas_call(functools.partial(conv_back_kernel, micros), name='conv_ba...  34.1 us
    pallas_call x1, Pallas kernels, inner_back(): pl.pallas_call(inner_back_kernel, name='inner_back', grid=(blocks, groups...  25.5 us
    dot_general x3, matrix products, nt(): lax.dot_general(a, b, (((1,), (1,)), ((), ())), preferred_element_type=f32)  23 us
    dot_general x3, matrix products, nn(): lax.dot_general(a, b, (((1,), (0,)), ((), ())), preferred_element_type=f32)  20.9 us
    pallas_call x1, Pallas kernels, inner_part(): pl.pallas_call(inner_kernel, name='inner_part', grid=(blocks, groups), in...  20.5 us
  transfers between devices with their start and end apart: 105, of which 29 were waited for; matrix products, arithmetic and copies ran while one was open for 25% of the time, Pallas kernels for 22%

profile of v1, /device:TPU:0, one launch (start us, length us, event | category | flops | bytes accessed | tf_op | source)
XLA Modules:
  0.0 586.9 jit_solution(12911291370110534345)
XLA Ops:
  7.9 3.6 collective-permute-start.1
  11.5 3.7 collective-permute-start.5
  25.6 3.0 collective-permute-done.8
  30.5 3.0 collective-permute-start.4
  33.6 5.6 collective-permute-done.3
  39.2 4.2 collective-permute-done.4
  47.6 2.3 maximum_select_fusion
  50.0 4.3 collective-permute-done.17
  54.9 6.1 %collective-permute-done.15 = bf16[2,96,768]{2,1,0:T(8,128)(2,1)S(1)} collective-permute-done((bf16[2,96,768]{2,1,0:T(8,128)(2,1)S(1)}, bf16[2,96,768]{2,1,0:T(8,128)(2,1)S(1)}, u32[]{:S(2)}, u32[]{:S(2)}) %collective-permute-start.15) | collective-permute-done | bytes 294944 | tf_op jit(solution)/shard_map/ppermute | solution.py:534
  61.1 2.4 collective-permute-start.18
  65.3 3.7 collective-permute-done.13
  71.6 2.4 collective-permute-start.22
  74.2 3.6 maximum_select_fusion.1
  78.0 6.7 %collective-permute-done.21 = bf16[96,768]{1,0:T(8,128)(2,1)} collective-permute-done((bf16[96,768]{1,0:T(8,128)(2,1)S(1)}, bf16[96,768]{1,0:T(8,128)(2,1)}, u32[]{:S(2)}, u32[]{:S(2)}) %collective-permute-start.21) | collective-permute-done | bytes 147488 | tf_op jit(solution)/shard_map/ppermute | solution.py:534
  92.5 4.5 collective-permute-done.26
  97.0 2.7 collective-permute-done.27
  99.8 2.2 collective-permute-start.29
  106.5 2.6 fusion
  109.2 4.0 fusion.2
  114.8 13.8 %collective-permute-done.28 = bf16[96,768]{1,0:T(8,128)(2,1)} collective-permute-done((bf16[96,768]{1,0:T(8,128)(2,1)}, bf16[96,768]{1,0:T(8,128)(2,1)}, u32[]{:S(2)}, u32[]{:S(2)}) %collective-permute-start.28) | collective-permute-done | bytes 147488 | tf_op jit(solution)/shard_map/ppermute | solution.py:534
  141.2 12.0 %collective-permute-done.34.refs_1_ = bf16[4,96,896]{2,1,0:T(8,128)(2,1)S(1)} collective-permute-done((bf16[4,96,896]{2,1,0:T(8,128)(2,1)S(1)}, bf16[4,96,896]{2,1,0:T(8,128)(2,1)S(1)}, u32[]{:S(2)}, u32[]{:S(2)}) %collective-permute-start.34) | collective-permute-done | bytes 688160 | tf_op jit(solution)/shard_map/ppermute | solution.py:534
  154.8 9.5 %collective-permute-done.35.refs_3_ = bf16[4,96,896]{2,1,0:T(8,128)(2,1)S(1)} collective-permute-done((bf16[4,96,896]{2,1,0:T(8,128)(2,1)}, bf16[4,96,896]{2,1,0:T(8,128)(2,1)S(1)}, u32[]{:S(2)}, u32[]{:S(2)}) %collective-permute-start.35) | collective-permute-done | bytes 688160 | tf_op jit(solution)/shard_map/ppermute | solution.py:534
  165.7 2.8 join.3
  168.5 9.0 %fusion.85.xbc.halo.prev = f32[1040,1920]{1,0:T(8,128)} fusion(bf16[1040,1536]{1,0:T(8,128)(2,1)S(1)} %copy-done.36, bf16[1536,1920]{1,0:T(8,128)(2,1)S(1)} %join.3), kind=kOutput, calls=%fused_computation.293 | convolution fusion | flops 6134169600 | bytes 17080320 | tf_op jit(solution)/shard_map/dot_general | solution.py:35
  182.6 13.4 %block_states.1 = (f32[1024,1536]{1,0:T(8,128)S(1)}, f32[1024,256]{1,0:T(8,128)S(1)}, f32[1024,256]{1,0:T(8,128)S(1)}, f32[1024,128]{1,0:T(8,128)S(1)}, f32[1024...) custom-call(f32[1040,1920]{1,0:T(8,128)} %fusion.85.xbc.halo.prev, ...), custom_call_target="tpu_custom_call" | custom-call | flops 402653184 | bytes 17432576 | tf_op jit(solution)/shard_map/block_states/pallas_call | solution.py:146
  196.1 2.6 copy-done.1
  202.5 20.5 %inner_part.1.yin = f32[1024,1536]{1,0:T(8,128)S(1)} custom-call(f32[1024,256]{1,0:T(8,128)S(1)} %get-tuple-element.400.s, f32[1024,128]{1,0:T(8,128)S(1)} %get-tuple-element.401.ld, f32[4,32,256]{2,1,0:T(8,128)S(1)} %get-tuple-element.402.ldt, f32[1024,128]{1,0:T(8,128)S(1)} %get-tuple-element.403.dt, f32[1024,1536]{1,0:T(8,128)} %copy-done.1, ...), custom_call_target="tpu_custom_call" | custom-call | flops 3221225472 | bytes 16777216 | tf_op jit(solution)/shard_map/inner_part/pallas_call | solution.py:210
  224.5 3.6 collective-permute-start.42
  229.7 6.9 %fusion.15.z = f32[1024,1536]{1,0:T(8,128)} fusion(bf16[1536,1536]{1,0:T(8,128)(2,1)S(1)} %join.4, bf16[1040,1536]{1,0:T(8,128)(2,1)S(1)} %copy-done.36), kind=kOutput, calls=%fused_computation.34 | convolution fusion | flops 4831838208 | bytes 14155776 | tf_op jit(solution)/shard_map/dot_general | solution.py:35
  237.8 7.1 %gate_part.1 = (f32[1024,1536]{1,0:T(8,128)S(1)}, f32[1024,128]{1,0:T(8,128)S(1)}) custom-call(f32[1024,1536]{1,0:T(8,128)S(1)} %inner_part.1.yin, f32[1024,256]{1,0:T(8,128)S(1)} %get-tuple-element.406.bc, bf16[4,128,1536]{2,1,0:T(8,128)(2,1)S(1)} %bitcast.234, f32[1024,128]{1,0:T(8,128)S(1)} %get-tuple-element.401.ld, ...), custom_call_target="tpu_custom_call", output_to_operand_aliasing={{0}: (0, {})} | custom-call | flops 402653184 | bytes 18874368 | tf_op jit(solution)/shard_map/gate_part/pallas_call | solution.py:249
  246.5 3.2 join.5
  250.4 4.6 fusion.67
  255.0 5.5 convolution_convert_fusion.1.refs_0_
  262.6 2.5 collective-permute-start.49
  265.0 7.0 %fusion.86.gfin = f32[1024,1536]{1,0:T(8,128)} fusion(bf16[1024,1536]{1,0:T(8,128)(2,1)S(1)} %bitcast.256, bf16[1536,1536]{1,0:T(8,128)(2,1)S(1)} %join.5), kind=kOutput, calls=%fused_computation.294 | convolution fusion | flops 4831838208 | bytes 14155776 | tf_op jit(solution)/shard_map/dot_general | solution.py:39
  272.0 5.2 multiply_reduce_fusion
  283.8 15.7 %gate_back.1 = (bf16[1024,1536]{1,0:T(8,128)(2,1)S(1)}, bf16[1024,1536]{1,0:T(8,128)(2,1)S(1)}, f32[1024,128]{1,0:T(8,128)S(1)}, f32[4,128,1536]{2,1,0:T(8,128)}...) custom-call(f32[1024,1536]{1,0:T(8,128)} %copy-done, f32[1024,1536]{1,0:T(8,128)} %fusion.15.z, ...), custom_call_target="tpu_custom_call" | custom-call | flops 1610612736 | bytes 37748736 | tf_op jit(solution)/shard_map/gate_back/pallas_call | solution.py:314
  299.5 4.6 add_convert_fusion.3
  304.1 5.4 convolution_convert_fusion.refs_0_
  315.1 2.7 collective-permute-start.57
  319.6 3.5 collective-permute-start.58
  327.0 25.5 %inner_back.1 = (f32[1024,1536]{1,0:T(8,128)S(1)}, f32[1024,128]{1,0:T(8,128)S(1)}, f32[1024,256]{1,0:T(8,128)S(1)}) custom-call(f32[1024,256]{1,0:T(8,128)S(1)} %get-tuple-element.400.s, f32[1024,256]{1,0:T(8,128)S(1)} %get-tuple-element.406.bc, f32[1024,128]{1,0:T(8,128)S(1)} %get-tuple-element.401.ld, f32[4,32,256]{2,1,0:T(8,128)S(1)} %get-tuple-element.402.ldt, ...), custom_call_target="tpu_custom_call" | custom-call | flops 6442450944 | bytes 16777216 | tf_op jit(solution)/shard_map/inner_back/pallas_call | solution.py:377
  357.4 4.9 collective-permute-done.60
  362.3 5.8 collective-permute-done.62
  378.9 34.1 %conv_back.1 = (bf16[1040,1920]{1,0:T(8,128)(2,1)}, f32[8,1792]{1,0:T(8,128)}, f32[8,128]{1,0:T(8,128)}) custom-call(f32[1040,1920]{1,0:T(8,128)} %fusion.85.xbc.halo.prev, f32[1040,1920]{1,0:T(8,128)} %fusion.85.xbc.halo.prev, f32[1024,1536]{1,0:T(8,128)} %copy-done.1, f32[1024,1536]{1,0:T(8,128)} %copy-done.5, f32[1024,128]{1,0:T(8,128)} %copy-done.20, ...), custom_call_target="tpu_custom_call" | custom-call | flops 1207959552 | bytes 28311552 | tf_op jit(solution)/shard_map/conv_back/pallas_call | solution.py:496
  416.6 2.4 collective-permute-start.71
  426.5 8.8 %convolution_convert_fusion.2.refs_0_ = bf16[1536,1920]{1,0:T(8,128)(2,1)S(1)} fusion(bf16[1040,1536]{1,0:T(8,128)(2,1)S(1)} %copy-done.38, bf16[1040,1920]{1,0:T(8,128)(2,1)S(1)} %copy-done.76), kind=kOutput, calls=%fused_computation.4 | convolution fusion | flops 6137118720 | bytes 13086720 | tf_op jit(solution)/shard_map/dot_general | solution.py:43
  438.6 7.2 %collective-permute-done.75 = bf16[96,768]{1,0:T(8,128)(2,1)S(1)} collective-permute-done((bf16[96,768]{1,0:T(8,128)(2,1)S(1)}, bf16[96,768]{1,0:T(8,128)(2,1)S(1)}, u32[]{:S(2)}, u32[]{:S(2)}) %collective-permute-start.75) | collective-permute-done | bytes 147488 | tf_op jit(solution)/shard_map/ppermute | solution.py:534
  448.4 8.8 %fusion.87 = f32[1040,1536]{1,0:T(8,128)} fusion(bf16[1040,1920]{1,0:T(8,128)(2,1)S(1)} %copy-done.76, bf16[1536,1920]{1,0:T(8,128)(2,1)S(1)} %bitcast.238), kind=kOutput, calls=%fused_computation.295 | convolution fusion | flops 6134169600 | bytes 16281600 | tf_op jit(solution)/shard_map/dot_general | solution.py:39
  457.3 7.2 %slice_add_fusion = f32[1024,1536]{1,0:T(8,128)S(1)} fusion(f32[1040,1536]{1,0:T(8,128)} %fusion.87, bf16[1024,1536]{1,0:T(8,128)(2,1)S(1)} %copy-done.24, bf16[1536,1536]{1,0:T(8,128)(2,1)S(1)} %bitcast.242), kind=kOutput, calls=%fused_computation.8 | convolution fusion | flops 4833411072 | bytes 20447232 | tf_op jit(solution)/shard_map/dot_general | solution.py:39
  467.6 4.3 collective-permute-done.80
  472.1 2.4 collective-permute-start.81
  481.3 5.0 fusion.88
  489.6 2.1 collective-permute-start.86
  495.1 2.8 fusion.10
  498.7 20.6 %collective-permute-done.85 = bf16[2,96,1024]{2,1,0:T(8,128)(2,1)} collective-permute-done((bf16[2,96,1024]{2,1,0:T(8,128)(2,1)}, bf16[2,96,1024]{2,1,0:T(8,128)(2,1)}, u32[]{:S(2)}, u32[]{:S(2)}) %collective-permute-start.85) | collective-permute-done | bytes 393248 | tf_op jit(solution)/shard_map/ppermute | solution.py:534
  527.6 2.2 collective-permute-start.93
  529.8 3.2 fusion.13
  533.1 3.3 collective-permute-done.93
  537.3 2.8 collective-permute-start.98
  541.6 3.0 collective-permute-start.95
  544.6 22.1 %collective-permute-done.96 = f32[16,1792]{1,0:T(8,128)S(1)} collective-permute-done((f32[16,1792]{1,0:T(8,128)S(1)}, f32[16,1792]{1,0:T(8,128)S(1)}, u32[]{:S(2)}, u32[]{:S(2)}) %collective-permute-start.96) | collective-permute-done | bytes 114720 | tf_op jit(solution)/shard_map/ppermute | solution.py:696
  568.9 3.5 collective-permute-done.101
  574.0 3.3 collective-permute-done.102
  (570 shorter events, 166.1 us)
Async XLA Ops:
  7.3 16.5 %collective-permute-start = (bf16[48,3456]{1,0:T(8,128)(2,1)}, bf16[48,3456]{1,0:T(8,128)(2,1)}, u32[]{:S(2)}, u32[]{:S(2)}) collective-permute-start(bf16[48,3456]{1,0:T(8,128)(2,1)} %get-tuple-element.634), channel_id=1, source_target_pairs={{0,1},{1,0},{2,3},{3,2},{4,5},{5,4},{6,7},{7,6},{8,9},{9,8},{10,11... | collective-permute-start | bytes 995336 | tf_op jit(solution)/shard_map/ppermute | solution.py:696
  15.2 28.2 %collective-permute-start.9 = (bf16[2,256,1536]{2,1,0:T(8,128)(2,1)S(1)}, bf16[2,256,1536]{2,1,0:T(8,128)(2,1)}, u32[]{:S(2)}, u32[]{:S(2)}) collective-permute-start(bf16[2,256,1536]{2,1,0:T(8,128)(2,1)S(1)} %bitcast.245), channel_id=1, source_target_pairs={{0,1},{1,0},{2,3},{3,2},{4,5},{5,4},{6,7},{7,6},{8,9},{9,8},{10,11... | collective-permute-start | bytes 4718600 | tf_op jit(solution)/shard_map/ppermute | solution.py:696
  15.3 28.2 %collective-permute-start.10 = (bf16[2,256,1536]{2,1,0:T(8,128)(2,1)S(1)}, bf16[2,256,1536]{2,1,0:T(8,128)(2,1)}, u32[]{:S(2)}, u32[]{:S(2)}) collective-permute-start(bf16[2,256,1536]{2,1,0:T(8,128)(2,1)S(1)} %bitcast.251), channel_id=1, source_target_pairs={{0,1},{1,0},{2,3},{3,2},{4,5},{5,4},{6,7},{7,6},{8,9},{9,8},{10,11... | collective-permute-start | bytes 4718600 | tf_op jit(solution)/shard_map/ppermute | solution.py:696
  43.4 21.8 %collective-permute-start.11 = (bf16[96,896]{1,0:T(8,128)(2,1)S(1)}, bf16[96,896]{1,0:T(8,128)(2,1)}, u32[]{:S(2)}, u32[]{:S(2)}) collective-permute-start(bf16[96,896]{1,0:T(8,128)(2,1)S(1)} %collective-permute-done.3), channel_id=1, source_target_pairs={{0,8},{8,16},{16,24},{24,0},{1,9},{9,17},{17,25},{25,1},{2,10},{10... | collective-permute-start | bytes 516104 | tf_op jit(solution)/shard_map/ppermute | solution.py:534
  43.5 25.5 %collective-permute-start.14 = (bf16[2,96,1024]{2,1,0:T(8,128)(2,1)S(1)}, bf16[2,96,1024]{2,1,0:T(8,128)(2,1)S(1)}, u32[]{:S(2)}, u32[]{:S(2)}) collective-permute-start(bf16[2,96,1024]{2,1,0:T(8,128)(2,1)S(1)} %pad_maximum_fusion.8), channel_id=1, source_target_pairs={{0,4},{4,0},{1,5},{5,1},{2,6},{6,2},{3,7},{7,3},{8,12},{12,8},{9,1... | collective-permute-start | bytes 1179656 | tf_op jit(solution)/shard_map/ppermute | solution.py:534
  44.0 17.0 %collective-permute-start.15 = (bf16[2,96,768]{2,1,0:T(8,128)(2,1)S(1)}, bf16[2,96,768]{2,1,0:T(8,128)(2,1)S(1)}, u32[]{:S(2)}, u32[]{:S(2)}) collective-permute-start(bf16[2,96,768]{2,1,0:T(8,128)(2,1)S(1)} %pad_maximum_fusion.12), channel_id=1, source_target_pairs={{0,4},{4,0},{1,5},{5,1},{2,6},{6,2},{3,7},{7,3},{8,12},{12,8},{9,1... | collective-permute-start | bytes 884744 | tf_op jit(solution)/shard_map/ppermute | solution.py:534
  69.0 17.3 %collective-permute-start.19 = (bf16[96,896]{1,0:T(8,128)(2,1)}, bf16[96,896]{1,0:T(8,128)(2,1)}, u32[]{:S(2)}, u32[]{:S(2)}) collective-permute-start(bf16[96,896]{1,0:T(8,128)(2,1)} %collective-permute-done.11), channel_id=1, source_target_pairs={{0,8},{8,16},{16,24},{24,0},{1,9},{9,17},{17,25},{25,1},{2,10},{10... | collective-permute-start | bytes 516104 | tf_op jit(solution)/shard_map/ppermute | solution.py:534
  69.0 17.3 %collective-permute-start.20 = (bf16[96,1024]{1,0:T(8,128)(2,1)}, bf16[96,1024]{1,0:T(8,128)(2,1)}, u32[]{:S(2)}, u32[]{:S(2)}) collective-permute-start(bf16[96,1024]{1,0:T(8,128)(2,1)} %collective-permute-done.13), channel_id=1, source_target_pairs={{0,8},{8,16},{16,24},{24,0},{1,9},{9,17},{17,25},{25,1},{2,10},{10... | collective-permute-start | bytes 589832 | tf_op jit(solution)/shard_map/ppermute | solution.py:534
  91.2 63.7 %collective-permute-start.36 = (bf16[4,96,1024]{2,1,0:T(8,128)(2,1)S(1)}, bf16[4,96,1024]{2,1,0:T(8,128)(2,1)}, u32[]{:S(2)}, u32[]{:S(2)}) collective-permute-start(bf16[4,96,1024]{2,1,0:T(8,128)(2,1)S(1)} %constant_dynamic-update-slice_fusion.2.refs_4_), channel_id=1, source_target_pairs={{0,2},{2,0},{1,3},{3,1},{4,6},{6,4},{5,7},{7,5},{8,10},{10,8},{9,1... | collective-permute-start | bytes 2359304 | tf_op jit(solution)/shard_map/ppermute | solution.py:534
  97.0 39.4 %collective-permute-start.30 = (bf16[4,96,768]{2,1,0:T(8,128)(2,1)S(1)}, bf16[4,96,768]{2,1,0:T(8,128)(2,1)}, u32[]{:S(2)}, u32[]{:S(2)}) collective-permute-start(bf16[4,96,768]{2,1,0:T(8,128)(2,1)S(1)} %pad_maximum_fusion.4.refs_0_), channel_id=1, source_target_pairs={{0,8},{8,16},{16,24},{24,0},{1,9},{9,17},{17,25},{25,1},{2,10},{10... | collective-permute-start | bytes 1769480 | tf_op jit(solution)/shard_map/ppermute | solution.py:534
  99.7 37.9 %collective-permute-start.31 = (bf16[4,96,768]{2,1,0:T(8,128)(2,1)S(1)}, bf16[4,96,768]{2,1,0:T(8,128)(2,1)}, u32[]{:S(2)}, u32[]{:S(2)}) collective-permute-start(bf16[4,96,768]{2,1,0:T(8,128)(2,1)S(1)} %pad_maximum_fusion.5.refs_4_), channel_id=1, source_target_pairs={{0,8},{8,16},{16,24},{24,0},{1,9},{9,17},{17,25},{25,1},{2,10},{10... | collective-permute-start | bytes 1769480 | tf_op jit(solution)/shard_map/ppermute | solution.py:534
  99.7 28.9 %collective-permute-start.28 = (bf16[96,768]{1,0:T(8,128)(2,1)}, bf16[96,768]{1,0:T(8,128)(2,1)}, u32[]{:S(2)}, u32[]{:S(2)}) collective-permute-start(bf16[96,768]{1,0:T(8,128)(2,1)} %collective-permute-done.26), channel_id=1, source_target_pairs={{0,8},{8,16},{16,24},{24,0},{1,9},{9,17},{17,25},{25,1},{2,10},{10... | collective-permute-start | bytes 442376 | tf_op jit(solution)/shard_map/ppermute | solution.py:534
  99.8 35.0 %collective-permute-start.29 = (bf16[96,768]{1,0:T(8,128)(2,1)}, bf16[96,768]{1,0:T(8,128)(2,1)}, u32[]{:S(2)}, u32[]{:S(2)}) collective-permute-start(bf16[96,768]{1,0:T(8,128)(2,1)} %collective-permute-done.27), channel_id=1, source_target_pairs={{0,8},{8,16},{16,24},{24,0},{1,9},{9,17},{17,25},{25,1},{2,10},{10... | collective-permute-start | bytes 442376 | tf_op jit(solution)/shard_map/ppermute | solution.py:534
  128.6 35.9 %collective-permute-start.37 = (bf16[4,96,1024]{2,1,0:T(8,128)(2,1)S(1)}, bf16[4,96,1024]{2,1,0:T(8,128)(2,1)}, u32[]{:S(2)}, u32[]{:S(2)}) collective-permute-start(bf16[4,96,1024]{2,1,0:T(8,128)(2,1)S(1)} %constant_dynamic-update-slice_fusion.6.refs_6_), channel_id=1, source_target_pairs={{0,2},{2,0},{1,3},{3,1},{4,6},{6,4},{5,7},{7,5},{8,10},{10,8},{9,1... | collective-permute-start | bytes 2359304 | tf_op jit(solution)/shard_map/ppermute | solution.py:534
  134.8 18.4 %collective-permute-start.34 = (bf16[4,96,896]{2,1,0:T(8,128)(2,1)S(1)}, bf16[4,96,896]{2,1,0:T(8,128)(2,1)S(1)}, u32[]{:S(2)}, u32[]{:S(2)}) collective-permute-start(bf16[4,96,896]{2,1,0:T(8,128)(2,1)S(1)} %constant_dynamic-update-slice_fusion.refs_0_), channel_id=1, source_target_pairs={{0,4},{4,0},{1,5},{5,1},{2,6},{6,2},{3,7},{7,3},{8,12},{12,8},{9,1... | collective-permute-start | bytes 2064392 | tf_op jit(solution)/shard_map/ppermute | solution.py:534
  136.5 27.9 %collective-permute-start.35 = (bf16[4,96,896]{2,1,0:T(8,128)(2,1)}, bf16[4,96,896]{2,1,0:T(8,128)(2,1)S(1)}, u32[]{:S(2)}, u32[]{:S(2)}) collective-permute-start(bf16[4,96,896]{2,1,0:T(8,128)(2,1)} %copy-done.15), channel_id=1, source_target_pairs={{0,4},{4,0},{1,5},{5,1},{2,6},{6,2},{3,7},{7,3},{8,12},{12,8},{9,1... | collective-permute-start | bytes 2064392 | tf_op jit(solution)/shard_map/ppermute | solution.py:534
  139.3 38.2 %collective-permute-start.32 = (bf16[2,96,768]{2,1,0:T(8,128)(2,1)S(1)}, bf16[2,96,768]{2,1,0:T(8,128)(2,1)S(1)}, u32[]{:S(2)}, u32[]{:S(2)}) collective-permute-start(bf16[2,96,768]{2,1,0:T(8,128)(2,1)S(1)} %pad_maximum_fusion.14), channel_id=1, source_target_pairs={{0,2},{2,0},{1,3},{3,1},{4,6},{6,4},{5,7},{7,5},{8,10},{10,8},{9,1... | collective-permute-start | bytes 884744 | tf_op jit(solution)/shard_map/ppermute | solution.py:534
  153.2 24.3 %collective-permute-start.33 = (bf16[2,96,768]{2,1,0:T(8,128)(2,1)S(1)}, bf16[2,96,768]{2,1,0:T(8,128)(2,1)S(1)}, u32[]{:S(2)}, u32[]{:S(2)}) collective-permute-start(bf16[2,96,768]{2,1,0:T(8,128)(2,1)S(1)} %pad_maximum_fusion.15), channel_id=1, source_target_pairs={{0,4},{4,0},{1,5},{5,1},{2,6},{6,2},{3,7},{7,3},{8,12},{12,8},{9,1... | collective-permute-start | bytes 884744 | tf_op jit(solution)/shard_map/ppermute | solution.py:534
  154.8 43.9 %collective-permute-start.40 = (bf16[4,96,768]{2,1,0:T(8,128)(2,1)}, bf16[4,96,768]{2,1,0:T(8,128)(2,1)S(1)}, u32[]{:S(2)}, u32[]{:S(2)}) collective-permute-start(bf16[4,96,768]{2,1,0:T(8,128)(2,1)} %collective-permute-done.30.refs_1_), channel_id=1, source_target_pairs={{0,8},{8,16},{16,24},{24,0},{1,9},{9,17},{17,25},{25,1},{2,10},{10... | collective-permute-start | bytes 1769480 | tf_op jit(solution)/shard_map/ppermute | solution.py:534
  164.4 35.6 %collective-permute-start.41 = (bf16[4,96,768]{2,1,0:T(8,128)(2,1)}, bf16[4,96,768]{2,1,0:T(8,128)(2,1)S(1)}, u32[]{:S(2)}, u32[]{:S(2)}) collective-permute-start(bf16[4,96,768]{2,1,0:T(8,128)(2,1)} %collective-permute-done.31.refs_5_), channel_id=1, source_target_pairs={{0,8},{8,16},{16,24},{24,0},{1,9},{9,17},{17,25},{25,1},{2,10},{10... | collective-permute-start | bytes 1769480 | tf_op jit(solution)/shard_map/ppermute | solution.py:534
  178.5 21.5 %collective-permute-start.38 = (bf16[2,96,768]{2,1,0:T(8,128)(2,1)S(1)}, bf16[2,96,768]{2,1,0:T(8,128)(2,1)S(1)}, u32[]{:S(2)}, u32[]{:S(2)}) collective-permute-start(bf16[2,96,768]{2,1,0:T(8,128)(2,1)S(1)} %pad_maximum_fusion.16), channel_id=1, source_target_pairs={{0,2},{2,0},{1,3},{3,1},{4,6},{6,4},{5,7},{7,5},{8,10},{10,8},{9,1... | collective-permute-start | bytes 884744 | tf_op jit(solution)/shard_map/ppermute | solution.py:534
  180.4 19.7 %collective-permute-start.39 = (bf16[2,96,768]{2,1,0:T(8,128)(2,1)S(1)}, bf16[2,96,768]{2,1,0:T(8,128)(2,1)S(1)}, u32[]{:S(2)}, u32[]{:S(2)}) collective-permute-start(bf16[2,96,768]{2,1,0:T(8,128)(2,1)S(1)} %pad_maximum_fusion.17), channel_id=1, source_target_pairs={{0,4},{4,0},{1,5},{5,1},{2,6},{6,2},{3,7},{7,3},{8,12},{12,8},{9,1... | collective-permute-start | bytes 884744 | tf_op jit(solution)/shard_map/ppermute | solution.py:534
  181.8 41.2 %collective-permute-start.43 = (bf16[4,96,768]{2,1,0:T(8,128)(2,1)S(1)}, bf16[4,96,768]{2,1,0:T(8,128)(2,1)S(1)}, u32[]{:S(2)}, u32[]{:S(2)}) collective-permute-start(bf16[4,96,768]{2,1,0:T(8,128)(2,1)S(1)} %constant_dynamic-update-slice_fusion.8.refs_0_), channel_id=1, source_target_pairs={{0,4},{4,0},{1,5},{5,1},{2,6},{6,2},{3,7},{7,3},{8,12},{12,8},{9,1... | collective-permute-start | bytes 1769480 | tf_op jit(solution)/shard_map/ppermute | solution.py:534
  198.7 25.8 %collective-permute-start.45 = (bf16[4,96,768]{2,1,0:T(8,128)(2,1)S(1)}, bf16[4,96,768]{2,1,0:T(8,128)(2,1)S(1)}, u32[]{:S(2)}, u32[]{:S(2)}) collective-permute-start(bf16[4,96,768]{2,1,0:T(8,128)(2,1)S(1)} %constant_dynamic-update-slice_fusion.10.refs_4_), channel_id=1, source_target_pairs={{0,2},{2,0},{1,3},{3,1},{4,6},{6,4},{5,7},{7,5},{8,10},{10,8},{9,1... | collective-permute-start | bytes 1769480 | tf_op jit(solution)/shard_map/ppermute | solution.py:534
  200.1 28.0 %collective-permute-start.44 = (bf16[4,96,768]{2,1,0:T(8,128)(2,1)S(1)}, bf16[4,96,768]{2,1,0:T(8,128)(2,1)S(1)}, u32[]{:S(2)}, u32[]{:S(2)}) collective-permute-start(bf16[4,96,768]{2,1,0:T(8,128)(2,1)S(1)} %constant_dynamic-update-slice_fusion.12.refs_2_), channel_id=1, source_target_pairs={{0,4},{4,0},{1,5},{5,1},{2,6},{6,2},{3,7},{7,3},{8,12},{12,8},{9,1... | collective-permute-start | bytes 1769480 | tf_op jit(solution)/shard_map/ppermute | solution.py:534
  201.8 26.4 %collective-permute-start.46 = (bf16[4,96,768]{2,1,0:T(8,128)(2,1)S(1)}, bf16[4,96,768]{2,1,0:T(8,128)(2,1)S(1)}, u32[]{:S(2)}, u32[]{:S(2)}) collective-permute-start(bf16[4,96,768]{2,1,0:T(8,128)(2,1)S(1)} %constant_dynamic-update-slice_fusion.14.refs_6_), channel_id=1, source_target_pairs={{0,2},{2,0},{1,3},{3,1},{4,6},{6,4},{5,7},{7,5},{8,10},{10,8},{9,1... | collective-permute-start | bytes 1769480 | tf_op jit(solution)/shard_map/ppermute | solution.py:534
  202.5 44.0 %collective-permute-start.50 = (bf16[4,96,768]{2,1,0:T(8,128)(2,1)S(1)}, bf16[4,96,768]{2,1,0:T(8,128)(2,1)S(1)}, u32[]{:S(2)}, u32[]{:S(2)}) collective-permute-start(bf16[4,96,768]{2,1,0:T(8,128)(2,1)S(1)} %collective-permute-done.40.refs_2_), channel_id=1, source_target_pairs={{0,8},{8,16},{16,24},{24,0},{1,9},{9,17},{17,25},{25,1},{2,10},{10... | collective-permute-start | bytes 1769480 | tf_op jit(solution)/shard_map/ppermute | solution.py:534
  223.0 23.4 %collective-permute-start.51 = (bf16[4,96,768]{2,1,0:T(8,128)(2,1)S(1)}, bf16[4,96,768]{2,1,0:T(8,128)(2,1)S(1)}, u32[]{:S(2)}, u32[]{:S(2)}) collective-permute-start(bf16[4,96,768]{2,1,0:T(8,128)(2,1)S(1)} %collective-permute-done.41.refs_6_), channel_id=1, source_target_pairs={{0,8},{8,16},{16,24},{24,0},{1,9},{9,17},{17,25},{25,1},{2,10},{10... | collective-permute-start | bytes 1769480 | tf_op jit(solution)/shard_map/ppermute | solution.py:534
  278.6 33.8 %collective-permute-start.52 = (bf16[2,96,768]{2,1,0:T(8,128)(2,1)}, bf16[2,96,768]{2,1,0:T(8,128)(2,1)S(1)}, u32[]{:S(2)}, u32[]{:S(2)}) collective-permute-start(bf16[2,96,768]{2,1,0:T(8,128)(2,1)} %get-tuple-element.658), channel_id=1, source_target_pairs={{0,2},{2,0},{1,3},{3,1},{4,6},{6,4},{5,7},{7,5},{8,10},{10,8},{9,1... | collective-permute-start | bytes 884744 | tf_op jit(solution)/shard_map/ppermute | solution.py:534
  280.4 32.1 %collective-permute-start.53 = (bf16[4,96,768]{2,1,0:T(8,128)(2,1)S(1)}, bf16[4,96,768]{2,1,0:T(8,128)(2,1)}, u32[]{:S(2)}, u32[]{:S(2)}) collective-permute-start(bf16[4,96,768]{2,1,0:T(8,128)(2,1)S(1)} %get-tuple-element.435), channel_id=1, source_target_pairs={{0,4},{4,0},{1,5},{5,1},{2,6},{6,2},{3,7},{7,3},{8,12},{12,8},{9,1... | collective-permute-start | bytes 1769480 | tf_op jit(solution)/shard_map/ppermute | solution.py:534
  282.9 29.6 %collective-permute-start.54 = (bf16[2,96,768]{2,1,0:T(8,128)(2,1)}, bf16[2,96,768]{2,1,0:T(8,128)(2,1)S(1)}, u32[]{:S(2)}, u32[]{:S(2)}) collective-permute-start(bf16[2,96,768]{2,1,0:T(8,128)(2,1)} %get-tuple-element.656), channel_id=1, source_target_pairs={{0,4},{4,0},{1,5},{5,1},{2,6},{6,2},{3,7},{7,3},{8,12},{12,8},{9,1... | collective-permute-start | bytes 884744 | tf_op jit(solution)/shard_map/ppermute | solution.py:534
  283.3 29.2 %collective-permute-start.55 = (bf16[4,96,768]{2,1,0:T(8,128)(2,1)S(1)}, bf16[4,96,768]{2,1,0:T(8,128)(2,1)S(1)}, u32[]{:S(2)}, u32[]{:S(2)}) collective-permute-start(bf16[4,96,768]{2,1,0:T(8,128)(2,1)S(1)} %get-tuple-element.439), channel_id=1, source_target_pairs={{0,2},{2,0},{1,3},{3,1},{4,6},{6,4},{5,7},{7,5},{8,10},{10,8},{9,1... | collective-permute-start | bytes 1769480 | tf_op jit(solution)/shard_map/ppermute | solution.py:534
  311.1 43.1 %collective-permute-start.63 = (bf16[2,128,1536]{2,1,0:T(8,128)(2,1)}, bf16[2,128,1536]{2,1,0:T(8,128)(2,1)S(1)}, u32[]{:S(2)}, u32[]{:S(2)}) collective-permute-start(bf16[2,128,1536]{2,1,0:T(8,128)(2,1)} %add_convert_fusion.3), channel_id=1, source_target_pairs={{2,0},{3,1},{6,4},{7,5},{10,8},{11,9},{14,12},{15,13},{18,16},{19,... | collective-permute-start | bytes 2359304 | tf_op jit(solution)/shard_map/ppermute | solution.py:925
  315.1 47.1 %collective-permute-start.57 = (bf16[2,96,768]{2,1,0:T(8,128)(2,1)}, bf16[2,96,768]{2,1,0:T(8,128)(2,1)}, u32[]{:S(2)}, u32[]{:S(2)}) collective-permute-start(bf16[2,96,768]{2,1,0:T(8,128)(2,1)} %get-tuple-element.654), channel_id=1, source_target_pairs={{0,2},{2,0},{1,3},{3,1},{4,6},{6,4},{5,7},{7,5},{8,10},{10,8},{9,1... | collective-permute-start | bytes 884744 | tf_op jit(solution)/shard_map/ppermute | solution.py:534
  319.6 34.9 %collective-permute-start.58 = (bf16[96,768]{1,0:T(8,128)(2,1)}, bf16[96,768]{1,0:T(8,128)(2,1)}, u32[]{:S(2)}, u32[]{:S(2)}) collective-permute-start(bf16[96,768]{1,0:T(8,128)(2,1)} %get-tuple-element.671), channel_id=1, source_target_pairs={{0,8},{8,16},{16,24},{24,0},{1,9},{9,17},{17,25},{25,1},{2,10},{10... | collective-permute-start | bytes 442376 | tf_op jit(solution)/shard_map/ppermute | solution.py:534
  324.2 38.1 %collective-permute-start.59 = (bf16[2,96,768]{2,1,0:T(8,128)(2,1)}, bf16[2,96,768]{2,1,0:T(8,128)(2,1)S(1)}, u32[]{:S(2)}, u32[]{:S(2)}) collective-permute-start(bf16[2,96,768]{2,1,0:T(8,128)(2,1)} %get-tuple-element.652), channel_id=1, source_target_pairs={{0,4},{4,0},{1,5},{5,1},{2,6},{6,2},{3,7},{7,3},{8,12},{12,8},{9,1... | collective-permute-start | bytes 884744 | tf_op jit(solution)/shard_map/ppermute | solution.py:534
  325.8 36.5 %collective-permute-start.61 = (bf16[4,96,768]{2,1,0:T(8,128)(2,1)S(1)}, bf16[4,96,768]{2,1,0:T(8,128)(2,1)S(1)}, u32[]{:S(2)}, u32[]{:S(2)}) collective-permute-start(bf16[4,96,768]{2,1,0:T(8,128)(2,1)S(1)} %get-tuple-element.465), channel_id=1, source_target_pairs={{0,4},{4,0},{1,5},{5,1},{2,6},{6,2},{3,7},{7,3},{8,12},{12,8},{9,1... | collective-permute-start | bytes 1769480 | tf_op jit(solution)/shard_map/ppermute | solution.py:534
  369.4 45.0 %collective-permute-start.65 = (bf16[96,768]{1,0:T(8,128)(2,1)S(1)}, bf16[96,768]{1,0:T(8,128)(2,1)}, u32[]{:S(2)}, u32[]{:S(2)}) collective-permute-start(bf16[96,768]{1,0:T(8,128)(2,1)S(1)} %add_convert_fusion.25), channel_id=1, source_target_pairs={{0,8},{8,16},{16,24},{24,0},{1,9},{9,17},{17,25},{25,1},{2,10},{10... | collective-permute-start | bytes 442376 | tf_op jit(solution)/shard_map/ppermute | solution.py:534
  370.4 44.0 %collective-permute-start.66 = (bf16[2,96,768]{2,1,0:T(8,128)(2,1)}, bf16[2,96,768]{2,1,0:T(8,128)(2,1)}, u32[]{:S(2)}, u32[]{:S(2)}) collective-permute-start(bf16[2,96,768]{2,1,0:T(8,128)(2,1)} %get-tuple-element.650), channel_id=1, source_target_pairs={{0,2},{2,0},{1,3},{3,1},{4,6},{6,4},{5,7},{7,5},{8,10},{10,8},{9,1... | collective-permute-start | bytes 884744 | tf_op jit(solution)/shard_map/ppermute | solution.py:534
  370.7 43.6 %collective-permute-start.67 = (bf16[4,96,768]{2,1,0:T(8,128)(2,1)S(1)}, bf16[4,96,768]{2,1,0:T(8,128)(2,1)}, u32[]{:S(2)}, u32[]{:S(2)}) collective-permute-start(bf16[4,96,768]{2,1,0:T(8,128)(2,1)S(1)} %get-tuple-element.486), channel_id=1, source_target_pairs={{0,4},{4,0},{1,5},{5,1},{2,6},{6,2},{3,7},{7,3},{8,12},{12,8},{9,1... | collective-permute-start | bytes 1769480 | tf_op jit(solution)/shard_map/ppermute | solution.py:534
  372.3 42.0 %collective-permute-start.69 = (bf16[4,96,768]{2,1,0:T(8,128)(2,1)S(1)}, bf16[4,96,768]{2,1,0:T(8,128)(2,1)}, u32[]{:S(2)}, u32[]{:S(2)}) collective-permute-start(bf16[4,96,768]{2,1,0:T(8,128)(2,1)S(1)} %get-tuple-element.490), channel_id=1, source_target_pairs={{0,2},{2,0},{1,3},{3,1},{4,6},{6,4},{5,7},{7,5},{8,10},{10,8},{9,1... | collective-permute-start | bytes 1769480 | tf_op jit(solution)/shard_map/ppermute | solution.py:534
  376.7 37.7 %collective-permute-start.68 = (bf16[2,96,768]{2,1,0:T(8,128)(2,1)}, bf16[2,96,768]{2,1,0:T(8,128)(2,1)}, u32[]{:S(2)}, u32[]{:S(2)}) collective-permute-start(bf16[2,96,768]{2,1,0:T(8,128)(2,1)} %get-tuple-element.648), channel_id=1, source_target_pairs={{0,4},{4,0},{1,5},{5,1},{2,6},{6,2},{3,7},{7,3},{8,12},{12,8},{9,1... | collective-permute-start | bytes 884744 | tf_op jit(solution)/shard_map/ppermute | solution.py:534
  415.5 21.8 %collective-permute-start.70 = (bf16[96,768]{1,0:T(8,128)(2,1)S(1)}, bf16[96,768]{1,0:T(8,128)(2,1)S(1)}, u32[]{:S(2)}, u32[]{:S(2)}) collective-permute-start(bf16[96,768]{1,0:T(8,128)(2,1)S(1)} %fusion.47), channel_id=1, source_target_pairs={{0,8},{8,16},{16,24},{24,0},{1,9},{9,17},{17,25},{25,1},{2,10},{10... | collective-permute-start | bytes 442376 | tf_op jit(solution)/shard_map/ppermute | solution.py:534
  416.6 22.0 %collective-permute-start.71 = (bf16[96,768]{1,0:T(8,128)(2,1)S(1)}, bf16[96,768]{1,0:T(8,128)(2,1)S(1)}, u32[]{:S(2)}, u32[]{:S(2)}) collective-permute-start(bf16[96,768]{1,0:T(8,128)(2,1)S(1)} %fusion.45), channel_id=1, source_target_pairs={{0,8},{8,16},{16,24},{24,0},{1,9},{9,17},{17,25},{25,1},{2,10},{10... | collective-permute-start | bytes 442376 | tf_op jit(solution)/shard_map/ppermute | solution.py:534
  420.4 25.4 %collective-permute-start.72 = (bf16[2,96,768]{2,1,0:T(8,128)(2,1)S(1)}, bf16[2,96,768]{2,1,0:T(8,128)(2,1)S(1)}, u32[]{:S(2)}, u32[]{:S(2)}) collective-permute-start(bf16[2,96,768]{2,1,0:T(8,128)(2,1)S(1)} %get-tuple-element.646), channel_id=1, source_target_pairs={{0,2},{2,0},{1,3},{3,1},{4,6},{6,4},{5,7},{7,5},{8,10},{10,8},{9,1... | collective-permute-start | bytes 884744 | tf_op jit(solution)/shard_map/ppermute | solution.py:534
  422.0 16.6 %collective-permute-start.73 = (bf16[96,768]{1,0:T(8,128)(2,1)S(1)}, bf16[96,768]{1,0:T(8,128)(2,1)S(1)}, u32[]{:S(2)}, u32[]{:S(2)}) collective-permute-start(bf16[96,768]{1,0:T(8,128)(2,1)S(1)} %get-tuple-element.667), channel_id=1, source_target_pairs={{0,8},{8,16},{16,24},{24,0},{1,9},{9,17},{17,25},{25,1},{2,10},{10... | collective-permute-start | bytes 442376 | tf_op jit(solution)/shard_map/ppermute | solution.py:534
  423.8 22.1 %collective-permute-start.74 = (bf16[2,96,768]{2,1,0:T(8,128)(2,1)S(1)}, bf16[2,96,768]{2,1,0:T(8,128)(2,1)S(1)}, u32[]{:S(2)}, u32[]{:S(2)}) collective-permute-start(bf16[2,96,768]{2,1,0:T(8,128)(2,1)S(1)} %get-tuple-element.644), channel_id=1, source_target_pairs={{0,4},{4,0},{1,5},{5,1},{2,6},{6,2},{3,7},{7,3},{8,12},{12,8},{9,1... | collective-permute-start | bytes 884744 | tf_op jit(solution)/shard_map/ppermute | solution.py:534
  445.9 26.1 %collective-permute-start.76 = (bf16[96,768]{1,0:T(8,128)(2,1)S(1)}, bf16[96,768]{1,0:T(8,128)(2,1)S(1)}, u32[]{:S(2)}, u32[]{:S(2)}) collective-permute-start(bf16[96,768]{1,0:T(8,128)(2,1)S(1)} %add_convert_fusion.24), channel_id=1, source_target_pairs={{0,8},{8,16},{16,24},{24,0},{1,9},{9,17},{17,25},{25,1},{2,10},{10... | collective-permute-start | bytes 442376 | tf_op jit(solution)/shard_map/ppermute | solution.py:534
  446.0 25.9 %collective-permute-start.77 = (bf16[96,768]{1,0:T(8,128)(2,1)S(1)}, bf16[96,768]{1,0:T(8,128)(2,1)S(1)}, u32[]{:S(2)}, u32[]{:S(2)}) collective-permute-start(bf16[96,768]{1,0:T(8,128)(2,1)S(1)} %add_convert_fusion.23), channel_id=1, source_target_pairs={{0,8},{8,16},{16,24},{24,0},{1,9},{9,17},{17,25},{25,1},{2,10},{10... | collective-permute-start | bytes 442376 | tf_op jit(solution)/shard_map/ppermute | solution.py:534
  446.2 25.7 %collective-permute-start.78 = (bf16[4,96,896]{2,1,0:T(8,128)(2,1)S(1)}, bf16[4,96,896]{2,1,0:T(8,128)(2,1)S(1)}, u32[]{:S(2)}, u32[]{:S(2)}) collective-permute-start(bf16[4,96,896]{2,1,0:T(8,128)(2,1)S(1)} %get-tuple-element.533), channel_id=1, source_target_pairs={{0,4},{4,0},{1,5},{5,1},{2,6},{6,2},{3,7},{7,3},{8,12},{12,8},{9,1... | collective-permute-start | bytes 2064392 | tf_op jit(solution)/shard_map/ppermute | solution.py:534
  447.1 24.8 %collective-permute-start.79 = (bf16[4,96,1024]{2,1,0:T(8,128)(2,1)S(1)}, bf16[4,96,1024]{2,1,0:T(8,128)(2,1)S(1)}, u32[]{:S(2)}, u32[]{:S(2)}) collective-permute-start(bf16[4,96,1024]{2,1,0:T(8,128)(2,1)S(1)} %get-tuple-element.537), channel_id=1, source_target_pairs={{0,2},{2,0},{1,3},{3,1},{4,6},{6,4},{5,7},{7,5},{8,10},{10,8},{9,1... | collective-permute-start | bytes 2359304 | tf_op jit(solution)/shard_map/ppermute | solution.py:534
  472.1 20.9 %collective-permute-start.81 = (bf16[96,768]{1,0:T(8,128)(2,1)S(1)}, bf16[96,768]{1,0:T(8,128)(2,1)S(1)}, u32[]{:S(2)}, u32[]{:S(2)}) collective-permute-start(bf16[96,768]{1,0:T(8,128)(2,1)S(1)} %fusion.43), channel_id=1, source_target_pairs={{0,8},{8,16},{16,24},{24,0},{1,9},{9,17},{17,25},{25,1},{2,10},{10... | collective-permute-start | bytes 442376 | tf_op jit(solution)/shard_map/ppermute | solution.py:534
  474.5 20.1 %collective-permute-start.82 = (bf16[96,768]{1,0:T(8,128)(2,1)S(1)}, bf16[96,768]{1,0:T(8,128)(2,1)S(1)}, u32[]{:S(2)}, u32[]{:S(2)}) collective-permute-start(bf16[96,768]{1,0:T(8,128)(2,1)S(1)} %fusion.41), channel_id=1, source_target_pairs={{0,8},{8,16},{16,24},{24,0},{1,9},{9,17},{17,25},{25,1},{2,10},{10... | collective-permute-start | bytes 442376 | tf_op jit(solution)/shard_map/ppermute | solution.py:534
  477.5 21.2 %collective-permute-start.83 = (bf16[2,96,896]{2,1,0:T(8,128)(2,1)}, bf16[2,96,896]{2,1,0:T(8,128)(2,1)}, u32[]{:S(2)}, u32[]{:S(2)}) collective-permute-start(bf16[2,96,896]{2,1,0:T(8,128)(2,1)} %get-tuple-element.629), channel_id=1, source_target_pairs={{0,2},{2,0},{1,3},{3,1},{4,6},{6,4},{5,7},{7,5},{8,10},{10,8},{9,1... | collective-permute-start | bytes 1032200 | tf_op jit(solution)/shard_map/ppermute | solution.py:534
  487.6 31.7 %collective-permute-start.88 = (bf16[2,256,1536]{2,1,0:T(8,128)(2,1)}, bf16[2,256,1536]{2,1,0:T(8,128)(2,1)}, u32[]{:S(2)}, u32[]{:S(2)}) collective-permute-start(bf16[2,256,1536]{2,1,0:T(8,128)(2,1)} %fusion.18), channel_id=1, source_target_pairs={{0,1},{1,0},{2,3},{3,2},{4,5},{5,4},{6,7},{7,6},{8,9},{9,8},{10,11... | collective-permute-start | bytes 4718600 | tf_op jit(solution)/shard_map/ppermute | solution.py:696
  489.6 29.7 %collective-permute-start.86 = (bf16[4,96,1024]{2,1,0:T(8,128)(2,1)S(1)}, bf16[4,96,1024]{2,1,0:T(8,128)(2,1)}, u32[]{:S(2)}, u32[]{:S(2)}) collective-permute-start(bf16[4,96,1024]{2,1,0:T(8,128)(2,1)S(1)} %get-tuple-element.558), channel_id=1, source_target_pairs={{0,2},{2,0},{1,3},{3,1},{4,6},{6,4},{5,7},{7,5},{8,10},{10,8},{9,1... | collective-permute-start | bytes 2359304 | tf_op jit(solution)/shard_map/ppermute | solution.py:534
  493.0 26.4 %collective-permute-start.84 = (bf16[4,96,896]{2,1,0:T(8,128)(2,1)}, bf16[4,96,896]{2,1,0:T(8,128)(2,1)}, u32[]{:S(2)}, u32[]{:S(2)}) collective-permute-start(bf16[4,96,896]{2,1,0:T(8,128)(2,1)} %get-tuple-element.554), channel_id=1, source_target_pairs={{0,4},{4,0},{1,5},{5,1},{2,6},{6,2},{3,7},{7,3},{8,12},{12,8},{9,1... | collective-permute-start | bytes 2064392 | tf_op jit(solution)/shard_map/ppermute | solution.py:534
  494.6 24.7 %collective-permute-start.85 = (bf16[2,96,1024]{2,1,0:T(8,128)(2,1)}, bf16[2,96,1024]{2,1,0:T(8,128)(2,1)}, u32[]{:S(2)}, u32[]{:S(2)}) collective-permute-start(bf16[2,96,1024]{2,1,0:T(8,128)(2,1)} %get-tuple-element.619), channel_id=1, source_target_pairs={{0,4},{4,0},{1,5},{5,1},{2,6},{6,2},{3,7},{7,3},{8,12},{12,8},{9,1... | collective-permute-start | bytes 1179656 | tf_op jit(solution)/shard_map/ppermute | solution.py:534
  520.7 15.8 %collective-permute-start.89 = (bf16[2,96,896]{2,1,0:T(8,128)(2,1)S(1)}, bf16[2,96,896]{2,1,0:T(8,128)(2,1)S(1)}, u32[]{:S(2)}, u32[]{:S(2)}) collective-permute-start(bf16[2,96,896]{2,1,0:T(8,128)(2,1)S(1)} %get-tuple-element.627), channel_id=1, source_target_pairs={{0,2},{2,0},{1,3},{3,1},{4,6},{6,4},{5,7},{7,5},{8,10},{10,8},{9,1... | collective-permute-start | bytes 1032200 | tf_op jit(solution)/shard_map/ppermute | solution.py:534
  536.5 30.4 %collective-permute-start.97 = (f32[96,1536]{1,0:T(8,128)S(1)}, f32[96,1536]{1,0:T(8,128)S(1)}, u32[]{:S(2)}, u32[]{:S(2)}) collective-permute-start(f32[96,1536]{1,0:T(8,128)S(1)} %copy-done.44), channel_id=1, source_target_pairs={{0,0},{1,16},{16,1},{17,17},{2,2},{3,18},{18,3},{19,19},{4,4},{5,2... | collective-permute-start | bytes 1769480 | tf_op jit(solution)/shard_map/ppermute | solution.py:1036
  537.3 29.5 %collective-permute-start.98 = (f32[48,1536]{1,0:T(8,128)S(1)}, f32[48,1536]{1,0:T(8,128)S(1)}, u32[]{:S(2)}, u32[]{:S(2)}) collective-permute-start(f32[48,1536]{1,0:T(8,128)S(1)} %get-tuple-element.643), channel_id=1, source_target_pairs={{0,1},{1,0},{2,3},{3,2},{4,5},{5,4},{6,7},{7,6},{8,9},{9,8},{10,11... | collective-permute-start | bytes 884744 | tf_op jit(solution)/shard_map/ppermute | solution.py:696
  540.1 26.8 %collective-permute-start.94 = (bf16[96,896]{1,0:T(8,128)(2,1)S(1)}, bf16[96,896]{1,0:T(8,128)(2,1)S(1)}, u32[]{:S(2)}, u32[]{:S(2)}) collective-permute-start(bf16[96,896]{1,0:T(8,128)(2,1)S(1)} %add_convert_fusion.22), channel_id=1, source_target_pairs={{0,8},{8,16},{16,24},{24,0},{1,9},{9,17},{17,25},{25,1},{2,10},{10... | collective-permute-start | bytes 516104 | tf_op jit(solution)/shard_map/ppermute | solution.py:534
  541.5 25.2 %collective-permute-start.96 = (f32[16,1792]{1,0:T(8,128)S(1)}, f32[16,1792]{1,0:T(8,128)S(1)}, u32[]{:S(2)}, u32[]{:S(2)}) collective-permute-start(f32[16,1792]{1,0:T(8,128)S(1)} %add.385), channel_id=1, source_target_pairs={{0,16},{16,0},{1,17},{17,1},{2,18},{18,2},{3,19},{19,3},{4,20},{20... | collective-permute-start | bytes 344072 | tf_op jit(solution)/shard_map/ppermute | solution.py:696
  541.6 25.3 %collective-permute-start.95 = (bf16[96,1024]{1,0:T(8,128)(2,1)S(1)}, bf16[96,1024]{1,0:T(8,128)(2,1)S(1)}, u32[]{:S(2)}, u32[]{:S(2)}) collective-permute-start(bf16[96,1024]{1,0:T(8,128)(2,1)S(1)} %add_convert_fusion.21), channel_id=1, source_target_pairs={{0,8},{8,16},{16,24},{24,0},{1,9},{9,17},{17,25},{25,1},{2,10},{10... | collective-permute-start | bytes 589832 | tf_op jit(solution)/shard_map/ppermute | solution.py:534
  (126 other events, 1740.8 us)

commit v2 on v1

--- a/solution.py
+++ b/solution.py
@@ -23,6 +23,8 @@
 XP = XC + 128
 EPS = 1e-05
 NEG = -1e30
+LOG2E = 1.4426950408889634
+HT = T // 2
 f32 = jnp.float32
 bf16 = jnp.bfloat16
 HIGH = lax.Precision.HIGHEST
@@ -94,6 +96,41 @@
 
 def cost(flops, nbytes, trans=0):
     return pl.CostEstimate(flops=int(flops), bytes_accessed=int(nbytes), transcendentals=int(trans))
+
+
+def norm_kernel(blocks, hid, rim, gain, out):
+    j = pl.program_id(0)
+
+    def scaled(v):
+        v = v.astype(f32)
+        return (v * lax.rsqrt(jnp.mean(v * v, axis=-1, keepdims=True) + EPS) * gain[0:1]).astype(bf16)
+
+    @pl.when(j < blocks)
+    def _():
+        out[...] = scaled(hid[...])
+
+    @pl.when(j == blocks)
+    def _():
+        out[: rim.shape[0]] = scaled(rim[...])
+
+
+def pre_norm(hid, rim, gain):
+    rows, extra = hid.shape[0], rim.shape[0]
+    blocks = rows // T
+    return pl.pallas_call(
+        functools.partial(norm_kernel, blocks),
+        name="pre_norm",
+        grid=(blocks + 1,),
+        in_specs=[
+            pl.BlockSpec((T, D), lambda j: (jnp.minimum(j, blocks - 1), 0)),
+            pl.BlockSpec((extra, D), lambda j: (0, 0)),
+            pl.BlockSpec((1, D), lambda j: (0, 0)),
+        ],
+        out_specs=pl.BlockSpec((T, D), lambda j: (j, 0)),
+        out_shape=jax.ShapeDtypeStruct((rows + extra, D), bf16),
+        compiler_params=params(),
+        cost_estimate=cost(6 * rows * D, 4 * rows * D),
+    )(hid, rim, gain)
 
 
 def states_kernel(xbc, halo, cw, hp, x, bc, s, dt, ld, ldt, st0, comb, dec, pad, tail, carry, xw):
@@ -188,25 +225,34 @@
 
 def inner_kernel(s, ld, ldt, dt, x, skip, y):
     g = pl.program_id(1)
-    causal = iota((T, T), 0) >= iota((T, T), 1)
+    shift = lax.rem(128 - 8 * g, 128)
+    logd = pltpu.roll(ld[...], shift, 1) * LOG2E
+    step = pltpu.roll(dt[...], shift, 1)
+    upper = iota((HT, HT), 0) >= iota((HT, HT), 1)
+    lower = iota((HT, T), 0) + HT >= iota((HT, T), 1)
     head = iota((T, 256), 1) // PS
-    shift = lax.rem(128 - 4 * g, 128)
-    logd = pltpu.roll(ld[...], shift, 1)
-    step = pltpu.roll(dt[...], shift, 1)
-    tile = x[...]
-    xdt = tile * spread(step, 0, 4)
-    scores = s[...]
-    total = skip[0:1, :] * tile
-    for i in range(4):
-        gap = logd[:, i : i + 1] - ldt[0, pl.ds(4 * g + i, 1), :]
-        mixing = (jnp.exp(jnp.where(causal, gap, NEG)) * scores).astype(bf16)
-        total = total + nn(mixing, jnp.where(head == i, xdt, 0.0).astype(bf16))
-    y[...] = total
+    for q in range(2):
+        lanes = slice(256 * q, 256 * q + 256)
+        tile = x[:, lanes]
+        xdt = tile * spread(step, 4 * q, 4)
+        top = skip[0:1, lanes] * tile[:HT]
+        bottom = skip[0:1, lanes] * tile[HT:]
+        for i in range(4):
+            h = 4 * q + i
+            row = ldt[0, pl.ds(8 * g + h, 1), :] * LOG2E
+            col = logd[:, h : h + 1]
+            mine = jnp.where(head == i, xdt, 0.0).astype(bf16)
+            decay = jnp.exp2(jnp.where(upper, col[:HT] - row[:, :HT], NEG))
+            top = top + nn((decay * s[:HT, :HT]).astype(bf16), mine[:HT])
+            decay = jnp.exp2(jnp.where(lower, col[HT:] - row, NEG))
+            bottom = bottom + nn((decay * s[HT:, :]).astype(bf16), mine)
+        y[:HT, lanes] = top
+        y[HT:, lanes] = bottom
 
 
 def inner_part(s, ld, ldt, dt, x, skip_row):
     rows = x.shape[0]
-    blocks, groups = rows // T, W // 256
+    blocks, groups = rows // T, W // 512
     return pl.pallas_call(
         inner_kernel,
         name="inner_part",
@@ -216,10 +262,10 @@
             pl.BlockSpec((T, 128), lambda j, g: (j, 0)),
             pl.BlockSpec((1, 32, T), lambda j, g: (j, 0, 0)),
             pl.BlockSpec((T, 128), lambda j, g: (j, 0)),
-            pl.BlockSpec((T, 256), lambda j, g: (j, g)),
-            pl.BlockSpec((8, 256), lambda j, g: (0, g)),
-        ],
-        out_specs=pl.BlockSpec((T, 256), lambda j, g: (j, g)),
+            pl.BlockSpec((T, 512), lambda j, g: (j, g)),
+            pl.BlockSpec((8, 512), lambda j, g: (0, g)),
+        ],
+        out_specs=pl.BlockSpec((T, 512), lambda j, g: (j, g)),
         out_shape=jax.ShapeDtypeStruct((rows, W), f32),
         compiler_params=params(),
         cost_estimate=cost(
@@ -268,7 +314,30 @@
     )(yin, bc, e, ld, z)
 
 
-def gate_back_kernel(y, z, gfin, x, sums, dots, bc, e, ld, gain, skip, dz, dy, dc, de, dl, ggain, gskip, dye):
+def out_back_kernel(cot, w, exact, gfin, dots):
+    g = nt(cot[...], w[...])
+    gfin[...] = g
+    dots[...] = jnp.broadcast_to(jnp.sum(g * exact[...], axis=1, keepdims=True), dots.shape)
+
+
+def out_back(cot, w, exact):
+    rows = cot.shape[0]
+    row = lambda c: pl.BlockSpec((T, c), lambda j: (j, 0))
+    return pl.pallas_call(
+        out_back_kernel,
+        name="out_back",
+        grid=(rows // T,),
+        in_specs=[row(D), pl.BlockSpec((W, D), lambda j: (0, 0)), row(W)],
+        out_specs=[row(W), row(128)],
+        out_shape=[jax.ShapeDtypeStruct((rows, W), f32), jax.ShapeDtypeStruct((rows, 128), f32)],
+        compiler_params=params(),
+        cost_estimate=cost(2 * rows * D * W, rows * W * 10 + 2 * D * W),
+    )(cot, w, exact)
+
+
+def gate_back_kernel(
+    y, z, gfin, x, sums, dots, bc, e, ld, gain, skip, dec, dz, dy, dc, de1, given, dl, ggain, gskip, dye, keep
+):
     j = pl.program_id(0)
 
     @pl.when(j == 0)
@@ -301,35 +370,50 @@
         dcs = dcs + (nt(high, e[0, :, lanes]) + nt(low, e[0, :, lanes]))
     dl[...] = dlog
     dc[...] = dcs
-    de[0] = tn(bc[:, N:].astype(bf16), dye[...])
-
-
-def gate_back(y, z, gfin, x, sums, dots, bc, e, ld, gain, skip_row):
+    de = tn(bc[:, N:].astype(bf16), dye[...])
+
+    @pl.when(j % 2 == 0)
+    def _():
+        de1[0] = de
+        keep[...] = de
+
+    @pl.when(j % 2 == 1)
+    def _():
+        given[0] = (de + dec[0, 0:1] * keep[...]).astype(bf16)
+
+
+def gate_back(y, z, gfin, x, sums, dots, bc, e, ld, gain, skip_row, dec, micros):
     rows = y.shape[0]
     blocks = rows // T
-    row = lambda c: pl.BlockSpec((T, c), lambda j: (j, 0))
-    fixed = pl.BlockSpec((8, W), lambda j: (0, 0))
-    state = pl.BlockSpec((1, N, W), lambda j: (j, 0, 0))
+    blk = lambda p: (1 - p % 2) * micros + p // 2
+    row = lambda c: pl.BlockSpec((T, c), lambda p: (blk(p), 0))
+    fixed = pl.BlockSpec((8, W), lambda p: (0, 0))
+    state = pl.BlockSpec((1, N, W), lambda p: (blk(p), 0, 0))
+    chip = pl.BlockSpec((1, N, W), lambda p: (p // 2, 0, 0))
     sh = jax.ShapeDtypeStruct
     return pl.pallas_call(
         gate_back_kernel,
         name="gate_back",
         grid=(blocks,),
-        in_specs=[row(W), row(W), row(W), row(W), row(128), row(128), row(2 * N), state, row(128), fixed, fixed],
-        out_specs=[row(W), row(W), row(N), state, row(128), fixed, fixed],
+        in_specs=[
+            row(W), row(W), row(W), row(W), row(128), row(128), row(2 * N), state, row(128),
+            fixed, fixed, pl.BlockSpec((1, 8, W), lambda p: (blk(p), 0, 0)),
+        ],
+        out_specs=[row(W), row(W), row(N), chip, chip, row(128), fixed, fixed],
         out_shape=[
             sh((rows, W), bf16),
             sh((rows, W), bf16),
             sh((rows, N), f32),
-            sh((blocks, N, W), f32),
+            sh((micros, N, W), f32),
+            sh((micros, N, W), bf16),
             sh((rows, 128), f32),
             sh((8, W), f32),
             sh((8, W), f32),
         ],
-        scratch_shapes=[pltpu.VMEM((T, W), bf16)],
+        scratch_shapes=[pltpu.VMEM((T, W), bf16), pltpu.VMEM((N, W), f32)],
         compiler_params=params(),
         cost_estimate=cost(8 * rows * N * W, rows * W * 24, rows * W * 2),
-    )(y, z, gfin, x, sums, dots, bc, e, ld, gain, skip_row)
+    )(y, z, gfin, x, sums, dots, bc, e, ld, gain, skip_row, dec)
 
 
 def inner_back_kernel(s, bc, ld, ldt, dt, x, dy, skip, dx, xv, dbc, st, dst):
@@ -341,26 +425,41 @@
         dst[...] = jnp.zeros_like(dst)
         xv[...] = jnp.zeros_like(xv)
 
-    causal = iota((T, T), 1) >= iota((T, T), 0)
+    shift = lax.rem(128 - 8 * g, 128)
+    logd = pltpu.roll(ld[...], shift, 1) * LOG2E
+    step = pltpu.roll(dt[...], shift, 1)
+    early = iota((HT, T), 1) >= iota((HT, T), 0)
+    late = iota((HT, HT), 1) >= iota((HT, HT), 0)
     head = iota((T, 256), 1) // PS
-    shift = lax.rem(128 - 4 * g, 128)
-    logd = pltpu.roll(ld[...], shift, 1)
-    steps = spread(pltpu.roll(dt[...], shift, 1), 0, 4)
-    tile = x[...]
-    xdt = tile * steps
-    dyt = dy[...]
-    scores = st[...]
-    total = jnp.zeros((T, 256), f32)
-    gscore = jnp.zeros((T, T), f32)
-    for i in range(4):
-        gap = ldt[0, pl.ds(4 * g + i, 1), :] - logd[:, i : i + 1]
-        decay = jnp.exp(jnp.where(causal, gap, NEG))
-        mine = head == i
-        total = total + nn((decay * scores).astype(bf16), jnp.where(mine, dyt, jnp.zeros_like(dyt)))
-        gscore = gscore + nt(jnp.where(mine, xdt, 0.0).astype(bf16), dyt) * decay
-    dst[...] += gscore
-    dx[...] = total * steps + skip[0:1, :] * dyt.astype(f32)
-    xv[...] += per_head(tile * total, 4 * g)
+    gtop = jnp.zeros((HT, T), f32)
+    gbottom = jnp.zeros((HT, HT), f32)
+    sums = jnp.zeros((T, 128), f32)
+    for q in range(2):
+        lanes = slice(256 * q, 256 * q + 256)
+        steps = spread(step, 4 * q, 4)
+        tile = x[:, lanes]
+        xdt = tile * steps
+        dyt = dy[:, lanes]
+        top = jnp.zeros((HT, 256), f32)
+        bottom = jnp.zeros((HT, 256), f32)
+        for i in range(4):
+            h = 4 * q + i
+            row = ldt[0, pl.ds(8 * g + h, 1), :] * LOG2E
+            col = logd[:, h : h + 1]
+            dmine = jnp.where(head == i, dyt, jnp.zeros_like(dyt))
+            xmine = jnp.where(head == i, xdt, 0.0).astype(bf16)
+            decay = jnp.exp2(jnp.where(early, row - col[:HT], NEG))
+            top = top + nn((decay * st[:HT, :]).astype(bf16), dmine)
+            gtop = gtop + nt(xmine[:HT], dyt) * decay
+            decay = jnp.exp2(jnp.where(late, row[:, HT:] - col[HT:], NEG))
+            bottom = bottom + nn((decay * st[HT:, HT:]).astype(bf16), dmine[HT:])
+            gbottom = gbottom + nt(xmine[HT:], dyt[HT:]) * decay
+        total = jnp.concatenate([top, bottom], axis=0)
+        dx[:, lanes] = total * steps + skip[0:1, lanes] * dyt.astype(f32)
+        sums = sums + per_head(tile * total, 8 * g + 4 * q)
+    xv[...] += sums
+    dst[:HT, :] += gtop
+    dst[HT:, HT:] += gbottom
 
     @pl.when(g == pl.num_programs(1) - 1)
     def _():
@@ -370,9 +469,9 @@
 
 def inner_back(s, bc, ld, ldt, dt, x, dy, skip_row):
     rows = x.shape[0]
-    blocks, groups = rows // T, W // 256
+    blocks, groups = rows // T, W // 512
     row = lambda c: pl.BlockSpec((T, c), lambda j, g: (j, 0))
-    tile = pl.BlockSpec((T, 256), lambda j, g: (j, g))
+    tile = pl.BlockSpec((T, 512), lambda j, g: (j, g))
     sh = jax.ShapeDtypeStruct
     return pl.pallas_call(
         inner_back_kernel,
@@ -386,7 +485,7 @@
             row(128),
             tile,
             tile,
-            pl.BlockSpec((8, 256), lambda j, g: (0, g)),
+            pl.BlockSpec((8, 512), lambda j, g: (0, g)),
         ],
         out_specs=[tile, row(128), row(2 * N)],
         out_shape=[sh((rows, W), f32), sh((rows, 128), f32), sh((rows, 2 * N), f32)],
@@ -399,7 +498,7 @@
 
 
 def conv_back_kernel(
-    micros, xbc, prev, x, dxi, xv, dbc, bc, dt, ld, later, e, dc, dla, cw, hp,
+    micros, xbc, prev, x, dxi, xv, dbc, bc, dt, ld, later1, de1, dec, e, dc, dla, cw, hp,
     gp, gcw, ghp, pad, dpre, nxt, edge,
 ):
     p = pl.program_id(0)
@@ -450,7 +549,9 @@
         ddec = jnp.zeros((8, 128), f32)
         for i in range(W // 256):
             lanes = slice(256 * i, 256 * i + 256)
-            lat = later[0, :, lanes]
+            lat = later1[0, :, lanes]
+            earlier = de1[0, :, lanes] + dec[0, 0:1, lanes] * lat.astype(f32)
+            lat = jnp.where(b == 1, lat, earlier.astype(bf16))
             spreadw = spread(tailw, 4 * i, 4)
             xt = x[:, lanes]
             bl = nn(bst, lat)
@@ -481,13 +582,16 @@
             edge[pl.ds(pl.multiple_of(8 * (p // 2), 8), 8), XC:XP] = jnp.zeros((8, 128), f32)
 
 
-def conv_back(xbc, x, dxi, xv, dbc, bc, dt, ld, later, e, dc, dla, cw, hp, micros):
+def conv_back(xbc, x, dxi, xv, dbc, bc, dt, ld, later1, de1, dec, e, dc, dla, cw, hp, micros):
     blocks = 2 * micros
     rows = blocks * T
     blk = lambda p: jnp.where(p < blocks, (1 - p % 2) * micros + p // 2, micros - 1)
     row = lambda c: pl.BlockSpec((T, c), lambda p: (blk(p), 0))
     whole = lambda a: pl.BlockSpec(a.shape, lambda p: (0, 0))
     state = pl.BlockSpec((1, N, W), lambda p: (blk(p), 0, 0))
+
+    unit = lambda p: jnp.minimum(p // 2, micros - 1)
+    chip = pl.BlockSpec((1, N, W), lambda p: (unit(p), 0, 0))
 
     def before(p):
         k = blk(p)
@@ -501,7 +605,8 @@
             row(XP),
             pl.BlockSpec((8, XP), before),
             row(W), row(W), row(128), row(2 * N), row(2 * N), row(128), row(128),
-            state, state, row(N), row(128), whole(cw), whole(hp),
+            chip, chip, pl.BlockSpec((1, 8, W), lambda p: (micros + unit(p), 0, 0)), state,
+            row(N), row(128), whole(cw), whole(hp),
         ],
         out_specs=[
             pl.BlockSpec((T, XP), lambda p: (jnp.where(p < blocks, blk(p), blocks), 0)),
@@ -521,7 +626,7 @@
         ],
         compiler_params=pltpu.CompilerParams(vmem_limit_bytes=58 * MB_),
         cost_estimate=cost(6 * rows * N * W, rows * W * 18, rows * XC * 2),
-    )(xbc, xbc, x, dxi, xv, dbc, bc, dt, ld, later, e, dc, dla, cw, hp)
+    )(xbc, xbc, x, dxi, xv, dbc, bc, dt, ld, later1, de1, dec, e, dc, dla, cw, hp)
 
 
 AXIS = {"z": Z, "l": "zl", "s": "s"}
@@ -557,9 +662,20 @@
         return hop(value, axis)
 
 
-class RingFirst(Moves):
-    def __init__(self, own, a, b):
-        self.a, self.b = a, b
+WAYS = (("s", "l"), ("l", "s"))
+
+
+def lanes_of(widths):
+    return [slice(sum(widths[:c]), sum(widths[: c + 1])) for c in range(len(widths))]
+
+
+def near(c, kl, ks):
+    return (ks, kl) if c == 0 else (kl, ks)
+
+
+class Gather(Moves):
+    def __init__(self, own, widths, turns):
+        self.widths, self.turns = widths, turns
         self.live = {"g0": own}
         self.n = 1
         self.parts = []
@@ -569,76 +685,102 @@
         self.n += 1
 
     def first(self, h):
-        pair = jnp.stack([self.live.pop(f"g{2 * h}"), self.live[f"g{2 * h + 1}"]], 0)
-        if h:
-            self.live.pop("g3")
-        self.live[f"p{h}"] = pair
-        self.live[f"q{h}"] = self.send(pair, self.a)
+        some = jnp.stack([self.live[f"g{k}"] for k in self.turns[h]], 0)
+        for k in self.turns[h]:
+            if k < self.n - 1 or self.n == RING:
+                self.live.pop(f"g{k}")
+        for c, lanes in enumerate(lanes_of(self.widths)):
+            self.live[f"p{h}{c}"] = some[:, :, lanes]
+            self.live[f"q{h}{c}"] = self.send(some[:, :, lanes], WAYS[c][0])
 
     def second(self, h):
-        four = jnp.concatenate([self.live.pop(f"p{h}"), self.live.pop(f"q{h}")], 0)
-        self.parts += [four, self.send(four, self.b)]
-
-    def entry(self, kz, kl, ks):
-        ka, kb = (kl, ks) if self.a == "l" else (ks, kl)
-        return (kz // 2) * 2 + kb, ka * 2 + kz % 2
+        for c in range(2):
+            more = jnp.concatenate([self.live.pop(f"p{h}{c}"), self.live.pop(f"q{h}{c}")], 0)
+            self.parts += [more, self.send(more, WAYS[c][1])]
+
+    def place(self, c, kz, kl, ks):
+        ka, kb = near(c, kl, ks)
+        h = [kz in t for t in self.turns].index(True)
+        turn = self.turns[h]
+        return (h * 2 + c) * 2 + kb, ka * len(turn) + turn.index(kz)
 
 
 class RingLast(Moves):
-    def __init__(self, own, a, b):
-        self.a, self.b = a, b
-        self.live = {"p": own[None]}
+    def __init__(self, own, widths):
+        self.widths = widths
+        self.live = {f"p{c}": own[None, :, lanes] for c, lanes in enumerate(lanes_of(widths))}
         self.parts = []
 
-    def step(self, axis):
-        self.live["p"] = jnp.concatenate([self.live["p"], self.send(self.live["p"], axis)], 0)
+    def step(self, n):
+        for c in range(2):
+            p = self.live[f"p{c}"]
+            self.live[f"p{c}"] = jnp.concatenate([p, self.send(p, WAYS[c][n])], 0)
 
     def z(self):
         if not self.parts:
+            self.live["p"] = jnp.concatenate([self.live.pop("p0"), self.live.pop("p1")], 0)
             self.parts = [self.live["p"]]
         self.live["p"] = self.send(self.live["p"], "z")
         self.parts.append(self.live["p"])
 
-    def entry(self, kz, kl, ks):
-        ka, kb = (kl, ks) if self.a == "l" else (ks, kl)
-        return kz, kb * 2 + ka
-
-
-class ExchangeFirst(Moves):
-    def __init__(self, a, b):
-        self.a, self.b = a, b
+    def place(self, c, kz, kl, ks):
+        ka, kb = near(c, kl, ks)
+        return kz, c * 4 + kb * 2 + ka
+
+
+class Scatter(Moves):
+    def __init__(self, widths, turns):
+        self.widths, self.turns = widths, turns
         self.live = {}
+        self.order = [k for t in turns for k in t]
 
     def load(self, parts):
-        for h in range(2):
-            self.live[f"k{h}"], self.live[f"s{h}"] = parts[2 * h], parts[2 * h + 1]
+        parts = iter(parts)
+        for h in range(len(self.turns)):
+            for c in range(2):
+                self.live[f"k{h}{c}"] = next(parts)
+                self.live[f"s{h}{c}"] = next(parts)
 
     def second(self, h):
-        got = self.send(self.live.pop(f"s{h}"), self.b)
-        self.live[f"r{h}"] = got
+        for c in range(2):
+            self.live[f"r{h}{c}"] = self.send(self.live.pop(f"s{h}{c}"), WAYS[c][1])
 
     def first(self, h):
-        total = self.live.pop(f"r{h}").astype(f32) + self.live.pop(f"k{h}").astype(f32)
-        self.live[f"m{h}"] = total[:2].astype(bf16)
-        self.live[f"n{h}"] = self.send(total[2:].astype(bf16), self.a)
+        n = len(self.turns[h])
+        for c in range(2):
+            got, kept = self.live.pop(f"r{h}{c}"), self.live.pop(f"k{h}{c}")
+            self.live[f"m{h}{c}"] = got[:n].astype(f32) + kept[:n].astype(f32)
+            give = (got[n:].astype(f32) + kept[n:].astype(f32)).astype(bf16)
+            self.live[f"n{h}{c}"] = self.send(give, WAYS[c][0])
 
     def ring(self, k):
-        if k in (0, 2):
-            h = k // 2
-            both = self.live.pop(f"m{h}").astype(f32) + self.live.pop(f"n{h}").astype(f32)
-            term, self.live["w"] = both[0], both[1].astype(bf16)
-        else:
-            term = self.live.pop("w").astype(f32)
+        h = [self.order[k] in t for t in self.turns].index(True)
+        at = self.turns[h].index(self.order[k])
+        if at == 0:
+            self.live["w"] = jnp.concatenate(
+                [self.live.pop(f"m{h}{c}") + self.live.pop(f"n{h}{c}").astype(f32) for c in range(2)], 2
+            )
+        total = self.live["w"][at]
         if k:
-            term = term + self.live.pop("t").astype(f32)
-        if k == 3:
-            return term
-        self.live["t"] = self.send(term.astype(bf16), "z")
-
-    def entry(self, kz, kl, ks):
-        ka, kb = (kl, ks) if self.a == "l" else (ks, kl)
-        h, at = ((0, kz - 1) if kz in (1, 2) else (1, (kz + 1) % 4))
-        return 2 * h + kb, ka * 2 + at
+            total = total + self.live.pop("t").astype(f32)
+        if k == RING - 1:
+            self.live.pop("w")
+            return total
+        self.live["t"] = self.send(total.astype(bf16), "z")
+
+    def place(self, c, kz, kl, ks):
+        ka, kb = near(c, kl, ks)
+        h = [kz in t for t in self.turns].index(True)
+        turn = self.turns[h]
+        return (h * 2 + c) * 2 + kb, ka * len(turn) + turn.index(kz)
+
+    def shapes(self, r):
+        return [
+            jax.ShapeDtypeStruct((2 * len(t), r, w), bf16)
+            for t in self.turns
+            for w in self.widths
+            for _ in range(2)
+        ]
 
 
 def move_kernel(table, r, out_of, where, *refs):
@@ -647,9 +789,9 @@
     whole = refs[-1] if out_of else refs[0]
     arrays = refs[:-1] if out_of else refs[1:]
     copies = []
-    for n, (array, entry, k, lane, width) in enumerate(table):
+    for n, (array, entry, k, lanes) in enumerate(table):
         row = pl.multiple_of(where[k] * r, 16)
-        place = whole.at[pl.ds(row, r), lane : lane + width]
+        place = whole.at[pl.ds(row, r), lanes]
         piece = arrays[array].at[entry]
         pair = (piece, place) if out_of else (place, piece)
         copies.append(pltpu.make_async_copy(*pair, sems.at[n]))
@@ -659,37 +801,31 @@
         c.wait()
 
 
-def move(groups, where, r, widths, whole=None, parts=None):
+def move(group, where, r, given, shapes, out_of):
     table = []
-    for g, group in enumerate(groups):
+    for c, lanes in enumerate(lanes_of(group.widths)):
         for k in range(CHIPS):
-            array, entry = group.entry(k // 4, k // 2 % 2, k % 2)
-            table.append((4 * g + array, entry, k, sum(widths[:g]), widths[g]))
-    wide = sum(widths)
-    shapes = [jax.ShapeDtypeStruct((4, r, w), bf16) for w in widths for _ in range(4)]
-    joined = jax.ShapeDtypeStruct((CHIPS * r, wide), bf16)
-    given = parts if parts else [whole]
+            table.append((*group.place(c, k // 4, k // 2 % 2, k % 2), k, lanes))
     any_ = pl.BlockSpec(memory_space=pl.ANY)
     return pl.pallas_call(
-        functools.partial(move_kernel, tuple(table), r, parts is not None),
-        name="join" if parts else "deal",
+        functools.partial(move_kernel, tuple(table), r, out_of),
+        name="join" if out_of else "deal",
         in_specs=[pl.BlockSpec(memory_space=pltpu.SMEM)] + [any_] * len(given),
-        out_specs=any_ if parts else [any_] * len(shapes),
-        out_shape=joined if parts else shapes,
+        out_specs=[any_] * len(shapes),
+        out_shape=shapes,
         scratch_shapes=[pltpu.SemaphoreType.DMA((len(table),))],
         compiler_params=pltpu.CompilerParams(vmem_limit_bytes=MB_),
-        cost_estimate=cost(0, 4 * CHIPS * r * wide),
+        cost_estimate=cost(0, 4 * CHIPS * r * sum(group.widths)),
     )(where, *given)
 
 
-def join(groups, where, r, widths):
-    return move(groups, where, r, widths, parts=[p for g in groups for p in g.parts])
-
-
-def deal(groups, where, r, widths, whole):
-    parts = move(groups, where, r, widths, whole=whole)
-    for g, group in enumerate(groups):
-        group.load(parts[4 * g : 4 * g + 4])
+def join(group, where, r):
+    shape = jax.ShapeDtypeStruct((CHIPS * r, sum(group.widths)), bf16)
+    return move(group, where, r, group.parts, [shape], True)[0]
+
+
+def deal(group, where, r, whole):
+    group.load(move(group, where, r, [whole], group.shapes(r), False))
 
 
 def swap(value, axis="c"):
@@ -698,14 +834,6 @@
 
 def two(mine, other, at):
     return jnp.where(at == 0, jnp.stack([mine, other]), jnp.stack([other, mine]))
-
-
-def cols(value, *widths):
-    out, at = [], 0
-    for w in widths:
-        out.append(value[:, at : at + w])
-        at += w
-    return out
 
 
 class Plain:
@@ -735,19 +863,24 @@
     turn = [(a * 2 + b, b * 2 + a) for a in range(2) for b in range(2)]
 
     def cut(k):
+        part = lambda at, width: lax.dynamic_slice_in_dim(in_weight, at + k * width, width, 1)
+        steps = in_weight[:, DI + CONV :]
+        steps = jnp.where(k == 0, steps[:, :HH], steps[:, HH:])
         return jnp.concatenate(
             [
-                in_weight[:, DI + k * W : DI + (k + 1) * W],
+                part(DI, W),
                 in_weight[:, 2 * DI : 2 * DI + 2 * N],
-                jnp.pad(in_weight[:, DI + CONV + k * HH : DI + CONV + (k + 1) * HH], ((0, 0), (0, 128 - HH))),
-                in_weight[:, k * W : (k + 1) * W],
+                jnp.pad(steps, ((0, 0), (0, 128 - HH))),
+                part(0, W),
             ],
             axis=1,
         )
 
-    cuts = jnp.stack([cut(0), cut(1)])
-    theirs = swap(lax.dynamic_index_in_dim(cuts, 1 - core, 0, False))
-    chip_rows = two(lax.dynamic_index_in_dim(cuts, core, 0, False), theirs, core).reshape(r, -1)
+    ours, theirs = cut(core), cut(1 - core)
+    theirs, out_weight, hidden, cotangent = lax.optimization_barrier(
+        (theirs, out_weight, hidden, cotangent)
+    )
+    chip_rows = two(ours, swap(theirs), core).reshape(r, -1)
     w_own = lax.ppermute(out_weight, ("za", "c"), turn)
 
     ins = Plain(ALL[:4])
@@ -782,49 +915,31 @@
         small = spread_out(packed, "za", 0)
         small = spread_out(small, "zb", 1)
         chip_rows, small = lax.optimization_barrier((chip_rows, small))
-        own = cols(chip_rows, *x_cols, *z_cols)
-        gx_ = [RingFirst(own[0], "s", "l"), RingFirst(own[1], "l", "s")]
-        gz_ = [RingFirst(own[2], "s", "l"), RingFirst(own[3], "l", "s")]
-        own = cols(w_own, *o_cols)
-        go_ = [RingLast(own[0], "s", "l"), RingLast(own[1], "l", "s")]
-        every = gx_ + gz_ + go_
+        halves_, ring_ = ((0, 1), (2, 3)), ((0, 1, 2, 3),)
+        gx_ = Gather(chip_rows[:, :XP], x_cols, halves_)
+        gz_ = Gather(chip_rows[:, XP:], z_cols, ring_)
+        go_ = RingLast(w_own, o_cols)
+        every = [gx_, gz_, go_]
         small = spread_out(small, "zl", 2)
-        for g in gx_:
-            g.z()
-        for g in go_:
-            g.step(g.a)
+        gx_.z()
+        go_.step(0)
         small, hid_other, cot_other = fence(every, small, hid_other, cot_other)
         small = spread_out(small, "s", 3)
-        for g in gx_:
-            g.z()
-            g.first(0)
-        for g in go_:
-            g.step(g.b)
+        gx_.z()
+        gx_.first(0)
+        go_.step(1)
         hid_own_, hid_other = after(every, hid_own, hid_other)
         hid_all = chip_tokens(hid_own_, hid_other)
         rim = rim_of(hid_all)
+        small = spread_out(small, "c", 4).reshape(-1, packed.shape[0])
         small, rim, hid_all = fence(every, small, rim, hid_all)
-        for g in gx_:
-            g.z()
-            g.second(0)
-        for g in gz_:
-            g.z()
-        small, cot_own_, cot_other = after(every, small, cot_own, cot_other)
-        small = spread_out(small, "c", 4).reshape(-1, packed.shape[0])
+        gx_.z()
+        gx_.second(0)
+        gz_.z()
+        small, rim, hid_all, cot_own_, cot_other = after(
+            every, small, rim, hid_all, cot_own, cot_other
+        )
         cot_all = chip_tokens(cot_own_, cot_other)
-        small, cot_all = fence(every, small, cot_all)
-        for g in gx_:
-            g.first(1)
-        for g in gz_:
-            g.z()
-        for g in go_:
-            g.z()
-        (small,) = fence(gx_ + gz_, small)
-        for g in gx_:
-            g.second(1)
-        for g in gz_:
-            g.z()
-        small, hid_all, rim = after(gx_ + gz_, small, hid_all, rim)
     else:
         small = lax.all_gather(packed, ALL)
         hid_all, cot_all = chip_tokens(hid_own, hid_other), chip_tokens(cot_own, cot_other)
@@ -832,8 +947,6 @@
         w_x, w_z = ins.gather(chip_rows[:, :XP]), ins.gather(chip_rows[:, XP:])
 
     rim = jnp.where(iota(rim.shape, 1) >= 5, rim, jnp.zeros_like(rim)).reshape(8 * micros, D)
-    tok_f = jnp.concatenate([hid_all, rim], axis=0).astype(f32)
-    scale = lax.rsqrt(jnp.mean(tok_f * tok_f, axis=-1, keepdims=True) + EPS)
     devices = small.shape[0]
     taps = small[:, : KC * n_c].reshape(devices, KC, n_c).transpose(1, 0, 2).reshape(KC, CONV)
     bias = small[:, KC * n_c : (KC + 1) * n_c].reshape(1, CONV)
@@ -848,34 +961,37 @@
     heads = lax.dynamic_slice_in_dim(heads, core * HH, HH, 1)
     hp = jnp.pad(heads, ((0, 5), (0, 128 - HH)))
     skip_row = jnp.broadcast_to(jnp.repeat(heads[2], PS)[None], (8, W))
-    normed = (tok_f * scale * norm_vec).astype(bf16)
-
-    if fast:
-        normed, cw, hp, gain, skip_row = fence(every, normed, cw, hp, gain, skip_row)
-        for g in gz_:
-            g.first(0)
-        for g in go_:
-            g.z()
-        (normed,) = after(gz_ + go_, normed)
-        w_x = join(gx_, in_place, r, x_cols)
+    normed = pre_norm(hid_all, rim, norm_vec[None])
+    if fast:
+        normed, cot_all, cw, hp, gain, skip_row = fence(
+            every, normed, cot_all, cw, hp, gain, skip_row
+        )
+        gx_.first(1)
+        gz_.z()
+        (normed,) = fence([gx_, gz_], normed)
+        gx_.second(1)
+        gz_.z()
+        (normed,) = after([gx_, gz_], normed)
+
+    if fast:
+        (normed,) = fence(every, normed)
+        gz_.first(0)
+        go_.z()
+        (normed,) = after([gz_, go_], normed)
+        w_x = join(gx_, in_place, r)
     xbc = nn(normed, w_x)
     if fast:
-        (xbc,) = fence(gz_, xbc)
-        for g in gz_:
-            g.second(0)
-            g.first(1)
-        (xbc,) = after(gz_, xbc)
+        (xbc,) = fence([gz_], xbc)
+        gz_.second(0)
+        (xbc,) = after([gz_], xbc)
     else:
         w_o = outs.gather(w_own)
-    x, bc, s, dt, ld, ldt, st0, comb, dec = block_states(xbc, cw, hp, micros)
-    dec = dec[:, 0].reshape(2, micros, 1, W)
-    if fast:
-        comb, s = fence(gz_ + go_, comb, s)
-        for g in gz_:
-            g.second(1)
-        for g in go_:
-            g.z()
-        (s,) = after(gz_ + go_, s)
+    x, bc, s, dt, ld, ldt, st0, comb, dec8 = block_states(xbc, cw, hp, micros)
+    dec = dec8[:, 0].reshape(2, micros, 1, W)
+    if fast:
+        comb, s = fence([go_], comb, s)
+        go_.z()
+        (s,) = after([go_], s)
     if ns == 2:
         first = lax.ppermute(comb, "s", onward)
     else:
@@ -885,10 +1001,14 @@
             out = (chip_decay * first.astype(f32) + comb.astype(f32)).astype(bf16)
             first = lax.ppermute(out, "s", onward)
     yin = inner_part(s, ld, ldt, dt, x, skip_row)
+    if fast:
+        (yin,) = fence([gz_, go_], yin)
+        go_.z()
+        (yin,) = after([go_], yin)
     second = (dec[0] * first.astype(f32) + st0).astype(bf16)
     entering = jnp.stack([first, second], 0).reshape(2 * micros, N, W)
     if fast:
-        w_z = join(gz_, in_place, r, z_cols)
+        w_z = join(gz_, in_place, r)
     z = nn(normed[:rows], w_z)
     y, sums = gate_part(yin, bc, entering, ld, z)
     sums = sums + swap(sums)
@@ -897,96 +1017,89 @@
     fin = exact.astype(bf16)
     g_out = tn(fin, cot_all).astype(bf16)
     if fast:
-        so_ = [ExchangeFirst("s", "l"), ExchangeFirst("l", "s")]
-        deal(so_, out_place, r, o_cols, g_out)
-        (cot_all,) = fence(so_, cot_all)
-        for g in so_:
-            g.second(0)
-        (cot_all,) = after(so_, cot_all)
-        w_o = join(go_, out_place, r, o_cols)
-
-    gfin = nt(cot_all, w_o)
-    dots = jnp.sum(gfin * exact, axis=1)
-    if fast:
-        dots, gfin = fence(so_, dots, gfin)
-        for g in so_:
-            g.second(1)
-            g.first(0)
-        (y,) = after(so_, y)
+        ring_back = ((1, 2, 3, 0),)
+        so_ = Scatter(o_cols, ring_back)
+        deal(so_, out_place, r, g_out)
+        (cot_all,) = fence([so_], cot_all)
+        so_.second(0)
+        (cot_all,) = after([so_], cot_all)
+        w_o = join(go_, out_place, r)
+
+    gfin, dots = out_back(cot_all, w_o, exact)
+
+    partial_out = nn(fin, w_o).reshape(2, micros, T, D)
+    give = lax.dynamic_index_in_dim(partial_out, 1 - core, 0, False).astype(bf16)
+    keep = lax.dynamic_index_in_dim(partial_out, core, 0, False)
+    given_out = swap(give)
+    block_out = (hid_own.astype(f32) + keep + given_out.astype(f32)).astype(bf16)
+    if fast:
+        dots, gfin, give = fence([so_], dots, gfin, give)
+        so_.first(0)
+        (y,) = after([so_], y)
     dots = dots + swap(dots)
-    dots = jnp.broadcast_to(dots[:, None], (rows, 128))
-    dz, dy, dc, de, dla, ggain, gskip = gate_back(
-        y, z, gfin, x, sums, dots, bc, entering, ld, gain, skip_row
+    dz, dy, dc, de1, given, dla, ggain, gskip = gate_back(
+        y, z, gfin, x, sums, dots, bc, entering, ld, gain, skip_row, dec8, micros
     )
-    de = de.reshape(2, micros, N, W)
     if ns == 2:
-        given = (de[0] + dec[0] * de[1]).astype(bf16)
         dz, given = lax.optimization_barrier((dz, given))
         later1 = lax.ppermute(given, "s", backward)
     else:
         later1 = jnp.zeros((micros, N, W), bf16)
         for _ in range(ns - 1):
-            out = de[0] + dec[0] * (de[1] + dec[1] * later1.astype(f32))
+            out = given.astype(f32) + dec[0] * dec[1] * later1.astype(f32)
             later1 = lax.ppermute(out.astype(bf16), "s", backward)
     gz = tn(normed[:rows], dz).astype(bf16)
     if fast:
-        sz_ = [ExchangeFirst("s", "l"), ExchangeFirst("l", "s")]
-        deal(sz_, in_place, r, z_cols, gz)
-        (dy,) = fence(so_ + sz_, dy)
-        for g in so_:
-            g.first(1)
-            g.ring(0)
-        for g in sz_:
-            g.second(0)
-        (dy,) = after(so_ + sz_, dy)
+        sz_ = Scatter(z_cols, ring_back)
+        deal(sz_, in_place, r, gz)
+        (dy,) = fence([so_, sz_], dy)
+        so_.ring(0)
+        sz_.second(0)
+        (dy,) = after([so_, sz_], dy)
 
     dxi, xv, dbc = inner_back(s, bc, ld, ldt, dt, x, dy, skip_row)
-    later0 = (de[1] + dec[1] * later1.astype(f32)).astype(bf16)
-    later = jnp.stack([later0, later1], 0).reshape(2 * micros, N, W)
-    if fast:
-        dxi, later = fence(so_ + sz_, dxi, later)
-        for g in so_:
-            g.ring(1)
-        for g in sz_:
-            g.second(1)
-            g.first(0)
-        (dxi,) = after(so_ + sz_, dxi)
+    if fast:
+        dxi, later1 = fence([so_, sz_], dxi, later1)
+        so_.ring(1)
+        sz_.first(0)
+        (dxi,) = after([so_, sz_], dxi)
     gp, gcw, ghp = conv_back(
-        xbc, x, dxi, xv, dbc, bc, dt, ld, later, entering, dc, dla, cw, hp, micros
+        xbc, x, dxi, xv, dbc, bc, dt, ld, later1, de1, dec8, entering, dc, dla, cw, hp, micros
     )
     if fast:
-        (gp,) = fence(so_ + sz_, gp)
-        for g in sz_:
-            g.first(1)
-            g.ring(0)
-        for g in so_:
-            g.ring(2)
-        (gp,) = after(so_ + sz_, gp)
+        (gp,) = fence([so_, sz_], gp)
+        so_.ring(2)
+        sz_.ring(0)
+        (gp,) = after([so_, sz_], gp)
     gx = tn(normed, gp).astype(bf16)
-    if fast:
-        sx_ = [ExchangeFirst("s", "l"), ExchangeFirst("l", "s")]
-        deal(sx_, in_place, r, x_cols, gx)
-        (gp,) = fence(so_ + sz_ + sx_, gp)
-        for g in sx_:
-            g.second(0)
-        for g in sz_:
-            g.ring(1)
-        (gp,) = after(sx_ + sz_, gp)
-        g_out = jnp.concatenate([g.ring(3) for g in so_], axis=1)
+
+    wide = lambda v: jnp.pad(v, ((0, 0), (0, XC - v.shape[1])))
+    tiny = jnp.concatenate(
+        [gcw[:5], wide(ggain[:1]), wide(gskip[:1]), wide(ghp[:2].reshape(1, 256))], axis=0
+    )
+    if fast:
+        sx_ = Scatter(x_cols, ((1, 2), (3, 0)))
+        deal(sx_, in_place, r, gx)
+        gp, tiny = fence([so_, sz_, sx_], gp, tiny)
+        sx_.second(0)
+        sz_.ring(1)
+        (gp,) = after([sx_, sz_], gp)
+        g_out = so_.ring(3)
     else:
         g_out = outs.reduce(g_out)
+    g_out = lax.ppermute(g_out, ("za", "c"), turn)
 
     gn = nt(gp, w_x)
     edge = lax.ppermute(gn[rows:].astype(bf16), "s", backward).reshape(1, micros, 8, D)
-    gn = (gn[:rows] + nt(dz, w_z)).reshape(2, micros, T, D)
-    if fast:
-        gn, edge, fin, g_out = fence(sz_ + sx_, gn, edge, fin, g_out)
-        for g in sx_:
-            g.second(1)
-            g.first(0)
-        for g in sz_:
-            g.ring(2)
-        gn, fin = after(sx_ + sz_, gn, fin)
+    gn = gn[:rows] + nt(dz, w_z)
+
+    if fast:
+        gn, g_out = fence([sz_, sx_], gn, g_out)
+        sx_.second(1)
+        sx_.first(0)
+        sz_.ring(2)
+        (gn,) = after([sx_, sz_], gn)
+    gn = gn.reshape(2, micros, T, D)
     edge = jnp.where(iota(edge.shape, 2) >= 5, edge.astype(f32), 0.0)
     gn = gn + jnp.pad(edge, ((1, 0), (0, 0), (T - 8, 0), (0, 0)))
     give = lax.dynamic_index_in_dim(gn, 1 - core, 0, False).astype(bf16)
@@ -999,29 +1112,15 @@
     g_hid = cot_own.astype(f32) + own_scale * (
         gq - unit * jnp.mean(gq * unit, axis=-1, keepdims=True)
     )
-    g_norm = jnp.sum(gn * unit, axis=(0, 1))
-
-    partial_out = nn(fin, w_o).reshape(2, micros, T, D)
-    give = lax.dynamic_index_in_dim(partial_out, 1 - core, 0, False).astype(bf16)
-    keep = lax.dynamic_index_in_dim(partial_out, core, 0, False)
-    given_out = swap(give)
-
-    wide = lambda v: jnp.pad(v, ((0, 0), (0, XC - v.shape[1])))
-    tiny = jnp.concatenate(
-        [
-            gcw[:5], wide(ggain[:1]), wide(gskip[:1]), wide(ghp[:2].reshape(1, 256)),
-            wide(g_norm[None]), jnp.zeros((7, XC), f32),
-        ],
-        axis=0,
-    )
-    if fast:
-        tiny, g_hid, given_out, keep = fence(sz_ + sx_, tiny, g_hid, given_out, keep)
-        tiny = tiny + swap(tiny, "zb")
-        for g in sx_:
-            g.first(1)
-            g.ring(0)
-        gz = jnp.concatenate([g.ring(3) for g in sz_], axis=1)
-    block_out = (hid_own.astype(f32) + keep + given_out.astype(f32)).astype(bf16)
+
+    if fast:
+        tiny, g_hid, block_out = fence([sz_, sx_], tiny, g_hid, block_out)
+        sx_.first(1)
+        sx_.ring(0)
+        (tiny,) = after([sx_], tiny)
+        tiny = tiny + swap(tiny, "s")
+        tiny = tiny + swap(tiny, "zl")
+        gz = sz_.ring(3)
 
     def exchanged(g):
         g = g.reshape(2, r_in, -1)
@@ -1029,30 +1128,26 @@
         return two(mine, swap(lax.dynamic_index_in_dim(g, 1 - core, 0, False)), core)
 
     if fast:
-        tiny, block_out, gz, g_out = fence(sx_, tiny, block_out, gz, g_out)
+        tiny, gz = fence([sx_], tiny, gz)
+        sx_.ring(1)
+        tiny, gz = after([sx_], tiny, gz)
+        tiny = tiny + swap(tiny, "zb")
+        gz = exchanged(gz)
+        tiny, gz = fence([sx_], tiny, gz)
+        sx_.ring(2)
+        (tiny,) = after([sx_], tiny)
         tiny = tiny + swap(tiny, "za")
-        for g in sx_:
-            g.ring(1)
-        g_out = lax.ppermute(g_out, ("za", "c"), turn)
-        gz = exchanged(gz)
-        tiny, g_out, gz = fence(sx_, tiny, g_out, gz)
-        tiny = tiny + swap(tiny, "s")
-        for g in sx_:
-            g.ring(2)
-        tiny = tiny + swap(tiny, "zl")
-        (tiny,) = fence(sx_, tiny)
-        gx = jnp.concatenate([g.ring(3) for g in sx_], axis=1)
+        (tiny,) = fence([sx_], tiny)
+        gx = sx_.ring(3)
     else:
         tiny = lax.psum(tiny, ALL[:4])
         gx, gz = ins.reduce(gx), ins.reduce(gz)
-        g_out = lax.ppermute(g_out, ("za", "c"), turn)
         gz = exchanged(gz)
     gx = exchanged(gx)
     both = two(tiny, swap(tiny), core)
     g_conv = jnp.concatenate([both[0, :5, :W], both[1, :5, :W], both[0, :5, W:] + both[1, :5, W:]], axis=1)
     me = lax.axis_index(ALL)
     g_conv = lax.dynamic_slice_in_dim(g_conv, me * n_c, n_c, 1)
-    g_norm = lax.dynamic_slice_in_dim(both[0, 8, :D] + both[1, 8, :D], me * r_in, r_in)
     g_gate = both[:, 5, :W].reshape(-1)
     g_gate = lax.dynamic_slice_in_dim(g_gate, me * r_out, r_out)
     g_skip = both[:, 6, :W].reshape(H, PS).sum(-1)
@@ -1067,6 +1162,7 @@
         ],
         axis=1,
     )
+    g_norm = jnp.sum(g_in * in_weight.astype(f32), axis=1) / norm_gain.astype(f32)
     return (
         block_out.reshape(hidden.shape),
         g_hid.reshape(hidden.shape),

time: 596 us -> 514 us (0.86)
  waiting for transfers between devices: 161 us -> 111 us
  starting transfers between devices: 111 us -> 96 us
  matrix products: 63.7 us -> 56.4 us
    ppermute x80 -> x50, waiting for transfers between devices: 112 us -> 76 us  [hop(): return lax.ppermute(value, AXIS[axis], [(i, (i + 1) % n) for i in range(n)])]
    another operation x30 -> x4, other arithmetic: 24 us -> 4.08 us  [the longest x3 4.03 us: first(): some = jnp.stack([self.live[f'g{k}'] for k in self.turns[h]], 0)]
    ppermute x80 -> x50, starting transfers between devices: 80.6 us -> 62.3 us  [hop(): return lax.ppermute(value, AXIS[axis], [(i, (i + 1) % n) for i in range(n)])]
    unnamed x181 -> x153, local copies, waits for them, and re-layouts: 12.4 us -> 25.1 us
    pallas_call x6 -> x8, Pallas kernels: 12.5 us -> 22.2 us  [the longest x6 11.3 us: move(): pl.pallas_call(functools.partial(move_kernel, tuple(table), r, out_of), n...]
    slice x20 -> x4, local copies, waits for them, and re-layouts: 10.3 us -> 0.86 us  [the longest x1 0.74 us: body(): gz_ = Gather(chip_rows[:, XP:], z_cols, ring_)]
    ppermute x19, starting transfers between devices: 16.9 us -> 25.8 us  [swap(): return lax.ppermute(value, axis, [(0, 1), (1, 0)])]
    reduce_sum x3 -> x1, other arithmetic: 9.16 us -> 0.26 us  [body(): jnp.sum(g_in * in_weight.astype(f32), axis=1) / norm_gain.astype(f32)]
  transfers between devices with their start and end apart: 105 -> 75, of which waited for: 29 -> 22; matrix products, arithmetic and copies ran while one was open for 25% -> 28% of each run, Pallas kernels for 22% -> 24%
where the time goes in v2:
time: 514 us; the launch traced here: 507 us
  Pallas kernels  128 us (25%)
  waiting for transfers between devices  111 us (22%)
  starting transfers between devices  96 us (19%)
  other arithmetic  66.6 us (13%)
  matrix products  56.4 us (11%)
  local copies, waits for them, and re-layouts  45.8 us (9%)
    ppermute x50, waiting for transfers between devices, hop(): return lax.ppermute(value, AXIS[axis], [(i, (i + 1) % n) for i in range(n)])  76 us
    ppermute x50, starting transfers between devices, hop(): return lax.ppermute(value, AXIS[axis], [(i, (i + 1) % n) for i in range(n)])  62.3 us
    pallas_call x1, Pallas kernels, conv_back(): pl.pallas_call(functools.partial(conv_back_kernel, micros), name='conv_ba...  35.1 us
    ppermute x19, waiting for transfers between devices, swap(): return lax.ppermute(value, axis, [(0, 1), (1, 0)])  33.5 us
    ppermute x19, starting transfers between devices, swap(): return lax.ppermute(value, axis, [(0, 1), (1, 0)])  25.8 us
    unnamed x153, local copies, waits for them, and re-layouts  25.1 us
    pallas_call x1, Pallas kernels, inner_back(): pl.pallas_call(inner_back_kernel, name='inner_back', grid=(blocks, groups...  21 us
    dot_general x3, matrix products, nn(): lax.dot_general(a, b, (((1,), (0,)), ((), ())), preferred_element_type=f32)  20.8 us
  transfers between devices with their start and end apart: 75, of which 22 were waited for; matrix products, arithmetic and copies ran while one was open for 28% of the time, Pallas kernels for 24%

profile of v2, /device:TPU:0, one launch (start us, length us, event | category | flops | bytes accessed | tf_op | source)
XLA Modules:
  0.0 506.8 jit_solution(5411860739841374506)
XLA Ops:
  2.4 4.0 collective-permute-start.1
  12.3 1.9 collective-permute-start.2
  24.1 2.8 collective-permute-done.5
  27.6 5.9 %collective-permute-done.3 = bf16[96,1920]{1,0:T(8,128)(2,1)} collective-permute-done((bf16[96,1920]{1,0:T(8,128)(2,1)S(1)}, bf16[96,1920]{1,0:T(8,128)(2,1)}, u32[]{:S(2)}, u32[]{:S(2)}) %collective-permute-start.3) | collective-permute-done | bytes 368672 | tf_op jit(solution)/shard_map/ppermute | solution.py:639
  36.2 2.1 collective-permute-start.15
  40.4 3.3 maximum_select_fusion
  45.7 2.0 collective-permute-start.11
  49.4 1.9 collective-permute-start.17
  66.2 4.8 maximum_select_fusion.1
  80.1 2.4 collective-permute-start.20
  82.5 3.5 collective-permute-start.22
  86.6 5.1 %collective-permute-done.22 = bf16[96,1536]{1,0:T(8,128)(2,1)S(1)} collective-permute-done((bf16[96,1536]{1,0:T(8,128)(2,1)}, bf16[96,1536]{1,0:T(8,128)(2,1)S(1)}, u32[]{:S(2)}, u32[]{:S(2)}) %collective-permute-start.22) | collective-permute-done | bytes 294944 | tf_op jit(solution)/shard_map/ppermute | solution.py:639
  91.8 3.2 collective-permute-start.23
  95.7 2.1 collective-permute-start.30
  97.8 2.5 collective-permute-done.23
  102.7 2.0 collective-permute-done.27.refs_1_
  104.7 2.0 collective-permute-start.25
  108.4 3.6 collective-permute-start.24
  112.0 7.4 %collective-permute-done.29.refs_5_ = bf16[4,96,896]{2,1,0:T(8,128)(2,1)S(1)} collective-permute-done((bf16[4,96,896]{2,1,0:T(8,128)(2,1)S(1)}, bf16[4,96,896]{2,1,0:T(8,128)(2,1)S(1)}, u32[]{:S(2)}, u32[]{:S(2)}) %collective-permute-start.29) | collective-permute-done | bytes 688160 | tf_op jit(solution)/shard_map/ppermute | solution.py:639
  119.4 5.8 %collective-permute-done.30.refs_7_ = bf16[4,96,1024]{2,1,0:T(8,128)(2,1)S(1)} collective-permute-done((bf16[4,96,1024]{2,1,0:T(8,128)(2,1)S(1)}, bf16[4,96,1024]{2,1,0:T(8,128)(2,1)S(1)}, u32[]{:S(2)}, u32[]{:S(2)}) %collective-permute-start.30) | collective-permute-done | bytes 786464 | tf_op jit(solution)/shard_map/ppermute | solution.py:639
  125.2 2.4 join.3
  127.6 8.9 %fusion.62.xbc.halo.prev = f32[1040,1920]{1,0:T(8,128)} fusion(bf16[1040,1536]{1,0:T(8,128)(2,1)S(1)} %copy-done.9, bf16[1536,1920]{1,0:T(8,128)(2,1)S(1)} %join.3), kind=kOutput, calls=%fused_computation.248 | convolution fusion | flops 6134169600 | bytes 17080320 | tf_op jit(solution)/shard_map/dot_general | solution.py:37
  136.6 2.1 collective-permute-start.34
  139.4 14.2 %block_states.1 = (f32[1024,1536]{1,0:T(8,128)S(1)}, f32[1024,256]{1,0:T(8,128)S(1)}, f32[1024,256]{1,0:T(8,128)S(1)}, f32[1024,128]{1,0:T(8,128)S(1)}, f32[1024...) custom-call(f32[1040,1920]{1,0:T(8,128)} %fusion.62.xbc.halo.prev, ...), custom_call_target="tpu_custom_call" | custom-call | flops 402653184 | bytes 17432576 | tf_op jit(solution)/shard_map/block_states/pallas_call | solution.py:183
  153.6 2.6 copy-done.1
  156.3 3.5 collective-permute-start.31
  159.8 2.0 collective-permute-start.32
  161.8 13.3 %inner_part.1.yin = f32[1024,1536]{1,0:T(8,128)S(1)} custom-call(f32[1024,256]{1,0:T(8,128)S(1)} %get-tuple-element.301.s, f32[1024,128]{1,0:T(8,128)S(1)} %get-tuple-element.302.ld, f32[4,32,256]{2,1,0:T(8,128)S(1)} %get-tuple-element.303.ldt, f32[1024,128]{1,0:T(8,128)S(1)} %get-tuple-element.304.dt, f32[1024,1536]{1,0:T(8,128)} %copy-done.1, ...), custom_call_target="tpu_custom_call" | custom-call | flops 3221225472 | bytes 16777216 | tf_op jit(solution)/shard_map/inner_part/pallas_call | solution.py:256
  176.7 6.9 %fusion.11.z = f32[1024,1536]{1,0:T(8,128)} fusion(bf16[1536,1536]{1,0:T(8,128)(2,1)S(1)} %join.4, bf16[1040,1536]{1,0:T(8,128)(2,1)S(1)} %copy-done.9), kind=kOutput, calls=%fused_computation.31 | convolution fusion | flops 4831838208 | bytes 14155776 | tf_op jit(solution)/shard_map/dot_general | solution.py:37
  183.9 7.7 %gate_part.1 = (f32[1024,1536]{1,0:T(8,128)S(1)}, f32[1024,128]{1,0:T(8,128)}) custom-call(f32[1024,1536]{1,0:T(8,128)S(1)} %inner_part.1.yin, f32[1024,256]{1,0:T(8,128)S(1)} %get-tuple-element.310.bc, bf16[4,128,1536]{2,1,0:T(8,128)(2,1)S(1)} %bitcast.175, f32[1024,128]{1,0:T(8,128)S(1)} %get-tuple-element.302.ld, ...), custom_call_target="tpu_custom_call", output_to_operand_aliasing={{0}: (0, {})} | custom-call | flops 402653184 | bytes 18874368 | tf_op jit(solution)/shard_map/gate_part/pallas_call | solution.py:295
  191.6 2.6 copy-done
  198.0 5.9 %multiply_multiply_fusion.exact = f32[1024,1536]{1,0:T(8,128)S(1)} fusion(f32[1024,1536]{1,0:T(8,128)} %copy-done, f32[1024,1536]{1,0:T(8,128)} %fusion.11.z, f32[1536]{0:T(1024)S(1)} %slice_reduce_fusion.1, f32[1024]{0:T(1024)S(1)} %fusion.37), kind=kLoop, calls=%fused_computation.5 | loop fusion | flops 11010048 | bytes 18884608 | tf_op jit(solution)/shard_map/mul | solution.py:1016
  203.9 5.4 %convolution_convert_fusion.1.refs_0_ = bf16[1536,1536]{1,0:T(8,128)(2,1)S(1)} fusion(bf16[1024,1536]{1,0:T(8,128)(2,1)S(1)} %bitcast.183, f32[1024,1536]{1,0:T(8,128)S(1)} %multiply_multiply_fusion.exact), kind=kOutput, calls=%fused_computation.1 | convolution fusion | flops 4835770368 | bytes 14155776 | tf_op jit(solution)/shard_map/dot_general | solution.py:45
  212.4 12.5 %collective-permute-done.38.refs_3_ = bf16[8,96,768]{2,1,0:T(8,128)(2,1)S(1)} collective-permute-done((bf16[8,96,768]{2,1,0:T(8,128)(2,1)}, bf16[8,96,768]{2,1,0:T(8,128)(2,1)S(1)}, u32[]{:S(2)}, u32[]{:S(2)}) %collective-permute-start.38) | collective-permute-done | bytes 1179680 | tf_op jit(solution)/shard_map/ppermute | solution.py:639
  224.9 2.6 join.5.w
  227.6 5.0 fusion.15
  235.7 9.0 %out_back.1 = (f32[1024,1536]{1,0:T(8,128)}, f32[1024,128]{1,0:T(8,128)S(1)}) custom-call(bf16[1024,1536]{1,0:T(8,128)(2,1)S(1)} %bitcast.184, bf16[1536,1536]{1,0:T(8,128)(2,1)S(1)} %join.5.w, f32[1024,1536]{1,0:T(8,128)} %copy-done.39), custom_call_target="tpu_custom_call" | custom-call | flops 4831838208 | bytes 20447232 | tf_op jit(solution)/shard_map/out_back/pallas_call | solution.py:326
  245.3 2.7 add_convert_fusion.4
  251.1 14.9 %gate_back.1 = (bf16[1024,1536]{1,0:T(8,128)(2,1)S(1)}, bf16[1024,1536]{1,0:T(8,128)(2,1)S(1)}, f32[1024,128]{1,0:T(8,128)S(1)}, f32[2,128,1536]{2,1,0:T(8,128)S...) custom-call(f32[1024,1536]{1,0:T(8,128)} %copy-done, ...), custom_call_target="tpu_custom_call" | custom-call | flops 1610612736 | bytes 37748736 | tf_op jit(solution)/shard_map/gate_back/pallas_call | solution.py:394
  268.9 5.4 %convolution_convert_fusion.refs_0_ = bf16[1536,1536]{1,0:T(8,128)(2,1)S(1)} fusion(bf16[1024,1536]{1,0:T(8,128)(2,1)S(1)} %get-tuple-element.339, bf16[1040,1536]{1,0:T(8,128)(2,1)S(1)} %copy-done.10), kind=kOutput, calls=%fused_computation | convolution fusion | flops 4834197504 | bytes 11010048 | tf_op jit(solution)/shard_map/dot_general | solution.py:45
  276.9 2.7 collective-permute-start.44
  282.7 21.0 %inner_back.1 = (f32[1024,1536]{1,0:T(8,128)S(1)}, f32[1024,128]{1,0:T(8,128)S(1)}, f32[1024,256]{1,0:T(8,128)S(1)}) custom-call(f32[1024,256]{1,0:T(8,128)S(1)} %copy-done.19, f32[1024,256]{1,0:T(8,128)S(1)} %get-tuple-element.310.bc, f32[1024,128]{1,0:T(8,128)S(1)} %get-tuple-element.302.ld, f32[4,32,256]{2,1,0:T(8,128)S(1)} %copy-done.27, ...), custom_call_target="tpu_custom_call" | custom-call | flops 6442450944 | bytes 16777216 | tf_op jit(solution)/shard_map/inner_back/pallas_call | solution.py:476
  303.6 2.6 copy-done.5
  307.5 6.5 %collective-permute-done.44 = bf16[8,96,768]{2,1,0:T(8,128)(2,1)S(1)} collective-permute-done((bf16[8,96,768]{2,1,0:T(8,128)(2,1)S(1)}, bf16[8,96,768]{2,1,0:T(8,128)(2,1)S(1)}, u32[]{:S(2)}, u32[]{:S(2)}) %collective-permute-start.44) | collective-permute-done | bytes 1179680 | tf_op jit(solution)/shard_map/ppermute | solution.py:639
  314.0 2.3 add_convert_fusion.2
  319.0 35.1 %conv_back.1 = (bf16[1040,1920]{1,0:T(8,128)(2,1)}, f32[8,1792]{1,0:T(8,128)}, f32[8,128]{1,0:T(8,128)}) custom-call(f32[1040,1920]{1,0:T(8,128)} %fusion.62.xbc.halo.prev, f32[1040,1920]{1,0:T(8,128)} %fusion.62.xbc.halo.prev, f32[1024,1536]{1,0:T(8,128)} %copy-done.1, f32[1024,1536]{1,0:T(8,128)} %copy-done.5, f32[1024,128]{1,0:T(8,128)} %copy-done.24, ...), custom_call_target="tpu_custom_call" | custom-call | flops 1207959552 | bytes 28311552 | tf_op jit(solution)/shard_map/conv_back/pallas_call | solution.py:600
  359.1 8.8 %convolution_convert_fusion.2.refs_0_ = bf16[1536,1920]{1,0:T(8,128)(2,1)S(1)} fusion(bf16[1040,1536]{1,0:T(8,128)(2,1)S(1)} %copy-done.11, bf16[1040,1920]{1,0:T(8,128)(2,1)S(1)} %copy-done.66), kind=kOutput, calls=%fused_computation.2 | convolution fusion | flops 6137118720 | bytes 13086720 | tf_op jit(solution)/shard_map/dot_general | solution.py:45
  374.8 8.9 %fusion.63 = f32[1040,1536]{1,0:T(8,128)} fusion(bf16[1040,1920]{1,0:T(8,128)(2,1)S(1)} %copy-done.66, bf16[1536,1920]{1,0:T(8,128)(2,1)S(1)} %bitcast.180), kind=kOutput, calls=%fused_computation.249 | convolution fusion | flops 6134169600 | bytes 16281600 | tf_op jit(solution)/shard_map/dot_general | solution.py:41
  387.8 7.2 %slice_add_fusion = f32[1024,1536]{1,0:T(8,128)S(1)} fusion(f32[1040,1536]{1,0:T(8,128)} %fusion.63, bf16[1024,1536]{1,0:T(8,128)(2,1)S(1)} %copy-done.30, bf16[1536,1536]{1,0:T(8,128)(2,1)S(1)} %bitcast.182), kind=kOutput, calls=%fused_computation.3 | convolution fusion | flops 4833411072 | bytes 20447232 | tf_op jit(solution)/shard_map/dot_general | solution.py:41
  395.0 3.0 collective-permute-start.51
  398.0 7.1 %collective-permute-done.51 = bf16[96,1536]{1,0:T(8,128)(2,1)S(1)} collective-permute-done((bf16[96,1536]{1,0:T(8,128)(2,1)S(1)}, bf16[96,1536]{1,0:T(8,128)(2,1)S(1)}, u32[]{:S(2)}, u32[]{:S(2)}) %collective-permute-start.51) | collective-permute-done | bytes 294944 | tf_op jit(solution)/shard_map/ppermute | solution.py:639
  407.9 2.6 copy-done.33
  411.9 7.6 %collective-permute-start.61 = (bf16[2,256,1536]{2,1,0:T(8,128)(2,1)}, bf16[2,256,1536]{2,1,0:T(8,128)(2,1)}, u32[]{:S(2)}, u32[]{:S(2)}) collective-permute-start(bf16[2,256,1536]{2,1,0:T(8,128)(2,1)} %fusion.14), channel_id=1, source_target_pairs={{0,1},{1,0},{2,3},{3,2},{4,5},{5,4},{6,7},{7,6},{8,9},{9,8},{10,11... | collective-permute-start | bytes 4718600 | tf_op jit(solution)/shard_map/ppermute | solution.py:832
  419.6 4.8 fusion.8
  425.4 2.6 collective-permute-start.59
  429.6 2.8 fusion.2
  432.4 4.3 fusion.5
  436.7 16.1 %collective-permute-done.56 = bf16[2,96,896]{2,1,0:T(8,128)(2,1)S(1)} collective-permute-done((bf16[2,96,896]{2,1,0:T(8,128)(2,1)S(1)}, bf16[2,96,896]{2,1,0:T(8,128)(2,1)S(1)}, u32[]{:S(2)}, u32[]{:S(2)}) %collective-permute-start.56) | collective-permute-done | bytes 344096 | tf_op jit(solution)/shard_map/ppermute | solution.py:639
  460.0 4.7 collective-permute-done.66
  466.4 2.6 collective-permute-done.67
  470.6 2.2 collective-permute-start.69
  472.8 10.1 %collective-permute-done.69 = f32[8,1792]{1,0:T(8,128)S(1)} collective-permute-done((f32[8,1792]{1,0:T(8,128)S(1)}, f32[8,1792]{1,0:T(8,128)S(1)}, u32[]{:S(2)}, u32[]{:S(2)}) %collective-permute-start.69) | collective-permute-done | bytes 57376 | tf_op jit(solution)/shard_map/ppermute | solution.py:832
  484.5 2.3 collective-permute-start.72
  486.8 10.6 %collective-permute-done.72 = f32[8,1792]{1,0:T(8,128)S(1)} collective-permute-done((f32[8,1792]{1,0:T(8,128)S(1)}, f32[8,1792]{1,0:T(8,128)S(1)}, u32[]{:S(2)}, u32[]{:S(2)}) %collective-permute-start.72) | collective-permute-done | bytes 57376 | tf_op jit(solution)/shard_map/ppermute | solution.py:832
  (424 shorter events, 127.4 us)
Async XLA Ops:
  2.4 9.9 %collective-permute-start.1 = (bf16[664]{0:T(1024)(128)(2,1)S(1)}, bf16[664]{0:T(1024)(128)(2,1)S(1)}, u32[]{:S(2)}, u32[]{:S(2)}) collective-permute-start(bf16[664]{0:T(1024)(128)(2,1)S(1)} %pad_maximum_fusion.17), channel_id=1, source_target_pairs={{0,16},{16,0},{1,17},{17,1},{2,18},{18,2},{3,19},{19,3},{4,20},{20... | collective-permute-start | bytes 3992 | tf_op jit(solution)/shard_map/ppermute | solution.py:832
  10.1 7.8 %collective-permute-start = (bf16[48,3456]{1,0:T(8,128)(2,1)S(1)}, bf16[48,3456]{1,0:T(8,128)(2,1)S(1)}, u32[]{:S(2)}, u32[]{:S(2)}) collective-permute-start(bf16[48,3456]{1,0:T(8,128)(2,1)S(1)} %get-tuple-element.233), channel_id=1, source_target_pairs={{0,1},{1,0},{2,3},{3,2},{4,5},{5,4},{6,7},{7,6},{8,9},{9,8},{10,11... | collective-permute-start | bytes 995336 | tf_op jit(solution)/shard_map/ppermute | solution.py:832
  11.6 21.9 %collective-permute-start.9 = (bf16[2,256,1536]{2,1,0:T(8,128)(2,1)}, bf16[2,256,1536]{2,1,0:T(8,128)(2,1)}, u32[]{:S(2)}, u32[]{:S(2)}) collective-permute-start(bf16[2,256,1536]{2,1,0:T(8,128)(2,1)} %bitcast.188), channel_id=1, source_target_pairs={{0,1},{1,0},{2,3},{3,2},{4,5},{5,4},{6,7},{7,6},{8,9},{9,8},{10,11... | collective-permute-start | bytes 4718600 | tf_op jit(solution)/shard_map/ppermute | solution.py:832
  11.7 21.9 %collective-permute-start.8 = (bf16[2,256,1536]{2,1,0:T(8,128)(2,1)S(1)}, bf16[2,256,1536]{2,1,0:T(8,128)(2,1)}, u32[]{:S(2)}, u32[]{:S(2)}) collective-permute-start(bf16[2,256,1536]{2,1,0:T(8,128)(2,1)S(1)} %bitcast.186), channel_id=1, source_target_pairs={{0,1},{1,0},{2,3},{3,2},{4,5},{5,4},{6,7},{7,6},{8,9},{9,8},{10,11... | collective-permute-start | bytes 4718600 | tf_op jit(solution)/shard_map/ppermute | solution.py:832
  16.2 7.2 %collective-permute-start.6 = (bf16[1,96,768]{2,1,0:T(8,128)(2,1)S(1)}, bf16[1,96,768]{2,1,0:T(8,128)(2,1)S(1)}, u32[]{:S(2)}, u32[]{:S(2)}) collective-permute-start(bf16[1,96,768]{2,1,0:T(8,128)(2,1)S(1)} %get-tuple-element.493), channel_id=1, source_target_pairs={{0,4},{4,0},{1,5},{5,1},{2,6},{6,2},{3,7},{7,3},{8,12},{12,8},{9,1... | collective-permute-start | bytes 442376 | tf_op jit(solution)/shard_map/ppermute | solution.py:639
  18.5 15.0 %collective-permute-start.3 = (bf16[96,1920]{1,0:T(8,128)(2,1)S(1)}, bf16[96,1920]{1,0:T(8,128)(2,1)}, u32[]{:S(2)}, u32[]{:S(2)}) collective-permute-start(bf16[96,1920]{1,0:T(8,128)(2,1)S(1)} %slice.300), channel_id=1, source_target_pairs={{0,8},{8,16},{16,24},{24,0},{1,9},{9,17},{17,25},{25,1},{2,10},{10... | collective-permute-start | bytes 1105928 | tf_op jit(solution)/shard_map/ppermute | solution.py:639
  33.5 23.0 %collective-permute-start.10 = (bf16[96,1920]{1,0:T(8,128)(2,1)}, bf16[96,1920]{1,0:T(8,128)(2,1)}, u32[]{:S(2)}, u32[]{:S(2)}) collective-permute-start(bf16[96,1920]{1,0:T(8,128)(2,1)} %collective-permute-done.3), channel_id=1, source_target_pairs={{0,8},{8,16},{16,24},{24,0},{1,9},{9,17},{17,25},{25,1},{2,10},{10... | collective-permute-start | bytes 1105928 | tf_op jit(solution)/shard_map/ppermute | solution.py:639
  36.2 8.2 %collective-permute-start.15 = (bf16[2,2,2,664]{3,1,0,2:T(2,128)(2,1)S(1)}, bf16[2,2,2,664]{3,1,0,2:T(2,128)(2,1)S(1)}, u32[]{:S(2)}, u32[]{:S(2)}) collective-permute-start(bf16[2,2,2,664]{3,1,0,2:T(2,128)(2,1)S(1)} %broadcast_select_fusion.3), channel_id=1, source_target_pairs={{0,2},{2,0},{1,3},{3,1},{4,6},{6,4},{5,7},{7,5},{8,10},{10,8},{9,1... | collective-permute-start | bytes 31880 | tf_op jit(solution)/shard_map/ppermute | solution.py:832
  38.4 11.0 %collective-permute-start.13 = (bf16[2,96,768]{2,1,0:T(8,128)(2,1)}, bf16[2,96,768]{2,1,0:T(8,128)(2,1)}, u32[]{:S(2)}, u32[]{:S(2)}) collective-permute-start(bf16[2,96,768]{2,1,0:T(8,128)(2,1)} %pad_maximum_fusion.14), channel_id=1, source_target_pairs={{0,4},{4,0},{1,5},{5,1},{2,6},{6,2},{3,7},{7,3},{8,12},{12,8},{9,1... | collective-permute-start | bytes 884744 | tf_op jit(solution)/shard_map/ppermute | solution.py:639
  39.9 13.3 %collective-permute-start.14 = (bf16[2,96,768]{2,1,0:T(8,128)(2,1)}, bf16[2,96,768]{2,1,0:T(8,128)(2,1)}, u32[]{:S(2)}, u32[]{:S(2)}) collective-permute-start(bf16[2,96,768]{2,1,0:T(8,128)(2,1)} %pad_maximum_fusion.15), channel_id=1, source_target_pairs={{0,2},{2,0},{1,3},{3,1},{4,6},{6,4},{5,7},{7,5},{8,10},{10,8},{9,1... | collective-permute-start | bytes 884744 | tf_op jit(solution)/shard_map/ppermute | solution.py:639
  40.4 16.1 %collective-permute-start.12 = (bf16[2,96,1024]{2,1,0:T(8,128)(2,1)}, bf16[2,96,1024]{2,1,0:T(8,128)(2,1)}, u32[]{:S(2)}, u32[]{:S(2)}) collective-permute-start(bf16[2,96,1024]{2,1,0:T(8,128)(2,1)} %pad_maximum_fusion.11), channel_id=1, source_target_pairs={{0,4},{4,0},{1,5},{5,1},{2,6},{6,2},{3,7},{7,3},{8,12},{12,8},{9,1... | collective-permute-start | bytes 1179656 | tf_op jit(solution)/shard_map/ppermute | solution.py:639
  45.7 10.8 %collective-permute-start.11 = (bf16[2,96,896]{2,1,0:T(8,128)(2,1)S(1)}, bf16[2,96,896]{2,1,0:T(8,128)(2,1)}, u32[]{:S(2)}, u32[]{:S(2)}) collective-permute-start(bf16[2,96,896]{2,1,0:T(8,128)(2,1)S(1)} %pad_maximum_fusion.13), channel_id=1, source_target_pairs={{0,2},{2,0},{1,3},{3,1},{4,6},{6,4},{5,7},{7,5},{8,10},{10,8},{9,1... | collective-permute-start | bytes 1032200 | tf_op jit(solution)/shard_map/ppermute | solution.py:639
  49.4 7.2 %collective-permute-start.17 = (bf16[2,8,1536]{2,1,0:T(8,128)(2,1)}, bf16[2,8,1536]{2,1,0:T(8,128)(2,1)S(1)}, u32[]{:S(2)}, u32[]{:S(2)}) collective-permute-start(bf16[2,8,1536]{2,1,0:T(8,128)(2,1)} %slice_bitcast_fusion.8), channel_id=1, source_target_pairs={{0,2},{1,3},{4,6},{5,7},{8,10},{9,11},{12,14},{13,15},{16,18},{17,... | collective-permute-start | bytes 147464 | tf_op jit(solution)/shard_map/ppermute | solution.py:905
  56.6 19.8 %collective-permute-start.19 = (bf16[96,1536]{1,0:T(8,128)(2,1)}, bf16[96,1536]{1,0:T(8,128)(2,1)}, u32[]{:S(2)}, u32[]{:S(2)}) collective-permute-start(bf16[96,1536]{1,0:T(8,128)(2,1)} %slice.301), channel_id=1, source_target_pairs={{0,8},{8,16},{16,24},{24,0},{1,9},{9,17},{17,25},{25,1},{2,10},{10... | collective-permute-start | bytes 884744 | tf_op jit(solution)/shard_map/ppermute | solution.py:639
  56.6 19.7 %collective-permute-start.18 = (bf16[96,1920]{1,0:T(8,128)(2,1)}, bf16[96,1920]{1,0:T(8,128)(2,1)}, u32[]{:S(2)}, u32[]{:S(2)}) collective-permute-start(bf16[96,1920]{1,0:T(8,128)(2,1)} %collective-permute-done.10), channel_id=1, source_target_pairs={{0,8},{8,16},{16,24},{24,0},{1,9},{9,17},{17,25},{25,1},{2,10},{10... | collective-permute-start | bytes 1105928 | tf_op jit(solution)/shard_map/ppermute | solution.py:639
  77.5 14.3 %collective-permute-start.21 = (bf16[2,96,1024]{2,1,0:T(8,128)(2,1)S(1)}, bf16[2,96,1024]{2,1,0:T(8,128)(2,1)S(1)}, u32[]{:S(2)}, u32[]{:S(2)}) collective-permute-start(bf16[2,96,1024]{2,1,0:T(8,128)(2,1)S(1)} %pad_maximum_fusion.10), channel_id=1, source_target_pairs={{0,4},{4,0},{1,5},{5,1},{2,6},{6,2},{3,7},{7,3},{8,12},{12,8},{9,1... | collective-permute-start | bytes 1179656 | tf_op jit(solution)/shard_map/ppermute | solution.py:639
  80.1 11.7 %collective-permute-start.20 = (bf16[2,96,896]{2,1,0:T(8,128)(2,1)S(1)}, bf16[2,96,896]{2,1,0:T(8,128)(2,1)S(1)}, u32[]{:S(2)}, u32[]{:S(2)}) collective-permute-start(bf16[2,96,896]{2,1,0:T(8,128)(2,1)S(1)} %pad_maximum_fusion.12), channel_id=1, source_target_pairs={{0,2},{2,0},{1,3},{3,1},{4,6},{6,4},{5,7},{7,5},{8,10},{10,8},{9,1... | collective-permute-start | bytes 1032200 | tf_op jit(solution)/shard_map/ppermute | solution.py:639
  82.5 9.2 %collective-permute-start.22 = (bf16[96,1536]{1,0:T(8,128)(2,1)}, bf16[96,1536]{1,0:T(8,128)(2,1)S(1)}, u32[]{:S(2)}, u32[]{:S(2)}) collective-permute-start(bf16[96,1536]{1,0:T(8,128)(2,1)} %collective-permute-done.19), channel_id=1, source_target_pairs={{0,8},{8,16},{16,24},{24,0},{1,9},{9,17},{17,25},{25,1},{2,10},{10... | collective-permute-start | bytes 884744 | tf_op jit(solution)/shard_map/ppermute | solution.py:639
  86.0 18.6 %collective-permute-start.27 = (bf16[4,96,896]{2,1,0:T(8,128)(2,1)}, bf16[4,96,896]{2,1,0:T(8,128)(2,1)S(1)}, u32[]{:S(2)}, u32[]{:S(2)}) collective-permute-start(bf16[4,96,896]{2,1,0:T(8,128)(2,1)} %constant_dynamic-update-slice_fusion.refs_0_), channel_id=1, source_target_pairs={{0,4},{4,0},{1,5},{5,1},{2,6},{6,2},{3,7},{7,3},{8,12},{12,8},{9,1... | collective-permute-start | bytes 2064392 | tf_op jit(solution)/shard_map/ppermute | solution.py:639
  86.6 21.8 %collective-permute-start.28 = (bf16[4,96,1024]{2,1,0:T(8,128)(2,1)}, bf16[4,96,1024]{2,1,0:T(8,128)(2,1)S(1)}, u32[]{:S(2)}, u32[]{:S(2)}) collective-permute-start(bf16[4,96,1024]{2,1,0:T(8,128)(2,1)} %constant_dynamic-update-slice_fusion.2.refs_2_), channel_id=1, source_target_pairs={{0,2},{2,0},{1,3},{3,1},{4,6},{6,4},{5,7},{7,5},{8,10},{10,8},{9,1... | collective-permute-start | bytes 2359304 | tf_op jit(solution)/shard_map/ppermute | solution.py:639
  91.8 8.5 %collective-permute-start.23 = (bf16[96,1536]{1,0:T(8,128)(2,1)S(1)}, bf16[96,1536]{1,0:T(8,128)(2,1)S(1)}, u32[]{:S(2)}, u32[]{:S(2)}) collective-permute-start(bf16[96,1536]{1,0:T(8,128)(2,1)S(1)} %collective-permute-done.22), channel_id=1, source_target_pairs={{0,8},{8,16},{16,24},{24,0},{1,9},{9,17},{17,25},{25,1},{2,10},{10... | collective-permute-start | bytes 884744 | tf_op jit(solution)/shard_map/ppermute | solution.py:639
  95.1 24.4 %collective-permute-start.29 = (bf16[4,96,896]{2,1,0:T(8,128)(2,1)S(1)}, bf16[4,96,896]{2,1,0:T(8,128)(2,1)S(1)}, u32[]{:S(2)}, u32[]{:S(2)}) collective-permute-start(bf16[4,96,896]{2,1,0:T(8,128)(2,1)S(1)} %constant_dynamic-update-slice_fusion.4.refs_4_), channel_id=1, source_target_pairs={{0,4},{4,0},{1,5},{5,1},{2,6},{6,2},{3,7},{7,3},{8,12},{12,8},{9,1... | collective-permute-start | bytes 2064392 | tf_op jit(solution)/shard_map/ppermute | solution.py:639
  95.7 29.5 %collective-permute-start.30 = (bf16[4,96,1024]{2,1,0:T(8,128)(2,1)S(1)}, bf16[4,96,1024]{2,1,0:T(8,128)(2,1)S(1)}, u32[]{:S(2)}, u32[]{:S(2)}) collective-permute-start(bf16[4,96,1024]{2,1,0:T(8,128)(2,1)S(1)} %constant_dynamic-update-slice_fusion.6.refs_6_), channel_id=1, source_target_pairs={{0,2},{2,0},{1,3},{3,1},{4,6},{6,4},{5,7},{7,5},{8,10},{10,8},{9,1... | collective-permute-start | bytes 2359304 | tf_op jit(solution)/shard_map/ppermute | solution.py:639
  101.7 34.9 %collective-permute-start.26 = (bf16[4,96,768]{2,1,0:T(8,128)(2,1)S(1)}, bf16[4,96,768]{2,1,0:T(8,128)(2,1)S(1)}, u32[]{:S(2)}, u32[]{:S(2)}) collective-permute-start(bf16[4,96,768]{2,1,0:T(8,128)(2,1)S(1)} %get-tuple-element.292), channel_id=1, source_target_pairs={{0,4},{4,0},{1,5},{5,1},{2,6},{6,2},{3,7},{7,3},{8,12},{12,8},{9,1... | collective-permute-start | bytes 1769480 | tf_op jit(solution)/shard_map/ppermute | solution.py:639
  104.7 31.9 %collective-permute-start.25 = (bf16[4,96,768]{2,1,0:T(8,128)(2,1)S(1)}, bf16[4,96,768]{2,1,0:T(8,128)(2,1)S(1)}, u32[]{:S(2)}, u32[]{:S(2)}) collective-permute-start(bf16[4,96,768]{2,1,0:T(8,128)(2,1)S(1)} %get-tuple-element.290), channel_id=1, source_target_pairs={{0,2},{2,0},{1,3},{3,1},{4,6},{6,4},{5,7},{7,5},{8,10},{10,8},{9,1... | collective-permute-start | bytes 1769480 | tf_op jit(solution)/shard_map/ppermute | solution.py:639
  108.4 47.9 %collective-permute-start.24 = (bf16[8,96,768]{2,1,0:T(8,128)(2,1)S(1)}, bf16[8,96,768]{2,1,0:T(8,128)(2,1)}, u32[]{:S(2)}, u32[]{:S(2)}) collective-permute-start(bf16[8,96,768]{2,1,0:T(8,128)(2,1)S(1)} %constant_dynamic-update-slice_fusion.8.refs_0_), channel_id=1, source_target_pairs={{0,8},{8,16},{16,24},{24,0},{1,9},{9,17},{17,25},{25,1},{2,10},{10... | collective-permute-start | bytes 3538952 | tf_op jit(solution)/shard_map/ppermute | solution.py:639
  136.6 38.5 %collective-permute-start.34 = (bf16[8,96,768]{2,1,0:T(8,128)(2,1)S(1)}, bf16[8,96,768]{2,1,0:T(8,128)(2,1)S(1)}, u32[]{:S(2)}, u32[]{:S(2)}) collective-permute-start(bf16[8,96,768]{2,1,0:T(8,128)(2,1)S(1)} %constant_dynamic-update-slice_fusion.12.refs_2_), channel_id=1, source_target_pairs={{0,2},{2,0},{1,3},{3,1},{4,6},{6,4},{5,7},{7,5},{8,10},{10,8},{9,1... | collective-permute-start | bytes 3538952 | tf_op jit(solution)/shard_map/ppermute | solution.py:639
  138.8 36.3 %collective-permute-start.33 = (bf16[8,96,768]{2,1,0:T(8,128)(2,1)S(1)}, bf16[8,96,768]{2,1,0:T(8,128)(2,1)S(1)}, u32[]{:S(2)}, u32[]{:S(2)}) collective-permute-start(bf16[8,96,768]{2,1,0:T(8,128)(2,1)S(1)} %constant_dynamic-update-slice_fusion.10.refs_0_), channel_id=1, source_target_pairs={{0,4},{4,0},{1,5},{5,1},{2,6},{6,2},{3,7},{7,3},{8,12},{12,8},{9,1... | collective-permute-start | bytes 3538952 | tf_op jit(solution)/shard_map/ppermute | solution.py:639
  156.3 27.6 %collective-permute-start.31 = (bf16[8,96,768]{2,1,0:T(8,128)(2,1)}, bf16[8,96,768]{2,1,0:T(8,128)(2,1)}, u32[]{:S(2)}, u32[]{:S(2)}) collective-permute-start(bf16[8,96,768]{2,1,0:T(8,128)(2,1)} %collective-permute-done.24.refs_1_), channel_id=1, source_target_pairs={{0,8},{8,16},{16,24},{24,0},{1,9},{9,17},{17,25},{25,1},{2,10},{10... | collective-permute-start | bytes 3538952 | tf_op jit(solution)/shard_map/ppermute | solution.py:639
  159.8 23.7 %collective-permute-start.32 = (bf16[2,128,1536]{2,1,0:T(8,128)(2,1)}, bf16[2,128,1536]{2,1,0:T(8,128)(2,1)S(1)}, u32[]{:S(2)}, u32[]{:S(2)}) collective-permute-start(bf16[2,128,1536]{2,1,0:T(8,128)(2,1)} %get-tuple-element.311), channel_id=1, source_target_pairs={{0,2},{1,3},{4,6},{5,7},{8,10},{9,11},{12,14},{13,15},{16,18},{17,... | collective-permute-start | bytes 2359304 | tf_op jit(solution)/shard_map/ppermute | solution.py:996
  194.3 30.7 %collective-permute-start.38 = (bf16[8,96,768]{2,1,0:T(8,128)(2,1)}, bf16[8,96,768]{2,1,0:T(8,128)(2,1)S(1)}, u32[]{:S(2)}, u32[]{:S(2)}) collective-permute-start(bf16[8,96,768]{2,1,0:T(8,128)(2,1)} %collective-permute-done.31.refs_2_), channel_id=1, source_target_pairs={{0,8},{8,16},{16,24},{24,0},{1,9},{9,17},{17,25},{25,1},{2,10},{10... | collective-permute-start | bytes 3538952 | tf_op jit(solution)/shard_map/ppermute | solution.py:639
  210.8 33.9 %collective-permute-start.36 = (bf16[8,96,768]{2,1,0:T(8,128)(2,1)S(1)}, bf16[8,96,768]{2,1,0:T(8,128)(2,1)}, u32[]{:S(2)}, u32[]{:S(2)}) collective-permute-start(bf16[8,96,768]{2,1,0:T(8,128)(2,1)S(1)} %get-tuple-element.324), channel_id=1, source_target_pairs={{0,4},{4,0},{1,5},{5,1},{2,6},{6,2},{3,7},{7,3},{8,12},{12,8},{9,1... | collective-permute-start | bytes 3538952 | tf_op jit(solution)/shard_map/ppermute | solution.py:639
  212.4 32.3 %collective-permute-start.37 = (bf16[8,96,768]{2,1,0:T(8,128)(2,1)S(1)}, bf16[8,96,768]{2,1,0:T(8,128)(2,1)S(1)}, u32[]{:S(2)}, u32[]{:S(2)}) collective-permute-start(bf16[8,96,768]{2,1,0:T(8,128)(2,1)S(1)} %get-tuple-element.325), channel_id=1, source_target_pairs={{0,2},{2,0},{1,3},{3,1},{4,6},{6,4},{5,7},{7,5},{8,10},{10,8},{9,1... | collective-permute-start | bytes 3538952 | tf_op jit(solution)/shard_map/ppermute | solution.py:639
  235.7 183.9 %collective-permute-start.62 = (bf16[2,256,1536]{2,1,0:T(8,128)(2,1)}, bf16[2,256,1536]{2,1,0:T(8,128)(2,1)}, u32[]{:S(2)}, u32[]{:S(2)}) collective-permute-start(bf16[2,256,1536]{2,1,0:T(8,128)(2,1)} %fusion.13), channel_id=1, source_target_pairs={{0,1},{1,0},{2,3},{3,2},{4,5},{5,4},{6,7},{7,6},{8,9},{9,8},{10,11... | collective-permute-start | bytes 4718600 | tf_op jit(solution)/shard_map/ppermute | solution.py:832
  248.0 27.9 %collective-permute-start.39 = (bf16[4,96,768]{2,1,0:T(8,128)(2,1)}, bf16[4,96,768]{2,1,0:T(8,128)(2,1)S(1)}, u32[]{:S(2)}, u32[]{:S(2)}) collective-permute-start(bf16[4,96,768]{2,1,0:T(8,128)(2,1)} %get-tuple-element.463), channel_id=1, source_target_pairs={{0,2},{2,0},{1,3},{3,1},{4,6},{6,4},{5,7},{7,5},{8,10},{10,8},{9,1... | collective-permute-start | bytes 1769480 | tf_op jit(solution)/shard_map/ppermute | solution.py:639
  249.5 26.4 %collective-permute-start.40 = (bf16[4,96,768]{2,1,0:T(8,128)(2,1)}, bf16[4,96,768]{2,1,0:T(8,128)(2,1)S(1)}, u32[]{:S(2)}, u32[]{:S(2)}) collective-permute-start(bf16[4,96,768]{2,1,0:T(8,128)(2,1)} %get-tuple-element.461), channel_id=1, source_target_pairs={{0,4},{4,0},{1,5},{5,1},{2,6},{6,2},{3,7},{7,3},{8,12},{12,8},{9,1... | collective-permute-start | bytes 1769480 | tf_op jit(solution)/shard_map/ppermute | solution.py:639
  267.6 39.9 %collective-permute-start.45 = (bf16[2,128,1536]{2,1,0:T(8,128)(2,1)S(1)}, bf16[2,128,1536]{2,1,0:T(8,128)(2,1)S(1)}, u32[]{:S(2)}, u32[]{:S(2)}) collective-permute-start(bf16[2,128,1536]{2,1,0:T(8,128)(2,1)S(1)} %get-tuple-element.356), channel_id=1, source_target_pairs={{2,0},{3,1},{6,4},{7,5},{10,8},{11,9},{14,12},{15,13},{18,16},{19,... | collective-permute-start | bytes 2359304 | tf_op jit(solution)/shard_map/ppermute | solution.py:1045
  275.9 31.6 %collective-permute-start.43 = (bf16[8,96,768]{2,1,0:T(8,128)(2,1)S(1)}, bf16[8,96,768]{2,1,0:T(8,128)(2,1)}, u32[]{:S(2)}, u32[]{:S(2)}) collective-permute-start(bf16[8,96,768]{2,1,0:T(8,128)(2,1)S(1)} %get-tuple-element.351), channel_id=1, source_target_pairs={{0,4},{4,0},{1,5},{5,1},{2,6},{6,2},{3,7},{7,3},{8,12},{12,8},{9,1... | collective-permute-start | bytes 3538952 | tf_op jit(solution)/shard_map/ppermute | solution.py:639
  276.9 37.1 %collective-permute-start.44 = (bf16[8,96,768]{2,1,0:T(8,128)(2,1)S(1)}, bf16[8,96,768]{2,1,0:T(8,128)(2,1)S(1)}, u32[]{:S(2)}, u32[]{:S(2)}) collective-permute-start(bf16[8,96,768]{2,1,0:T(8,128)(2,1)S(1)} %get-tuple-element.352), channel_id=1, source_target_pairs={{0,2},{2,0},{1,3},{3,1},{4,6},{6,4},{5,7},{7,5},{8,10},{10,8},{9,1... | collective-permute-start | bytes 3538952 | tf_op jit(solution)/shard_map/ppermute | solution.py:639
  281.9 25.5 %collective-permute-start.42 = (bf16[96,1536]{1,0:T(8,128)(2,1)}, bf16[96,1536]{1,0:T(8,128)(2,1)}, u32[]{:S(2)}, u32[]{:S(2)}) collective-permute-start(bf16[96,1536]{1,0:T(8,128)(2,1)} %fusion.46), channel_id=1, source_target_pairs={{0,8},{8,16},{16,24},{24,0},{1,9},{9,17},{17,25},{25,1},{2,10},{10... | collective-permute-start | bytes 884744 | tf_op jit(solution)/shard_map/ppermute | solution.py:639
  316.3 39.3 %collective-permute-start.47 = (bf16[4,96,768]{2,1,0:T(8,128)(2,1)}, bf16[4,96,768]{2,1,0:T(8,128)(2,1)}, u32[]{:S(2)}, u32[]{:S(2)}) collective-permute-start(bf16[4,96,768]{2,1,0:T(8,128)(2,1)} %get-tuple-element.459), channel_id=1, source_target_pairs={{0,2},{2,0},{1,3},{3,1},{4,6},{6,4},{5,7},{7,5},{8,10},{10,8},{9,1... | collective-permute-start | bytes 1769480 | tf_op jit(solution)/shard_map/ppermute | solution.py:639
  317.4 38.3 %collective-permute-start.48 = (bf16[4,96,768]{2,1,0:T(8,128)(2,1)}, bf16[4,96,768]{2,1,0:T(8,128)(2,1)S(1)}, u32[]{:S(2)}, u32[]{:S(2)}) collective-permute-start(bf16[4,96,768]{2,1,0:T(8,128)(2,1)} %get-tuple-element.457), channel_id=1, source_target_pairs={{0,4},{4,0},{1,5},{5,1},{2,6},{6,2},{3,7},{7,3},{8,12},{12,8},{9,1... | collective-permute-start | bytes 1769480 | tf_op jit(solution)/shard_map/ppermute | solution.py:639
  318.9 36.7 %collective-permute-start.46 = (bf16[96,1536]{1,0:T(8,128)(2,1)S(1)}, bf16[96,1536]{1,0:T(8,128)(2,1)S(1)}, u32[]{:S(2)}, u32[]{:S(2)}) collective-permute-start(bf16[96,1536]{1,0:T(8,128)(2,1)S(1)} %fusion.34), channel_id=1, source_target_pairs={{0,8},{8,16},{16,24},{24,0},{1,9},{9,17},{17,25},{25,1},{2,10},{10... | collective-permute-start | bytes 884744 | tf_op jit(solution)/shard_map/ppermute | solution.py:639
  355.8 15.0 %collective-permute-start.49 = (bf16[96,1536]{1,0:T(8,128)(2,1)S(1)}, bf16[96,1536]{1,0:T(8,128)(2,1)S(1)}, u32[]{:S(2)}, u32[]{:S(2)}) collective-permute-start(bf16[96,1536]{1,0:T(8,128)(2,1)S(1)} %fusion.33), channel_id=1, source_target_pairs={{0,8},{8,16},{16,24},{24,0},{1,9},{9,17},{17,25},{25,1},{2,10},{10... | collective-permute-start | bytes 884744 | tf_op jit(solution)/shard_map/ppermute | solution.py:639
  357.4 14.0 %collective-permute-start.50 = (bf16[96,1536]{1,0:T(8,128)(2,1)S(1)}, bf16[96,1536]{1,0:T(8,128)(2,1)S(1)}, u32[]{:S(2)}, u32[]{:S(2)}) collective-permute-start(bf16[96,1536]{1,0:T(8,128)(2,1)S(1)} %fusion.47), channel_id=1, source_target_pairs={{0,8},{8,16},{16,24},{24,0},{1,9},{9,17},{17,25},{25,1},{2,10},{10... | collective-permute-start | bytes 884744 | tf_op jit(solution)/shard_map/ppermute | solution.py:639
  371.4 33.8 %collective-permute-start.52 = (bf16[4,96,896]{2,1,0:T(8,128)(2,1)S(1)}, bf16[4,96,896]{2,1,0:T(8,128)(2,1)S(1)}, u32[]{:S(2)}, u32[]{:S(2)}) collective-permute-start(bf16[4,96,896]{2,1,0:T(8,128)(2,1)S(1)} %get-tuple-element.398), channel_id=1, source_target_pairs={{0,4},{4,0},{1,5},{5,1},{2,6},{6,2},{3,7},{7,3},{8,12},{12,8},{9,1... | collective-permute-start | bytes 2064392 | tf_op jit(solution)/shard_map/ppermute | solution.py:639
  372.9 32.2 %collective-permute-start.53 = (bf16[4,96,1024]{2,1,0:T(8,128)(2,1)S(1)}, bf16[4,96,1024]{2,1,0:T(8,128)(2,1)S(1)}, u32[]{:S(2)}, u32[]{:S(2)}) collective-permute-start(bf16[4,96,1024]{2,1,0:T(8,128)(2,1)S(1)} %get-tuple-element.399), channel_id=1, source_target_pairs={{0,2},{2,0},{1,3},{3,1},{4,6},{6,4},{5,7},{7,5},{8,10},{10,8},{9,1... | collective-permute-start | bytes 2359304 | tf_op jit(solution)/shard_map/ppermute | solution.py:639
  384.6 10.4 %collective-permute-start.60 = (bf16[16,1536]{1,0:T(8,128)(2,1)S(1)}, bf16[16,1536]{1,0:T(8,128)(2,1)S(1)}, u32[]{:S(2)}, u32[]{:S(2)}) collective-permute-start(bf16[16,1536]{1,0:T(8,128)(2,1)S(1)} %slice.552), channel_id=1, source_target_pairs={{2,0},{3,1},{6,4},{7,5},{10,8},{11,9},{14,12},{15,13},{18,16},{19,... | collective-permute-start | bytes 147464 | tf_op jit(solution)/shard_map/ppermute | solution.py:1093
  387.0 18.1 %collective-permute-start.54 = (f32[96,1536]{1,0:T(8,128)S(1)}, f32[96,1536]{1,0:T(8,128)S(1)}, u32[]{:S(2)}, u32[]{:S(2)}) collective-permute-start(f32[96,1536]{1,0:T(8,128)S(1)} %bitcast_add_fusion.5), channel_id=1, source_target_pairs={{0,0},{1,16},{16,1},{17,17},{2,2},{3,18},{18,3},{19,19},{4,4},{5,2... | collective-permute-start | bytes 1769480 | tf_op jit(solution)/shard_map/ppermute | solution.py:1090
  395.0 10.2 %collective-permute-start.51 = (bf16[96,1536]{1,0:T(8,128)(2,1)S(1)}, bf16[96,1536]{1,0:T(8,128)(2,1)S(1)}, u32[]{:S(2)}, u32[]{:S(2)}) collective-permute-start(bf16[96,1536]{1,0:T(8,128)(2,1)S(1)} %fusion.32), channel_id=1, source_target_pairs={{0,8},{8,16},{16,24},{24,0},{1,9},{9,17},{17,25},{25,1},{2,10},{10... | collective-permute-start | bytes 884744 | tf_op jit(solution)/shard_map/ppermute | solution.py:639
  411.9 16.2 %collective-permute-start.61 = (bf16[2,256,1536]{2,1,0:T(8,128)(2,1)}, bf16[2,256,1536]{2,1,0:T(8,128)(2,1)}, u32[]{:S(2)}, u32[]{:S(2)}) collective-permute-start(bf16[2,256,1536]{2,1,0:T(8,128)(2,1)} %fusion.14), channel_id=1, source_target_pairs={{0,1},{1,0},{2,3},{3,2},{4,5},{5,4},{6,7},{7,6},{8,9},{9,8},{10,11... | collective-permute-start | bytes 4718600 | tf_op jit(solution)/shard_map/ppermute | solution.py:832
  424.5 12.3 %collective-permute-start.55 = (bf16[96,1536]{1,0:T(8,128)(2,1)S(1)}, bf16[96,1536]{1,0:T(8,128)(2,1)S(1)}, u32[]{:S(2)}, u32[]{:S(2)}) collective-permute-start(bf16[96,1536]{1,0:T(8,128)(2,1)S(1)} %copy-done.54), channel_id=1, source_target_pairs={{0,8},{8,16},{16,24},{24,0},{1,9},{9,17},{17,25},{25,1},{2,10},{10... | collective-permute-start | bytes 884744 | tf_op jit(solution)/shard_map/ppermute | solution.py:639
  424.8 28.0 %collective-permute-start.58 = (bf16[4,96,896]{2,1,0:T(8,128)(2,1)S(1)}, bf16[4,96,896]{2,1,0:T(8,128)(2,1)S(1)}, u32[]{:S(2)}, u32[]{:S(2)}) collective-permute-start(bf16[4,96,896]{2,1,0:T(8,128)(2,1)S(1)} %copy-done.32), channel_id=1, source_target_pairs={{0,4},{4,0},{1,5},{5,1},{2,6},{6,2},{3,7},{7,3},{8,12},{12,8},{9,1... | collective-permute-start | bytes 2064392 | tf_op jit(solution)/shard_map/ppermute | solution.py:639
  425.4 27.4 %collective-permute-start.59 = (bf16[4,96,1024]{2,1,0:T(8,128)(2,1)S(1)}, bf16[4,96,1024]{2,1,0:T(8,128)(2,1)S(1)}, u32[]{:S(2)}, u32[]{:S(2)}) collective-permute-start(bf16[4,96,1024]{2,1,0:T(8,128)(2,1)S(1)} %get-tuple-element.415), channel_id=1, source_target_pairs={{0,2},{2,0},{1,3},{3,1},{4,6},{6,4},{5,7},{7,5},{8,10},{10,8},{9,1... | collective-permute-start | bytes 2359304 | tf_op jit(solution)/shard_map/ppermute | solution.py:639
  428.0 24.8 %collective-permute-start.56 = (bf16[2,96,896]{2,1,0:T(8,128)(2,1)S(1)}, bf16[2,96,896]{2,1,0:T(8,128)(2,1)S(1)}, u32[]{:S(2)}, u32[]{:S(2)}) collective-permute-start(bf16[2,96,896]{2,1,0:T(8,128)(2,1)S(1)} %copy-done.53), channel_id=1, source_target_pairs={{0,2},{2,0},{1,3},{3,1},{4,6},{6,4},{5,7},{7,5},{8,10},{10,8},{9,1... | collective-permute-start | bytes 1032200 | tf_op jit(solution)/shard_map/ppermute | solution.py:639
  428.0 24.8 %collective-permute-start.57 = (bf16[2,96,1024]{2,1,0:T(8,128)(2,1)S(1)}, bf16[2,96,1024]{2,1,0:T(8,128)(2,1)S(1)}, u32[]{:S(2)}, u32[]{:S(2)}) collective-permute-start(bf16[2,96,1024]{2,1,0:T(8,128)(2,1)S(1)} %get-tuple-element.469), channel_id=1, source_target_pairs={{0,4},{4,0},{1,5},{5,1},{2,6},{6,2},{3,7},{7,3},{8,12},{12,8},{9,1... | collective-permute-start | bytes 1179656 | tf_op jit(solution)/shard_map/ppermute | solution.py:639
  453.0 16.0 %collective-permute-start.65 = (bf16[96,1920]{1,0:T(8,128)(2,1)S(1)}, bf16[96,1920]{1,0:T(8,128)(2,1)S(1)}, u32[]{:S(2)}, u32[]{:S(2)}) collective-permute-start(bf16[96,1920]{1,0:T(8,128)(2,1)S(1)} %fusion.40), channel_id=1, source_target_pairs={{0,8},{8,16},{16,24},{24,0},{1,9},{9,17},{17,25},{25,1},{2,10},{10... | collective-permute-start | bytes 1105928 | tf_op jit(solution)/shard_map/ppermute | solution.py:639
  454.9 14.1 %collective-permute-start.63 = (bf16[2,96,896]{2,1,0:T(8,128)(2,1)S(1)}, bf16[2,96,896]{2,1,0:T(8,128)(2,1)S(1)}, u32[]{:S(2)}, u32[]{:S(2)}) collective-permute-start(bf16[2,96,896]{2,1,0:T(8,128)(2,1)S(1)} %get-tuple-element.471), channel_id=1, source_target_pairs={{0,2},{2,0},{1,3},{3,1},{4,6},{6,4},{5,7},{7,5},{8,10},{10,8},{9,1... | collective-permute-start | bytes 1032200 | tf_op jit(solution)/shard_map/ppermute | solution.py:639
  457.0 12.0 %collective-permute-start.64 = (bf16[2,96,1024]{2,1,0:T(8,128)(2,1)S(1)}, bf16[2,96,1024]{2,1,0:T(8,128)(2,1)S(1)}, u32[]{:S(2)}, u32[]{:S(2)}) collective-permute-start(bf16[2,96,1024]{2,1,0:T(8,128)(2,1)S(1)} %get-tuple-element.465), channel_id=1, source_target_pairs={{0,4},{4,0},{1,5},{5,1},{2,6},{6,2},{3,7},{7,3},{8,12},{12,8},{9,1... | collective-permute-start | bytes 1179656 | tf_op jit(solution)/shard_map/ppermute | solution.py:639
  469.9 13.1 %collective-permute-start.70 = (f32[48,1536]{1,0:T(8,128)}, f32[48,1536]{1,0:T(8,128)}, u32[]{:S(2)}, u32[]{:S(2)}) collective-permute-start(f32[48,1536]{1,0:T(8,128)} %get-tuple-element.492), channel_id=1, source_target_pairs={{0,1},{1,0},{2,3},{3,2},{4,5},{5,4},{6,7},{7,6},{8,9},{9,8},{10,11... | collective-permute-start | bytes 884744 | tf_op jit(solution)/shard_map/ppermute | solution.py:832
  469.9 14.2 %collective-permute-start.68 = (bf16[96,1920]{1,0:T(8,128)(2,1)S(1)}, bf16[96,1920]{1,0:T(8,128)(2,1)S(1)}, u32[]{:S(2)}, u32[]{:S(2)}) collective-permute-start(bf16[96,1920]{1,0:T(8,128)(2,1)S(1)} %fusion.25), channel_id=1, source_target_pairs={{0,8},{8,16},{16,24},{24,0},{1,9},{9,17},{17,25},{25,1},{2,10},{10... | collective-permute-start | bytes 1105928 | tf_op jit(solution)/shard_map/ppermute | solution.py:639
  470.6 12.4 %collective-permute-start.69 = (f32[8,1792]{1,0:T(8,128)S(1)}, f32[8,1792]{1,0:T(8,128)S(1)}, u32[]{:S(2)}, u32[]{:S(2)}) collective-permute-start(f32[8,1792]{1,0:T(8,128)S(1)} %add.348), channel_id=1, source_target_pairs={{0,8},{8,0},{1,9},{9,1},{2,10},{10,2},{3,11},{11,3},{4,12},{12,4},... | collective-permute-start | bytes 172040 | tf_op jit(solution)/shard_map/ppermute | solution.py:832
  484.3 13.1 %collective-permute-start.71 = (bf16[96,1920]{1,0:T(8,128)(2,1)S(1)}, bf16[96,1920]{1,0:T(8,128)(2,1)S(1)}, u32[]{:S(2)}, u32[]{:S(2)}) collective-permute-start(bf16[96,1920]{1,0:T(8,128)(2,1)S(1)} %fusion.22), channel_id=1, source_target_pairs={{0,8},{8,16},{16,24},{24,0},{1,9},{9,17},{17,25},{25,1},{2,10},{10... | collective-permute-start | bytes 1105928 | tf_op jit(solution)/shard_map/ppermute | solution.py:639
  484.5 13.0 %collective-permute-start.72 = (f32[8,1792]{1,0:T(8,128)S(1)}, f32[8,1792]{1,0:T(8,128)S(1)}, u32[]{:S(2)}, u32[]{:S(2)}) collective-permute-start(f32[8,1792]{1,0:T(8,128)S(1)} %add.351), channel_id=1, source_target_pairs={{0,16},{16,0},{1,17},{17,1},{2,18},{18,2},{3,19},{19,3},{4,20},{20... | collective-permute-start | bytes 172040 | tf_op jit(solution)/shard_map/ppermute | solution.py:832
  (84 other events, 1280.5 us)

commit v3 on v2

--- a/solution.py
+++ b/solution.py
@@ -651,6 +651,13 @@
     values, _ = lax.optimization_barrier((values, [v for g in groups for v in g.sent]))
     for g in groups:
         g.sent = ()
+    return values
+
+
+def partly(group, names, *values):
+    held = {k: group.live[k] for k in group.live if k[:-1] in names}
+    held, values = lax.optimization_barrier((held, values))
+    group.live.update(held)
     return values
 
 
@@ -984,14 +991,15 @@
         (xbc,) = fence([gz_], xbc)
         gz_.second(0)
         (xbc,) = after([gz_], xbc)
+        go_.live, xbc = lax.optimization_barrier((go_.live, xbc))
+        go_.z()
+        (xbc,) = after([go_], xbc)
     else:
         w_o = outs.gather(w_own)
     x, bc, s, dt, ld, ldt, st0, comb, dec8 = block_states(xbc, cw, hp, micros)
     dec = dec8[:, 0].reshape(2, micros, 1, W)
     if fast:
-        comb, s = fence([go_], comb, s)
-        go_.z()
-        (s,) = after([go_], s)
+        comb, s = lax.optimization_barrier((comb, s))
     if ns == 2:
         first = lax.ppermute(comb, "s", onward)
     else:
@@ -1083,7 +1091,8 @@
         gp, tiny = fence([so_, sz_, sx_], gp, tiny)
         sx_.second(0)
         sz_.ring(1)
-        (gp,) = after([sx_, sz_], gp)
+        gp, tiny = after([sx_, sz_], gp, tiny)
+        tiny = tiny + swap(tiny, "zb")
         g_out = so_.ring(3)
     else:
         g_out = outs.reduce(g_out)
@@ -1091,12 +1100,15 @@
 
     gn = nt(gp, w_x)
     edge = lax.ppermute(gn[rows:].astype(bf16), "s", backward).reshape(1, micros, 8, D)
+    if fast:
+        gn, dz, tiny = fence([sz_], gn, dz, tiny)
+        tiny = tiny + swap(tiny, "za")
     gn = gn[:rows] + nt(dz, w_z)
 
     if fast:
-        gn, g_out = fence([sz_, sx_], gn, g_out)
+        gn, g_out, tiny = fence([sz_, sx_], gn, g_out, tiny)
+        sx_.first(0)
         sx_.second(1)
-        sx_.first(0)
         sz_.ring(2)
         (gn,) = after([sx_, sz_], gn)
     gn = gn.reshape(2, micros, T, D)
@@ -1104,7 +1116,12 @@
     gn = gn + jnp.pad(edge, ((1, 0), (0, 0), (T - 8, 0), (0, 0)))
     give = lax.dynamic_index_in_dim(gn, 1 - core, 0, False).astype(bf16)
     keep = lax.dynamic_index_in_dim(gn, core, 0, False)
-    gn = keep + swap(give).astype(f32)
+    other = swap(give)
+    if fast:
+        keep, other = partly(sx_, ("m0", "n0"), keep, other)
+        sx_.ring(0)
+        keep, other = after([sx_], keep, other)
+    gn = keep + other.astype(f32)
     hid_f = hid_own.astype(f32)
     own_scale = lax.rsqrt(jnp.mean(hid_f * hid_f, axis=-1, keepdims=True) + EPS)
     unit = hid_f * own_scale
@@ -1116,10 +1133,9 @@
     if fast:
         tiny, g_hid, block_out = fence([sz_, sx_], tiny, g_hid, block_out)
         sx_.first(1)
-        sx_.ring(0)
+        sx_.ring(1)
         (tiny,) = after([sx_], tiny)
         tiny = tiny + swap(tiny, "s")
-        tiny = tiny + swap(tiny, "zl")
         gz = sz_.ring(3)
 
     def exchanged(g):
@@ -1129,15 +1145,11 @@
 
     if fast:
         tiny, gz = fence([sx_], tiny, gz)
-        sx_.ring(1)
+        sx_.ring(2)
         tiny, gz = after([sx_], tiny, gz)
-        tiny = tiny + swap(tiny, "zb")
         gz = exchanged(gz)
+        tiny = tiny + swap(tiny, "zl")
         tiny, gz = fence([sx_], tiny, gz)
-        sx_.ring(2)
-        (tiny,) = after([sx_], tiny)
-        tiny = tiny + swap(tiny, "za")
-        (tiny,) = fence([sx_], tiny)
         gx = sx_.ring(3)
     else:
         tiny = lax.psum(tiny, ALL[:4])

time: 514 us -> 499 us (0.971)
  starting transfers between devices: 96 us -> 82.6 us
    ppermute x19, starting transfers between devices: 25.8 us -> 18.5 us  [swap(): return lax.ppermute(value, axis, [(0, 1), (1, 0)])]
    ppermute x19, waiting for transfers between devices: 33.5 us -> 26.5 us  [swap(): return lax.ppermute(value, axis, [(0, 1), (1, 0)])]
    ppermute x50, starting transfers between devices: 62.3 us -> 56.3 us  [hop(): return lax.ppermute(value, AXIS[axis], [(i, (i + 1) % n) for i in range(n)])]
    ppermute x50, waiting for transfers between devices: 76 us -> 81.7 us  [hop(): return lax.ppermute(value, AXIS[axis], [(i, (i + 1) % n) for i in range(n)])]
    unnamed x153 -> x157, local copies, waits for them, and re-layouts: 25.1 us -> 23.1 us
  transfers between devices with their start and end apart: 75 -> 75, of which waited for: 22 -> 27; matrix products, arithmetic and copies ran while one was open for 28% -> 28% of each run, Pallas kernels for 24% -> 25%
where the time goes in v3:
time: 499 us; the launch traced here: 490 us
  Pallas kernels  128 us (26%)
  waiting for transfers between devices  114 us (23%)
  starting transfers between devices  82.6 us (17%)
  other arithmetic  63 us (13%)
  matrix products  56.5 us (11%)
  local copies, waits for them, and re-layouts  43.4 us (9%)
    ppermute x50, waiting for transfers between devices, hop(): return lax.ppermute(value, AXIS[axis], [(i, (i + 1) % n) for i in range(n)])  81.7 us
    ppermute x50, starting transfers between devices, hop(): return lax.ppermute(value, AXIS[axis], [(i, (i + 1) % n) for i in range(n)])  56.3 us
    pallas_call x1, Pallas kernels, conv_back(): pl.pallas_call(functools.partial(conv_back_kernel, micros), name='conv_ba...  35.3 us
    ppermute x19, waiting for transfers between devices, swap(): return lax.ppermute(value, axis, [(0, 1), (1, 0)])  26.5 us
    unnamed x157, local copies, waits for them, and re-layouts  23.1 us
    pallas_call x1, Pallas kernels, inner_back(): pl.pallas_call(inner_back_kernel, name='inner_back', grid=(blocks, groups...  21 us
    dot_general x3, matrix products, nn(): lax.dot_general(a, b, (((1,), (0,)), ((), ())), preferred_element_type=f32)  20.8 us
    dot_general x3, matrix products, tn(): lax.dot_general(a, b, (((0,), (0,)), ((), ())), preferred_element_type=f32)  19.7 us
  transfers between devices with their start and end apart: 75, of which 27 were waited for; matrix products, arithmetic and copies ran while one was open for 28% of the time, Pallas kernels for 25%

profile of v3, /device:TPU:0, one launch (start us, length us, event | category | flops | bytes accessed | tf_op | source)
XLA Modules:
  0.0 490.3 jit_solution(13242111374395259445)
XLA Ops:
  2.4 4.0 collective-permute-start.1
  12.3 1.9 collective-permute-start.2
  24.1 2.8 collective-permute-done.5
  27.6 5.9 %collective-permute-done.3 = bf16[96,1920]{1,0:T(8,128)(2,1)} collective-permute-done((bf16[96,1920]{1,0:T(8,128)(2,1)S(1)}, bf16[96,1920]{1,0:T(8,128)(2,1)}, u32[]{:S(2)}, u32[]{:S(2)}) %collective-permute-start.3) | collective-permute-done | bytes 368672 | tf_op jit(solution)/shard_map/ppermute | solution.py:639
  36.2 2.1 collective-permute-start.15
  40.4 3.2 maximum_select_fusion
  45.7 2.0 collective-permute-start.11
  66.1 4.8 maximum_select_fusion.1
  80.1 2.4 collective-permute-start.20
  82.5 3.5 collective-permute-start.22
  86.6 5.1 %collective-permute-done.22 = bf16[96,1536]{1,0:T(8,128)(2,1)S(1)} collective-permute-done((bf16[96,1536]{1,0:T(8,128)(2,1)}, bf16[96,1536]{1,0:T(8,128)(2,1)S(1)}, u32[]{:S(2)}, u32[]{:S(2)}) %collective-permute-start.22) | collective-permute-done | bytes 294944 | tf_op jit(solution)/shard_map/ppermute | solution.py:639
  91.8 3.2 collective-permute-start.23
  95.7 2.1 collective-permute-start.30
  97.8 2.5 collective-permute-done.23
  102.7 2.0 collective-permute-done.27.refs_1_
  104.6 2.0 collective-permute-start.25
  108.3 3.5 collective-permute-start.24
  111.8 7.6 %collective-permute-done.29.refs_5_ = bf16[4,96,896]{2,1,0:T(8,128)(2,1)S(1)} collective-permute-done((bf16[4,96,896]{2,1,0:T(8,128)(2,1)S(1)}, bf16[4,96,896]{2,1,0:T(8,128)(2,1)S(1)}, u32[]{:S(2)}, u32[]{:S(2)}) %collective-permute-start.29) | collective-permute-done | bytes 688160 | tf_op jit(solution)/shard_map/ppermute | solution.py:639
  119.4 5.8 %collective-permute-done.30.refs_7_ = bf16[4,96,1024]{2,1,0:T(8,128)(2,1)S(1)} collective-permute-done((bf16[4,96,1024]{2,1,0:T(8,128)(2,1)S(1)}, bf16[4,96,1024]{2,1,0:T(8,128)(2,1)S(1)}, u32[]{:S(2)}, u32[]{:S(2)}) %collective-permute-start.30) | collective-permute-done | bytes 786464 | tf_op jit(solution)/shard_map/ppermute | solution.py:639
  125.2 2.4 join.3
  127.6 8.9 %fusion.61.xbc.halo.prev = f32[1040,1920]{1,0:T(8,128)} fusion(bf16[1040,1536]{1,0:T(8,128)(2,1)S(1)} %copy-done.9, bf16[1536,1920]{1,0:T(8,128)(2,1)S(1)} %join.3), kind=kOutput, calls=%fused_computation.248 | convolution fusion | flops 6134169600 | bytes 17080320 | tf_op jit(solution)/shard_map/dot_general | solution.py:37
  136.6 2.1 collective-permute-start.34
  139.4 4.0 collective-permute-start.31
  143.3 13.4 %block_states.1 = (f32[1024,1536]{1,0:T(8,128)S(1)}, f32[1024,256]{1,0:T(8,128)S(1)}, f32[1024,256]{1,0:T(8,128)S(1)}, f32[1024,128]{1,0:T(8,128)S(1)}, f32[1024...) custom-call(f32[1040,1920]{1,0:T(8,128)} %fusion.61.xbc.halo.prev, ...), custom_call_target="tpu_custom_call" | custom-call | flops 402653184 | bytes 17432576 | tf_op jit(solution)/shard_map/block_states/pallas_call | solution.py:183
  156.8 2.6 copy-done.1
  159.5 2.0 collective-permute-start.32
  161.4 13.3 %inner_part.1.yin = f32[1024,1536]{1,0:T(8,128)S(1)} custom-call(f32[1024,256]{1,0:T(8,128)S(1)} %get-tuple-element.308.s, f32[1024,128]{1,0:T(8,128)S(1)} %get-tuple-element.309.ld, f32[4,32,256]{2,1,0:T(8,128)S(1)} %get-tuple-element.310.ldt, f32[1024,128]{1,0:T(8,128)S(1)} %get-tuple-element.311.dt, f32[1024,1536]{1,0:T(8,128)} %copy-done.1, ...), custom_call_target="tpu_custom_call" | custom-call | flops 3221225472 | bytes 16777216 | tf_op jit(solution)/shard_map/inner_part/pallas_call | solution.py:256
  176.3 6.9 %fusion.10.z = f32[1024,1536]{1,0:T(8,128)} fusion(bf16[1536,1536]{1,0:T(8,128)(2,1)S(1)} %join.4, bf16[1040,1536]{1,0:T(8,128)(2,1)S(1)} %copy-done.9), kind=kOutput, calls=%fused_computation.31 | convolution fusion | flops 4831838208 | bytes 14155776 | tf_op jit(solution)/shard_map/dot_general | solution.py:37
  183.6 7.7 %gate_part.1 = (f32[1024,1536]{1,0:T(8,128)S(1)}, f32[1024,128]{1,0:T(8,128)}) custom-call(f32[1024,1536]{1,0:T(8,128)S(1)} %inner_part.1.yin, f32[1024,256]{1,0:T(8,128)S(1)} %get-tuple-element.317.bc, bf16[4,128,1536]{2,1,0:T(8,128)(2,1)S(1)} %bitcast.169, f32[1024,128]{1,0:T(8,128)S(1)} %get-tuple-element.309.ld, ...), custom_call_target="tpu_custom_call", output_to_operand_aliasing={{0}: (0, {})} | custom-call | flops 402653184 | bytes 18874368 | tf_op jit(solution)/shard_map/gate_part/pallas_call | solution.py:295
  191.3 2.6 copy-done
  197.7 5.9 %multiply_multiply_fusion.exact = f32[1024,1536]{1,0:T(8,128)S(1)} fusion(f32[1024,1536]{1,0:T(8,128)} %copy-done, f32[1024,1536]{1,0:T(8,128)} %fusion.10.z, f32[1536]{0:T(1024)S(1)} %slice_reduce_fusion.1, f32[1024]{0:T(1024)S(1)} %fusion.36), kind=kLoop, calls=%fused_computation.5 | loop fusion | flops 11010048 | bytes 18884608 | tf_op jit(solution)/shard_map/mul | solution.py:1024
  203.6 5.4 %convolution_convert_fusion.1.refs_0_ = bf16[1536,1536]{1,0:T(8,128)(2,1)S(1)} fusion(bf16[1024,1536]{1,0:T(8,128)(2,1)S(1)} %bitcast.177, f32[1024,1536]{1,0:T(8,128)S(1)} %multiply_multiply_fusion.exact), kind=kOutput, calls=%fused_computation.1 | convolution fusion | flops 4835770368 | bytes 14155776 | tf_op jit(solution)/shard_map/dot_general | solution.py:45
  212.2 12.4 %collective-permute-done.38.refs_3_ = bf16[8,96,768]{2,1,0:T(8,128)(2,1)S(1)} collective-permute-done((bf16[8,96,768]{2,1,0:T(8,128)(2,1)}, bf16[8,96,768]{2,1,0:T(8,128)(2,1)S(1)}, u32[]{:S(2)}, u32[]{:S(2)}) %collective-permute-start.38) | collective-permute-done | bytes 1179680 | tf_op jit(solution)/shard_map/ppermute | solution.py:639
  224.6 2.4 join.5.w
  227.0 5.0 %fusion.14 = f32[1024,1536]{1,0:T(8,128)S(1)} fusion(bf16[1536,1536]{1,0:T(8,128)(2,1)S(1)} %join.5.w, f32[1024,1536]{1,0:T(8,128)S(1)} %multiply_multiply_fusion.exact), kind=kOutput, calls=%fused_computation.42 | convolution fusion | flops 4833411072 | bytes 17301504 | tf_op jit(solution)/shard_map/dot_general | solution.py:37
  233.5 10.1 %out_back.1 = (f32[1024,1536]{1,0:T(8,128)}, f32[1024,128]{1,0:T(8,128)S(1)}) custom-call(bf16[1024,1536]{1,0:T(8,128)(2,1)S(1)} %bitcast.178, bf16[1536,1536]{1,0:T(8,128)(2,1)S(1)} %join.5.w, f32[1024,1536]{1,0:T(8,128)} %copy-done.43), custom_call_target="tpu_custom_call" | custom-call | flops 4831838208 | bytes 20447232 | tf_op jit(solution)/shard_map/out_back/pallas_call | solution.py:326
  244.7 2.4 add_convert_fusion.4
  250.2 14.7 %gate_back.1 = (bf16[1024,1536]{1,0:T(8,128)(2,1)S(1)}, bf16[1024,1536]{1,0:T(8,128)(2,1)S(1)}, f32[1024,128]{1,0:T(8,128)S(1)}, f32[2,128,1536]{2,1,0:T(8,128)S...) custom-call(f32[1024,1536]{1,0:T(8,128)} %copy-done, ...), custom_call_target="tpu_custom_call" | custom-call | flops 1610612736 | bytes 37748736 | tf_op jit(solution)/shard_map/gate_back/pallas_call | solution.py:394
  266.3 5.4 %convolution_convert_fusion.refs_0_ = bf16[1536,1536]{1,0:T(8,128)(2,1)S(1)} fusion(bf16[1024,1536]{1,0:T(8,128)(2,1)S(1)} %get-tuple-element.416, bf16[1040,1536]{1,0:T(8,128)(2,1)S(1)} %copy-done.10), kind=kOutput, calls=%fused_computation | convolution fusion | flops 4834197504 | bytes 11010048 | tf_op jit(solution)/shard_map/dot_general | solution.py:45
  273.8 4.1 collective-permute-start.44
  281.0 21.0 %inner_back.1 = (f32[1024,1536]{1,0:T(8,128)S(1)}, f32[1024,128]{1,0:T(8,128)S(1)}, f32[1024,256]{1,0:T(8,128)S(1)}) custom-call(f32[1024,256]{1,0:T(8,128)S(1)} %copy-done.21, f32[1024,256]{1,0:T(8,128)S(1)} %get-tuple-element.317.bc, f32[1024,128]{1,0:T(8,128)S(1)} %get-tuple-element.309.ld, f32[4,32,256]{2,1,0:T(8,128)S(1)} %copy-done.29, ...), custom_call_target="tpu_custom_call" | custom-call | flops 6442450944 | bytes 16777216 | tf_op jit(solution)/shard_map/inner_back/pallas_call | solution.py:476
  301.9 2.6 copy-done.5
  305.7 6.1 %collective-permute-done.44 = bf16[8,96,768]{2,1,0:T(8,128)(2,1)S(1)} collective-permute-done((bf16[8,96,768]{2,1,0:T(8,128)(2,1)S(1)}, bf16[8,96,768]{2,1,0:T(8,128)(2,1)S(1)}, u32[]{:S(2)}, u32[]{:S(2)}) %collective-permute-start.44) | collective-permute-done | bytes 1179680 | tf_op jit(solution)/shard_map/ppermute | solution.py:639
  311.8 2.3 add_convert_fusion.2
  315.8 35.3 %conv_back.1 = (bf16[1040,1920]{1,0:T(8,128)(2,1)}, f32[8,1792]{1,0:T(8,128)}, f32[8,128]{1,0:T(8,128)}) custom-call(f32[1040,1920]{1,0:T(8,128)} %fusion.61.xbc.halo.prev, f32[1040,1920]{1,0:T(8,128)} %fusion.61.xbc.halo.prev, f32[1024,1536]{1,0:T(8,128)} %copy-done.1, f32[1024,1536]{1,0:T(8,128)} %copy-done.5, f32[1024,128]{1,0:T(8,128)} %copy-done.26, ...), custom_call_target="tpu_custom_call" | custom-call | flops 1207959552 | bytes 28311552 | tf_op jit(solution)/shard_map/conv_back/pallas_call | solution.py:600
  356.2 8.9 %convolution_convert_fusion.2.refs_0_ = bf16[1536,1920]{1,0:T(8,128)(2,1)S(1)} fusion(bf16[1040,1536]{1,0:T(8,128)(2,1)S(1)} %copy-done.11, bf16[1040,1920]{1,0:T(8,128)(2,1)S(1)} %copy-done.68), kind=kOutput, calls=%fused_computation.2 | convolution fusion | flops 6137118720 | bytes 13086720 | tf_op jit(solution)/shard_map/dot_general | solution.py:45
  372.5 2.0 collective-permute-start.54
  374.5 8.9 %fusion.62 = f32[1040,1536]{1,0:T(8,128)} fusion(bf16[1040,1920]{1,0:T(8,128)(2,1)S(1)} %copy-done.68, bf16[1536,1920]{1,0:T(8,128)(2,1)S(1)} %bitcast.174), kind=kOutput, calls=%fused_computation.249 | convolution fusion | flops 6134169600 | bytes 16281600 | tf_op jit(solution)/shard_map/dot_general | solution.py:41
  386.7 4.0 collective-permute-done.62
  390.7 2.0 collective-permute-start.52
  392.8 2.1 collective-permute-done.52
  395.6 3.1 collective-permute-start.56
  398.7 7.2 %slice_add_fusion = f32[1024,1536]{1,0:T(8,128)S(1)} fusion(f32[1040,1536]{1,0:T(8,128)} %fusion.62, bf16[1024,1536]{1,0:T(8,128)(2,1)S(1)} %copy-done.32, bf16[1536,1536]{1,0:T(8,128)(2,1)S(1)} %bitcast.176), kind=kOutput, calls=%fused_computation.4 | convolution fusion | flops 4833411072 | bytes 20447232 | tf_op jit(solution)/shard_map/dot_general | solution.py:41
  405.9 9.3 %collective-permute-done.56 = f32[8,1792]{1,0:T(8,128)S(1)} collective-permute-done((f32[8,1792]{1,0:T(8,128)S(1)}, f32[8,1792]{1,0:T(8,128)S(1)}, u32[]{:S(2)}, u32[]{:S(2)}) %collective-permute-start.56) | collective-permute-done | bytes 57376 | tf_op jit(solution)/shard_map/ppermute | solution.py:839
  418.0 2.6 copy-done.39
  422.1 4.8 fusion.8
  429.4 8.0 %collective-permute-done.60 = bf16[2,96,896]{2,1,0:T(8,128)(2,1)S(1)} collective-permute-done((bf16[2,96,896]{2,1,0:T(8,128)(2,1)S(1)}, bf16[2,96,896]{2,1,0:T(8,128)(2,1)S(1)}, u32[]{:S(2)}, u32[]{:S(2)}) %collective-permute-start.60) | collective-permute-done | bytes 344096 | tf_op jit(solution)/shard_map/ppermute | solution.py:639
  440.3 2.3 fusion.2
  442.6 4.2 fusion.5
  447.0 6.3 %collective-permute-done.58 = bf16[4,96,896]{2,1,0:T(8,128)(2,1)S(1)} collective-permute-done((bf16[4,96,896]{2,1,0:T(8,128)(2,1)S(1)}, bf16[4,96,896]{2,1,0:T(8,128)(2,1)S(1)}, u32[]{:S(2)}, u32[]{:S(2)}) %collective-permute-start.58) | collective-permute-done | bytes 688160 | tf_op jit(solution)/shard_map/ppermute | solution.py:639
  453.2 3.3 collective-permute-done.59
  460.9 6.0 %collective-permute-done.69 = f32[8,1792]{1,0:T(8,128)S(1)} collective-permute-done((f32[8,1792]{1,0:T(8,128)S(1)}, f32[8,1792]{1,0:T(8,128)S(1)}, u32[]{:S(2)}, u32[]{:S(2)}) %collective-permute-start.69) | collective-permute-done | bytes 57376 | tf_op jit(solution)/shard_map/ppermute | solution.py:839
  469.0 3.6 collective-permute-done.71
  472.6 8.4 %collective-permute-done.70 = bf16[96,1920]{1,0:T(8,128)(2,1)S(1)} collective-permute-done((bf16[96,1920]{1,0:T(8,128)(2,1)S(1)}, bf16[96,1920]{1,0:T(8,128)(2,1)S(1)}, u32[]{:S(2)}, u32[]{:S(2)}) %collective-permute-start.70) | collective-permute-done | bytes 368672 | tf_op jit(solution)/shard_map/ppermute | solution.py:639
  (429 shorter events, 123.1 us)
Async XLA Ops:
  2.4 9.9 %collective-permute-start.1 = (bf16[664]{0:T(1024)(128)(2,1)S(1)}, bf16[664]{0:T(1024)(128)(2,1)S(1)}, u32[]{:S(2)}, u32[]{:S(2)}) collective-permute-start(bf16[664]{0:T(1024)(128)(2,1)S(1)} %pad_maximum_fusion.17), channel_id=1, source_target_pairs={{0,16},{16,0},{1,17},{17,1},{2,18},{18,2},{3,19},{19,3},{4,20},{20... | collective-permute-start | bytes 3992 | tf_op jit(solution)/shard_map/ppermute | solution.py:839
  9.5 6.7 %collective-permute-start.4 = (bf16[96,1536]{1,0:T(8,128)(2,1)S(1)}, bf16[96,1536]{1,0:T(8,128)(2,1)S(1)}, u32[]{:S(2)}, u32[]{:S(2)}) collective-permute-start(bf16[96,1536]{1,0:T(8,128)(2,1)S(1)} %copy-done.69), channel_id=1, source_target_pairs={{0,0},{1,16},{16,1},{17,17},{2,2},{3,18},{18,3},{19,19},{4,4},{5,2... | collective-permute-start | bytes 884744 | tf_op jit(solution)/shard_map/ppermute | solution.py:891
  10.1 7.8 %collective-permute-start = (bf16[48,3456]{1,0:T(8,128)(2,1)S(1)}, bf16[48,3456]{1,0:T(8,128)(2,1)S(1)}, u32[]{:S(2)}, u32[]{:S(2)}) collective-permute-start(bf16[48,3456]{1,0:T(8,128)(2,1)S(1)} %get-tuple-element.239), channel_id=1, source_target_pairs={{0,1},{1,0},{2,3},{3,2},{4,5},{5,4},{6,7},{7,6},{8,9},{9,8},{10,11... | collective-permute-start | bytes 995336 | tf_op jit(solution)/shard_map/ppermute | solution.py:839
  11.6 21.9 %collective-permute-start.9 = (bf16[2,256,1536]{2,1,0:T(8,128)(2,1)}, bf16[2,256,1536]{2,1,0:T(8,128)(2,1)}, u32[]{:S(2)}, u32[]{:S(2)}) collective-permute-start(bf16[2,256,1536]{2,1,0:T(8,128)(2,1)} %bitcast.182), channel_id=1, source_target_pairs={{0,1},{1,0},{2,3},{3,2},{4,5},{5,4},{6,7},{7,6},{8,9},{9,8},{10,11... | collective-permute-start | bytes 4718600 | tf_op jit(solution)/shard_map/ppermute | solution.py:839
  11.7 21.9 %collective-permute-start.8 = (bf16[2,256,1536]{2,1,0:T(8,128)(2,1)S(1)}, bf16[2,256,1536]{2,1,0:T(8,128)(2,1)}, u32[]{:S(2)}, u32[]{:S(2)}) collective-permute-start(bf16[2,256,1536]{2,1,0:T(8,128)(2,1)S(1)} %bitcast.180), channel_id=1, source_target_pairs={{0,1},{1,0},{2,3},{3,2},{4,5},{5,4},{6,7},{7,6},{8,9},{9,8},{10,11... | collective-permute-start | bytes 4718600 | tf_op jit(solution)/shard_map/ppermute | solution.py:839
  16.2 7.2 %collective-permute-start.6 = (bf16[1,96,768]{2,1,0:T(8,128)(2,1)S(1)}, bf16[1,96,768]{2,1,0:T(8,128)(2,1)S(1)}, u32[]{:S(2)}, u32[]{:S(2)}) collective-permute-start(bf16[1,96,768]{2,1,0:T(8,128)(2,1)S(1)} %get-tuple-element.505), channel_id=1, source_target_pairs={{0,4},{4,0},{1,5},{5,1},{2,6},{6,2},{3,7},{7,3},{8,12},{12,8},{9,1... | collective-permute-start | bytes 442376 | tf_op jit(solution)/shard_map/ppermute | solution.py:639
  18.5 15.0 %collective-permute-start.3 = (bf16[96,1920]{1,0:T(8,128)(2,1)S(1)}, bf16[96,1920]{1,0:T(8,128)(2,1)}, u32[]{:S(2)}, u32[]{:S(2)}) collective-permute-start(bf16[96,1920]{1,0:T(8,128)(2,1)S(1)} %slice.300), channel_id=1, source_target_pairs={{0,8},{8,16},{16,24},{24,0},{1,9},{9,17},{17,25},{25,1},{2,10},{10... | collective-permute-start | bytes 1105928 | tf_op jit(solution)/shard_map/ppermute | solution.py:639
  33.5 22.9 %collective-permute-start.10 = (bf16[96,1920]{1,0:T(8,128)(2,1)}, bf16[96,1920]{1,0:T(8,128)(2,1)}, u32[]{:S(2)}, u32[]{:S(2)}) collective-permute-start(bf16[96,1920]{1,0:T(8,128)(2,1)} %collective-permute-done.3), channel_id=1, source_target_pairs={{0,8},{8,16},{16,24},{24,0},{1,9},{9,17},{17,25},{25,1},{2,10},{10... | collective-permute-start | bytes 1105928 | tf_op jit(solution)/shard_map/ppermute | solution.py:639
  36.2 8.1 %collective-permute-start.15 = (bf16[2,2,2,664]{3,1,0,2:T(2,128)(2,1)S(1)}, bf16[2,2,2,664]{3,1,0,2:T(2,128)(2,1)S(1)}, u32[]{:S(2)}, u32[]{:S(2)}) collective-permute-start(bf16[2,2,2,664]{3,1,0,2:T(2,128)(2,1)S(1)} %broadcast_select_fusion.3), channel_id=1, source_target_pairs={{0,2},{2,0},{1,3},{3,1},{4,6},{6,4},{5,7},{7,5},{8,10},{10,8},{9,1... | collective-permute-start | bytes 31880 | tf_op jit(solution)/shard_map/ppermute | solution.py:839
  38.4 10.9 %collective-permute-start.13 = (bf16[2,96,768]{2,1,0:T(8,128)(2,1)}, bf16[2,96,768]{2,1,0:T(8,128)(2,1)}, u32[]{:S(2)}, u32[]{:S(2)}) collective-permute-start(bf16[2,96,768]{2,1,0:T(8,128)(2,1)} %pad_maximum_fusion.14), channel_id=1, source_target_pairs={{0,4},{4,0},{1,5},{5,1},{2,6},{6,2},{3,7},{7,3},{8,12},{12,8},{9,1... | collective-permute-start | bytes 884744 | tf_op jit(solution)/shard_map/ppermute | solution.py:639
  39.9 13.3 %collective-permute-start.14 = (bf16[2,96,768]{2,1,0:T(8,128)(2,1)}, bf16[2,96,768]{2,1,0:T(8,128)(2,1)}, u32[]{:S(2)}, u32[]{:S(2)}) collective-permute-start(bf16[2,96,768]{2,1,0:T(8,128)(2,1)} %pad_maximum_fusion.15), channel_id=1, source_target_pairs={{0,2},{2,0},{1,3},{3,1},{4,6},{6,4},{5,7},{7,5},{8,10},{10,8},{9,1... | collective-permute-start | bytes 884744 | tf_op jit(solution)/shard_map/ppermute | solution.py:639
  40.4 16.0 %collective-permute-start.12 = (bf16[2,96,1024]{2,1,0:T(8,128)(2,1)}, bf16[2,96,1024]{2,1,0:T(8,128)(2,1)}, u32[]{:S(2)}, u32[]{:S(2)}) collective-permute-start(bf16[2,96,1024]{2,1,0:T(8,128)(2,1)} %pad_maximum_fusion.11), channel_id=1, source_target_pairs={{0,4},{4,0},{1,5},{5,1},{2,6},{6,2},{3,7},{7,3},{8,12},{12,8},{9,1... | collective-permute-start | bytes 1179656 | tf_op jit(solution)/shard_map/ppermute | solution.py:639
  45.7 10.8 %collective-permute-start.11 = (bf16[2,96,896]{2,1,0:T(8,128)(2,1)S(1)}, bf16[2,96,896]{2,1,0:T(8,128)(2,1)}, u32[]{:S(2)}, u32[]{:S(2)}) collective-permute-start(bf16[2,96,896]{2,1,0:T(8,128)(2,1)S(1)} %pad_maximum_fusion.13), channel_id=1, source_target_pairs={{0,2},{2,0},{1,3},{3,1},{4,6},{6,4},{5,7},{7,5},{8,10},{10,8},{9,1... | collective-permute-start | bytes 1032200 | tf_op jit(solution)/shard_map/ppermute | solution.py:639
  49.3 7.2 %collective-permute-start.17 = (bf16[2,8,1536]{2,1,0:T(8,128)(2,1)}, bf16[2,8,1536]{2,1,0:T(8,128)(2,1)S(1)}, u32[]{:S(2)}, u32[]{:S(2)}) collective-permute-start(bf16[2,8,1536]{2,1,0:T(8,128)(2,1)} %slice_bitcast_fusion.8), channel_id=1, source_target_pairs={{0,2},{1,3},{4,6},{5,7},{8,10},{9,11},{12,14},{13,15},{16,18},{17,... | collective-permute-start | bytes 147464 | tf_op jit(solution)/shard_map/ppermute | solution.py:912
  56.5 19.9 %collective-permute-start.19 = (bf16[96,1536]{1,0:T(8,128)(2,1)}, bf16[96,1536]{1,0:T(8,128)(2,1)}, u32[]{:S(2)}, u32[]{:S(2)}) collective-permute-start(bf16[96,1536]{1,0:T(8,128)(2,1)} %slice.301), channel_id=1, source_target_pairs={{0,8},{8,16},{16,24},{24,0},{1,9},{9,17},{17,25},{25,1},{2,10},{10... | collective-permute-start | bytes 884744 | tf_op jit(solution)/shard_map/ppermute | solution.py:639
  56.6 19.8 %collective-permute-start.18 = (bf16[96,1920]{1,0:T(8,128)(2,1)}, bf16[96,1920]{1,0:T(8,128)(2,1)}, u32[]{:S(2)}, u32[]{:S(2)}) collective-permute-start(bf16[96,1920]{1,0:T(8,128)(2,1)} %collective-permute-done.10), channel_id=1, source_target_pairs={{0,8},{8,16},{16,24},{24,0},{1,9},{9,17},{17,25},{25,1},{2,10},{10... | collective-permute-start | bytes 1105928 | tf_op jit(solution)/shard_map/ppermute | solution.py:639
  77.4 14.3 %collective-permute-start.21 = (bf16[2,96,1024]{2,1,0:T(8,128)(2,1)S(1)}, bf16[2,96,1024]{2,1,0:T(8,128)(2,1)S(1)}, u32[]{:S(2)}, u32[]{:S(2)}) collective-permute-start(bf16[2,96,1024]{2,1,0:T(8,128)(2,1)S(1)} %pad_maximum_fusion.10), channel_id=1, source_target_pairs={{0,4},{4,0},{1,5},{5,1},{2,6},{6,2},{3,7},{7,3},{8,12},{12,8},{9,1... | collective-permute-start | bytes 1179656 | tf_op jit(solution)/shard_map/ppermute | solution.py:639
  80.1 11.7 %collective-permute-start.20 = (bf16[2,96,896]{2,1,0:T(8,128)(2,1)S(1)}, bf16[2,96,896]{2,1,0:T(8,128)(2,1)S(1)}, u32[]{:S(2)}, u32[]{:S(2)}) collective-permute-start(bf16[2,96,896]{2,1,0:T(8,128)(2,1)S(1)} %pad_maximum_fusion.12), channel_id=1, source_target_pairs={{0,2},{2,0},{1,3},{3,1},{4,6},{6,4},{5,7},{7,5},{8,10},{10,8},{9,1... | collective-permute-start | bytes 1032200 | tf_op jit(solution)/shard_map/ppermute | solution.py:639
  82.5 9.2 %collective-permute-start.22 = (bf16[96,1536]{1,0:T(8,128)(2,1)}, bf16[96,1536]{1,0:T(8,128)(2,1)S(1)}, u32[]{:S(2)}, u32[]{:S(2)}) collective-permute-start(bf16[96,1536]{1,0:T(8,128)(2,1)} %collective-permute-done.19), channel_id=1, source_target_pairs={{0,8},{8,16},{16,24},{24,0},{1,9},{9,17},{17,25},{25,1},{2,10},{10... | collective-permute-start | bytes 884744 | tf_op jit(solution)/shard_map/ppermute | solution.py:639
  86.0 18.6 %collective-permute-start.27 = (bf16[4,96,896]{2,1,0:T(8,128)(2,1)}, bf16[4,96,896]{2,1,0:T(8,128)(2,1)S(1)}, u32[]{:S(2)}, u32[]{:S(2)}) collective-permute-start(bf16[4,96,896]{2,1,0:T(8,128)(2,1)} %constant_dynamic-update-slice_fusion.refs_0_), channel_id=1, source_target_pairs={{0,4},{4,0},{1,5},{5,1},{2,6},{6,2},{3,7},{7,3},{8,12},{12,8},{9,1... | collective-permute-start | bytes 2064392 | tf_op jit(solution)/shard_map/ppermute | solution.py:639
  86.6 21.8 %collective-permute-start.28 = (bf16[4,96,1024]{2,1,0:T(8,128)(2,1)}, bf16[4,96,1024]{2,1,0:T(8,128)(2,1)S(1)}, u32[]{:S(2)}, u32[]{:S(2)}) collective-permute-start(bf16[4,96,1024]{2,1,0:T(8,128)(2,1)} %constant_dynamic-update-slice_fusion.2.refs_2_), channel_id=1, source_target_pairs={{0,2},{2,0},{1,3},{3,1},{4,6},{6,4},{5,7},{7,5},{8,10},{10,8},{9,1... | collective-permute-start | bytes 2359304 | tf_op jit(solution)/shard_map/ppermute | solution.py:639
  91.8 8.5 %collective-permute-start.23 = (bf16[96,1536]{1,0:T(8,128)(2,1)S(1)}, bf16[96,1536]{1,0:T(8,128)(2,1)S(1)}, u32[]{:S(2)}, u32[]{:S(2)}) collective-permute-start(bf16[96,1536]{1,0:T(8,128)(2,1)S(1)} %collective-permute-done.22), channel_id=1, source_target_pairs={{0,8},{8,16},{16,24},{24,0},{1,9},{9,17},{17,25},{25,1},{2,10},{10... | collective-permute-start | bytes 884744 | tf_op jit(solution)/shard_map/ppermute | solution.py:639
  95.0 24.3 %collective-permute-start.29 = (bf16[4,96,896]{2,1,0:T(8,128)(2,1)S(1)}, bf16[4,96,896]{2,1,0:T(8,128)(2,1)S(1)}, u32[]{:S(2)}, u32[]{:S(2)}) collective-permute-start(bf16[4,96,896]{2,1,0:T(8,128)(2,1)S(1)} %constant_dynamic-update-slice_fusion.4.refs_4_), channel_id=1, source_target_pairs={{0,4},{4,0},{1,5},{5,1},{2,6},{6,2},{3,7},{7,3},{8,12},{12,8},{9,1... | collective-permute-start | bytes 2064392 | tf_op jit(solution)/shard_map/ppermute | solution.py:639
  95.7 29.5 %collective-permute-start.30 = (bf16[4,96,1024]{2,1,0:T(8,128)(2,1)S(1)}, bf16[4,96,1024]{2,1,0:T(8,128)(2,1)S(1)}, u32[]{:S(2)}, u32[]{:S(2)}) collective-permute-start(bf16[4,96,1024]{2,1,0:T(8,128)(2,1)S(1)} %constant_dynamic-update-slice_fusion.6.refs_6_), channel_id=1, source_target_pairs={{0,2},{2,0},{1,3},{3,1},{4,6},{6,4},{5,7},{7,5},{8,10},{10,8},{9,1... | collective-permute-start | bytes 2359304 | tf_op jit(solution)/shard_map/ppermute | solution.py:639
  101.6 34.8 %collective-permute-start.26 = (bf16[4,96,768]{2,1,0:T(8,128)(2,1)S(1)}, bf16[4,96,768]{2,1,0:T(8,128)(2,1)S(1)}, u32[]{:S(2)}, u32[]{:S(2)}) collective-permute-start(bf16[4,96,768]{2,1,0:T(8,128)(2,1)S(1)} %get-tuple-element.298), channel_id=1, source_target_pairs={{0,4},{4,0},{1,5},{5,1},{2,6},{6,2},{3,7},{7,3},{8,12},{12,8},{9,1... | collective-permute-start | bytes 1769480 | tf_op jit(solution)/shard_map/ppermute | solution.py:639
  104.6 31.9 %collective-permute-start.25 = (bf16[4,96,768]{2,1,0:T(8,128)(2,1)S(1)}, bf16[4,96,768]{2,1,0:T(8,128)(2,1)S(1)}, u32[]{:S(2)}, u32[]{:S(2)}) collective-permute-start(bf16[4,96,768]{2,1,0:T(8,128)(2,1)S(1)} %get-tuple-element.296), channel_id=1, source_target_pairs={{0,2},{2,0},{1,3},{3,1},{4,6},{6,4},{5,7},{7,5},{8,10},{10,8},{9,1... | collective-permute-start | bytes 1769480 | tf_op jit(solution)/shard_map/ppermute | solution.py:639
  108.3 31.0 %collective-permute-start.24 = (bf16[8,96,768]{2,1,0:T(8,128)(2,1)S(1)}, bf16[8,96,768]{2,1,0:T(8,128)(2,1)S(1)}, u32[]{:S(2)}, u32[]{:S(2)}) collective-permute-start(bf16[8,96,768]{2,1,0:T(8,128)(2,1)S(1)} %constant_dynamic-update-slice_fusion.8.refs_0_), channel_id=1, source_target_pairs={{0,8},{8,16},{16,24},{24,0},{1,9},{9,17},{17,25},{25,1},{2,10},{10... | collective-permute-start | bytes 3538952 | tf_op jit(solution)/shard_map/ppermute | solution.py:639
  136.6 38.2 %collective-permute-start.34 = (bf16[8,96,768]{2,1,0:T(8,128)(2,1)S(1)}, bf16[8,96,768]{2,1,0:T(8,128)(2,1)S(1)}, u32[]{:S(2)}, u32[]{:S(2)}) collective-permute-start(bf16[8,96,768]{2,1,0:T(8,128)(2,1)S(1)} %constant_dynamic-update-slice_fusion.12.refs_2_), channel_id=1, source_target_pairs={{0,2},{2,0},{1,3},{3,1},{4,6},{6,4},{5,7},{7,5},{8,10},{10,8},{9,1... | collective-permute-start | bytes 3538952 | tf_op jit(solution)/shard_map/ppermute | solution.py:639
  138.8 36.0 %collective-permute-start.33 = (bf16[8,96,768]{2,1,0:T(8,128)(2,1)S(1)}, bf16[8,96,768]{2,1,0:T(8,128)(2,1)S(1)}, u32[]{:S(2)}, u32[]{:S(2)}) collective-permute-start(bf16[8,96,768]{2,1,0:T(8,128)(2,1)S(1)} %constant_dynamic-update-slice_fusion.10.refs_0_), channel_id=1, source_target_pairs={{0,4},{4,0},{1,5},{5,1},{2,6},{6,2},{3,7},{7,3},{8,12},{12,8},{9,1... | collective-permute-start | bytes 3538952 | tf_op jit(solution)/shard_map/ppermute | solution.py:639
  139.4 44.2 %collective-permute-start.31 = (bf16[8,96,768]{2,1,0:T(8,128)(2,1)S(1)}, bf16[8,96,768]{2,1,0:T(8,128)(2,1)}, u32[]{:S(2)}, u32[]{:S(2)}) collective-permute-start(bf16[8,96,768]{2,1,0:T(8,128)(2,1)S(1)} %collective-permute-done.24.refs_1_), channel_id=1, source_target_pairs={{0,8},{8,16},{16,24},{24,0},{1,9},{9,17},{17,25},{25,1},{2,10},{10... | collective-permute-start | bytes 3538952 | tf_op jit(solution)/shard_map/ppermute | solution.py:639
  159.5 23.7 %collective-permute-start.32 = (bf16[2,128,1536]{2,1,0:T(8,128)(2,1)S(1)}, bf16[2,128,1536]{2,1,0:T(8,128)(2,1)S(1)}, u32[]{:S(2)}, u32[]{:S(2)}) collective-permute-start(bf16[2,128,1536]{2,1,0:T(8,128)(2,1)S(1)} %get-tuple-element.318), channel_id=1, source_target_pairs={{0,2},{1,3},{4,6},{5,7},{8,10},{9,11},{12,14},{13,15},{16,18},{17,... | collective-permute-start | bytes 2359304 | tf_op jit(solution)/shard_map/ppermute | solution.py:1004
  194.0 30.6 %collective-permute-start.38 = (bf16[8,96,768]{2,1,0:T(8,128)(2,1)}, bf16[8,96,768]{2,1,0:T(8,128)(2,1)S(1)}, u32[]{:S(2)}, u32[]{:S(2)}) collective-permute-start(bf16[8,96,768]{2,1,0:T(8,128)(2,1)} %collective-permute-done.31.refs_2_), channel_id=1, source_target_pairs={{0,8},{8,16},{16,24},{24,0},{1,9},{9,17},{17,25},{25,1},{2,10},{10... | collective-permute-start | bytes 3538952 | tf_op jit(solution)/shard_map/ppermute | solution.py:639
  210.6 33.1 %collective-permute-start.36 = (bf16[8,96,768]{2,1,0:T(8,128)(2,1)S(1)}, bf16[8,96,768]{2,1,0:T(8,128)(2,1)}, u32[]{:S(2)}, u32[]{:S(2)}) collective-permute-start(bf16[8,96,768]{2,1,0:T(8,128)(2,1)S(1)} %get-tuple-element.331), channel_id=1, source_target_pairs={{0,4},{4,0},{1,5},{5,1},{2,6},{6,2},{3,7},{7,3},{8,12},{12,8},{9,1... | collective-permute-start | bytes 3538952 | tf_op jit(solution)/shard_map/ppermute | solution.py:639
  212.2 31.5 %collective-permute-start.37 = (bf16[8,96,768]{2,1,0:T(8,128)(2,1)S(1)}, bf16[8,96,768]{2,1,0:T(8,128)(2,1)S(1)}, u32[]{:S(2)}, u32[]{:S(2)}) collective-permute-start(bf16[8,96,768]{2,1,0:T(8,128)(2,1)S(1)} %get-tuple-element.332), channel_id=1, source_target_pairs={{0,2},{2,0},{1,3},{3,1},{4,6},{6,4},{5,7},{7,5},{8,10},{10,8},{9,1... | collective-permute-start | bytes 3538952 | tf_op jit(solution)/shard_map/ppermute | solution.py:639
  233.5 188.6 %collective-permute-start.65 = (bf16[2,256,1536]{2,1,0:T(8,128)(2,1)}, bf16[2,256,1536]{2,1,0:T(8,128)(2,1)}, u32[]{:S(2)}, u32[]{:S(2)}) collective-permute-start(bf16[2,256,1536]{2,1,0:T(8,128)(2,1)} %fusion.12), channel_id=1, source_target_pairs={{0,1},{1,0},{2,3},{3,2},{4,5},{5,4},{6,7},{7,6},{8,9},{9,8},{10,11... | collective-permute-start | bytes 4718600 | tf_op jit(solution)/shard_map/ppermute | solution.py:839
  247.1 26.1 %collective-permute-start.39 = (bf16[4,96,768]{2,1,0:T(8,128)(2,1)}, bf16[4,96,768]{2,1,0:T(8,128)(2,1)S(1)}, u32[]{:S(2)}, u32[]{:S(2)}) collective-permute-start(bf16[4,96,768]{2,1,0:T(8,128)(2,1)} %get-tuple-element.475), channel_id=1, source_target_pairs={{0,2},{2,0},{1,3},{3,1},{4,6},{6,4},{5,7},{7,5},{8,10},{10,8},{9,1... | collective-permute-start | bytes 1769480 | tf_op jit(solution)/shard_map/ppermute | solution.py:639
  248.6 24.6 %collective-permute-start.40 = (bf16[4,96,768]{2,1,0:T(8,128)(2,1)}, bf16[4,96,768]{2,1,0:T(8,128)(2,1)}, u32[]{:S(2)}, u32[]{:S(2)}) collective-permute-start(bf16[4,96,768]{2,1,0:T(8,128)(2,1)} %get-tuple-element.473), channel_id=1, source_target_pairs={{0,4},{4,0},{1,5},{5,1},{2,6},{6,2},{3,7},{7,3},{8,12},{12,8},{9,1... | collective-permute-start | bytes 1769480 | tf_op jit(solution)/shard_map/ppermute | solution.py:639
  265.0 40.8 %collective-permute-start.45 = (bf16[2,128,1536]{2,1,0:T(8,128)(2,1)S(1)}, bf16[2,128,1536]{2,1,0:T(8,128)(2,1)}, u32[]{:S(2)}, u32[]{:S(2)}) collective-permute-start(bf16[2,128,1536]{2,1,0:T(8,128)(2,1)S(1)} %get-tuple-element.363), channel_id=1, source_target_pairs={{2,0},{3,1},{6,4},{7,5},{10,8},{11,9},{14,12},{15,13},{18,16},{19,... | collective-permute-start | bytes 2359304 | tf_op jit(solution)/shard_map/ppermute | solution.py:1053
  273.2 32.5 %collective-permute-start.43 = (bf16[8,96,768]{2,1,0:T(8,128)(2,1)S(1)}, bf16[8,96,768]{2,1,0:T(8,128)(2,1)}, u32[]{:S(2)}, u32[]{:S(2)}) collective-permute-start(bf16[8,96,768]{2,1,0:T(8,128)(2,1)S(1)} %get-tuple-element.358), channel_id=1, source_target_pairs={{0,4},{4,0},{1,5},{5,1},{2,6},{6,2},{3,7},{7,3},{8,12},{12,8},{9,1... | collective-permute-start | bytes 3538952 | tf_op jit(solution)/shard_map/ppermute | solution.py:639
  273.8 38.0 %collective-permute-start.44 = (bf16[8,96,768]{2,1,0:T(8,128)(2,1)S(1)}, bf16[8,96,768]{2,1,0:T(8,128)(2,1)S(1)}, u32[]{:S(2)}, u32[]{:S(2)}) collective-permute-start(bf16[8,96,768]{2,1,0:T(8,128)(2,1)S(1)} %get-tuple-element.359), channel_id=1, source_target_pairs={{0,2},{2,0},{1,3},{3,1},{4,6},{6,4},{5,7},{7,5},{8,10},{10,8},{9,1... | collective-permute-start | bytes 3538952 | tf_op jit(solution)/shard_map/ppermute | solution.py:639
  279.5 26.2 %collective-permute-start.42 = (bf16[96,1536]{1,0:T(8,128)(2,1)S(1)}, bf16[96,1536]{1,0:T(8,128)(2,1)S(1)}, u32[]{:S(2)}, u32[]{:S(2)}) collective-permute-start(bf16[96,1536]{1,0:T(8,128)(2,1)S(1)} %fusion.45), channel_id=1, source_target_pairs={{0,8},{8,16},{16,24},{24,0},{1,9},{9,17},{17,25},{25,1},{2,10},{10... | collective-permute-start | bytes 884744 | tf_op jit(solution)/shard_map/ppermute | solution.py:639
  314.1 38.6 %collective-permute-start.47 = (bf16[4,96,768]{2,1,0:T(8,128)(2,1)}, bf16[4,96,768]{2,1,0:T(8,128)(2,1)}, u32[]{:S(2)}, u32[]{:S(2)}) collective-permute-start(bf16[4,96,768]{2,1,0:T(8,128)(2,1)} %get-tuple-element.471), channel_id=1, source_target_pairs={{0,2},{2,0},{1,3},{3,1},{4,6},{6,4},{5,7},{7,5},{8,10},{10,8},{9,1... | collective-permute-start | bytes 1769480 | tf_op jit(solution)/shard_map/ppermute | solution.py:639
  315.2 37.5 %collective-permute-start.48 = (bf16[4,96,768]{2,1,0:T(8,128)(2,1)}, bf16[4,96,768]{2,1,0:T(8,128)(2,1)S(1)}, u32[]{:S(2)}, u32[]{:S(2)}) collective-permute-start(bf16[4,96,768]{2,1,0:T(8,128)(2,1)} %get-tuple-element.469), channel_id=1, source_target_pairs={{0,4},{4,0},{1,5},{5,1},{2,6},{6,2},{3,7},{7,3},{8,12},{12,8},{9,1... | collective-permute-start | bytes 1769480 | tf_op jit(solution)/shard_map/ppermute | solution.py:639
  315.8 36.9 %collective-permute-start.46 = (bf16[96,1536]{1,0:T(8,128)(2,1)S(1)}, bf16[96,1536]{1,0:T(8,128)(2,1)S(1)}, u32[]{:S(2)}, u32[]{:S(2)}) collective-permute-start(bf16[96,1536]{1,0:T(8,128)(2,1)S(1)} %fusion.33), channel_id=1, source_target_pairs={{0,8},{8,16},{16,24},{24,0},{1,9},{9,17},{17,25},{25,1},{2,10},{10... | collective-permute-start | bytes 884744 | tf_op jit(solution)/shard_map/ppermute | solution.py:639
  352.8 14.3 %collective-permute-start.49 = (bf16[96,1536]{1,0:T(8,128)(2,1)S(1)}, bf16[96,1536]{1,0:T(8,128)(2,1)S(1)}, u32[]{:S(2)}, u32[]{:S(2)}) collective-permute-start(bf16[96,1536]{1,0:T(8,128)(2,1)S(1)} %fusion.32), channel_id=1, source_target_pairs={{0,8},{8,16},{16,24},{24,0},{1,9},{9,17},{17,25},{25,1},{2,10},{10... | collective-permute-start | bytes 884744 | tf_op jit(solution)/shard_map/ppermute | solution.py:639
  354.4 14.6 %collective-permute-start.50 = (bf16[96,1536]{1,0:T(8,128)(2,1)S(1)}, bf16[96,1536]{1,0:T(8,128)(2,1)S(1)}, u32[]{:S(2)}, u32[]{:S(2)}) collective-permute-start(bf16[96,1536]{1,0:T(8,128)(2,1)S(1)} %fusion.46), channel_id=1, source_target_pairs={{0,8},{8,16},{16,24},{24,0},{1,9},{9,17},{17,25},{25,1},{2,10},{10... | collective-permute-start | bytes 884744 | tf_op jit(solution)/shard_map/ppermute | solution.py:639
  369.1 26.5 %collective-permute-start.51 = (bf16[96,1536]{1,0:T(8,128)(2,1)S(1)}, bf16[96,1536]{1,0:T(8,128)(2,1)S(1)}, u32[]{:S(2)}, u32[]{:S(2)}) collective-permute-start(bf16[96,1536]{1,0:T(8,128)(2,1)S(1)} %fusion.31), channel_id=1, source_target_pairs={{0,8},{8,16},{16,24},{24,0},{1,9},{9,17},{17,25},{25,1},{2,10},{10... | collective-permute-start | bytes 884744 | tf_op jit(solution)/shard_map/ppermute | solution.py:639
  371.0 44.2 %collective-permute-start.53 = (bf16[4,96,896]{2,1,0:T(8,128)(2,1)S(1)}, bf16[4,96,896]{2,1,0:T(8,128)(2,1)S(1)}, u32[]{:S(2)}, u32[]{:S(2)}) collective-permute-start(bf16[4,96,896]{2,1,0:T(8,128)(2,1)S(1)} %get-tuple-element.403), channel_id=1, source_target_pairs={{0,4},{4,0},{1,5},{5,1},{2,6},{6,2},{3,7},{7,3},{8,12},{12,8},{9,1... | collective-permute-start | bytes 2064392 | tf_op jit(solution)/shard_map/ppermute | solution.py:639
  372.5 42.7 %collective-permute-start.54 = (bf16[4,96,1024]{2,1,0:T(8,128)(2,1)S(1)}, bf16[4,96,1024]{2,1,0:T(8,128)(2,1)S(1)}, u32[]{:S(2)}, u32[]{:S(2)}) collective-permute-start(bf16[4,96,1024]{2,1,0:T(8,128)(2,1)S(1)} %get-tuple-element.404), channel_id=1, source_target_pairs={{0,2},{2,0},{1,3},{3,1},{4,6},{6,4},{5,7},{7,5},{8,10},{10,8},{9,1... | collective-permute-start | bytes 2359304 | tf_op jit(solution)/shard_map/ppermute | solution.py:639
  384.3 6.4 %collective-permute-start.62 = (bf16[16,1536]{1,0:T(8,128)(2,1)S(1)}, bf16[16,1536]{1,0:T(8,128)(2,1)S(1)}, u32[]{:S(2)}, u32[]{:S(2)}) collective-permute-start(bf16[16,1536]{1,0:T(8,128)(2,1)S(1)} %slice.551), channel_id=1, source_target_pairs={{2,0},{3,1},{6,4},{7,5},{10,8},{11,9},{14,12},{15,13},{18,16},{19,... | collective-permute-start | bytes 147464 | tf_op jit(solution)/shard_map/ppermute | solution.py:1102
  394.9 20.3 %collective-permute-start.55 = (f32[96,1536]{1,0:T(8,128)S(1)}, f32[96,1536]{1,0:T(8,128)S(1)}, u32[]{:S(2)}, u32[]{:S(2)}) collective-permute-start(f32[96,1536]{1,0:T(8,128)S(1)} %bitcast_add_fusion.4), channel_id=1, source_target_pairs={{0,0},{1,16},{16,1},{17,17},{2,2},{3,18},{18,3},{19,19},{4,4},{5,2... | collective-permute-start | bytes 1769480 | tf_op jit(solution)/shard_map/ppermute | solution.py:1099
  395.6 19.6 %collective-permute-start.56 = (f32[8,1792]{1,0:T(8,128)S(1)}, f32[8,1792]{1,0:T(8,128)S(1)}, u32[]{:S(2)}, u32[]{:S(2)}) collective-permute-start(f32[8,1792]{1,0:T(8,128)S(1)} %add.326), channel_id=1, source_target_pairs={{0,16},{16,0},{1,17},{17,1},{2,18},{18,2},{3,19},{19,3},{4,20},{20... | collective-permute-start | bytes 172040 | tf_op jit(solution)/shard_map/ppermute | solution.py:839
  422.0 16.9 %collective-permute-start.63 = (bf16[2,256,1536]{2,1,0:T(8,128)(2,1)}, bf16[2,256,1536]{2,1,0:T(8,128)(2,1)}, u32[]{:S(2)}, u32[]{:S(2)}) collective-permute-start(bf16[2,256,1536]{2,1,0:T(8,128)(2,1)} %fusion.13), channel_id=1, source_target_pairs={{0,1},{1,0},{2,3},{3,2},{4,5},{5,4},{6,7},{7,6},{8,9},{9,8},{10,11... | collective-permute-start | bytes 4718600 | tf_op jit(solution)/shard_map/ppermute | solution.py:839
  426.9 10.5 %collective-permute-start.60 = (bf16[2,96,896]{2,1,0:T(8,128)(2,1)S(1)}, bf16[2,96,896]{2,1,0:T(8,128)(2,1)S(1)}, u32[]{:S(2)}, u32[]{:S(2)}) collective-permute-start(bf16[2,96,896]{2,1,0:T(8,128)(2,1)S(1)} %copy-done.55), channel_id=1, source_target_pairs={{0,2},{2,0},{1,3},{3,1},{4,6},{6,4},{5,7},{7,5},{8,10},{10,8},{9,1... | collective-permute-start | bytes 1032200 | tf_op jit(solution)/shard_map/ppermute | solution.py:639
  426.9 12.0 %collective-permute-start.61 = (bf16[2,96,1024]{2,1,0:T(8,128)(2,1)S(1)}, bf16[2,96,1024]{2,1,0:T(8,128)(2,1)S(1)}, u32[]{:S(2)}, u32[]{:S(2)}) collective-permute-start(bf16[2,96,1024]{2,1,0:T(8,128)(2,1)S(1)} %get-tuple-element.481), channel_id=1, source_target_pairs={{0,4},{4,0},{1,5},{5,1},{2,6},{6,2},{3,7},{7,3},{8,12},{12,8},{9,1... | collective-permute-start | bytes 1179656 | tf_op jit(solution)/shard_map/ppermute | solution.py:639
  427.5 19.5 %collective-permute-start.57 = (bf16[96,1536]{1,0:T(8,128)(2,1)S(1)}, bf16[96,1536]{1,0:T(8,128)(2,1)S(1)}, u32[]{:S(2)}, u32[]{:S(2)}) collective-permute-start(bf16[96,1536]{1,0:T(8,128)(2,1)S(1)} %copy-done.56), channel_id=1, source_target_pairs={{0,8},{8,16},{16,24},{24,0},{1,9},{9,17},{17,25},{25,1},{2,10},{10... | collective-permute-start | bytes 884744 | tf_op jit(solution)/shard_map/ppermute | solution.py:639
  427.6 25.7 %collective-permute-start.58 = (bf16[4,96,896]{2,1,0:T(8,128)(2,1)S(1)}, bf16[4,96,896]{2,1,0:T(8,128)(2,1)S(1)}, u32[]{:S(2)}, u32[]{:S(2)}) collective-permute-start(bf16[4,96,896]{2,1,0:T(8,128)(2,1)S(1)} %copy-done.36), channel_id=1, source_target_pairs={{0,4},{4,0},{1,5},{5,1},{2,6},{6,2},{3,7},{7,3},{8,12},{12,8},{9,1... | collective-permute-start | bytes 2064392 | tf_op jit(solution)/shard_map/ppermute | solution.py:639
  437.4 19.2 %collective-permute-start.59 = (bf16[4,96,1024]{2,1,0:T(8,128)(2,1)S(1)}, bf16[4,96,1024]{2,1,0:T(8,128)(2,1)S(1)}, u32[]{:S(2)}, u32[]{:S(2)}) collective-permute-start(bf16[4,96,1024]{2,1,0:T(8,128)(2,1)S(1)} %get-tuple-element.425), channel_id=1, source_target_pairs={{0,2},{2,0},{1,3},{3,1},{4,6},{6,4},{5,7},{7,5},{8,10},{10,8},{9,1... | collective-permute-start | bytes 2359304 | tf_op jit(solution)/shard_map/ppermute | solution.py:639
  439.1 17.4 %collective-permute-start.64 = (bf16[96,1920]{1,0:T(8,128)(2,1)S(1)}, bf16[96,1920]{1,0:T(8,128)(2,1)S(1)}, u32[]{:S(2)}, u32[]{:S(2)}) collective-permute-start(bf16[96,1920]{1,0:T(8,128)(2,1)S(1)} %fusion.39), channel_id=1, source_target_pairs={{0,8},{8,16},{16,24},{24,0},{1,9},{9,17},{17,25},{25,1},{2,10},{10... | collective-permute-start | bytes 1105928 | tf_op jit(solution)/shard_map/ppermute | solution.py:639
  456.6 11.2 %collective-permute-start.68 = (bf16[96,1920]{1,0:T(8,128)(2,1)S(1)}, bf16[96,1920]{1,0:T(8,128)(2,1)S(1)}, u32[]{:S(2)}, u32[]{:S(2)}) collective-permute-start(bf16[96,1920]{1,0:T(8,128)(2,1)S(1)} %fusion.24), channel_id=1, source_target_pairs={{0,8},{8,16},{16,24},{24,0},{1,9},{9,17},{17,25},{25,1},{2,10},{10... | collective-permute-start | bytes 1105928 | tf_op jit(solution)/shard_map/ppermute | solution.py:639
  456.9 10.1 %collective-permute-start.66 = (bf16[2,96,896]{2,1,0:T(8,128)(2,1)S(1)}, bf16[2,96,896]{2,1,0:T(8,128)(2,1)S(1)}, u32[]{:S(2)}, u32[]{:S(2)}) collective-permute-start(bf16[2,96,896]{2,1,0:T(8,128)(2,1)S(1)} %get-tuple-element.483), channel_id=1, source_target_pairs={{0,2},{2,0},{1,3},{3,1},{4,6},{6,4},{5,7},{7,5},{8,10},{10,8},{9,1... | collective-permute-start | bytes 1032200 | tf_op jit(solution)/shard_map/ppermute | solution.py:639
  457.7 10.1 %collective-permute-start.67 = (bf16[2,96,1024]{2,1,0:T(8,128)(2,1)S(1)}, bf16[2,96,1024]{2,1,0:T(8,128)(2,1)S(1)}, u32[]{:S(2)}, u32[]{:S(2)}) collective-permute-start(bf16[2,96,1024]{2,1,0:T(8,128)(2,1)S(1)} %get-tuple-element.477), channel_id=1, source_target_pairs={{0,4},{4,0},{1,5},{5,1},{2,6},{6,2},{3,7},{7,3},{8,12},{12,8},{9,1... | collective-permute-start | bytes 1179656 | tf_op jit(solution)/shard_map/ppermute | solution.py:639
  458.3 8.7 %collective-permute-start.69 = (f32[8,1792]{1,0:T(8,128)S(1)}, f32[8,1792]{1,0:T(8,128)S(1)}, u32[]{:S(2)}, u32[]{:S(2)}) collective-permute-start(f32[8,1792]{1,0:T(8,128)S(1)} %add.329), channel_id=1, source_target_pairs={{0,2},{2,0},{1,3},{3,1},{4,6},{6,4},{5,7},{7,5},{8,10},{10,8},{9,1... | collective-permute-start | bytes 172040 | tf_op jit(solution)/shard_map/ppermute | solution.py:839
  468.2 12.8 %collective-permute-start.70 = (bf16[96,1920]{1,0:T(8,128)(2,1)S(1)}, bf16[96,1920]{1,0:T(8,128)(2,1)S(1)}, u32[]{:S(2)}, u32[]{:S(2)}) collective-permute-start(bf16[96,1920]{1,0:T(8,128)(2,1)S(1)} %fusion.21), channel_id=1, source_target_pairs={{0,8},{8,16},{16,24},{24,0},{1,9},{9,17},{17,25},{25,1},{2,10},{10... | collective-permute-start | bytes 1105928 | tf_op jit(solution)/shard_map/ppermute | solution.py:639
  (86 other events, 1350.2 us)

commit v4 on v3

--- a/solution.py
+++ b/solution.py
@@ -27,7 +27,6 @@
 HT = T // 2
 f32 = jnp.float32
 bf16 = jnp.bfloat16
-HIGH = lax.Precision.HIGHEST
 ALL = ("za", "zb", "zl", "s", "c")
 Z = ("za", "zb")
 MB_ = 1 << 20
@@ -68,11 +67,20 @@
     return out
 
 
+def head_place(lanes, first):
+    return (iota((lanes, 128), 0) // PS + first == iota((lanes, 128), 1)).astype(bf16)
+
+
 def per_head(values, first):
-    lanes = values.shape[1]
-    place = (iota((lanes, 128), 0) // PS + first == iota((lanes, 128), 1)).astype(bf16)
+    place = head_place(values.shape[1], first)
     high, low = halves(values)
     return nn(high, place) + nn(low, place)
+
+
+def masked_sums(mask, values):
+    high, low = halves(values)
+    ones = mask.astype(bf16)
+    return nn(ones, high) + nn(ones, low)
 
 
 def row_sum(values):
@@ -133,7 +141,7 @@
     )(hid, rim, gain)
 
 
-def states_kernel(xbc, halo, cw, hp, x, bc, s, dt, ld, ldt, st0, comb, dec, pad, tail, carry, xw):
+def states_kernel(xbc, halo, cw, hp, x, pre, bc, s, dt, ld, ldt, st0, comb, dec, pad, tail, carry, xw):
     j = pl.program_id(0)
     m, b = j // 2, j % 2
     before = jnp.where(b == 0, halo[pl.ds(8 * m, 8), :XC], tail[...])
@@ -142,20 +150,21 @@
     tail[...] = xbc[T - 8 : T, :XC]
     step = softplus(xbc[:, XC:XP] + hp[0:1, :])
     step = jnp.where(iota((T, 128), 1) < HH, step, 0.0)
-    tri = (iota((T, T), 0) >= iota((T, T), 1)).astype(f32)
-    logd = jnp.dot(tri, -hp[1:2, :] * step, precision=HIGH, preferred_element_type=f32)
+    logd = masked_sums(iota((T, T), 0) >= iota((T, T), 1), -hp[1:2, :] * step)
     dt[...] = step
     ld[...] = logd
     ldt[0] = logd.T[:32]
     tailw = jnp.exp(logd[T - 1 : T] - logd) * step
     lanes = slice(W, XC)
     a = conv_taps(pad, cw, lanes)
+    pre[:, lanes] = a
     act = a * lax.logistic(a)
     bc[...] = act
     s[...] = fine(nt, act[:, N:], act[:, :N])
     for i in range(W // 128):
         lanes = slice(128 * i, 128 * i + 128)
         a = conv_taps(pad, cw, lanes)
+        pre[:, lanes] = a
         act_x = a * lax.logistic(a)
         x[:, lanes] = act_x
         xw[:, lanes] = (act_x * spread(tailw, 2 * i, 2)).astype(bf16)
@@ -192,6 +201,7 @@
         ],
         out_specs=[
             pl.BlockSpec((T, W), lambda j: (blk(j), 0)),
+            pl.BlockSpec((T, XC), lambda j: (blk(j), 0)),
             pl.BlockSpec((T, 2 * N), lambda j: (blk(j), 0)),
             pl.BlockSpec((T, T), lambda j: (blk(j), 0)),
             pl.BlockSpec((T, 128), lambda j: (blk(j), 0)),
@@ -203,6 +213,7 @@
         ],
         out_shape=[
             out(rows, W),
+            out(rows, XC),
             out(rows, 2 * N),
             out(rows, T),
             out(rows, 128),
@@ -225,13 +236,13 @@
 
 def inner_kernel(s, ld, ldt, dt, x, skip, y):
     g = pl.program_id(1)
-    shift = lax.rem(128 - 8 * g, 128)
+    shift = lax.rem(128 - 24 * g, 128)
     logd = pltpu.roll(ld[...], shift, 1) * LOG2E
     step = pltpu.roll(dt[...], shift, 1)
     upper = iota((HT, HT), 0) >= iota((HT, HT), 1)
     lower = iota((HT, T), 0) + HT >= iota((HT, T), 1)
     head = iota((T, 256), 1) // PS
-    for q in range(2):
+    for q in range(6):
         lanes = slice(256 * q, 256 * q + 256)
         tile = x[:, lanes]
         xdt = tile * spread(step, 4 * q, 4)
@@ -239,7 +250,7 @@
         bottom = skip[0:1, lanes] * tile[HT:]
         for i in range(4):
             h = 4 * q + i
-            row = ldt[0, pl.ds(8 * g + h, 1), :] * LOG2E
+            row = ldt[0, pl.ds(24 * g + h, 1), :] * LOG2E
             col = logd[:, h : h + 1]
             mine = jnp.where(head == i, xdt, 0.0).astype(bf16)
             decay = jnp.exp2(jnp.where(upper, col[:HT] - row[:, :HT], NEG))
@@ -252,7 +263,7 @@
 
 def inner_part(s, ld, ldt, dt, x, skip_row):
     rows = x.shape[0]
-    blocks, groups = rows // T, W // 512
+    blocks, groups = rows // T, W // 1536
     return pl.pallas_call(
         inner_kernel,
         name="inner_part",
@@ -262,10 +273,10 @@
             pl.BlockSpec((T, 128), lambda j, g: (j, 0)),
             pl.BlockSpec((1, 32, T), lambda j, g: (j, 0, 0)),
             pl.BlockSpec((T, 128), lambda j, g: (j, 0)),
-            pl.BlockSpec((T, 512), lambda j, g: (j, g)),
-            pl.BlockSpec((8, 512), lambda j, g: (0, g)),
-        ],
-        out_specs=pl.BlockSpec((T, 512), lambda j, g: (j, g)),
+            pl.BlockSpec((T, 1536), lambda j, g: (j, g)),
+            pl.BlockSpec((8, 1536), lambda j, g: (0, g)),
+        ],
+        out_specs=pl.BlockSpec((T, 1536), lambda j, g: (j, g)),
         out_shape=jax.ShapeDtypeStruct((rows, W), f32),
         compiler_params=params(),
         cost_estimate=cost(
@@ -425,7 +436,7 @@
         dst[...] = jnp.zeros_like(dst)
         xv[...] = jnp.zeros_like(xv)
 
-    shift = lax.rem(128 - 8 * g, 128)
+    shift = lax.rem(128 - 24 * g, 128)
     logd = pltpu.roll(ld[...], shift, 1) * LOG2E
     step = pltpu.roll(dt[...], shift, 1)
     early = iota((HT, T), 1) >= iota((HT, T), 0)
@@ -434,7 +445,7 @@
     gtop = jnp.zeros((HT, T), f32)
     gbottom = jnp.zeros((HT, HT), f32)
     sums = jnp.zeros((T, 128), f32)
-    for q in range(2):
+    for q in range(6):
         lanes = slice(256 * q, 256 * q + 256)
         steps = spread(step, 4 * q, 4)
         tile = x[:, lanes]
@@ -444,7 +455,7 @@
         bottom = jnp.zeros((HT, 256), f32)
         for i in range(4):
             h = 4 * q + i
-            row = ldt[0, pl.ds(8 * g + h, 1), :] * LOG2E
+            row = ldt[0, pl.ds(24 * g + h, 1), :] * LOG2E
             col = logd[:, h : h + 1]
             dmine = jnp.where(head == i, dyt, jnp.zeros_like(dyt))
             xmine = jnp.where(head == i, xdt, 0.0).astype(bf16)
@@ -456,7 +467,7 @@
             gbottom = gbottom + nt(xmine[HT:], dyt[HT:]) * decay
         total = jnp.concatenate([top, bottom], axis=0)
         dx[:, lanes] = total * steps + skip[0:1, lanes] * dyt.astype(f32)
-        sums = sums + per_head(tile * total, 8 * g + 4 * q)
+        sums = sums + per_head(tile * total, 24 * g + 4 * q)
     xv[...] += sums
     dst[:HT, :] += gtop
     dst[HT:, HT:] += gbottom
@@ -469,9 +480,9 @@
 
 def inner_back(s, bc, ld, ldt, dt, x, dy, skip_row):
     rows = x.shape[0]
-    blocks, groups = rows // T, W // 512
+    blocks, groups = rows // T, W // 1536
     row = lambda c: pl.BlockSpec((T, c), lambda j, g: (j, 0))
-    tile = pl.BlockSpec((T, 512), lambda j, g: (j, g))
+    tile = pl.BlockSpec((T, 1536), lambda j, g: (j, g))
     sh = jax.ShapeDtypeStruct
     return pl.pallas_call(
         inner_back_kernel,
@@ -485,7 +496,7 @@
             row(128),
             tile,
             tile,
-            pl.BlockSpec((8, 512), lambda j, g: (0, g)),
+            pl.BlockSpec((8, 1536), lambda j, g: (0, g)),
         ],
         out_specs=[tile, row(128), row(2 * N)],
         out_shape=[sh((rows, W), f32), sh((rows, 128), f32), sh((rows, 2 * N), f32)],
@@ -498,7 +509,7 @@
 
 
 def conv_back_kernel(
-    micros, xbc, prev, x, dxi, xv, dbc, bc, dt, ld, later1, de1, dec, e, dc, dla, cw, hp,
+    micros, xbc, prev, pre, dxi, xv, dbc, bc, dt, ld, later1, de1, dec, e, dc, dla, cw, hp,
     gp, gcw, ghp, pad, dpre, nxt, edge,
 ):
     p = pl.program_id(0)
@@ -524,9 +535,7 @@
         tailw = fade * step
         bst = bc[:, :N].astype(bf16)
 
-        def through_conv(grad, lanes):
-            a = conv_taps(pad, cw, lanes)
-            sg = lax.logistic(a)
+        def through_conv(grad, lanes, a, sg):
             d = grad * (sg * (1.0 + a * (1.0 - sg)))
             dpre[8 : 8 + T, lanes] = d
             gcw[4:5, lanes] += row_sum(d)
@@ -553,23 +562,24 @@
             earlier = de1[0, :, lanes] + dec[0, 0:1, lanes] * lat.astype(f32)
             lat = jnp.where(b == 1, lat, earlier.astype(bf16))
             spreadw = spread(tailw, 4 * i, 4)
-            xt = x[:, lanes]
+            a = pre[:, lanes]
+            sg = lax.logistic(a)
+            xt = a * sg
             bl = nn(bst, lat)
-            dw = dw + per_head(xt * bl, 4 * i)
+            dw = dw + nn((xt * bl).astype(bf16), head_place(256, 4 * i))
             high, low = halves(xt * spreadw)
             dbs = dbs + (nt(high, lat) + nt(low, lat))
             both = row_sum(lat.astype(f32) * e[0, :, lanes].astype(f32))
             ddec = ddec + per_head(jnp.broadcast_to(both, (8, 256)), 4 * i)
-            through_conv(dxi[:, lanes] + bl * spreadw, lanes)
-        through_conv(
-            jnp.concatenate([dbc[:, :N] + dbs, dbc[:, N:] + dc[...]], axis=1), slice(W, XC)
-        )
+            through_conv(dxi[:, lanes] + bl * spreadw, lanes, a, sg)
+        a = pre[:, W:]
+        both = jnp.concatenate([dbc[:, :N] + dbs, dbc[:, N:] + dc[...]], axis=1)
+        through_conv(both, slice(W, XC), a, lax.logistic(a))
         q = dw * tailw
         dlog = dla[...] - step * xv[...] - q
         dlast = row_sum(q) + ddec[0:1] * jnp.exp(logd[T - 1 : T])
         dlog = dlog + jnp.where(iota((T, 128), 0) == T - 1, dlast, 0.0)
-        tri = (iota((T, T), 1) >= iota((T, T), 0)).astype(f32)
-        dcum = jnp.dot(tri, dlog, precision=HIGH, preferred_element_type=f32)
+        dcum = masked_sums(iota((T, T), 1) >= iota((T, T), 0), dlog)
         dstep = xv[...] + dw * fade - hp[1:2, :] * dcum
         draw = dstep * lax.logistic(xbc[:, XC:XP] + hp[0:1, :])
         draw = jnp.where(iota((T, 128), 1) < HH, draw, 0.0)
@@ -582,7 +592,7 @@
             edge[pl.ds(pl.multiple_of(8 * (p // 2), 8), 8), XC:XP] = jnp.zeros((8, 128), f32)
 
 
-def conv_back(xbc, x, dxi, xv, dbc, bc, dt, ld, later1, de1, dec, e, dc, dla, cw, hp, micros):
+def conv_back(xbc, pre, dxi, xv, dbc, bc, dt, ld, later1, de1, dec, e, dc, dla, cw, hp, micros):
     blocks = 2 * micros
     rows = blocks * T
     blk = lambda p: jnp.where(p < blocks, (1 - p % 2) * micros + p // 2, micros - 1)
@@ -604,7 +614,7 @@
         in_specs=[
             row(XP),
             pl.BlockSpec((8, XP), before),
-            row(W), row(W), row(128), row(2 * N), row(2 * N), row(128), row(128),
+            row(XC), row(W), row(128), row(2 * N), row(2 * N), row(128), row(128),
             chip, chip, pl.BlockSpec((1, 8, W), lambda p: (micros + unit(p), 0, 0)), state,
             row(N), row(128), whole(cw), whole(hp),
         ],
@@ -626,7 +636,7 @@
         ],
         compiler_params=pltpu.CompilerParams(vmem_limit_bytes=58 * MB_),
         cost_estimate=cost(6 * rows * N * W, rows * W * 18, rows * XC * 2),
-    )(xbc, xbc, x, dxi, xv, dbc, bc, dt, ld, later1, de1, dec, e, dc, dla, cw, hp)
+    )(xbc, xbc, pre, dxi, xv, dbc, bc, dt, ld, later1, de1, dec, e, dc, dla, cw, hp)
 
 
 AXIS = {"z": Z, "l": "zl", "s": "s"}
@@ -934,7 +944,6 @@
         small = spread_out(small, "s", 3)
         gx_.z()
         gx_.first(0)
-        go_.step(1)
         hid_own_, hid_other = after(every, hid_own, hid_other)
         hid_all = chip_tokens(hid_own_, hid_other)
         rim = rim_of(hid_all)
@@ -974,6 +983,7 @@
             every, normed, cot_all, cw, hp, gain, skip_row
         )
         gx_.first(1)
+        go_.step(1)
         gz_.z()
         (normed,) = fence([gx_, gz_], normed)
         gx_.second(1)
@@ -996,7 +1006,7 @@
         (xbc,) = after([go_], xbc)
     else:
         w_o = outs.gather(w_own)
-    x, bc, s, dt, ld, ldt, st0, comb, dec8 = block_states(xbc, cw, hp, micros)
+    x, pre, bc, s, dt, ld, ldt, st0, comb, dec8 = block_states(xbc, cw, hp, micros)
     dec = dec8[:, 0].reshape(2, micros, 1, W)
     if fast:
         comb, s = lax.optimization_barrier((comb, s))
@@ -1072,7 +1082,7 @@
         sz_.first(0)
         (dxi,) = after([so_, sz_], dxi)
     gp, gcw, ghp = conv_back(
-        xbc, x, dxi, xv, dbc, bc, dt, ld, later1, de1, dec8, entering, dc, dla, cw, hp, micros
+        xbc, pre, dxi, xv, dbc, bc, dt, ld, later1, de1, dec8, entering, dc, dla, cw, hp, micros
     )
     if fast:
         (gp,) = fence([so_, sz_], gp)

time: 499 us -> 485 us (0.972)
  Pallas kernels: 128 us -> 114 us
  waiting for transfers between devices: 114 us -> 126 us
  starting transfers between devices: 82.6 us -> 76.6 us
    ppermute x50, waiting for transfers between devices: 81.7 us -> 97.8 us  [hop(): return lax.ppermute(value, AXIS[axis], [(i, (i + 1) % n) for i in range(n)])]
    ppermute x50, starting transfers between devices: 56.3 us -> 45.9 us  [hop(): return lax.ppermute(value, AXIS[axis], [(i, (i + 1) % n) for i in range(n)])]
    pallas_call x1, Pallas kernels: 35.3 us -> 27.3 us  [conv_back(): pl.pallas_call(functools.partial(conv_back_kernel, micros), name='conv_ba...]
    unnamed x157 -> x155, local copies, waits for them, and re-layouts: 23.1 us -> 21.4 us
  transfers between devices with their start and end apart: 75 -> 75, of which waited for: 27 -> 30; matrix products, arithmetic and copies ran while one was open for 28% -> 28% of each run, Pallas kernels for 25% -> 22%
where the time goes in v4:
time: 485 us; the launch traced here: 477 us
  waiting for transfers between devices  126 us (26%)
  Pallas kernels  114 us (24%)
  starting transfers between devices  76.6 us (16%)
  other arithmetic  59.1 us (12%)
  matrix products  56.6 us (12%)
  local copies, waits for them, and re-layouts  41.6 us (9%)
    ppermute x50, waiting for transfers between devices, hop(): return lax.ppermute(value, AXIS[axis], [(i, (i + 1) % n) for i in range(n)])  97.8 us
    ppermute x50, starting transfers between devices, hop(): return lax.ppermute(value, AXIS[axis], [(i, (i + 1) % n) for i in range(n)])  45.9 us
    pallas_call x1, Pallas kernels, conv_back(): pl.pallas_call(functools.partial(conv_back_kernel, micros), name='conv_ba...  27.3 us
    ppermute x19, waiting for transfers between devices, swap(): return lax.ppermute(value, axis, [(0, 1), (1, 0)])  24.1 us
    unnamed x155, local copies, waits for them, and re-layouts  21.4 us
    dot_general x3, matrix products, nn(): lax.dot_general(a, b, (((1,), (0,)), ((), ())), preferred_element_type=f32)  20.8 us
    dot_general x3, matrix products, tn(): lax.dot_general(a, b, (((0,), (0,)), ((), ())), preferred_element_type=f32)  19.5 us
    ppermute x19, starting transfers between devices, swap(): return lax.ppermute(value, axis, [(0, 1), (1, 0)])  19.5 us
  transfers between devices with their start and end apart: 75, of which 30 were waited for; matrix products, arithmetic and copies ran while one was open for 28% of the time, Pallas kernels for 22%

profile of v4, /device:TPU:0, one launch (start us, length us, event | category | flops | bytes accessed | tf_op | source)
XLA Modules:
  0.0 476.7 jit_solution(12902097658489459565)
XLA Ops:
  2.4 4.0 collective-permute-start.1
  12.3 1.9 collective-permute-start.2
  24.1 2.8 collective-permute-done.5
  27.7 5.9 %collective-permute-done.3 = bf16[96,1920]{1,0:T(8,128)(2,1)} collective-permute-done((bf16[96,1920]{1,0:T(8,128)(2,1)S(1)}, bf16[96,1920]{1,0:T(8,128)(2,1)}, u32[]{:S(2)}, u32[]{:S(2)}) %collective-permute-start.3) | collective-permute-done | bytes 368672 | tf_op jit(solution)/shard_map/ppermute | solution.py:649
  36.2 2.2 collective-permute-start.13
  38.4 2.0 collective-permute-start.12
  40.4 3.2 maximum_select_fusion
  44.3 4.0 collective-permute-start.15
  61.0 4.7 maximum_select_fusion.1
  75.0 3.0 collective-permute-start.20
  81.5 3.6 collective-permute-done.20
  85.1 3.9 collective-permute-done.18
  89.2 2.2 collective-permute-start.21
  93.5 4.3 collective-permute-done.21
  100.0 4.0 collective-permute-done.27.refs_1_
  104.0 2.0 collective-permute-done.28.refs_3_
  107.7 11.0 %collective-permute-done.29.refs_5_ = bf16[4,96,896]{2,1,0:T(8,128)(2,1)S(1)} collective-permute-done((bf16[4,96,896]{2,1,0:T(8,128)(2,1)S(1)}, bf16[4,96,896]{2,1,0:T(8,128)(2,1)S(1)}, u32[]{:S(2)}, u32[]{:S(2)}) %collective-permute-start.29) | collective-permute-done | bytes 688160 | tf_op jit(solution)/shard_map/ppermute | solution.py:649
  118.7 4.1 collective-permute-done.30.refs_7_
  122.8 2.4 join.3
  125.2 8.9 %fusion.61.xbc.halo.prev = f32[1040,1920]{1,0:T(8,128)} fusion(bf16[1040,1536]{1,0:T(8,128)(2,1)S(1)} %pre_norm.1, bf16[1536,1920]{1,0:T(8,128)(2,1)S(1)} %join.3), kind=kOutput, calls=%fused_computation.248 | convolution fusion | flops 6134169600 | bytes 17080320 | tf_op jit(solution)/shard_map/dot_general | solution.py:36
  136.2 2.6 collective-permute-start.31
  138.7 14.5 %block_states.1 = (f32[1024,1536]{1,0:T(8,128)S(1)}, f32[1024,1792]{1,0:T(8,128)}, f32[1024,256]{1,0:T(8,128)S(1)}, f32[1024,256]{1,0:T(8,128)S(1)}, f32[1024,12...) custom-call(f32[1040,1920]{1,0:T(8,128)} %fusion.61.xbc.halo.prev, ...), custom_call_target="tpu_custom_call" | custom-call | flops 402653184 | bytes 17432576 | tf_op jit(solution)/shard_map/block_states/pallas_call | solution.py:192
  153.2 2.7 copy-done.2
  155.9 3.2 collective-permute-start.32
  159.1 10.7 %inner_part.1.yin = f32[1024,1536]{1,0:T(8,128)S(1)} custom-call(f32[1024,256]{1,0:T(8,128)S(1)} %get-tuple-element.309.s, f32[1024,128]{1,0:T(8,128)S(1)} %get-tuple-element.310.ld, f32[4,32,256]{2,1,0:T(8,128)S(1)} %get-tuple-element.311.ldt, f32[1024,128]{1,0:T(8,128)S(1)} %get-tuple-element.312.dt, f32[1024,1536]{1,0:T(8,128)} %copy-done.2, ...), custom_call_target="tpu_custom_call" | custom-call | flops 3221225472 | bytes 16777216 | tf_op jit(solution)/shard_map/inner_part/pallas_call | solution.py:267
  171.4 6.8 %fusion.10.z = f32[1024,1536]{1,0:T(8,128)} fusion(bf16[1536,1536]{1,0:T(8,128)(2,1)S(1)} %join.4, bf16[1040,1536]{1,0:T(8,128)(2,1)S(1)} %pre_norm.1), kind=kOutput, calls=%fused_computation.31 | convolution fusion | flops 4831838208 | bytes 14155776 | tf_op jit(solution)/shard_map/dot_general | solution.py:36
  178.7 7.8 %gate_part.1 = (f32[1024,1536]{1,0:T(8,128)S(1)}, f32[1024,128]{1,0:T(8,128)}) custom-call(f32[1024,1536]{1,0:T(8,128)S(1)} %inner_part.1.yin, f32[1024,256]{1,0:T(8,128)S(1)} %get-tuple-element.318.bc, bf16[4,128,1536]{2,1,0:T(8,128)(2,1)S(1)} %bitcast.169, f32[1024,128]{1,0:T(8,128)S(1)} %get-tuple-element.310.ld, ...), custom_call_target="tpu_custom_call", output_to_operand_aliasing={{0}: (0, {})} | custom-call | flops 402653184 | bytes 18874368 | tf_op jit(solution)/shard_map/gate_part/pallas_call | solution.py:306
  186.4 2.6 copy-done
  192.8 5.9 %multiply_multiply_fusion.exact = f32[1024,1536]{1,0:T(8,128)S(1)} fusion(f32[1024,1536]{1,0:T(8,128)} %copy-done, f32[1024,1536]{1,0:T(8,128)} %fusion.10.z, f32[1536]{0:T(1024)S(1)} %slice_reduce_fusion.1, f32[1024]{0:T(1024)S(1)} %fusion.36), kind=kLoop, calls=%fused_computation.5 | loop fusion | flops 11010048 | bytes 18884608 | tf_op jit(solution)/shard_map/mul | solution.py:1034
  198.8 5.4 %convolution_convert_fusion.1.refs_0_ = bf16[1536,1536]{1,0:T(8,128)(2,1)S(1)} fusion(bf16[1024,1536]{1,0:T(8,128)(2,1)S(1)} %bitcast.177, f32[1024,1536]{1,0:T(8,128)S(1)} %multiply_multiply_fusion.exact), kind=kOutput, calls=%fused_computation.1 | convolution fusion | flops 4835770368 | bytes 14155776 | tf_op jit(solution)/shard_map/dot_general | solution.py:44
  206.4 13.5 %collective-permute-done.38.refs_3_ = bf16[8,96,768]{2,1,0:T(8,128)(2,1)S(1)} collective-permute-done((bf16[8,96,768]{2,1,0:T(8,128)(2,1)}, bf16[8,96,768]{2,1,0:T(8,128)(2,1)S(1)}, u32[]{:S(2)}, u32[]{:S(2)}) %collective-permute-start.38) | collective-permute-done | bytes 1179680 | tf_op jit(solution)/shard_map/ppermute | solution.py:649
  220.0 2.4 join.5.w
  222.4 5.0 %fusion.14 = f32[1024,1536]{1,0:T(8,128)S(1)} fusion(bf16[1536,1536]{1,0:T(8,128)(2,1)S(1)} %join.5.w, f32[1024,1536]{1,0:T(8,128)S(1)} %multiply_multiply_fusion.exact), kind=kOutput, calls=%fused_computation.42 | convolution fusion | flops 4833411072 | bytes 17301504 | tf_op jit(solution)/shard_map/dot_general | solution.py:36
  228.9 10.2 %out_back.1 = (f32[1024,1536]{1,0:T(8,128)}, f32[1024,128]{1,0:T(8,128)S(1)}) custom-call(bf16[1024,1536]{1,0:T(8,128)(2,1)S(1)} %bitcast.178, bf16[1536,1536]{1,0:T(8,128)(2,1)S(1)} %join.5.w, f32[1024,1536]{1,0:T(8,128)} %copy-done.42), custom_call_target="tpu_custom_call" | custom-call | flops 4831838208 | bytes 20447232 | tf_op jit(solution)/shard_map/out_back/pallas_call | solution.py:337
  240.1 2.4 add_convert_fusion.4
  244.6 14.6 %gate_back.1 = (bf16[1024,1536]{1,0:T(8,128)(2,1)S(1)}, bf16[1024,1536]{1,0:T(8,128)(2,1)S(1)}, f32[1024,128]{1,0:T(8,128)S(1)}, f32[2,128,1536]{2,1,0:T(8,128)S...) custom-call(f32[1024,1536]{1,0:T(8,128)} %copy-done, ...), custom_call_target="tpu_custom_call" | custom-call | flops 1610612736 | bytes 37748736 | tf_op jit(solution)/shard_map/gate_back/pallas_call | solution.py:405
  260.6 5.4 %convolution_convert_fusion.refs_0_ = bf16[1536,1536]{1,0:T(8,128)(2,1)S(1)} fusion(bf16[1024,1536]{1,0:T(8,128)(2,1)S(1)} %get-tuple-element.418, bf16[1040,1536]{1,0:T(8,128)(2,1)S(1)} %copy-done.9), kind=kOutput, calls=%fused_computation | convolution fusion | flops 4834197504 | bytes 11010048 | tf_op jit(solution)/shard_map/dot_general | solution.py:44
  269.2 4.1 collective-permute-start.44
  276.3 16.3 %inner_back.1 = (f32[1024,1536]{1,0:T(8,128)S(1)}, f32[1024,128]{1,0:T(8,128)S(1)}, f32[1024,256]{1,0:T(8,128)S(1)}) custom-call(f32[1024,256]{1,0:T(8,128)S(1)} %copy-done.20, f32[1024,256]{1,0:T(8,128)S(1)} %get-tuple-element.318.bc, f32[1024,128]{1,0:T(8,128)S(1)} %get-tuple-element.310.ld, f32[4,32,256]{2,1,0:T(8,128)S(1)} %copy-done.28, ...), custom_call_target="tpu_custom_call" | custom-call | flops 6442450944 | bytes 16777216 | tf_op jit(solution)/shard_map/inner_back/pallas_call | solution.py:487
  292.6 2.7 copy-done.5
  296.4 9.7 %collective-permute-done.44 = bf16[8,96,768]{2,1,0:T(8,128)(2,1)S(1)} collective-permute-done((bf16[8,96,768]{2,1,0:T(8,128)(2,1)S(1)}, bf16[8,96,768]{2,1,0:T(8,128)(2,1)S(1)}, u32[]{:S(2)}, u32[]{:S(2)}) %collective-permute-start.44) | collective-permute-done | bytes 1179680 | tf_op jit(solution)/shard_map/ppermute | solution.py:649
  306.1 2.3 add_convert_fusion.2
  311.2 27.3 %conv_back.1 = (bf16[1040,1920]{1,0:T(8,128)(2,1)}, f32[8,1792]{1,0:T(8,128)}, f32[8,128]{1,0:T(8,128)}) custom-call(f32[1040,1920]{1,0:T(8,128)} %fusion.61.xbc.halo.prev, f32[1040,1920]{1,0:T(8,128)} %fusion.61.xbc.halo.prev, f32[1024,1792]{1,0:T(8,128)} %get-tuple-element.371.pre, f32[1024,1536]{1,0:T(8,128)} %copy-done.5, f32[1024,128]{1,0:T(8,128)} %copy-done.25, ...), custom_call_target="tpu_custom_call" | custom-call | flops 1207959552 | bytes 28311552 | tf_op jit(solution)/shard_map/conv_back/pallas_call | solution.py:610
  343.5 8.7 %convolution_convert_fusion.2.refs_0_ = bf16[1536,1920]{1,0:T(8,128)(2,1)S(1)} fusion(bf16[1040,1536]{1,0:T(8,128)(2,1)S(1)} %copy-done.10, bf16[1040,1920]{1,0:T(8,128)(2,1)S(1)} %copy-done.67), kind=kOutput, calls=%fused_computation.2 | convolution fusion | flops 6137118720 | bytes 13086720 | tf_op jit(solution)/shard_map/dot_general | solution.py:44
  354.3 2.1 collective-permute-done.50
  358.6 2.0 collective-permute-start.54
  360.7 9.1 %fusion.62 = f32[1040,1536]{1,0:T(8,128)} fusion(bf16[1040,1920]{1,0:T(8,128)(2,1)S(1)} %copy-done.67, bf16[1536,1920]{1,0:T(8,128)(2,1)S(1)} %bitcast.174), kind=kOutput, calls=%fused_computation.249 | convolution fusion | flops 6134169600 | bytes 16281600 | tf_op jit(solution)/shard_map/dot_general | solution.py:40
  373.1 3.8 collective-permute-done.62
  376.9 2.0 collective-permute-start.52
  378.9 2.1 collective-permute-done.52
  381.8 3.1 collective-permute-start.56
  384.8 7.2 %slice_add_fusion = f32[1024,1536]{1,0:T(8,128)S(1)} fusion(f32[1040,1536]{1,0:T(8,128)} %fusion.62, bf16[1024,1536]{1,0:T(8,128)(2,1)S(1)} %copy-done.31, bf16[1536,1536]{1,0:T(8,128)(2,1)S(1)} %bitcast.176), kind=kOutput, calls=%fused_computation.4 | convolution fusion | flops 4833411072 | bytes 20447232 | tf_op jit(solution)/shard_map/dot_general | solution.py:40
  392.0 9.3 %collective-permute-done.56 = f32[8,1792]{1,0:T(8,128)S(1)} collective-permute-done((f32[8,1792]{1,0:T(8,128)S(1)}, f32[8,1792]{1,0:T(8,128)S(1)}, u32[]{:S(2)}, u32[]{:S(2)}) %collective-permute-start.56) | collective-permute-done | bytes 57376 | tf_op jit(solution)/shard_map/ppermute | solution.py:849
  404.2 2.6 copy-done.38
  408.3 4.8 %fusion.8 = (bf16[2,256,1536]{2,1,0:T(8,128)(2,1)}, f32[2,256]{1,0:T(2,128)S(1)}) fusion(bf16[2,256,1536]{2,1,0:T(8,128)(2,1)} %collective-permute-done.65, f32[2,2,256,1536]{3,2,1,0:T(8,128)} %bitcast.185, s32[]{:T(128)S(6)} %select_n.268, bf16[2,1,256,1536]{3,2,1,0:T(8,128)(2,1)} %param.11), kind=kLoop, calls=%fused_computation.17 | loop fusion | flops 5504512 | bytes 7866372 | tf_op jit(solution)/shard_map/convert_element_type | solution.py:1052
  415.5 8.0 %collective-permute-done.60 = bf16[2,96,896]{2,1,0:T(8,128)(2,1)S(1)} collective-permute-done((bf16[2,96,896]{2,1,0:T(8,128)(2,1)S(1)}, bf16[2,96,896]{2,1,0:T(8,128)(2,1)S(1)}, u32[]{:S(2)}, u32[]{:S(2)}) %collective-permute-start.60) | collective-permute-done | bytes 344096 | tf_op jit(solution)/shard_map/ppermute | solution.py:649
  426.5 2.3 fusion.2
  428.8 4.2 fusion.5
  433.1 6.3 %collective-permute-done.58 = bf16[4,96,896]{2,1,0:T(8,128)(2,1)S(1)} collective-permute-done((bf16[4,96,896]{2,1,0:T(8,128)(2,1)S(1)}, bf16[4,96,896]{2,1,0:T(8,128)(2,1)S(1)}, u32[]{:S(2)}, u32[]{:S(2)}) %collective-permute-start.58) | collective-permute-done | bytes 688160 | tf_op jit(solution)/shard_map/ppermute | solution.py:649
  439.4 3.3 collective-permute-done.59
  448.1 5.0 %collective-permute-done.69 = f32[8,1792]{1,0:T(8,128)S(1)} collective-permute-done((f32[8,1792]{1,0:T(8,128)S(1)}, f32[8,1792]{1,0:T(8,128)S(1)}, u32[]{:S(2)}, u32[]{:S(2)}) %collective-permute-start.69) | collective-permute-done | bytes 57376 | tf_op jit(solution)/shard_map/ppermute | solution.py:849
  456.2 2.5 collective-permute-done.71
  458.8 8.4 %collective-permute-done.70 = bf16[96,1920]{1,0:T(8,128)(2,1)S(1)} collective-permute-done((bf16[96,1920]{1,0:T(8,128)(2,1)S(1)}, bf16[96,1920]{1,0:T(8,128)(2,1)S(1)}, u32[]{:S(2)}, u32[]{:S(2)}) %collective-permute-start.70) | collective-permute-done | bytes 368672 | tf_op jit(solution)/shard_map/ppermute | solution.py:649
  474.3 1.9 copy.67
  (427 shorter events, 116.8 us)
Async XLA Ops:
  2.4 9.9 %collective-permute-start.1 = (bf16[664]{0:T(1024)(128)(2,1)S(1)}, bf16[664]{0:T(1024)(128)(2,1)S(1)}, u32[]{:S(2)}, u32[]{:S(2)}) collective-permute-start(bf16[664]{0:T(1024)(128)(2,1)S(1)} %pad_maximum_fusion.17), channel_id=1, source_target_pairs={{0,16},{16,0},{1,17},{17,1},{2,18},{18,2},{3,19},{19,3},{4,20},{20... | collective-permute-start | bytes 3992 | tf_op jit(solution)/shard_map/ppermute | solution.py:849
  9.5 6.7 %collective-permute-start.4 = (bf16[96,1536]{1,0:T(8,128)(2,1)S(1)}, bf16[96,1536]{1,0:T(8,128)(2,1)S(1)}, u32[]{:S(2)}, u32[]{:S(2)}) collective-permute-start(bf16[96,1536]{1,0:T(8,128)(2,1)S(1)} %copy-done.68), channel_id=1, source_target_pairs={{0,0},{1,16},{16,1},{17,17},{2,2},{3,18},{18,3},{19,19},{4,4},{5,2... | collective-permute-start | bytes 884744 | tf_op jit(solution)/shard_map/ppermute | solution.py:901
  10.1 7.8 %collective-permute-start = (bf16[48,3456]{1,0:T(8,128)(2,1)S(1)}, bf16[48,3456]{1,0:T(8,128)(2,1)S(1)}, u32[]{:S(2)}, u32[]{:S(2)}) collective-permute-start(bf16[48,3456]{1,0:T(8,128)(2,1)S(1)} %get-tuple-element.240), channel_id=1, source_target_pairs={{0,1},{1,0},{2,3},{3,2},{4,5},{5,4},{6,7},{7,6},{8,9},{9,8},{10,11... | collective-permute-start | bytes 995336 | tf_op jit(solution)/shard_map/ppermute | solution.py:849
  11.6 21.9 %collective-permute-start.9 = (bf16[2,256,1536]{2,1,0:T(8,128)(2,1)}, bf16[2,256,1536]{2,1,0:T(8,128)(2,1)}, u32[]{:S(2)}, u32[]{:S(2)}) collective-permute-start(bf16[2,256,1536]{2,1,0:T(8,128)(2,1)} %bitcast.182), channel_id=1, source_target_pairs={{0,1},{1,0},{2,3},{3,2},{4,5},{5,4},{6,7},{7,6},{8,9},{9,8},{10,11... | collective-permute-start | bytes 4718600 | tf_op jit(solution)/shard_map/ppermute | solution.py:849
  11.7 21.9 %collective-permute-start.8 = (bf16[2,256,1536]{2,1,0:T(8,128)(2,1)S(1)}, bf16[2,256,1536]{2,1,0:T(8,128)(2,1)}, u32[]{:S(2)}, u32[]{:S(2)}) collective-permute-start(bf16[2,256,1536]{2,1,0:T(8,128)(2,1)S(1)} %bitcast.180), channel_id=1, source_target_pairs={{0,1},{1,0},{2,3},{3,2},{4,5},{5,4},{6,7},{7,6},{8,9},{9,8},{10,11... | collective-permute-start | bytes 4718600 | tf_op jit(solution)/shard_map/ppermute | solution.py:849
  16.2 7.2 %collective-permute-start.6 = (bf16[1,96,768]{2,1,0:T(8,128)(2,1)S(1)}, bf16[1,96,768]{2,1,0:T(8,128)(2,1)S(1)}, u32[]{:S(2)}, u32[]{:S(2)}) collective-permute-start(bf16[1,96,768]{2,1,0:T(8,128)(2,1)S(1)} %get-tuple-element.507), channel_id=1, source_target_pairs={{0,4},{4,0},{1,5},{5,1},{2,6},{6,2},{3,7},{7,3},{8,12},{12,8},{9,1... | collective-permute-start | bytes 442376 | tf_op jit(solution)/shard_map/ppermute | solution.py:649
  18.5 15.0 %collective-permute-start.3 = (bf16[96,1920]{1,0:T(8,128)(2,1)S(1)}, bf16[96,1920]{1,0:T(8,128)(2,1)}, u32[]{:S(2)}, u32[]{:S(2)}) collective-permute-start(bf16[96,1920]{1,0:T(8,128)(2,1)S(1)} %slice.300), channel_id=1, source_target_pairs={{0,8},{8,16},{16,24},{24,0},{1,9},{9,17},{17,25},{25,1},{2,10},{10... | collective-permute-start | bytes 1105928 | tf_op jit(solution)/shard_map/ppermute | solution.py:649
  33.5 17.8 %collective-permute-start.10 = (bf16[96,1920]{1,0:T(8,128)(2,1)}, bf16[96,1920]{1,0:T(8,128)(2,1)}, u32[]{:S(2)}, u32[]{:S(2)}) collective-permute-start(bf16[96,1920]{1,0:T(8,128)(2,1)} %collective-permute-done.3), channel_id=1, source_target_pairs={{0,8},{8,16},{16,24},{24,0},{1,9},{9,17},{17,25},{25,1},{2,10},{10... | collective-permute-start | bytes 1105928 | tf_op jit(solution)/shard_map/ppermute | solution.py:649
  36.2 12.1 %collective-permute-start.13 = (bf16[2,2,2,664]{3,1,0,2:T(2,128)(2,1)S(1)}, bf16[2,2,2,664]{3,1,0,2:T(2,128)(2,1)S(1)}, u32[]{:S(2)}, u32[]{:S(2)}) collective-permute-start(bf16[2,2,2,664]{3,1,0,2:T(2,128)(2,1)S(1)} %broadcast_select_fusion.3), channel_id=1, source_target_pairs={{0,2},{2,0},{1,3},{3,1},{4,6},{6,4},{5,7},{7,5},{8,10},{10,8},{9,1... | collective-permute-start | bytes 31880 | tf_op jit(solution)/shard_map/ppermute | solution.py:849
  38.4 12.9 %collective-permute-start.11 = (bf16[2,96,896]{2,1,0:T(8,128)(2,1)S(1)}, bf16[2,96,896]{2,1,0:T(8,128)(2,1)}, u32[]{:S(2)}, u32[]{:S(2)}) collective-permute-start(bf16[2,96,896]{2,1,0:T(8,128)(2,1)S(1)} %pad_maximum_fusion.13), channel_id=1, source_target_pairs={{0,2},{2,0},{1,3},{3,1},{4,6},{6,4},{5,7},{7,5},{8,10},{10,8},{9,1... | collective-permute-start | bytes 1032200 | tf_op jit(solution)/shard_map/ppermute | solution.py:649
  38.4 12.9 %collective-permute-start.12 = (bf16[2,96,1024]{2,1,0:T(8,128)(2,1)}, bf16[2,96,1024]{2,1,0:T(8,128)(2,1)}, u32[]{:S(2)}, u32[]{:S(2)}) collective-permute-start(bf16[2,96,1024]{2,1,0:T(8,128)(2,1)} %pad_maximum_fusion.11), channel_id=1, source_target_pairs={{0,4},{4,0},{1,5},{5,1},{2,6},{6,2},{3,7},{7,3},{8,12},{12,8},{9,1... | collective-permute-start | bytes 1179656 | tf_op jit(solution)/shard_map/ppermute | solution.py:649
  44.3 7.0 %collective-permute-start.15 = (bf16[2,8,1536]{2,1,0:T(8,128)(2,1)}, bf16[2,8,1536]{2,1,0:T(8,128)(2,1)}, u32[]{:S(2)}, u32[]{:S(2)}) collective-permute-start(bf16[2,8,1536]{2,1,0:T(8,128)(2,1)} %slice_bitcast_fusion.8), channel_id=1, source_target_pairs={{0,2},{1,3},{4,6},{5,7},{8,10},{9,11},{12,14},{13,15},{16,18},{17,... | collective-permute-start | bytes 147464 | tf_op jit(solution)/shard_map/ppermute | solution.py:922
  51.4 18.1 %collective-permute-start.17 = (bf16[96,1536]{1,0:T(8,128)(2,1)}, bf16[96,1536]{1,0:T(8,128)(2,1)}, u32[]{:S(2)}, u32[]{:S(2)}) collective-permute-start(bf16[96,1536]{1,0:T(8,128)(2,1)} %slice.301), channel_id=1, source_target_pairs={{0,8},{8,16},{16,24},{24,0},{1,9},{9,17},{17,25},{25,1},{2,10},{10... | collective-permute-start | bytes 884744 | tf_op jit(solution)/shard_map/ppermute | solution.py:649
  51.4 19.4 %collective-permute-start.16 = (bf16[96,1920]{1,0:T(8,128)(2,1)}, bf16[96,1920]{1,0:T(8,128)(2,1)}, u32[]{:S(2)}, u32[]{:S(2)}) collective-permute-start(bf16[96,1920]{1,0:T(8,128)(2,1)} %collective-permute-done.10), channel_id=1, source_target_pairs={{0,8},{8,16},{16,24},{24,0},{1,9},{9,17},{17,25},{25,1},{2,10},{10... | collective-permute-start | bytes 1105928 | tf_op jit(solution)/shard_map/ppermute | solution.py:649
  70.8 10.0 %collective-permute-start.22 = (bf16[2,96,768]{2,1,0:T(8,128)(2,1)S(1)}, bf16[2,96,768]{2,1,0:T(8,128)(2,1)S(1)}, u32[]{:S(2)}, u32[]{:S(2)}) collective-permute-start(bf16[2,96,768]{2,1,0:T(8,128)(2,1)S(1)} %copy-done.51), channel_id=1, source_target_pairs={{0,4},{4,0},{1,5},{5,1},{2,6},{6,2},{3,7},{7,3},{8,12},{12,8},{9,1... | collective-permute-start | bytes 884744 | tf_op jit(solution)/shard_map/ppermute | solution.py:649
  71.4 10.0 %collective-permute-start.23 = (bf16[2,96,768]{2,1,0:T(8,128)(2,1)S(1)}, bf16[2,96,768]{2,1,0:T(8,128)(2,1)S(1)}, u32[]{:S(2)}, u32[]{:S(2)}) collective-permute-start(bf16[2,96,768]{2,1,0:T(8,128)(2,1)S(1)} %copy-done.50), channel_id=1, source_target_pairs={{0,2},{2,0},{1,3},{3,1},{4,6},{6,4},{5,7},{7,5},{8,10},{10,8},{9,1... | collective-permute-start | bytes 884744 | tf_op jit(solution)/shard_map/ppermute | solution.py:649
  72.4 16.8 %collective-permute-start.19 = (bf16[2,96,1024]{2,1,0:T(8,128)(2,1)S(1)}, bf16[2,96,1024]{2,1,0:T(8,128)(2,1)S(1)}, u32[]{:S(2)}, u32[]{:S(2)}) collective-permute-start(bf16[2,96,1024]{2,1,0:T(8,128)(2,1)S(1)} %pad_maximum_fusion.10), channel_id=1, source_target_pairs={{0,4},{4,0},{1,5},{5,1},{2,6},{6,2},{3,7},{7,3},{8,12},{12,8},{9,1... | collective-permute-start | bytes 1179656 | tf_op jit(solution)/shard_map/ppermute | solution.py:649
  75.0 10.1 %collective-permute-start.20 = (bf16[96,1536]{1,0:T(8,128)(2,1)}, bf16[96,1536]{1,0:T(8,128)(2,1)S(1)}, u32[]{:S(2)}, u32[]{:S(2)}) collective-permute-start(bf16[96,1536]{1,0:T(8,128)(2,1)} %collective-permute-done.17), channel_id=1, source_target_pairs={{0,8},{8,16},{16,24},{24,0},{1,9},{9,17},{17,25},{25,1},{2,10},{10... | collective-permute-start | bytes 884744 | tf_op jit(solution)/shard_map/ppermute | solution.py:649
  78.1 11.0 %collective-permute-start.18 = (bf16[2,96,896]{2,1,0:T(8,128)(2,1)S(1)}, bf16[2,96,896]{2,1,0:T(8,128)(2,1)S(1)}, u32[]{:S(2)}, u32[]{:S(2)}) collective-permute-start(bf16[2,96,896]{2,1,0:T(8,128)(2,1)S(1)} %pad_maximum_fusion.12), channel_id=1, source_target_pairs={{0,2},{2,0},{1,3},{3,1},{4,6},{6,4},{5,7},{7,5},{8,10},{10,8},{9,1... | collective-permute-start | bytes 1032200 | tf_op jit(solution)/shard_map/ppermute | solution.py:649
  80.8 23.2 %collective-permute-start.27 = (bf16[4,96,896]{2,1,0:T(8,128)(2,1)}, bf16[4,96,896]{2,1,0:T(8,128)(2,1)S(1)}, u32[]{:S(2)}, u32[]{:S(2)}) collective-permute-start(bf16[4,96,896]{2,1,0:T(8,128)(2,1)} %constant_dynamic-update-slice_fusion.refs_0_), channel_id=1, source_target_pairs={{0,4},{4,0},{1,5},{5,1},{2,6},{6,2},{3,7},{7,3},{8,12},{12,8},{9,1... | collective-permute-start | bytes 2064392 | tf_op jit(solution)/shard_map/ppermute | solution.py:649
  81.4 24.6 %collective-permute-start.28 = (bf16[4,96,1024]{2,1,0:T(8,128)(2,1)}, bf16[4,96,1024]{2,1,0:T(8,128)(2,1)S(1)}, u32[]{:S(2)}, u32[]{:S(2)}) collective-permute-start(bf16[4,96,1024]{2,1,0:T(8,128)(2,1)} %constant_dynamic-update-slice_fusion.2.refs_2_), channel_id=1, source_target_pairs={{0,2},{2,0},{1,3},{3,1},{4,6},{6,4},{5,7},{7,5},{8,10},{10,8},{9,1... | collective-permute-start | bytes 2359304 | tf_op jit(solution)/shard_map/ppermute | solution.py:649
  89.2 8.5 %collective-permute-start.21 = (bf16[96,1536]{1,0:T(8,128)(2,1)S(1)}, bf16[96,1536]{1,0:T(8,128)(2,1)S(1)}, u32[]{:S(2)}, u32[]{:S(2)}) collective-permute-start(bf16[96,1536]{1,0:T(8,128)(2,1)S(1)} %collective-permute-done.20), channel_id=1, source_target_pairs={{0,8},{8,16},{16,24},{24,0},{1,9},{9,17},{17,25},{25,1},{2,10},{10... | collective-permute-start | bytes 884744 | tf_op jit(solution)/shard_map/ppermute | solution.py:649
  91.5 27.2 %collective-permute-start.29 = (bf16[4,96,896]{2,1,0:T(8,128)(2,1)S(1)}, bf16[4,96,896]{2,1,0:T(8,128)(2,1)S(1)}, u32[]{:S(2)}, u32[]{:S(2)}) collective-permute-start(bf16[4,96,896]{2,1,0:T(8,128)(2,1)S(1)} %constant_dynamic-update-slice_fusion.4.refs_4_), channel_id=1, source_target_pairs={{0,4},{4,0},{1,5},{5,1},{2,6},{6,2},{3,7},{7,3},{8,12},{12,8},{9,1... | collective-permute-start | bytes 2064392 | tf_op jit(solution)/shard_map/ppermute | solution.py:649
  92.6 30.2 %collective-permute-start.30 = (bf16[4,96,1024]{2,1,0:T(8,128)(2,1)S(1)}, bf16[4,96,1024]{2,1,0:T(8,128)(2,1)S(1)}, u32[]{:S(2)}, u32[]{:S(2)}) collective-permute-start(bf16[4,96,1024]{2,1,0:T(8,128)(2,1)S(1)} %constant_dynamic-update-slice_fusion.6.refs_6_), channel_id=1, source_target_pairs={{0,2},{2,0},{1,3},{3,1},{4,6},{6,4},{5,7},{7,5},{8,10},{10,8},{9,1... | collective-permute-start | bytes 2359304 | tf_op jit(solution)/shard_map/ppermute | solution.py:649
  98.9 35.1 %collective-permute-start.26 = (bf16[4,96,768]{2,1,0:T(8,128)(2,1)S(1)}, bf16[4,96,768]{2,1,0:T(8,128)(2,1)S(1)}, u32[]{:S(2)}, u32[]{:S(2)}) collective-permute-start(bf16[4,96,768]{2,1,0:T(8,128)(2,1)S(1)} %get-tuple-element.299), channel_id=1, source_target_pairs={{0,4},{4,0},{1,5},{5,1},{2,6},{6,2},{3,7},{7,3},{8,12},{12,8},{9,1... | collective-permute-start | bytes 1769480 | tf_op jit(solution)/shard_map/ppermute | solution.py:649
  104.0 30.1 %collective-permute-start.25 = (bf16[4,96,768]{2,1,0:T(8,128)(2,1)S(1)}, bf16[4,96,768]{2,1,0:T(8,128)(2,1)S(1)}, u32[]{:S(2)}, u32[]{:S(2)}) collective-permute-start(bf16[4,96,768]{2,1,0:T(8,128)(2,1)S(1)} %get-tuple-element.297), channel_id=1, source_target_pairs={{0,2},{2,0},{1,3},{3,1},{4,6},{6,4},{5,7},{7,5},{8,10},{10,8},{9,1... | collective-permute-start | bytes 1769480 | tf_op jit(solution)/shard_map/ppermute | solution.py:649
  105.9 30.2 %collective-permute-start.24 = (bf16[8,96,768]{2,1,0:T(8,128)(2,1)S(1)}, bf16[8,96,768]{2,1,0:T(8,128)(2,1)S(1)}, u32[]{:S(2)}, u32[]{:S(2)}) collective-permute-start(bf16[8,96,768]{2,1,0:T(8,128)(2,1)S(1)} %constant_dynamic-update-slice_fusion.8.refs_0_), channel_id=1, source_target_pairs={{0,8},{8,16},{16,24},{24,0},{1,9},{9,17},{17,25},{25,1},{2,10},{10... | collective-permute-start | bytes 3538952 | tf_op jit(solution)/shard_map/ppermute | solution.py:649
  134.2 35.7 %collective-permute-start.34 = (bf16[8,96,768]{2,1,0:T(8,128)(2,1)S(1)}, bf16[8,96,768]{2,1,0:T(8,128)(2,1)S(1)}, u32[]{:S(2)}, u32[]{:S(2)}) collective-permute-start(bf16[8,96,768]{2,1,0:T(8,128)(2,1)S(1)} %constant_dynamic-update-slice_fusion.12.refs_2_), channel_id=1, source_target_pairs={{0,2},{2,0},{1,3},{3,1},{4,6},{6,4},{5,7},{7,5},{8,10},{10,8},{9,1... | collective-permute-start | bytes 3538952 | tf_op jit(solution)/shard_map/ppermute | solution.py:649
  135.6 34.3 %collective-permute-start.33 = (bf16[8,96,768]{2,1,0:T(8,128)(2,1)S(1)}, bf16[8,96,768]{2,1,0:T(8,128)(2,1)S(1)}, u32[]{:S(2)}, u32[]{:S(2)}) collective-permute-start(bf16[8,96,768]{2,1,0:T(8,128)(2,1)S(1)} %constant_dynamic-update-slice_fusion.10.refs_0_), channel_id=1, source_target_pairs={{0,4},{4,0},{1,5},{5,1},{2,6},{6,2},{3,7},{7,3},{8,12},{12,8},{9,1... | collective-permute-start | bytes 3538952 | tf_op jit(solution)/shard_map/ppermute | solution.py:649
  136.2 42.5 %collective-permute-start.31 = (bf16[8,96,768]{2,1,0:T(8,128)(2,1)S(1)}, bf16[8,96,768]{2,1,0:T(8,128)(2,1)}, u32[]{:S(2)}, u32[]{:S(2)}) collective-permute-start(bf16[8,96,768]{2,1,0:T(8,128)(2,1)S(1)} %collective-permute-done.24.refs_1_), channel_id=1, source_target_pairs={{0,8},{8,16},{16,24},{24,0},{1,9},{9,17},{17,25},{25,1},{2,10},{10... | collective-permute-start | bytes 3538952 | tf_op jit(solution)/shard_map/ppermute | solution.py:649
  155.9 22.4 %collective-permute-start.32 = (bf16[2,128,1536]{2,1,0:T(8,128)(2,1)S(1)}, bf16[2,128,1536]{2,1,0:T(8,128)(2,1)S(1)}, u32[]{:S(2)}, u32[]{:S(2)}) collective-permute-start(bf16[2,128,1536]{2,1,0:T(8,128)(2,1)S(1)} %get-tuple-element.319), channel_id=1, source_target_pairs={{0,2},{1,3},{4,6},{5,7},{8,10},{9,11},{12,14},{13,15},{16,18},{17,... | collective-permute-start | bytes 2359304 | tf_op jit(solution)/shard_map/ppermute | solution.py:1014
  189.1 30.8 %collective-permute-start.38 = (bf16[8,96,768]{2,1,0:T(8,128)(2,1)}, bf16[8,96,768]{2,1,0:T(8,128)(2,1)S(1)}, u32[]{:S(2)}, u32[]{:S(2)}) collective-permute-start(bf16[8,96,768]{2,1,0:T(8,128)(2,1)} %collective-permute-done.31.refs_2_), channel_id=1, source_target_pairs={{0,8},{8,16},{16,24},{24,0},{1,9},{9,17},{17,25},{25,1},{2,10},{10... | collective-permute-start | bytes 3538952 | tf_op jit(solution)/shard_map/ppermute | solution.py:649
  205.8 33.3 %collective-permute-start.36 = (bf16[8,96,768]{2,1,0:T(8,128)(2,1)S(1)}, bf16[8,96,768]{2,1,0:T(8,128)(2,1)}, u32[]{:S(2)}, u32[]{:S(2)}) collective-permute-start(bf16[8,96,768]{2,1,0:T(8,128)(2,1)S(1)} %get-tuple-element.332), channel_id=1, source_target_pairs={{0,4},{4,0},{1,5},{5,1},{2,6},{6,2},{3,7},{7,3},{8,12},{12,8},{9,1... | collective-permute-start | bytes 3538952 | tf_op jit(solution)/shard_map/ppermute | solution.py:649
  206.3 32.7 %collective-permute-start.37 = (bf16[8,96,768]{2,1,0:T(8,128)(2,1)S(1)}, bf16[8,96,768]{2,1,0:T(8,128)(2,1)S(1)}, u32[]{:S(2)}, u32[]{:S(2)}) collective-permute-start(bf16[8,96,768]{2,1,0:T(8,128)(2,1)S(1)} %get-tuple-element.333), channel_id=1, source_target_pairs={{0,2},{2,0},{1,3},{3,1},{4,6},{6,4},{5,7},{7,5},{8,10},{10,8},{9,1... | collective-permute-start | bytes 3538952 | tf_op jit(solution)/shard_map/ppermute | solution.py:649
  228.9 179.4 %collective-permute-start.65 = (bf16[2,256,1536]{2,1,0:T(8,128)(2,1)}, bf16[2,256,1536]{2,1,0:T(8,128)(2,1)}, u32[]{:S(2)}, u32[]{:S(2)}) collective-permute-start(bf16[2,256,1536]{2,1,0:T(8,128)(2,1)} %fusion.12), channel_id=1, source_target_pairs={{0,1},{1,0},{2,3},{3,2},{4,5},{5,4},{6,7},{7,6},{8,9},{9,8},{10,11... | collective-permute-start | bytes 4718600 | tf_op jit(solution)/shard_map/ppermute | solution.py:849
  242.5 25.0 %collective-permute-start.39 = (bf16[4,96,768]{2,1,0:T(8,128)(2,1)}, bf16[4,96,768]{2,1,0:T(8,128)(2,1)S(1)}, u32[]{:S(2)}, u32[]{:S(2)}) collective-permute-start(bf16[4,96,768]{2,1,0:T(8,128)(2,1)} %get-tuple-element.477), channel_id=1, source_target_pairs={{0,2},{2,0},{1,3},{3,1},{4,6},{6,4},{5,7},{7,5},{8,10},{10,8},{9,1... | collective-permute-start | bytes 1769480 | tf_op jit(solution)/shard_map/ppermute | solution.py:649
  244.0 23.6 %collective-permute-start.40 = (bf16[4,96,768]{2,1,0:T(8,128)(2,1)}, bf16[4,96,768]{2,1,0:T(8,128)(2,1)}, u32[]{:S(2)}, u32[]{:S(2)}) collective-permute-start(bf16[4,96,768]{2,1,0:T(8,128)(2,1)} %get-tuple-element.475), channel_id=1, source_target_pairs={{0,4},{4,0},{1,5},{5,1},{2,6},{6,2},{3,7},{7,3},{8,12},{12,8},{9,1... | collective-permute-start | bytes 1769480 | tf_op jit(solution)/shard_map/ppermute | solution.py:649
  259.3 37.1 %collective-permute-start.45 = (bf16[2,128,1536]{2,1,0:T(8,128)(2,1)S(1)}, bf16[2,128,1536]{2,1,0:T(8,128)(2,1)}, u32[]{:S(2)}, u32[]{:S(2)}) collective-permute-start(bf16[2,128,1536]{2,1,0:T(8,128)(2,1)S(1)} %get-tuple-element.364), channel_id=1, source_target_pairs={{2,0},{3,1},{6,4},{7,5},{10,8},{11,9},{14,12},{15,13},{18,16},{19,... | collective-permute-start | bytes 2359304 | tf_op jit(solution)/shard_map/ppermute | solution.py:1063
  267.6 28.8 %collective-permute-start.43 = (bf16[8,96,768]{2,1,0:T(8,128)(2,1)S(1)}, bf16[8,96,768]{2,1,0:T(8,128)(2,1)}, u32[]{:S(2)}, u32[]{:S(2)}) collective-permute-start(bf16[8,96,768]{2,1,0:T(8,128)(2,1)S(1)} %get-tuple-element.359), channel_id=1, source_target_pairs={{0,4},{4,0},{1,5},{5,1},{2,6},{6,2},{3,7},{7,3},{8,12},{12,8},{9,1... | collective-permute-start | bytes 3538952 | tf_op jit(solution)/shard_map/ppermute | solution.py:649
  269.2 37.0 %collective-permute-start.44 = (bf16[8,96,768]{2,1,0:T(8,128)(2,1)S(1)}, bf16[8,96,768]{2,1,0:T(8,128)(2,1)S(1)}, u32[]{:S(2)}, u32[]{:S(2)}) collective-permute-start(bf16[8,96,768]{2,1,0:T(8,128)(2,1)S(1)} %get-tuple-element.360), channel_id=1, source_target_pairs={{0,2},{2,0},{1,3},{3,1},{4,6},{6,4},{5,7},{7,5},{8,10},{10,8},{9,1... | collective-permute-start | bytes 3538952 | tf_op jit(solution)/shard_map/ppermute | solution.py:649
  274.8 21.6 %collective-permute-start.42 = (bf16[96,1536]{1,0:T(8,128)(2,1)S(1)}, bf16[96,1536]{1,0:T(8,128)(2,1)S(1)}, u32[]{:S(2)}, u32[]{:S(2)}) collective-permute-start(bf16[96,1536]{1,0:T(8,128)(2,1)S(1)} %fusion.45), channel_id=1, source_target_pairs={{0,8},{8,16},{16,24},{24,0},{1,9},{9,17},{17,25},{25,1},{2,10},{10... | collective-permute-start | bytes 884744 | tf_op jit(solution)/shard_map/ppermute | solution.py:649
  308.4 31.6 %collective-permute-start.47 = (bf16[4,96,768]{2,1,0:T(8,128)(2,1)}, bf16[4,96,768]{2,1,0:T(8,128)(2,1)}, u32[]{:S(2)}, u32[]{:S(2)}) collective-permute-start(bf16[4,96,768]{2,1,0:T(8,128)(2,1)} %get-tuple-element.473), channel_id=1, source_target_pairs={{0,2},{2,0},{1,3},{3,1},{4,6},{6,4},{5,7},{7,5},{8,10},{10,8},{9,1... | collective-permute-start | bytes 1769480 | tf_op jit(solution)/shard_map/ppermute | solution.py:649
  309.5 30.5 %collective-permute-start.48 = (bf16[4,96,768]{2,1,0:T(8,128)(2,1)}, bf16[4,96,768]{2,1,0:T(8,128)(2,1)S(1)}, u32[]{:S(2)}, u32[]{:S(2)}) collective-permute-start(bf16[4,96,768]{2,1,0:T(8,128)(2,1)} %get-tuple-element.471), channel_id=1, source_target_pairs={{0,4},{4,0},{1,5},{5,1},{2,6},{6,2},{3,7},{7,3},{8,12},{12,8},{9,1... | collective-permute-start | bytes 1769480 | tf_op jit(solution)/shard_map/ppermute | solution.py:649
  311.1 28.9 %collective-permute-start.46 = (bf16[96,1536]{1,0:T(8,128)(2,1)S(1)}, bf16[96,1536]{1,0:T(8,128)(2,1)S(1)}, u32[]{:S(2)}, u32[]{:S(2)}) collective-permute-start(bf16[96,1536]{1,0:T(8,128)(2,1)S(1)} %fusion.33), channel_id=1, source_target_pairs={{0,8},{8,16},{16,24},{24,0},{1,9},{9,17},{17,25},{25,1},{2,10},{10... | collective-permute-start | bytes 884744 | tf_op jit(solution)/shard_map/ppermute | solution.py:649
  340.1 14.2 %collective-permute-start.49 = (bf16[96,1536]{1,0:T(8,128)(2,1)S(1)}, bf16[96,1536]{1,0:T(8,128)(2,1)S(1)}, u32[]{:S(2)}, u32[]{:S(2)}) collective-permute-start(bf16[96,1536]{1,0:T(8,128)(2,1)S(1)} %fusion.32), channel_id=1, source_target_pairs={{0,8},{8,16},{16,24},{24,0},{1,9},{9,17},{17,25},{25,1},{2,10},{10... | collective-permute-start | bytes 884744 | tf_op jit(solution)/shard_map/ppermute | solution.py:649
  341.7 14.6 %collective-permute-start.50 = (bf16[96,1536]{1,0:T(8,128)(2,1)S(1)}, bf16[96,1536]{1,0:T(8,128)(2,1)S(1)}, u32[]{:S(2)}, u32[]{:S(2)}) collective-permute-start(bf16[96,1536]{1,0:T(8,128)(2,1)S(1)} %fusion.46), channel_id=1, source_target_pairs={{0,8},{8,16},{16,24},{24,0},{1,9},{9,17},{17,25},{25,1},{2,10},{10... | collective-permute-start | bytes 884744 | tf_op jit(solution)/shard_map/ppermute | solution.py:649
  356.4 25.3 %collective-permute-start.51 = (bf16[96,1536]{1,0:T(8,128)(2,1)S(1)}, bf16[96,1536]{1,0:T(8,128)(2,1)S(1)}, u32[]{:S(2)}, u32[]{:S(2)}) collective-permute-start(bf16[96,1536]{1,0:T(8,128)(2,1)S(1)} %fusion.31), channel_id=1, source_target_pairs={{0,8},{8,16},{16,24},{24,0},{1,9},{9,17},{17,25},{25,1},{2,10},{10... | collective-permute-start | bytes 884744 | tf_op jit(solution)/shard_map/ppermute | solution.py:649
  358.1 43.2 %collective-permute-start.53 = (bf16[4,96,896]{2,1,0:T(8,128)(2,1)S(1)}, bf16[4,96,896]{2,1,0:T(8,128)(2,1)S(1)}, u32[]{:S(2)}, u32[]{:S(2)}) collective-permute-start(bf16[4,96,896]{2,1,0:T(8,128)(2,1)S(1)} %get-tuple-element.405), channel_id=1, source_target_pairs={{0,4},{4,0},{1,5},{5,1},{2,6},{6,2},{3,7},{7,3},{8,12},{12,8},{9,1... | collective-permute-start | bytes 2064392 | tf_op jit(solution)/shard_map/ppermute | solution.py:649
  358.6 42.7 %collective-permute-start.54 = (bf16[4,96,1024]{2,1,0:T(8,128)(2,1)S(1)}, bf16[4,96,1024]{2,1,0:T(8,128)(2,1)S(1)}, u32[]{:S(2)}, u32[]{:S(2)}) collective-permute-start(bf16[4,96,1024]{2,1,0:T(8,128)(2,1)S(1)} %get-tuple-element.406), channel_id=1, source_target_pairs={{0,2},{2,0},{1,3},{3,1},{4,6},{6,4},{5,7},{7,5},{8,10},{10,8},{9,1... | collective-permute-start | bytes 2359304 | tf_op jit(solution)/shard_map/ppermute | solution.py:649
  370.7 6.2 %collective-permute-start.62 = (bf16[16,1536]{1,0:T(8,128)(2,1)S(1)}, bf16[16,1536]{1,0:T(8,128)(2,1)S(1)}, u32[]{:S(2)}, u32[]{:S(2)}) collective-permute-start(bf16[16,1536]{1,0:T(8,128)(2,1)S(1)} %slice.551), channel_id=1, source_target_pairs={{2,0},{3,1},{6,4},{7,5},{10,8},{11,9},{14,12},{15,13},{18,16},{19,... | collective-permute-start | bytes 147464 | tf_op jit(solution)/shard_map/ppermute | solution.py:1112
  381.0 20.3 %collective-permute-start.55 = (f32[96,1536]{1,0:T(8,128)S(1)}, f32[96,1536]{1,0:T(8,128)S(1)}, u32[]{:S(2)}, u32[]{:S(2)}) collective-permute-start(f32[96,1536]{1,0:T(8,128)S(1)} %bitcast_add_fusion.4), channel_id=1, source_target_pairs={{0,0},{1,16},{16,1},{17,17},{2,2},{3,18},{18,3},{19,19},{4,4},{5,2... | collective-permute-start | bytes 1769480 | tf_op jit(solution)/shard_map/ppermute | solution.py:1109
  381.8 19.6 %collective-permute-start.56 = (f32[8,1792]{1,0:T(8,128)S(1)}, f32[8,1792]{1,0:T(8,128)S(1)}, u32[]{:S(2)}, u32[]{:S(2)}) collective-permute-start(f32[8,1792]{1,0:T(8,128)S(1)} %add.326), channel_id=1, source_target_pairs={{0,16},{16,0},{1,17},{17,1},{2,18},{18,2},{3,19},{19,3},{4,20},{20... | collective-permute-start | bytes 172040 | tf_op jit(solution)/shard_map/ppermute | solution.py:849
  408.1 16.9 %collective-permute-start.63 = (bf16[2,256,1536]{2,1,0:T(8,128)(2,1)}, bf16[2,256,1536]{2,1,0:T(8,128)(2,1)}, u32[]{:S(2)}, u32[]{:S(2)}) collective-permute-start(bf16[2,256,1536]{2,1,0:T(8,128)(2,1)} %fusion.13), channel_id=1, source_target_pairs={{0,1},{1,0},{2,3},{3,2},{4,5},{5,4},{6,7},{7,6},{8,9},{9,8},{10,11... | collective-permute-start | bytes 4718600 | tf_op jit(solution)/shard_map/ppermute | solution.py:849
  413.1 10.5 %collective-permute-start.60 = (bf16[2,96,896]{2,1,0:T(8,128)(2,1)S(1)}, bf16[2,96,896]{2,1,0:T(8,128)(2,1)S(1)}, u32[]{:S(2)}, u32[]{:S(2)}) collective-permute-start(bf16[2,96,896]{2,1,0:T(8,128)(2,1)S(1)} %copy-done.55), channel_id=1, source_target_pairs={{0,2},{2,0},{1,3},{3,1},{4,6},{6,4},{5,7},{7,5},{8,10},{10,8},{9,1... | collective-permute-start | bytes 1032200 | tf_op jit(solution)/shard_map/ppermute | solution.py:649
  413.1 12.0 %collective-permute-start.61 = (bf16[2,96,1024]{2,1,0:T(8,128)(2,1)S(1)}, bf16[2,96,1024]{2,1,0:T(8,128)(2,1)S(1)}, u32[]{:S(2)}, u32[]{:S(2)}) collective-permute-start(bf16[2,96,1024]{2,1,0:T(8,128)(2,1)S(1)} %get-tuple-element.483), channel_id=1, source_target_pairs={{0,4},{4,0},{1,5},{5,1},{2,6},{6,2},{3,7},{7,3},{8,12},{12,8},{9,1... | collective-permute-start | bytes 1179656 | tf_op jit(solution)/shard_map/ppermute | solution.py:649
  414.7 18.4 %collective-permute-start.57 = (bf16[96,1536]{1,0:T(8,128)(2,1)S(1)}, bf16[96,1536]{1,0:T(8,128)(2,1)S(1)}, u32[]{:S(2)}, u32[]{:S(2)}) collective-permute-start(bf16[96,1536]{1,0:T(8,128)(2,1)S(1)} %copy-done.56), channel_id=1, source_target_pairs={{0,8},{8,16},{16,24},{24,0},{1,9},{9,17},{17,25},{25,1},{2,10},{10... | collective-permute-start | bytes 884744 | tf_op jit(solution)/shard_map/ppermute | solution.py:649
  414.7 24.6 %collective-permute-start.58 = (bf16[4,96,896]{2,1,0:T(8,128)(2,1)S(1)}, bf16[4,96,896]{2,1,0:T(8,128)(2,1)S(1)}, u32[]{:S(2)}, u32[]{:S(2)}) collective-permute-start(bf16[4,96,896]{2,1,0:T(8,128)(2,1)S(1)} %copy-done.35), channel_id=1, source_target_pairs={{0,4},{4,0},{1,5},{5,1},{2,6},{6,2},{3,7},{7,3},{8,12},{12,8},{9,1... | collective-permute-start | bytes 2064392 | tf_op jit(solution)/shard_map/ppermute | solution.py:649
  423.5 19.2 %collective-permute-start.59 = (bf16[4,96,1024]{2,1,0:T(8,128)(2,1)S(1)}, bf16[4,96,1024]{2,1,0:T(8,128)(2,1)S(1)}, u32[]{:S(2)}, u32[]{:S(2)}) collective-permute-start(bf16[4,96,1024]{2,1,0:T(8,128)(2,1)S(1)} %get-tuple-element.427), channel_id=1, source_target_pairs={{0,2},{2,0},{1,3},{3,1},{4,6},{6,4},{5,7},{7,5},{8,10},{10,8},{9,1... | collective-permute-start | bytes 2359304 | tf_op jit(solution)/shard_map/ppermute | solution.py:649
  425.3 17.4 %collective-permute-start.64 = (bf16[96,1920]{1,0:T(8,128)(2,1)S(1)}, bf16[96,1920]{1,0:T(8,128)(2,1)S(1)}, u32[]{:S(2)}, u32[]{:S(2)}) collective-permute-start(bf16[96,1920]{1,0:T(8,128)(2,1)S(1)} %fusion.39), channel_id=1, source_target_pairs={{0,8},{8,16},{16,24},{24,0},{1,9},{9,17},{17,25},{25,1},{2,10},{10... | collective-permute-start | bytes 1105928 | tf_op jit(solution)/shard_map/ppermute | solution.py:649
  442.8 11.2 %collective-permute-start.68 = (bf16[96,1920]{1,0:T(8,128)(2,1)S(1)}, bf16[96,1920]{1,0:T(8,128)(2,1)S(1)}, u32[]{:S(2)}, u32[]{:S(2)}) collective-permute-start(bf16[96,1920]{1,0:T(8,128)(2,1)S(1)} %fusion.24), channel_id=1, source_target_pairs={{0,8},{8,16},{16,24},{24,0},{1,9},{9,17},{17,25},{25,1},{2,10},{10... | collective-permute-start | bytes 1105928 | tf_op jit(solution)/shard_map/ppermute | solution.py:649
  443.0 10.1 %collective-permute-start.66 = (bf16[2,96,896]{2,1,0:T(8,128)(2,1)S(1)}, bf16[2,96,896]{2,1,0:T(8,128)(2,1)S(1)}, u32[]{:S(2)}, u32[]{:S(2)}) collective-permute-start(bf16[2,96,896]{2,1,0:T(8,128)(2,1)S(1)} %get-tuple-element.485), channel_id=1, source_target_pairs={{0,2},{2,0},{1,3},{3,1},{4,6},{6,4},{5,7},{7,5},{8,10},{10,8},{9,1... | collective-permute-start | bytes 1032200 | tf_op jit(solution)/shard_map/ppermute | solution.py:649
  443.8 10.1 %collective-permute-start.67 = (bf16[2,96,1024]{2,1,0:T(8,128)(2,1)S(1)}, bf16[2,96,1024]{2,1,0:T(8,128)(2,1)S(1)}, u32[]{:S(2)}, u32[]{:S(2)}) collective-permute-start(bf16[2,96,1024]{2,1,0:T(8,128)(2,1)S(1)} %get-tuple-element.479), channel_id=1, source_target_pairs={{0,4},{4,0},{1,5},{5,1},{2,6},{6,2},{3,7},{7,3},{8,12},{12,8},{9,1... | collective-permute-start | bytes 1179656 | tf_op jit(solution)/shard_map/ppermute | solution.py:649
  445.4 7.7 %collective-permute-start.69 = (f32[8,1792]{1,0:T(8,128)S(1)}, f32[8,1792]{1,0:T(8,128)S(1)}, u32[]{:S(2)}, u32[]{:S(2)}) collective-permute-start(f32[8,1792]{1,0:T(8,128)S(1)} %add.329), channel_id=1, source_target_pairs={{0,2},{2,0},{1,3},{3,1},{4,6},{6,4},{5,7},{7,5},{8,10},{10,8},{9,1... | collective-permute-start | bytes 172040 | tf_op jit(solution)/shard_map/ppermute | solution.py:849
  454.4 12.8 %collective-permute-start.70 = (bf16[96,1920]{1,0:T(8,128)(2,1)S(1)}, bf16[96,1920]{1,0:T(8,128)(2,1)S(1)}, u32[]{:S(2)}, u32[]{:S(2)}) collective-permute-start(bf16[96,1920]{1,0:T(8,128)(2,1)S(1)} %fusion.21), channel_id=1, source_target_pairs={{0,8},{8,16},{16,24},{24,0},{1,9},{9,17},{17,25},{25,1},{2,10},{10... | collective-permute-start | bytes 1105928 | tf_op jit(solution)/shard_map/ppermute | solution.py:649
  (85 other events, 1403.3 us)

commit v5 on v4

--- a/solution.py
+++ b/solution.py
@@ -1045,13 +1045,8 @@
 
     gfin, dots = out_back(cot_all, w_o, exact)
 
-    partial_out = nn(fin, w_o).reshape(2, micros, T, D)
-    give = lax.dynamic_index_in_dim(partial_out, 1 - core, 0, False).astype(bf16)
-    keep = lax.dynamic_index_in_dim(partial_out, core, 0, False)
-    given_out = swap(give)
-    block_out = (hid_own.astype(f32) + keep + given_out.astype(f32)).astype(bf16)
-    if fast:
-        dots, gfin, give = fence([so_], dots, gfin, give)
+    if fast:
+        dots, gfin = fence([so_], dots, gfin)
         so_.first(0)
         (y,) = after([so_], y)
     dots = dots + swap(dots)
@@ -1141,12 +1136,18 @@
     )
 
     if fast:
-        tiny, g_hid, block_out = fence([sz_, sx_], tiny, g_hid, block_out)
+        tiny, g_hid, fin = fence([sz_, sx_], tiny, g_hid, fin)
         sx_.first(1)
         sx_.ring(1)
-        (tiny,) = after([sx_], tiny)
+        tiny, fin = after([sx_], tiny, fin)
         tiny = tiny + swap(tiny, "s")
         gz = sz_.ring(3)
+
+    partial_out = nn(fin, w_o).reshape(2, micros, T, D)
+    give = lax.dynamic_index_in_dim(partial_out, 1 - core, 0, False).astype(bf16)
+    keep = lax.dynamic_index_in_dim(partial_out, core, 0, False)
+    given_out = swap(give)
+    block_out = (hid_own.astype(f32) + keep + given_out.astype(f32)).astype(bf16)
 
     def exchanged(g):
         g = g.reshape(2, r_in, -1)
@@ -1154,7 +1155,7 @@
         return two(mine, swap(lax.dynamic_index_in_dim(g, 1 - core, 0, False)), core)
 
     if fast:
-        tiny, gz = fence([sx_], tiny, gz)
+        tiny, gz, give, keep = fence([sx_], tiny, gz, give, keep)
         sx_.ring(2)
         tiny, gz = after([sx_], tiny, gz)
         gz = exchanged(gz)

time: 485 us -> 483 us (level)
  waiting for transfers between devices: 126 us -> 118 us
    ppermute x50, waiting for transfers between devices: 97.8 us -> 90.8 us  [hop(): return lax.ppermute(value, AXIS[axis], [(i, (i + 1) % n) for i in range(n)])]
    mul x1 -> x0, other arithmetic: 5.93 us -> none  [body(): exact = y * (z * lax.logistic(z)) * root * gain[:1]]
    unnamed x155 -> x181, local copies, waits for them, and re-layouts: 21.4 us -> 25.1 us
    convert_element_type x8 -> x6, other arithmetic: 9.04 us -> 10.4 us  [first(): give = (got[n:].astype(f32) + kept[n:].astype(f32)).astype(bf16)]
  transfers between devices with their start and end apart: 75 -> 75, of which waited for: 30 -> 29; matrix products, arithmetic and copies ran while one was open for 28% -> 26% of each run, Pallas kernels for 22% -> 23%
where the time goes in v5:
time: 483 us; the launch traced here: 475 us
  waiting for transfers between devices  118 us (24%)
  Pallas kernels  114 us (24%)
  starting transfers between devices  79.3 us (16%)
  other arithmetic  57.9 us (12%)
  matrix products  56.5 us (12%)
  local copies, waits for them, and re-layouts  45.8 us (9%)
    ppermute x50, waiting for transfers between devices, hop(): return lax.ppermute(value, AXIS[axis], [(i, (i + 1) % n) for i in range(n)])  90.8 us
    ppermute x50, starting transfers between devices, hop(): return lax.ppermute(value, AXIS[axis], [(i, (i + 1) % n) for i in range(n)])  49.5 us
    pallas_call x1, Pallas kernels, conv_back(): pl.pallas_call(functools.partial(conv_back_kernel, micros), name='conv_ba...  27.2 us
    unnamed x181, local copies, waits for them, and re-layouts  25.1 us
    ppermute x19, waiting for transfers between devices, swap(): return lax.ppermute(value, axis, [(0, 1), (1, 0)])  24.9 us
    dot_general x3, matrix products, nn(): lax.dot_general(a, b, (((1,), (0,)), ((), ())), preferred_element_type=f32)  21 us
    dot_general x3, matrix products, tn(): lax.dot_general(a, b, (((0,), (0,)), ((), ())), preferred_element_type=f32)  19.5 us
    ppermute x19, starting transfers between devices, swap(): return lax.ppermute(value, axis, [(0, 1), (1, 0)])  18.2 us
  transfers between devices with their start and end apart: 75, of which 29 were waited for; matrix products, arithmetic and copies ran while one was open for 26% of the time, Pallas kernels for 23%

profile of v5, /device:TPU:0, one launch (start us, length us, event | category | flops | bytes accessed | tf_op | source)
XLA Modules:
  0.0 475.0 jit_solution(14824178958003261855)
XLA Ops:
  2.4 4.0 collective-permute-start.1
  12.3 1.9 collective-permute-start.2
  24.1 2.8 collective-permute-done.5
  27.6 5.9 %collective-permute-done.3 = bf16[96,1920]{1,0:T(8,128)(2,1)} collective-permute-done((bf16[96,1920]{1,0:T(8,128)(2,1)S(1)}, bf16[96,1920]{1,0:T(8,128)(2,1)}, u32[]{:S(2)}, u32[]{:S(2)}) %collective-permute-start.3) | collective-permute-done | bytes 368672 | tf_op jit(solution)/shard_map/ppermute | solution.py:649
  36.2 2.2 collective-permute-start.13
  38.4 2.0 collective-permute-start.12
  40.4 3.4 maximum_select_fusion
  44.5 4.0 collective-permute-start.15
  61.2 4.7 maximum_select_fusion.1
  75.3 3.0 collective-permute-start.20
  81.7 3.6 collective-permute-done.20
  85.3 3.9 collective-permute-done.18
  89.4 2.2 collective-permute-start.21
  93.6 4.3 collective-permute-done.21
  100.2 4.0 collective-permute-done.27.refs_1_
  104.2 1.9 collective-permute-done.28.refs_3_
  107.9 11.0 %collective-permute-done.29.refs_5_ = bf16[4,96,896]{2,1,0:T(8,128)(2,1)S(1)} collective-permute-done((bf16[4,96,896]{2,1,0:T(8,128)(2,1)S(1)}, bf16[4,96,896]{2,1,0:T(8,128)(2,1)S(1)}, u32[]{:S(2)}, u32[]{:S(2)}) %collective-permute-start.29) | collective-permute-done | bytes 688160 | tf_op jit(solution)/shard_map/ppermute | solution.py:649
  118.9 4.0 collective-permute-done.30.refs_7_
  122.9 2.4 join.3
  125.4 8.9 %fusion.60.xbc.halo.prev = f32[1040,1920]{1,0:T(8,128)} fusion(bf16[1040,1536]{1,0:T(8,128)(2,1)S(1)} %pre_norm.1, bf16[1536,1920]{1,0:T(8,128)(2,1)S(1)} %join.3), kind=kOutput, calls=%fused_computation.248 | convolution fusion | flops 6134169600 | bytes 17080320 | tf_op jit(solution)/shard_map/dot_general | solution.py:36
  136.4 2.5 collective-permute-start.31
  138.9 14.5 %block_states.1 = (f32[1024,1536]{1,0:T(8,128)S(1)}, f32[1024,1792]{1,0:T(8,128)}, f32[1024,256]{1,0:T(8,128)S(1)}, f32[1024,256]{1,0:T(8,128)S(1)}, f32[1024,12...) custom-call(f32[1040,1920]{1,0:T(8,128)} %fusion.60.xbc.halo.prev, ...), custom_call_target="tpu_custom_call" | custom-call | flops 402653184 | bytes 17432576 | tf_op jit(solution)/shard_map/block_states/pallas_call | solution.py:192
  153.4 2.6 copy-done.2
  157.2 3.2 collective-permute-start.32
  160.4 10.2 %inner_part.1.yin = f32[1024,1536]{1,0:T(8,128)S(1)} custom-call(f32[1024,256]{1,0:T(8,128)S(1)} %get-tuple-element.310.s, f32[1024,128]{1,0:T(8,128)S(1)} %get-tuple-element.311.ld, f32[4,32,256]{2,1,0:T(8,128)S(1)} %get-tuple-element.312.ldt, f32[1024,128]{1,0:T(8,128)S(1)} %get-tuple-element.313.dt, f32[1024,1536]{1,0:T(8,128)} %copy-done.2, ...), custom_call_target="tpu_custom_call" | custom-call | flops 3221225472 | bytes 16777216 | tf_op jit(solution)/shard_map/inner_part/pallas_call | solution.py:267
  176.9 7.0 %fusion.10.z = f32[1024,1536]{1,0:T(8,128)} fusion(bf16[1536,1536]{1,0:T(8,128)(2,1)S(1)} %join.4, bf16[1040,1536]{1,0:T(8,128)(2,1)S(1)} %copy-done.12), kind=kOutput, calls=%fused_computation.32 | convolution fusion | flops 4831838208 | bytes 14155776 | tf_op jit(solution)/shard_map/dot_general | solution.py:36
  184.3 7.1 %gate_part.1 = (f32[1024,1536]{1,0:T(8,128)S(1)}, f32[1024,128]{1,0:T(8,128)S(1)}) custom-call(f32[1024,1536]{1,0:T(8,128)S(1)} %inner_part.1.yin, f32[1024,256]{1,0:T(8,128)S(1)} %get-tuple-element.319.bc, bf16[4,128,1536]{2,1,0:T(8,128)(2,1)S(1)} %bitcast.173, f32[1024,128]{1,0:T(8,128)S(1)} %get-tuple-element.311.ld, ...), custom_call_target="tpu_custom_call", output_to_operand_aliasing={{0}: (0, {})} | custom-call | flops 402653184 | bytes 18874368 | tf_op jit(solution)/shard_map/gate_part/pallas_call | solution.py:306
  193.7 4.4 fusion.58
  198.1 5.4 %convolution_convert_fusion.1.refs_0_ = bf16[1536,1536]{1,0:T(8,128)(2,1)S(1)} fusion(bf16[1024,1536]{1,0:T(8,128)(2,1)S(1)} %get-tuple-element.452, bf16[1024,1536]{1,0:T(8,128)(2,1)S(1)} %bitcast.183), kind=kOutput, calls=%fused_computation.1 | convolution fusion | flops 4834197504 | bytes 11010048 | tf_op jit(solution)/shard_map/dot_general | solution.py:44
  203.6 2.3 deal.3
  208.4 13.9 %collective-permute-done.38.refs_3_ = bf16[8,96,768]{2,1,0:T(8,128)(2,1)} collective-permute-done((bf16[8,96,768]{2,1,0:T(8,128)(2,1)}, bf16[8,96,768]{2,1,0:T(8,128)(2,1)}, u32[]{:S(2)}, u32[]{:S(2)}) %collective-permute-start.38) | collective-permute-done | bytes 1179680 | tf_op jit(solution)/shard_map/ppermute | solution.py:649
  223.6 3.0 join.5.w
  226.6 10.3 %out_back.1 = (f32[1024,1536]{1,0:T(8,128)}, f32[1024,128]{1,0:T(8,128)S(1)}) custom-call(bf16[1024,1536]{1,0:T(8,128)(2,1)S(1)} %bitcast.184, bf16[1536,1536]{1,0:T(8,128)(2,1)S(1)} %join.5.w, f32[1024,1536]{1,0:T(8,128)} %get-tuple-element.476.exact), custom_call_target="tpu_custom_call" | custom-call | flops 4831838208 | bytes 20447232 | tf_op jit(solution)/shard_map/out_back/pallas_call | solution.py:337
  237.0 2.4 add_convert_fusion.4
  239.4 2.4 add_convert_fusion.3
  243.0 14.5 %gate_back.1 = (bf16[1024,1536]{1,0:T(8,128)(2,1)S(1)}, bf16[1024,1536]{1,0:T(8,128)(2,1)S(1)}, f32[1024,128]{1,0:T(8,128)S(1)}, f32[2,128,1536]{2,1,0:T(8,128)S...) custom-call(f32[1024,1536]{1,0:T(8,128)} %copy-done, ...), custom_call_target="tpu_custom_call" | custom-call | flops 1610612736 | bytes 37748736 | tf_op jit(solution)/shard_map/gate_back/pallas_call | solution.py:405
  259.3 5.4 %convolution_convert_fusion.refs_0_ = bf16[1536,1536]{1,0:T(8,128)(2,1)S(1)} fusion(bf16[1024,1536]{1,0:T(8,128)(2,1)S(1)} %get-tuple-element.419, bf16[1040,1536]{1,0:T(8,128)(2,1)S(1)} %copy-done.13), kind=kOutput, calls=%fused_computation | convolution fusion | flops 4834197504 | bytes 11010048 | tf_op jit(solution)/shard_map/dot_general | solution.py:44
  267.1 3.5 collective-permute-start.44
  273.5 16.3 %inner_back.1 = (f32[1024,1536]{1,0:T(8,128)S(1)}, f32[1024,128]{1,0:T(8,128)S(1)}, f32[1024,256]{1,0:T(8,128)S(1)}) custom-call(f32[1024,256]{1,0:T(8,128)S(1)} %copy-done.35, f32[1024,256]{1,0:T(8,128)S(1)} %get-tuple-element.319.bc, f32[1024,128]{1,0:T(8,128)S(1)} %get-tuple-element.311.ld, f32[4,32,256]{2,1,0:T(8,128)S(1)} %copy-done.43, ...), custom_call_target="tpu_custom_call" | custom-call | flops 6442450944 | bytes 16777216 | tf_op jit(solution)/shard_map/inner_back/pallas_call | solution.py:487
  289.9 2.6 copy-done.5
  294.3 9.9 %collective-permute-done.44 = bf16[8,96,768]{2,1,0:T(8,128)(2,1)S(1)} collective-permute-done((bf16[8,96,768]{2,1,0:T(8,128)(2,1)S(1)}, bf16[8,96,768]{2,1,0:T(8,128)(2,1)S(1)}, u32[]{:S(2)}, u32[]{:S(2)}) %collective-permute-start.44) | collective-permute-done | bytes 1179680 | tf_op jit(solution)/shard_map/ppermute | solution.py:649
  304.2 2.3 add_convert_fusion.2
  308.9 27.2 %conv_back.1 = (bf16[1040,1920]{1,0:T(8,128)(2,1)}, f32[8,1792]{1,0:T(8,128)}, f32[8,128]{1,0:T(8,128)}) custom-call(f32[1040,1920]{1,0:T(8,128)} %fusion.60.xbc.halo.prev, f32[1040,1920]{1,0:T(8,128)} %fusion.60.xbc.halo.prev, f32[1024,1792]{1,0:T(8,128)} %get-tuple-element.372.pre, f32[1024,1536]{1,0:T(8,128)} %copy-done.5, f32[1024,128]{1,0:T(8,128)} %copy-done.40, ...), custom_call_target="tpu_custom_call" | custom-call | flops 1207959552 | bytes 28311552 | tf_op jit(solution)/shard_map/conv_back/pallas_call | solution.py:610
  342.3 8.7 %convolution_convert_fusion.2.refs_0_ = bf16[1536,1920]{1,0:T(8,128)(2,1)S(1)} fusion(bf16[1040,1536]{1,0:T(8,128)(2,1)S(1)} %copy-done.14, bf16[1040,1920]{1,0:T(8,128)(2,1)S(1)} %copy-done.76), kind=kOutput, calls=%fused_computation.2 | convolution fusion | flops 6137118720 | bytes 13086720 | tf_op jit(solution)/shard_map/dot_general | solution.py:44
  353.9 2.0 collective-permute-start.51
  357.2 2.0 collective-permute-start.54
  359.2 8.8 %fusion.61 = f32[1040,1536]{1,0:T(8,128)} fusion(bf16[1040,1920]{1,0:T(8,128)(2,1)S(1)} %copy-done.76, bf16[1536,1920]{1,0:T(8,128)(2,1)S(1)} %bitcast.178), kind=kOutput, calls=%fused_computation.249 | convolution fusion | flops 6134169600 | bytes 16281600 | tf_op jit(solution)/shard_map/dot_general | solution.py:40
  372.9 2.5 collective-permute-done.62
  376.3 2.6 collective-permute-start.56
  378.9 7.2 %slice_add_fusion = f32[1024,1536]{1,0:T(8,128)S(1)} fusion(f32[1040,1536]{1,0:T(8,128)} %fusion.61, bf16[1024,1536]{1,0:T(8,128)(2,1)S(1)} %copy-done.46, bf16[1536,1536]{1,0:T(8,128)(2,1)S(1)} %bitcast.182), kind=kOutput, calls=%fused_computation.4 | convolution fusion | flops 4833411072 | bytes 20447232 | tf_op jit(solution)/shard_map/dot_general | solution.py:40
  386.1 9.2 %collective-permute-done.56 = f32[8,1792]{1,0:T(8,128)S(1)} collective-permute-done((f32[8,1792]{1,0:T(8,128)S(1)}, f32[8,1792]{1,0:T(8,128)S(1)}, u32[]{:S(2)}, u32[]{:S(2)}) %collective-permute-start.56) | collective-permute-done | bytes 57376 | tf_op jit(solution)/shard_map/ppermute | solution.py:849
  404.7 2.1 dynamic-slice_bitcast_fusion.1
  406.8 5.0 %collective-permute-done.60 = bf16[2,96,896]{2,1,0:T(8,128)(2,1)} collective-permute-done((bf16[2,96,896]{2,1,0:T(8,128)(2,1)}, bf16[2,96,896]{2,1,0:T(8,128)(2,1)}, u32[]{:S(2)}, u32[]{:S(2)}) %collective-permute-start.60) | collective-permute-done | bytes 344096 | tf_op jit(solution)/shard_map/ppermute | solution.py:649
  412.1 2.5 collective-permute-done.61
  417.0 2.4 fusion.2
  419.5 4.3 fusion.5
  423.9 3.4 collective-permute-done.58
  427.3 2.2 collective-permute-done.59
  431.5 5.0 %fusion.62 = f32[1024,1536]{1,0:T(8,128)S(1)} fusion(bf16[1024,1536]{1,0:T(8,128)(2,1)S(1)} %copy-done.59, bf16[1536,1536]{1,0:T(8,128)(2,1)S(1)} %bitcast.180), kind=kOutput, calls=%fused_computation.250 | convolution fusion | flops 4831838208 | bytes 14155776 | tf_op jit(solution)/shard_map/dot_general | solution.py:36
  436.8 2.6 collective-permute-start.68
  443.3 7.4 %collective-permute-done.69 = f32[8,1792]{1,0:T(8,128)S(1)} collective-permute-done((f32[8,1792]{1,0:T(8,128)S(1)}, f32[8,1792]{1,0:T(8,128)S(1)}, u32[]{:S(2)}, u32[]{:S(2)}) %collective-permute-start.69) | collective-permute-done | bytes 57376 | tf_op jit(solution)/shard_map/ppermute | solution.py:849
  454.3 3.3 collective-permute-done.71
  457.6 8.1 %collective-permute-done.70 = bf16[96,1920]{1,0:T(8,128)(2,1)S(1)} collective-permute-done((bf16[96,1920]{1,0:T(8,128)(2,1)S(1)}, bf16[96,1920]{1,0:T(8,128)(2,1)S(1)}, u32[]{:S(2)}, u32[]{:S(2)}) %collective-permute-start.70) | collective-permute-done | bytes 368672 | tf_op jit(solution)/shard_map/ppermute | solution.py:649
  472.9 1.9 copy.67
  (456 shorter events, 125.8 us)
Async XLA Ops:
  2.4 9.9 %collective-permute-start.1 = (bf16[664]{0:T(1024)(128)(2,1)S(1)}, bf16[664]{0:T(1024)(128)(2,1)S(1)}, u32[]{:S(2)}, u32[]{:S(2)}) collective-permute-start(bf16[664]{0:T(1024)(128)(2,1)S(1)} %pad_maximum_fusion.17), channel_id=1, source_target_pairs={{0,16},{16,0},{1,17},{17,1},{2,18},{18,2},{3,19},{19,3},{4,20},{20... | collective-permute-start | bytes 3992 | tf_op jit(solution)/shard_map/ppermute | solution.py:849
  9.5 6.7 %collective-permute-start.4 = (bf16[96,1536]{1,0:T(8,128)(2,1)S(1)}, bf16[96,1536]{1,0:T(8,128)(2,1)S(1)}, u32[]{:S(2)}, u32[]{:S(2)}) collective-permute-start(bf16[96,1536]{1,0:T(8,128)(2,1)S(1)} %copy-done.77), channel_id=1, source_target_pairs={{0,0},{1,16},{16,1},{17,17},{2,2},{3,18},{18,3},{19,19},{4,4},{5,2... | collective-permute-start | bytes 884744 | tf_op jit(solution)/shard_map/ppermute | solution.py:901
  10.1 7.8 %collective-permute-start = (bf16[48,3456]{1,0:T(8,128)(2,1)S(1)}, bf16[48,3456]{1,0:T(8,128)(2,1)S(1)}, u32[]{:S(2)}, u32[]{:S(2)}) collective-permute-start(bf16[48,3456]{1,0:T(8,128)(2,1)S(1)} %get-tuple-element.242), channel_id=1, source_target_pairs={{0,1},{1,0},{2,3},{3,2},{4,5},{5,4},{6,7},{7,6},{8,9},{9,8},{10,11... | collective-permute-start | bytes 995336 | tf_op jit(solution)/shard_map/ppermute | solution.py:849
  11.6 21.9 %collective-permute-start.9 = (bf16[2,256,1536]{2,1,0:T(8,128)(2,1)}, bf16[2,256,1536]{2,1,0:T(8,128)(2,1)}, u32[]{:S(2)}, u32[]{:S(2)}) collective-permute-start(bf16[2,256,1536]{2,1,0:T(8,128)(2,1)} %bitcast.190), channel_id=1, source_target_pairs={{0,1},{1,0},{2,3},{3,2},{4,5},{5,4},{6,7},{7,6},{8,9},{9,8},{10,11... | collective-permute-start | bytes 4718600 | tf_op jit(solution)/shard_map/ppermute | solution.py:849
  11.7 21.9 %collective-permute-start.8 = (bf16[2,256,1536]{2,1,0:T(8,128)(2,1)S(1)}, bf16[2,256,1536]{2,1,0:T(8,128)(2,1)}, u32[]{:S(2)}, u32[]{:S(2)}) collective-permute-start(bf16[2,256,1536]{2,1,0:T(8,128)(2,1)S(1)} %bitcast.188), channel_id=1, source_target_pairs={{0,1},{1,0},{2,3},{3,2},{4,5},{5,4},{6,7},{7,6},{8,9},{9,8},{10,11... | collective-permute-start | bytes 4718600 | tf_op jit(solution)/shard_map/ppermute | solution.py:849
  16.2 7.2 %collective-permute-start.6 = (bf16[1,96,768]{2,1,0:T(8,128)(2,1)S(1)}, bf16[1,96,768]{2,1,0:T(8,128)(2,1)S(1)}, u32[]{:S(2)}, u32[]{:S(2)}) collective-permute-start(bf16[1,96,768]{2,1,0:T(8,128)(2,1)S(1)} %get-tuple-element.511), channel_id=1, source_target_pairs={{0,4},{4,0},{1,5},{5,1},{2,6},{6,2},{3,7},{7,3},{8,12},{12,8},{9,1... | collective-permute-start | bytes 442376 | tf_op jit(solution)/shard_map/ppermute | solution.py:649
  18.5 15.0 %collective-permute-start.3 = (bf16[96,1920]{1,0:T(8,128)(2,1)S(1)}, bf16[96,1920]{1,0:T(8,128)(2,1)}, u32[]{:S(2)}, u32[]{:S(2)}) collective-permute-start(bf16[96,1920]{1,0:T(8,128)(2,1)S(1)} %slice.300), channel_id=1, source_target_pairs={{0,8},{8,16},{16,24},{24,0},{1,9},{9,17},{17,25},{25,1},{2,10},{10... | collective-permute-start | bytes 1105928 | tf_op jit(solution)/shard_map/ppermute | solution.py:649
  33.5 18.0 %collective-permute-start.10 = (bf16[96,1920]{1,0:T(8,128)(2,1)}, bf16[96,1920]{1,0:T(8,128)(2,1)}, u32[]{:S(2)}, u32[]{:S(2)}) collective-permute-start(bf16[96,1920]{1,0:T(8,128)(2,1)} %collective-permute-done.3), channel_id=1, source_target_pairs={{0,8},{8,16},{16,24},{24,0},{1,9},{9,17},{17,25},{25,1},{2,10},{10... | collective-permute-start | bytes 1105928 | tf_op jit(solution)/shard_map/ppermute | solution.py:649
  36.2 12.3 %collective-permute-start.13 = (bf16[2,2,2,664]{3,1,0,2:T(2,128)(2,1)S(1)}, bf16[2,2,2,664]{3,1,0,2:T(2,128)(2,1)S(1)}, u32[]{:S(2)}, u32[]{:S(2)}) collective-permute-start(bf16[2,2,2,664]{3,1,0,2:T(2,128)(2,1)S(1)} %broadcast_select_fusion.3), channel_id=1, source_target_pairs={{0,2},{2,0},{1,3},{3,1},{4,6},{6,4},{5,7},{7,5},{8,10},{10,8},{9,1... | collective-permute-start | bytes 31880 | tf_op jit(solution)/shard_map/ppermute | solution.py:849
  38.4 13.1 %collective-permute-start.11 = (bf16[2,96,896]{2,1,0:T(8,128)(2,1)S(1)}, bf16[2,96,896]{2,1,0:T(8,128)(2,1)}, u32[]{:S(2)}, u32[]{:S(2)}) collective-permute-start(bf16[2,96,896]{2,1,0:T(8,128)(2,1)S(1)} %pad_maximum_fusion.13), channel_id=1, source_target_pairs={{0,2},{2,0},{1,3},{3,1},{4,6},{6,4},{5,7},{7,5},{8,10},{10,8},{9,1... | collective-permute-start | bytes 1032200 | tf_op jit(solution)/shard_map/ppermute | solution.py:649
  38.4 13.1 %collective-permute-start.12 = (bf16[2,96,1024]{2,1,0:T(8,128)(2,1)}, bf16[2,96,1024]{2,1,0:T(8,128)(2,1)}, u32[]{:S(2)}, u32[]{:S(2)}) collective-permute-start(bf16[2,96,1024]{2,1,0:T(8,128)(2,1)} %pad_maximum_fusion.11), channel_id=1, source_target_pairs={{0,4},{4,0},{1,5},{5,1},{2,6},{6,2},{3,7},{7,3},{8,12},{12,8},{9,1... | collective-permute-start | bytes 1179656 | tf_op jit(solution)/shard_map/ppermute | solution.py:649
  44.5 7.0 %collective-permute-start.15 = (bf16[2,8,1536]{2,1,0:T(8,128)(2,1)}, bf16[2,8,1536]{2,1,0:T(8,128)(2,1)}, u32[]{:S(2)}, u32[]{:S(2)}) collective-permute-start(bf16[2,8,1536]{2,1,0:T(8,128)(2,1)} %slice_bitcast_fusion.8), channel_id=1, source_target_pairs={{0,2},{1,3},{4,6},{5,7},{8,10},{9,11},{12,14},{13,15},{16,18},{17,... | collective-permute-start | bytes 147464 | tf_op jit(solution)/shard_map/ppermute | solution.py:922
  51.6 18.1 %collective-permute-start.17 = (bf16[96,1536]{1,0:T(8,128)(2,1)}, bf16[96,1536]{1,0:T(8,128)(2,1)}, u32[]{:S(2)}, u32[]{:S(2)}) collective-permute-start(bf16[96,1536]{1,0:T(8,128)(2,1)} %slice.301), channel_id=1, source_target_pairs={{0,8},{8,16},{16,24},{24,0},{1,9},{9,17},{17,25},{25,1},{2,10},{10... | collective-permute-start | bytes 884744 | tf_op jit(solution)/shard_map/ppermute | solution.py:649
  51.6 19.4 %collective-permute-start.16 = (bf16[96,1920]{1,0:T(8,128)(2,1)}, bf16[96,1920]{1,0:T(8,128)(2,1)}, u32[]{:S(2)}, u32[]{:S(2)}) collective-permute-start(bf16[96,1920]{1,0:T(8,128)(2,1)} %collective-permute-done.10), channel_id=1, source_target_pairs={{0,8},{8,16},{16,24},{24,0},{1,9},{9,17},{17,25},{25,1},{2,10},{10... | collective-permute-start | bytes 1105928 | tf_op jit(solution)/shard_map/ppermute | solution.py:649
  71.0 10.0 %collective-permute-start.22 = (bf16[2,96,768]{2,1,0:T(8,128)(2,1)S(1)}, bf16[2,96,768]{2,1,0:T(8,128)(2,1)S(1)}, u32[]{:S(2)}, u32[]{:S(2)}) collective-permute-start(bf16[2,96,768]{2,1,0:T(8,128)(2,1)S(1)} %copy-done.64), channel_id=1, source_target_pairs={{0,4},{4,0},{1,5},{5,1},{2,6},{6,2},{3,7},{7,3},{8,12},{12,8},{9,1... | collective-permute-start | bytes 884744 | tf_op jit(solution)/shard_map/ppermute | solution.py:649
  71.6 10.0 %collective-permute-start.23 = (bf16[2,96,768]{2,1,0:T(8,128)(2,1)S(1)}, bf16[2,96,768]{2,1,0:T(8,128)(2,1)S(1)}, u32[]{:S(2)}, u32[]{:S(2)}) collective-permute-start(bf16[2,96,768]{2,1,0:T(8,128)(2,1)S(1)} %copy-done.63), channel_id=1, source_target_pairs={{0,2},{2,0},{1,3},{3,1},{4,6},{6,4},{5,7},{7,5},{8,10},{10,8},{9,1... | collective-permute-start | bytes 884744 | tf_op jit(solution)/shard_map/ppermute | solution.py:649
  72.6 16.8 %collective-permute-start.19 = (bf16[2,96,1024]{2,1,0:T(8,128)(2,1)S(1)}, bf16[2,96,1024]{2,1,0:T(8,128)(2,1)S(1)}, u32[]{:S(2)}, u32[]{:S(2)}) collective-permute-start(bf16[2,96,1024]{2,1,0:T(8,128)(2,1)S(1)} %pad_maximum_fusion.10), channel_id=1, source_target_pairs={{0,4},{4,0},{1,5},{5,1},{2,6},{6,2},{3,7},{7,3},{8,12},{12,8},{9,1... | collective-permute-start | bytes 1179656 | tf_op jit(solution)/shard_map/ppermute | solution.py:649
  75.3 10.1 %collective-permute-start.20 = (bf16[96,1536]{1,0:T(8,128)(2,1)}, bf16[96,1536]{1,0:T(8,128)(2,1)S(1)}, u32[]{:S(2)}, u32[]{:S(2)}) collective-permute-start(bf16[96,1536]{1,0:T(8,128)(2,1)} %collective-permute-done.17), channel_id=1, source_target_pairs={{0,8},{8,16},{16,24},{24,0},{1,9},{9,17},{17,25},{25,1},{2,10},{10... | collective-permute-start | bytes 884744 | tf_op jit(solution)/shard_map/ppermute | solution.py:649
  78.2 11.0 %collective-permute-start.18 = (bf16[2,96,896]{2,1,0:T(8,128)(2,1)S(1)}, bf16[2,96,896]{2,1,0:T(8,128)(2,1)S(1)}, u32[]{:S(2)}, u32[]{:S(2)}) collective-permute-start(bf16[2,96,896]{2,1,0:T(8,128)(2,1)S(1)} %pad_maximum_fusion.12), channel_id=1, source_target_pairs={{0,2},{2,0},{1,3},{3,1},{4,6},{6,4},{5,7},{7,5},{8,10},{10,8},{9,1... | collective-permute-start | bytes 1032200 | tf_op jit(solution)/shard_map/ppermute | solution.py:649
  81.0 23.2 %collective-permute-start.27 = (bf16[4,96,896]{2,1,0:T(8,128)(2,1)}, bf16[4,96,896]{2,1,0:T(8,128)(2,1)S(1)}, u32[]{:S(2)}, u32[]{:S(2)}) collective-permute-start(bf16[4,96,896]{2,1,0:T(8,128)(2,1)} %constant_dynamic-update-slice_fusion.refs_0_), channel_id=1, source_target_pairs={{0,4},{4,0},{1,5},{5,1},{2,6},{6,2},{3,7},{7,3},{8,12},{12,8},{9,1... | collective-permute-start | bytes 2064392 | tf_op jit(solution)/shard_map/ppermute | solution.py:649
  81.6 24.5 %collective-permute-start.28 = (bf16[4,96,1024]{2,1,0:T(8,128)(2,1)}, bf16[4,96,1024]{2,1,0:T(8,128)(2,1)S(1)}, u32[]{:S(2)}, u32[]{:S(2)}) collective-permute-start(bf16[4,96,1024]{2,1,0:T(8,128)(2,1)} %constant_dynamic-update-slice_fusion.2.refs_2_), channel_id=1, source_target_pairs={{0,2},{2,0},{1,3},{3,1},{4,6},{6,4},{5,7},{7,5},{8,10},{10,8},{9,1... | collective-permute-start | bytes 2359304 | tf_op jit(solution)/shard_map/ppermute | solution.py:649
  89.4 8.5 %collective-permute-start.21 = (bf16[96,1536]{1,0:T(8,128)(2,1)S(1)}, bf16[96,1536]{1,0:T(8,128)(2,1)S(1)}, u32[]{:S(2)}, u32[]{:S(2)}) collective-permute-start(bf16[96,1536]{1,0:T(8,128)(2,1)S(1)} %collective-permute-done.20), channel_id=1, source_target_pairs={{0,8},{8,16},{16,24},{24,0},{1,9},{9,17},{17,25},{25,1},{2,10},{10... | collective-permute-start | bytes 884744 | tf_op jit(solution)/shard_map/ppermute | solution.py:649
  91.7 27.2 %collective-permute-start.29 = (bf16[4,96,896]{2,1,0:T(8,128)(2,1)S(1)}, bf16[4,96,896]{2,1,0:T(8,128)(2,1)S(1)}, u32[]{:S(2)}, u32[]{:S(2)}) collective-permute-start(bf16[4,96,896]{2,1,0:T(8,128)(2,1)S(1)} %constant_dynamic-update-slice_fusion.4.refs_4_), channel_id=1, source_target_pairs={{0,4},{4,0},{1,5},{5,1},{2,6},{6,2},{3,7},{7,3},{8,12},{12,8},{9,1... | collective-permute-start | bytes 2064392 | tf_op jit(solution)/shard_map/ppermute | solution.py:649
  92.8 30.1 %collective-permute-start.30 = (bf16[4,96,1024]{2,1,0:T(8,128)(2,1)S(1)}, bf16[4,96,1024]{2,1,0:T(8,128)(2,1)S(1)}, u32[]{:S(2)}, u32[]{:S(2)}) collective-permute-start(bf16[4,96,1024]{2,1,0:T(8,128)(2,1)S(1)} %constant_dynamic-update-slice_fusion.6.refs_6_), channel_id=1, source_target_pairs={{0,2},{2,0},{1,3},{3,1},{4,6},{6,4},{5,7},{7,5},{8,10},{10,8},{9,1... | collective-permute-start | bytes 2359304 | tf_op jit(solution)/shard_map/ppermute | solution.py:649
  99.1 35.1 %collective-permute-start.26 = (bf16[4,96,768]{2,1,0:T(8,128)(2,1)S(1)}, bf16[4,96,768]{2,1,0:T(8,128)(2,1)S(1)}, u32[]{:S(2)}, u32[]{:S(2)}) collective-permute-start(bf16[4,96,768]{2,1,0:T(8,128)(2,1)S(1)} %get-tuple-element.300), channel_id=1, source_target_pairs={{0,4},{4,0},{1,5},{5,1},{2,6},{6,2},{3,7},{7,3},{8,12},{12,8},{9,1... | collective-permute-start | bytes 1769480 | tf_op jit(solution)/shard_map/ppermute | solution.py:649
  104.2 30.1 %collective-permute-start.25 = (bf16[4,96,768]{2,1,0:T(8,128)(2,1)S(1)}, bf16[4,96,768]{2,1,0:T(8,128)(2,1)S(1)}, u32[]{:S(2)}, u32[]{:S(2)}) collective-permute-start(bf16[4,96,768]{2,1,0:T(8,128)(2,1)S(1)} %get-tuple-element.298), channel_id=1, source_target_pairs={{0,2},{2,0},{1,3},{3,1},{4,6},{6,4},{5,7},{7,5},{8,10},{10,8},{9,1... | collective-permute-start | bytes 1769480 | tf_op jit(solution)/shard_map/ppermute | solution.py:649
  106.1 30.3 %collective-permute-start.24 = (bf16[8,96,768]{2,1,0:T(8,128)(2,1)S(1)}, bf16[8,96,768]{2,1,0:T(8,128)(2,1)}, u32[]{:S(2)}, u32[]{:S(2)}) collective-permute-start(bf16[8,96,768]{2,1,0:T(8,128)(2,1)S(1)} %constant_dynamic-update-slice_fusion.8.refs_0_), channel_id=1, source_target_pairs={{0,8},{8,16},{16,24},{24,0},{1,9},{9,17},{17,25},{25,1},{2,10},{10... | collective-permute-start | bytes 3538952 | tf_op jit(solution)/shard_map/ppermute | solution.py:649
  134.4 36.3 %collective-permute-start.34 = (bf16[8,96,768]{2,1,0:T(8,128)(2,1)S(1)}, bf16[8,96,768]{2,1,0:T(8,128)(2,1)S(1)}, u32[]{:S(2)}, u32[]{:S(2)}) collective-permute-start(bf16[8,96,768]{2,1,0:T(8,128)(2,1)S(1)} %constant_dynamic-update-slice_fusion.12.refs_2_), channel_id=1, source_target_pairs={{0,2},{2,0},{1,3},{3,1},{4,6},{6,4},{5,7},{7,5},{8,10},{10,8},{9,1... | collective-permute-start | bytes 3538952 | tf_op jit(solution)/shard_map/ppermute | solution.py:649
  135.8 35.9 %collective-permute-start.33 = (bf16[8,96,768]{2,1,0:T(8,128)(2,1)S(1)}, bf16[8,96,768]{2,1,0:T(8,128)(2,1)S(1)}, u32[]{:S(2)}, u32[]{:S(2)}) collective-permute-start(bf16[8,96,768]{2,1,0:T(8,128)(2,1)S(1)} %constant_dynamic-update-slice_fusion.10.refs_0_), channel_id=1, source_target_pairs={{0,4},{4,0},{1,5},{5,1},{2,6},{6,2},{3,7},{7,3},{8,12},{12,8},{9,1... | collective-permute-start | bytes 3538952 | tf_op jit(solution)/shard_map/ppermute | solution.py:649
  136.4 47.9 %collective-permute-start.31 = (bf16[8,96,768]{2,1,0:T(8,128)(2,1)}, bf16[8,96,768]{2,1,0:T(8,128)(2,1)}, u32[]{:S(2)}, u32[]{:S(2)}) collective-permute-start(bf16[8,96,768]{2,1,0:T(8,128)(2,1)} %collective-permute-done.24.refs_1_), channel_id=1, source_target_pairs={{0,8},{8,16},{16,24},{24,0},{1,9},{9,17},{17,25},{25,1},{2,10},{10... | collective-permute-start | bytes 3538952 | tf_op jit(solution)/shard_map/ppermute | solution.py:649
  157.2 26.6 %collective-permute-start.32 = (bf16[2,128,1536]{2,1,0:T(8,128)(2,1)S(1)}, bf16[2,128,1536]{2,1,0:T(8,128)(2,1)S(1)}, u32[]{:S(2)}, u32[]{:S(2)}) collective-permute-start(bf16[2,128,1536]{2,1,0:T(8,128)(2,1)S(1)} %get-tuple-element.320), channel_id=1, source_target_pairs={{0,2},{1,3},{4,6},{5,7},{8,10},{9,11},{12,14},{13,15},{16,18},{17,... | collective-permute-start | bytes 2359304 | tf_op jit(solution)/shard_map/ppermute | solution.py:1014
  191.6 30.7 %collective-permute-start.38 = (bf16[8,96,768]{2,1,0:T(8,128)(2,1)}, bf16[8,96,768]{2,1,0:T(8,128)(2,1)}, u32[]{:S(2)}, u32[]{:S(2)}) collective-permute-start(bf16[8,96,768]{2,1,0:T(8,128)(2,1)} %collective-permute-done.31.refs_2_), channel_id=1, source_target_pairs={{0,8},{8,16},{16,24},{24,0},{1,9},{9,17},{17,25},{25,1},{2,10},{10... | collective-permute-start | bytes 3538952 | tf_op jit(solution)/shard_map/ppermute | solution.py:649
  207.9 28.9 %collective-permute-start.36 = (bf16[8,96,768]{2,1,0:T(8,128)(2,1)}, bf16[8,96,768]{2,1,0:T(8,128)(2,1)}, u32[]{:S(2)}, u32[]{:S(2)}) collective-permute-start(bf16[8,96,768]{2,1,0:T(8,128)(2,1)} %get-tuple-element.333), channel_id=1, source_target_pairs={{0,4},{4,0},{1,5},{5,1},{2,6},{6,2},{3,7},{7,3},{8,12},{12,8},{9,1... | collective-permute-start | bytes 3538952 | tf_op jit(solution)/shard_map/ppermute | solution.py:649
  208.4 28.4 %collective-permute-start.37 = (bf16[8,96,768]{2,1,0:T(8,128)(2,1)}, bf16[8,96,768]{2,1,0:T(8,128)(2,1)}, u32[]{:S(2)}, u32[]{:S(2)}) collective-permute-start(bf16[8,96,768]{2,1,0:T(8,128)(2,1)} %get-tuple-element.334), channel_id=1, source_target_pairs={{0,2},{2,0},{1,3},{3,1},{4,6},{6,4},{5,7},{7,5},{8,10},{10,8},{9,1... | collective-permute-start | bytes 3538952 | tf_op jit(solution)/shard_map/ppermute | solution.py:649
  239.4 26.8 %collective-permute-start.39 = (bf16[4,96,768]{2,1,0:T(8,128)(2,1)}, bf16[4,96,768]{2,1,0:T(8,128)(2,1)}, u32[]{:S(2)}, u32[]{:S(2)}) collective-permute-start(bf16[4,96,768]{2,1,0:T(8,128)(2,1)} %get-tuple-element.483), channel_id=1, source_target_pairs={{0,2},{2,0},{1,3},{3,1},{4,6},{6,4},{5,7},{7,5},{8,10},{10,8},{9,1... | collective-permute-start | bytes 1769480 | tf_op jit(solution)/shard_map/ppermute | solution.py:649
  241.7 24.5 %collective-permute-start.40 = (bf16[4,96,768]{2,1,0:T(8,128)(2,1)}, bf16[4,96,768]{2,1,0:T(8,128)(2,1)}, u32[]{:S(2)}, u32[]{:S(2)}) collective-permute-start(bf16[4,96,768]{2,1,0:T(8,128)(2,1)} %get-tuple-element.481), channel_id=1, source_target_pairs={{0,4},{4,0},{1,5},{5,1},{2,6},{6,2},{3,7},{7,3},{8,12},{12,8},{9,1... | collective-permute-start | bytes 1769480 | tf_op jit(solution)/shard_map/ppermute | solution.py:649
  257.6 36.1 %collective-permute-start.45 = (bf16[2,128,1536]{2,1,0:T(8,128)(2,1)S(1)}, bf16[2,128,1536]{2,1,0:T(8,128)(2,1)}, u32[]{:S(2)}, u32[]{:S(2)}) collective-permute-start(bf16[2,128,1536]{2,1,0:T(8,128)(2,1)S(1)} %get-tuple-element.365), channel_id=1, source_target_pairs={{2,0},{3,1},{6,4},{7,5},{10,8},{11,9},{14,12},{15,13},{18,16},{19,... | collective-permute-start | bytes 2359304 | tf_op jit(solution)/shard_map/ppermute | solution.py:1058
  266.2 28.0 %collective-permute-start.43 = (bf16[8,96,768]{2,1,0:T(8,128)(2,1)S(1)}, bf16[8,96,768]{2,1,0:T(8,128)(2,1)}, u32[]{:S(2)}, u32[]{:S(2)}) collective-permute-start(bf16[8,96,768]{2,1,0:T(8,128)(2,1)S(1)} %get-tuple-element.360), channel_id=1, source_target_pairs={{0,4},{4,0},{1,5},{5,1},{2,6},{6,2},{3,7},{7,3},{8,12},{12,8},{9,1... | collective-permute-start | bytes 3538952 | tf_op jit(solution)/shard_map/ppermute | solution.py:649
  267.1 37.0 %collective-permute-start.44 = (bf16[8,96,768]{2,1,0:T(8,128)(2,1)S(1)}, bf16[8,96,768]{2,1,0:T(8,128)(2,1)S(1)}, u32[]{:S(2)}, u32[]{:S(2)}) collective-permute-start(bf16[8,96,768]{2,1,0:T(8,128)(2,1)S(1)} %get-tuple-element.361), channel_id=1, source_target_pairs={{0,2},{2,0},{1,3},{3,1},{4,6},{6,4},{5,7},{7,5},{8,10},{10,8},{9,1... | collective-permute-start | bytes 3538952 | tf_op jit(solution)/shard_map/ppermute | solution.py:649
  272.2 21.4 %collective-permute-start.42 = (bf16[96,1536]{1,0:T(8,128)(2,1)S(1)}, bf16[96,1536]{1,0:T(8,128)(2,1)S(1)}, u32[]{:S(2)}, u32[]{:S(2)}) collective-permute-start(bf16[96,1536]{1,0:T(8,128)(2,1)S(1)} %fusion.43), channel_id=1, source_target_pairs={{0,8},{8,16},{16,24},{24,0},{1,9},{9,17},{17,25},{25,1},{2,10},{10... | collective-permute-start | bytes 884744 | tf_op jit(solution)/shard_map/ppermute | solution.py:649
  306.5 31.1 %collective-permute-start.47 = (bf16[4,96,768]{2,1,0:T(8,128)(2,1)}, bf16[4,96,768]{2,1,0:T(8,128)(2,1)}, u32[]{:S(2)}, u32[]{:S(2)}) collective-permute-start(bf16[4,96,768]{2,1,0:T(8,128)(2,1)} %get-tuple-element.479), channel_id=1, source_target_pairs={{0,2},{2,0},{1,3},{3,1},{4,6},{6,4},{5,7},{7,5},{8,10},{10,8},{9,1... | collective-permute-start | bytes 1769480 | tf_op jit(solution)/shard_map/ppermute | solution.py:649
  307.6 30.1 %collective-permute-start.48 = (bf16[4,96,768]{2,1,0:T(8,128)(2,1)}, bf16[4,96,768]{2,1,0:T(8,128)(2,1)S(1)}, u32[]{:S(2)}, u32[]{:S(2)}) collective-permute-start(bf16[4,96,768]{2,1,0:T(8,128)(2,1)} %get-tuple-element.477), channel_id=1, source_target_pairs={{0,4},{4,0},{1,5},{5,1},{2,6},{6,2},{3,7},{7,3},{8,12},{12,8},{9,1... | collective-permute-start | bytes 1769480 | tf_op jit(solution)/shard_map/ppermute | solution.py:649
  308.6 29.0 %collective-permute-start.46 = (bf16[96,1536]{1,0:T(8,128)(2,1)S(1)}, bf16[96,1536]{1,0:T(8,128)(2,1)S(1)}, u32[]{:S(2)}, u32[]{:S(2)}) collective-permute-start(bf16[96,1536]{1,0:T(8,128)(2,1)S(1)} %fusion.31), channel_id=1, source_target_pairs={{0,8},{8,16},{16,24},{24,0},{1,9},{9,17},{17,25},{25,1},{2,10},{10... | collective-permute-start | bytes 884744 | tf_op jit(solution)/shard_map/ppermute | solution.py:649
  337.7 15.4 %collective-permute-start.49 = (bf16[96,1536]{1,0:T(8,128)(2,1)S(1)}, bf16[96,1536]{1,0:T(8,128)(2,1)S(1)}, u32[]{:S(2)}, u32[]{:S(2)}) collective-permute-start(bf16[96,1536]{1,0:T(8,128)(2,1)S(1)} %fusion.30), channel_id=1, source_target_pairs={{0,8},{8,16},{16,24},{24,0},{1,9},{9,17},{17,25},{25,1},{2,10},{10... | collective-permute-start | bytes 884744 | tf_op jit(solution)/shard_map/ppermute | solution.py:649
  340.4 13.4 %collective-permute-start.50 = (bf16[96,1536]{1,0:T(8,128)(2,1)S(1)}, bf16[96,1536]{1,0:T(8,128)(2,1)S(1)}, u32[]{:S(2)}, u32[]{:S(2)}) collective-permute-start(bf16[96,1536]{1,0:T(8,128)(2,1)S(1)} %fusion.44), channel_id=1, source_target_pairs={{0,8},{8,16},{16,24},{24,0},{1,9},{9,17},{17,25},{25,1},{2,10},{10... | collective-permute-start | bytes 884744 | tf_op jit(solution)/shard_map/ppermute | solution.py:649
  353.9 22.3 %collective-permute-start.51 = (bf16[96,1536]{1,0:T(8,128)(2,1)S(1)}, bf16[96,1536]{1,0:T(8,128)(2,1)S(1)}, u32[]{:S(2)}, u32[]{:S(2)}) collective-permute-start(bf16[96,1536]{1,0:T(8,128)(2,1)S(1)} %fusion.29), channel_id=1, source_target_pairs={{0,8},{8,16},{16,24},{24,0},{1,9},{9,17},{17,25},{25,1},{2,10},{10... | collective-permute-start | bytes 884744 | tf_op jit(solution)/shard_map/ppermute | solution.py:649
  356.0 39.3 %collective-permute-start.53 = (bf16[4,96,896]{2,1,0:T(8,128)(2,1)S(1)}, bf16[4,96,896]{2,1,0:T(8,128)(2,1)S(1)}, u32[]{:S(2)}, u32[]{:S(2)}) collective-permute-start(bf16[4,96,896]{2,1,0:T(8,128)(2,1)S(1)} %get-tuple-element.406), channel_id=1, source_target_pairs={{0,4},{4,0},{1,5},{5,1},{2,6},{6,2},{3,7},{7,3},{8,12},{12,8},{9,1... | collective-permute-start | bytes 2064392 | tf_op jit(solution)/shard_map/ppermute | solution.py:649
  357.2 38.1 %collective-permute-start.54 = (bf16[4,96,1024]{2,1,0:T(8,128)(2,1)S(1)}, bf16[4,96,1024]{2,1,0:T(8,128)(2,1)S(1)}, u32[]{:S(2)}, u32[]{:S(2)}) collective-permute-start(bf16[4,96,1024]{2,1,0:T(8,128)(2,1)S(1)} %get-tuple-element.407), channel_id=1, source_target_pairs={{0,2},{2,0},{1,3},{3,1},{4,6},{6,4},{5,7},{7,5},{8,10},{10,8},{9,1... | collective-permute-start | bytes 2359304 | tf_op jit(solution)/shard_map/ppermute | solution.py:649
  369.0 6.5 %collective-permute-start.62 = (bf16[16,1536]{1,0:T(8,128)(2,1)S(1)}, bf16[16,1536]{1,0:T(8,128)(2,1)S(1)}, u32[]{:S(2)}, u32[]{:S(2)}) collective-permute-start(bf16[16,1536]{1,0:T(8,128)(2,1)S(1)} %slice.551), channel_id=1, source_target_pairs={{2,0},{3,1},{6,4},{7,5},{10,8},{11,9},{14,12},{15,13},{18,16},{19,... | collective-permute-start | bytes 147464 | tf_op jit(solution)/shard_map/ppermute | solution.py:1107
  375.5 19.8 %collective-permute-start.55 = (f32[96,1536]{1,0:T(8,128)S(1)}, f32[96,1536]{1,0:T(8,128)S(1)}, u32[]{:S(2)}, u32[]{:S(2)}) collective-permute-start(f32[96,1536]{1,0:T(8,128)S(1)} %bitcast_add_fusion.4), channel_id=1, source_target_pairs={{0,0},{1,16},{16,1},{17,17},{2,2},{3,18},{18,3},{19,19},{4,4},{5,2... | collective-permute-start | bytes 1769480 | tf_op jit(solution)/shard_map/ppermute | solution.py:1104
  376.3 19.0 %collective-permute-start.56 = (f32[8,1792]{1,0:T(8,128)S(1)}, f32[8,1792]{1,0:T(8,128)S(1)}, u32[]{:S(2)}, u32[]{:S(2)}) collective-permute-start(f32[8,1792]{1,0:T(8,128)S(1)} %add.325), channel_id=1, source_target_pairs={{0,16},{16,0},{1,17},{17,1},{2,18},{18,2},{3,19},{19,3},{4,20},{20... | collective-permute-start | bytes 172040 | tf_op jit(solution)/shard_map/ppermute | solution.py:849
  400.3 14.3 %collective-permute-start.63 = (bf16[2,256,1536]{2,1,0:T(8,128)(2,1)}, bf16[2,256,1536]{2,1,0:T(8,128)(2,1)}, u32[]{:S(2)}, u32[]{:S(2)}) collective-permute-start(bf16[2,256,1536]{2,1,0:T(8,128)(2,1)} %fusion.12), channel_id=1, source_target_pairs={{0,1},{1,0},{2,3},{3,2},{4,5},{5,4},{6,7},{7,6},{8,9},{9,8},{10,11... | collective-permute-start | bytes 4718600 | tf_op jit(solution)/shard_map/ppermute | solution.py:849
  402.3 9.5 %collective-permute-start.60 = (bf16[2,96,896]{2,1,0:T(8,128)(2,1)}, bf16[2,96,896]{2,1,0:T(8,128)(2,1)}, u32[]{:S(2)}, u32[]{:S(2)}) collective-permute-start(bf16[2,96,896]{2,1,0:T(8,128)(2,1)} %get-tuple-element.491), channel_id=1, source_target_pairs={{0,2},{2,0},{1,3},{3,1},{4,6},{6,4},{5,7},{7,5},{8,10},{10,8},{9,1... | collective-permute-start | bytes 1032200 | tf_op jit(solution)/shard_map/ppermute | solution.py:649
  402.4 12.2 %collective-permute-start.61 = (bf16[2,96,1024]{2,1,0:T(8,128)(2,1)S(1)}, bf16[2,96,1024]{2,1,0:T(8,128)(2,1)}, u32[]{:S(2)}, u32[]{:S(2)}) collective-permute-start(bf16[2,96,1024]{2,1,0:T(8,128)(2,1)S(1)} %get-tuple-element.487), channel_id=1, source_target_pairs={{0,4},{4,0},{1,5},{5,1},{2,6},{6,2},{3,7},{7,3},{8,12},{12,8},{9,1... | collective-permute-start | bytes 1179656 | tf_op jit(solution)/shard_map/ppermute | solution.py:649
  403.6 20.3 %collective-permute-start.57 = (bf16[96,1536]{1,0:T(8,128)(2,1)}, bf16[96,1536]{1,0:T(8,128)(2,1)S(1)}, u32[]{:S(2)}, u32[]{:S(2)}) collective-permute-start(bf16[96,1536]{1,0:T(8,128)(2,1)} %fusion.28), channel_id=1, source_target_pairs={{0,8},{8,16},{16,24},{24,0},{1,9},{9,17},{17,25},{25,1},{2,10},{10... | collective-permute-start | bytes 884744 | tf_op jit(solution)/shard_map/ppermute | solution.py:649
  403.7 23.6 %collective-permute-start.58 = (bf16[4,96,896]{2,1,0:T(8,128)(2,1)S(1)}, bf16[4,96,896]{2,1,0:T(8,128)(2,1)S(1)}, u32[]{:S(2)}, u32[]{:S(2)}) collective-permute-start(bf16[4,96,896]{2,1,0:T(8,128)(2,1)S(1)} %copy-done.48), channel_id=1, source_target_pairs={{0,4},{4,0},{1,5},{5,1},{2,6},{6,2},{3,7},{7,3},{8,12},{12,8},{9,1... | collective-permute-start | bytes 2064392 | tf_op jit(solution)/shard_map/ppermute | solution.py:649
  411.8 17.7 %collective-permute-start.59 = (bf16[4,96,1024]{2,1,0:T(8,128)(2,1)S(1)}, bf16[4,96,1024]{2,1,0:T(8,128)(2,1)S(1)}, u32[]{:S(2)}, u32[]{:S(2)}) collective-permute-start(bf16[4,96,1024]{2,1,0:T(8,128)(2,1)S(1)} %get-tuple-element.428), channel_id=1, source_target_pairs={{0,2},{2,0},{1,3},{3,1},{4,6},{6,4},{5,7},{7,5},{8,10},{10,8},{9,1... | collective-permute-start | bytes 2359304 | tf_op jit(solution)/shard_map/ppermute | solution.py:649
  417.0 12.6 %collective-permute-start.64 = (bf16[96,1920]{1,0:T(8,128)(2,1)S(1)}, bf16[96,1920]{1,0:T(8,128)(2,1)S(1)}, u32[]{:S(2)}, u32[]{:S(2)}) collective-permute-start(bf16[96,1920]{1,0:T(8,128)(2,1)S(1)} %fusion.37), channel_id=1, source_target_pairs={{0,8},{8,16},{16,24},{24,0},{1,9},{9,17},{17,25},{25,1},{2,10},{10... | collective-permute-start | bytes 1105928 | tf_op jit(solution)/shard_map/ppermute | solution.py:649
  436.7 14.0 %collective-permute-start.65 = (bf16[2,256,1536]{2,1,0:T(8,128)(2,1)S(1)}, bf16[2,256,1536]{2,1,0:T(8,128)(2,1)S(1)}, u32[]{:S(2)}, u32[]{:S(2)}) collective-permute-start(bf16[2,256,1536]{2,1,0:T(8,128)(2,1)S(1)} %fusion.13), channel_id=1, source_target_pairs={{0,1},{1,0},{2,3},{3,2},{4,5},{5,4},{6,7},{7,6},{8,9},{9,8},{10,11... | collective-permute-start | bytes 4718600 | tf_op jit(solution)/shard_map/ppermute | solution.py:849
  436.8 15.7 %collective-permute-start.68 = (bf16[96,1920]{1,0:T(8,128)(2,1)S(1)}, bf16[96,1920]{1,0:T(8,128)(2,1)S(1)}, u32[]{:S(2)}, u32[]{:S(2)}) collective-permute-start(bf16[96,1920]{1,0:T(8,128)(2,1)S(1)} %fusion.22), channel_id=1, source_target_pairs={{0,8},{8,16},{16,24},{24,0},{1,9},{9,17},{17,25},{25,1},{2,10},{10... | collective-permute-start | bytes 1105928 | tf_op jit(solution)/shard_map/ppermute | solution.py:649
  439.4 13.2 %collective-permute-start.66 = (bf16[2,96,896]{2,1,0:T(8,128)(2,1)S(1)}, bf16[2,96,896]{2,1,0:T(8,128)(2,1)S(1)}, u32[]{:S(2)}, u32[]{:S(2)}) collective-permute-start(bf16[2,96,896]{2,1,0:T(8,128)(2,1)S(1)} %get-tuple-element.490), channel_id=1, source_target_pairs={{0,2},{2,0},{1,3},{3,1},{4,6},{6,4},{5,7},{7,5},{8,10},{10,8},{9,1... | collective-permute-start | bytes 1032200 | tf_op jit(solution)/shard_map/ppermute | solution.py:649
  439.6 12.9 %collective-permute-start.67 = (bf16[2,96,1024]{2,1,0:T(8,128)(2,1)S(1)}, bf16[2,96,1024]{2,1,0:T(8,128)(2,1)S(1)}, u32[]{:S(2)}, u32[]{:S(2)}) collective-permute-start(bf16[2,96,1024]{2,1,0:T(8,128)(2,1)S(1)} %get-tuple-element.486), channel_id=1, source_target_pairs={{0,4},{4,0},{1,5},{5,1},{2,6},{6,2},{3,7},{7,3},{8,12},{12,8},{9,1... | collective-permute-start | bytes 1179656 | tf_op jit(solution)/shard_map/ppermute | solution.py:649
  440.5 10.3 %collective-permute-start.69 = (f32[8,1792]{1,0:T(8,128)S(1)}, f32[8,1792]{1,0:T(8,128)S(1)}, u32[]{:S(2)}, u32[]{:S(2)}) collective-permute-start(f32[8,1792]{1,0:T(8,128)S(1)} %add.328), channel_id=1, source_target_pairs={{0,2},{2,0},{1,3},{3,1},{4,6},{6,4},{5,7},{7,5},{8,10},{10,8},{9,1... | collective-permute-start | bytes 172040 | tf_op jit(solution)/shard_map/ppermute | solution.py:849
  452.9 12.8 %collective-permute-start.70 = (bf16[96,1920]{1,0:T(8,128)(2,1)S(1)}, bf16[96,1920]{1,0:T(8,128)(2,1)S(1)}, u32[]{:S(2)}, u32[]{:S(2)}) collective-permute-start(bf16[96,1920]{1,0:T(8,128)(2,1)S(1)} %fusion.19), channel_id=1, source_target_pairs={{0,8},{8,16},{16,24},{24,0},{1,9},{9,17},{17,25},{25,1},{2,10},{10... | collective-permute-start | bytes 1105928 | tf_op jit(solution)/shard_map/ppermute | solution.py:649
  (98 other events, 1373.2 us)
